TPU v7x, 32 devices: a whole 2x2x4 slice. The times are simulated.
32 devices in a mesh: dp: 8 (over y, x, core), tensor: 4 (over z).
Axes of the slice: x: 2, y: 2, z: 4, core: 2. Of those that a mesh axis runs over, the one named last changes fastest.
Arguments:
- inputs: bfloat16 [24, 1024, 768], P('dp', 'tensor'), may hold values from -6 to 6
- condition: bfloat16 [24, 128], P('dp'), may hold values from -6 to 6
- doc_ids: int32 [24, 1024], P('dp'), may hold values from 0 to 7, as said below
- positions: int32 [24, 1024], P('dp'), may hold values from 0 to 1023, as said below
- w_qkv: bfloat16 [3, 768, 768], P(None, 'dp', 'tensor'), may hold values from -0.21875 to 0.21875
- w_out: bfloat16 [768, 768], P('tensor', 'dp'), may hold values from -1.75 to 1.75
- w_up: bfloat16 [768, 3072], P('dp', 'tensor'), may hold values from -0.21875 to 0.21875
- bias_up: bfloat16 [4, 768], P('tensor', 'dp'), may hold values from -3 to 3
- w_down: bfloat16 [3072, 768], P('tensor', 'dp'), may hold values from -0.109375 to 0.109375
- bias_down: bfloat16 [768], P('dp'), may hold values from -3 to 3
- gain_one: bfloat16 [768], P('dp'), may hold values from 0.5 to 1.5
- gain_two: bfloat16 [768], P('dp'), may hold values from 0.5 to 1.5
- w_ada: bfloat16 [128, 4608], P(None, 'dp'), may hold values from -0.5 to 0.5
- bias_ada: bfloat16 [4608], P('dp'), may hold values from -2 to 2
- out_grad: bfloat16 [24, 1024, 768], P('dp', 'tensor'), may hold values from -6 to 6
Outputs:
- block_out: bfloat16 [24, 1024, 768], P('dp', 'tensor')
- input_grad: bfloat16 [24, 1024, 768], P('dp', 'tensor')
- cond_grad: float32 [24, 128], P('dp')
- grad_qkv: float32 [3, 768, 768], P(None, 'dp', 'tensor')
- grad_out: float32 [768, 768], P('tensor', 'dp')
- grad_up: float32 [768, 3072], P('dp', 'tensor')
- grad_bias_up: float32 [4, 768], P('tensor', 'dp')
- grad_down: float32 [3072, 768], P('tensor', 'dp')
- grad_bias_down: float32 [768], P('dp')
- grad_gain_one: float32 [768], P('dp')
- grad_gain_two: float32 [768], P('dp')
- grad_ada: float32 [128, 4608], P(None, 'dp')
- grad_bias_ada: float32 [4608], P('dp')
Inputs may be any that keep to these rules, and one draw needn't show every extreme that they name: `doc_ids`: within each sequence the document numbers begin at 0 at the first token and rise by one at the first token of each further document; each document is a run of consecutive tokens; a sequence holds at most 8 documents. `positions`: each token's offset from the first token of its document.
All inputs are finite; a program needn't handle non-finite values.
Results may differ from a plain program's by a relative error of at most 0.013.
The roundings to bfloat16 on the way count: a program that leaves them out, or rounds other values in their place, can miss the bound.
Values may be sent and summed in bfloat16 or wider, within the bound.
No kernel may reach another device: no remote copies, remote signals or barrier semaphores. Data moves between devices by JAX's collectives and lax.ppermute only.
A program may use at most 128 MiB of HBM per device.

v0:
```python
from functools import partial

import jax
import jax.numpy as jnp
from jax import lax
from jax.sharding import PartitionSpec as P

HEAD = 64


PRECISE = lax.Precision.HIGHEST
EPSILON = 1e-05


def layer_norm(features, gain_vec):
    average = jnp.mean(features, axis=-1, keepdims=True)
    centred = features - average
    spread = jnp.mean(centred * centred, axis=-1, keepdims=True)
    return centred * lax.rsqrt(spread + EPSILON) * gain_vec


def norm_mod(features, gain_vec, scale_vec, shift_vec):
    return layer_norm(features, gain_vec) * (1.0 + scale_vec) + shift_vec


def angles(places):
    half_size = HEAD // 2
    frequencies = 10000.0 ** (-2.0 * jnp.arange(half_size, dtype=jnp.float32) / HEAD)
    turned = places.astype(jnp.float32)[:, None] * frequencies[None, :]
    return (jnp.cos(turned)[:, None, :], jnp.sin(turned)[:, None, :])


def rotate(vectors, cosine, sine_vals):
    half_size = vectors.shape[-1] // 2
    first_half = vectors[..., :half_size]
    second_half = vectors[..., half_size:]
    return jnp.concatenate(
        [
            first_half * cosine - second_half * sine_vals,
            second_half * cosine + first_half * sine_vals,
        ],
        axis=-1,
    )


def unrotate(vectors, cosine, sine_vals):
    half_size = vectors.shape[-1] // 2
    first_half = vectors[..., :half_size]
    second_half = vectors[..., half_size:]
    return jnp.concatenate(
        [
            first_half * cosine + second_half * sine_vals,
            second_half * cosine - first_half * sine_vals,
        ],
        axis=-1,
    )


def block_scores(query_blk, key_rows, doc_blk, documents):
    scores = jnp.einsum(
        "qhe,khe->hqk", query_blk, key_rows, preferred_element_type=jnp.float32
    ) * HEAD ** (-0.5)
    same_doc = (doc_blk[:, None] == documents[None, :])[None]
    return jnp.where(same_doc, scores, -1e30)


def attend(queries, key_rows, values, documents):
    length = queries.shape[0]
    block_rows = min(512, length)
    block_count = length // block_rows

    def one_block(block_index):
        first_row = block_index * block_rows
        query_blk = lax.dynamic_slice_in_dim(queries, first_row, block_rows, 0)
        doc_blk = lax.dynamic_slice_in_dim(documents, first_row, block_rows, 0)
        scores = block_scores(query_blk, key_rows, doc_blk, documents)
        log_total = jax.nn.logsumexp(scores, axis=-1, keepdims=True)
        probabilities = jnp.exp(scores - log_total).astype(jnp.bfloat16)
        mixed_blk = jnp.einsum(
            "hqk,khe->qhe", probabilities, values, preferred_element_type=jnp.float32
        )
        return (mixed_blk.astype(jnp.bfloat16), log_total)

    mixture, log_totals = lax.map(one_block, jnp.arange(block_count, dtype=jnp.int32))
    return (mixture.reshape(length, -1), log_totals)


def attend_back(queries, key_rows, values, documents, log_totals, d_mixture):
    length, local_heads, head_size = queries.shape
    block_rows = min(512, length)
    block_count = length // block_rows
    d_output = d_mixture.reshape(length, local_heads, head_size)
    scale_value = HEAD ** (-0.5)

    def one_block(running, block_index):
        d_key_rows, d_values = running
        first_row = block_index * block_rows
        query_blk = lax.dynamic_slice_in_dim(queries, first_row, block_rows, 0)
        doc_blk = lax.dynamic_slice_in_dim(documents, first_row, block_rows, 0)
        d_out_blk = lax.dynamic_slice_in_dim(d_output, first_row, block_rows, 0)
        scores = block_scores(query_blk, key_rows, doc_blk, documents)
        probabilities = jnp.exp(scores - log_totals[block_index])
        d_probs = jnp.einsum("qhe,khe->hqk", d_out_blk, values, preferred_element_type=jnp.float32)
        row_dot = jnp.sum(probabilities * d_probs, axis=-1, keepdims=True)
        d_scores = (probabilities * (d_probs - row_dot)).astype(jnp.bfloat16)
        d_query_blk = (
            jnp.einsum("hqk,khe->qhe", d_scores, key_rows, preferred_element_type=jnp.float32)
            * scale_value
        )
        d_key_rows = (
            d_key_rows
            + jnp.einsum("hqk,qhe->khe", d_scores, query_blk, preferred_element_type=jnp.float32)
            * scale_value
        )
        d_values = d_values + jnp.einsum(
            "hqk,qhe->khe",
            probabilities.astype(jnp.bfloat16),
            d_out_blk,
            preferred_element_type=jnp.float32,
        )
        return ((d_key_rows, d_values), d_query_blk)

    empty = jnp.zeros((length, local_heads, head_size), jnp.float32)
    (d_key_rows, d_values), d_queries = lax.scan(
        one_block, (empty, empty), jnp.arange(block_count, dtype=jnp.int32)
    )
    return (d_queries.reshape(length, local_heads, head_size), d_key_rows, d_values)


def shards(
    inputs,
    condition,
    doc_ids,
    positions,
    w_qkv,
    w_out,
    w_up,
    bias_up,
    w_down,
    bias_down,
    gain_one,
    gain_two,
    w_ada,
    bias_ada,
    out_grad,
):
    dp_count = lax.axis_size("dp")
    tensor_count = lax.axis_size("tensor")
    model_width = w_out.shape[1] * dp_count

    def micro_step(running, items):
        tokens, cotangent, cond_row, documents, places = items
        weights = (
            lax.all_gather(w_qkv, "dp", axis=1, tiled=True),
            lax.all_gather(w_out, "dp", axis=1, tiled=True),
            lax.all_gather(w_up, "dp", axis=0, tiled=True),
            lax.all_gather(bias_up, "dp", axis=1, tiled=True),
            lax.all_gather(w_down, "dp", axis=1, tiled=True),
            lax.all_gather(bias_down, "dp", axis=0, tiled=True),
            lax.all_gather(gain_one, "dp", axis=0, tiled=True),
            lax.all_gather(gain_two, "dp", axis=0, tiled=True),
            lax.all_gather(w_ada, "dp", axis=1, tiled=True),
            lax.all_gather(bias_ada, "dp", axis=0, tiled=True),
        )
        (
            qkv_full,
            out_full,
            up_full,
            bup_full,
            down_full,
            bdown_full,
            gone_full,
            gtwo_full,
            ada_full,
            bada_full,
        ) = weights
        cond_vals = cond_row.astype(jnp.float32)
        act_cond = jax.nn.silu(cond_vals)
        modulation = jnp.dot(
            act_cond[None, :],
            ada_full.astype(jnp.float32),
            precision=PRECISE,
            preferred_element_type=jnp.float32,
        )[0] + bada_full.astype(jnp.float32)
        shift_one, scale_one, gate_one, shift_two, scale_two, gate_two = jnp.split(modulation, 6)
        gone_vals = gone_full.astype(jnp.float32)
        gtwo_vals = gtwo_full.astype(jnp.float32)
        token_vals = tokens.astype(jnp.float32)
        normed = norm_mod(token_vals, gone_vals, scale_one, shift_one).astype(jnp.bfloat16)
        gathered = lax.all_gather(normed, "tensor", axis=0, tiled=True)
        length = gathered.shape[0]
        local_heads = qkv_full.shape[2] // HEAD
        cosine, sine_vals = angles(places)
        projected = jnp.einsum(
            "ld,cde->cle", gathered, qkv_full, preferred_element_type=jnp.float32
        )
        queries = rotate(projected[0].reshape(length, local_heads, HEAD), cosine, sine_vals).astype(
            jnp.bfloat16
        )
        key_rows = rotate(
            projected[1].reshape(length, local_heads, HEAD), cosine, sine_vals
        ).astype(jnp.bfloat16)
        values = projected[2].reshape(length, local_heads, HEAD).astype(jnp.bfloat16)
        mixture, log_totals = attend(queries, key_rows, values, documents)
        out_whole = lax.all_gather(out_full, "tensor", axis=0, tiled=True)
        mixture_local = lax.all_to_all(mixture, "tensor", split_axis=0, concat_axis=1, tiled=True)
        attention = jnp.dot(mixture_local, out_whole, preferred_element_type=jnp.float32)
        middle = token_vals + gate_one * attention
        normed_two = norm_mod(middle, gtwo_vals, scale_two, shift_two).astype(jnp.bfloat16)
        gathered_two = lax.all_gather(normed_two, "tensor", axis=0, tiled=True)
        hidden = jnp.dot(
            gathered_two, up_full, preferred_element_type=jnp.float32
        ) + bup_full.astype(jnp.float32)
        activated = jax.nn.gelu(hidden, approximate=True).astype(jnp.bfloat16)
        down_sum = lax.psum_scatter(
            jnp.dot(activated, down_full, preferred_element_type=jnp.float32).astype(jnp.bfloat16),
            "tensor",
            scatter_dimension=0,
            tiled=True,
        ).astype(jnp.float32)
        branch = down_sum + bdown_full.astype(jnp.float32)
        block_out = (middle + gate_two * branch).astype(jnp.bfloat16)
        weights = (
            lax.all_gather(w_qkv, "dp", axis=1, tiled=True),
            lax.all_gather(w_out, "dp", axis=1, tiled=True),
            lax.all_gather(w_up, "dp", axis=0, tiled=True),
            lax.all_gather(bias_up, "dp", axis=1, tiled=True),
            lax.all_gather(w_down, "dp", axis=1, tiled=True),
            lax.all_gather(bias_down, "dp", axis=0, tiled=True),
            lax.all_gather(gain_one, "dp", axis=0, tiled=True),
            lax.all_gather(gain_two, "dp", axis=0, tiled=True),
            lax.all_gather(w_ada, "dp", axis=1, tiled=True),
            lax.all_gather(bias_ada, "dp", axis=0, tiled=True),
        )
        (
            qkv_full,
            out_full,
            up_full,
            bup_full,
            down_full,
            bdown_full,
            gone_full,
            gtwo_full,
            ada_full,
            bada_full,
        ) = weights
        acc_qkv, acc_out, acc_up, acc_bup, acc_down, acc_bdown, acc_gone, acc_gtwo, ada_keep = (
            running
        )
        grad_res = cotangent.astype(jnp.float32)
        d_gate_two = jnp.sum(grad_res * branch, axis=0)
        d_down = grad_res * gate_two
        acc_bdown = acc_bdown + jnp.sum(d_down, axis=0)
        grad_rows = lax.all_gather(d_down.astype(jnp.bfloat16), "tensor", axis=0, tiled=True)
        acc_down = acc_down + jnp.einsum(
            "lf,ld->fd", activated, grad_rows, preferred_element_type=jnp.float32
        )
        d_activated = jnp.einsum(
            "ld,fd->lf", grad_rows, down_full, preferred_element_type=jnp.float32
        )
        gelu_pull = jax.vjp(partial(jax.nn.gelu, approximate=True), hidden)[1]
        d_hidden = gelu_pull(d_activated)[0].astype(jnp.bfloat16)
        acc_bup = acc_bup + jnp.sum(d_hidden.astype(jnp.float32), axis=0, keepdims=True)
        acc_up = acc_up + jnp.einsum(
            "ld,lf->df", gathered_two, d_hidden, preferred_element_type=jnp.float32
        )
        d_normed_two = lax.psum_scatter(
            jnp.einsum("lf,df->ld", d_hidden, up_full, preferred_element_type=jnp.float32),
            "tensor",
            scatter_dimension=0,
            tiled=True,
        )
        pull_two = jax.vjp(norm_mod, middle, gtwo_vals, scale_two, shift_two)[1]
        d_mid_norm, d_gain_two, d_scale_two, d_shift_two = pull_two(d_normed_two)
        d_middle = grad_res + d_mid_norm
        d_gate_one = jnp.sum(d_middle * attention, axis=0)
        d_attention = (d_middle * gate_one).astype(jnp.bfloat16)
        acc_out = acc_out + jnp.einsum(
            "lh,ld->hd", mixture_local, d_attention, preferred_element_type=jnp.float32
        )
        d_mix_local = jnp.einsum(
            "ld,hd->lh", d_attention, out_whole, preferred_element_type=jnp.float32
        ).astype(jnp.bfloat16)
        d_mixture = lax.all_to_all(d_mix_local, "tensor", split_axis=1, concat_axis=0, tiled=True)
        d_queries, d_key_rows, d_values = attend_back(
            queries, key_rows, values, documents, log_totals, d_mixture
        )
        d_proj_query = (
            unrotate(d_queries, cosine, sine_vals).reshape(length, -1).astype(jnp.bfloat16)
        )
        d_proj_key = (
            unrotate(d_key_rows, cosine, sine_vals).reshape(length, -1).astype(jnp.bfloat16)
        )
        d_proj_value = d_values.reshape(length, -1).astype(jnp.bfloat16)
        d_projected = jnp.stack([d_proj_query, d_proj_key, d_proj_value])
        acc_qkv = acc_qkv + jnp.einsum(
            "ld,cle->cde", gathered, d_projected, preferred_element_type=jnp.float32
        )
        d_normed = lax.psum_scatter(
            jnp.einsum("cle,cde->ld", d_projected, qkv_full, preferred_element_type=jnp.float32),
            "tensor",
            scatter_dimension=0,
            tiled=True,
        )
        pull_one = jax.vjp(norm_mod, token_vals, gone_vals, scale_one, shift_one)[1]
        d_tok_norm, d_gain_one, d_scale_one, d_shift_one = pull_one(d_normed)
        input_grad = (d_middle + d_tok_norm).astype(jnp.bfloat16)
        d_modulation = jnp.concatenate(
            [d_shift_one, d_scale_one, d_gate_one, d_shift_two, d_scale_two, d_gate_two]
        )
        acc_gone = acc_gone + d_gain_one
        acc_gtwo = acc_gtwo + d_gain_two
        running = (
            acc_qkv,
            acc_out,
            acc_up,
            acc_bup,
            acc_down,
            acc_bdown,
            acc_gone,
            acc_gtwo,
            ada_full,
        )
        return (running, (block_out, input_grad, d_modulation))

    out_start = jnp.zeros((w_out.shape[0] * tensor_count, model_width), jnp.float32)
    start_state = (
        jnp.zeros((3, w_qkv.shape[1] * dp_count, w_qkv.shape[2]), jnp.float32),
        out_start,
        jnp.zeros((w_up.shape[0] * dp_count, w_up.shape[1]), jnp.float32),
        jnp.zeros((1, bias_up.shape[1] * dp_count), jnp.float32),
        jnp.zeros((w_down.shape[0], model_width), jnp.float32),
        jnp.zeros((model_width,), jnp.float32),
        jnp.zeros((model_width,), jnp.float32),
        jnp.zeros((model_width,), jnp.float32),
        jnp.zeros((w_ada.shape[0], w_ada.shape[1] * dp_count), jnp.bfloat16),
    )
    final_state, (block_out, input_grad, mod_parts) = lax.scan(
        micro_step, start_state, (inputs, out_grad, condition, doc_ids, positions)
    )
    acc_qkv, acc_out, acc_up, acc_bup, acc_down, acc_bdown, acc_gone, acc_gtwo, ada_whole = (
        final_state
    )
    acc_out = lax.psum_scatter(acc_out, "tensor", scatter_dimension=0, tiled=True)
    mod_sum, gone_sum, gtwo_sum, bdown_sum = lax.psum(
        (mod_parts, acc_gone, acc_gtwo, acc_bdown), "tensor"
    )
    cond_vals = condition.astype(jnp.float32)
    act_cond, silu_pull = jax.vjp(jax.nn.silu, cond_vals)
    d_act = jnp.dot(
        mod_sum,
        ada_whole.astype(jnp.float32).T,
        precision=PRECISE,
        preferred_element_type=jnp.float32,
    )
    cond_grad = silu_pull(d_act)[0]
    ada_part = jnp.dot(act_cond.T, mod_sum, precision=PRECISE, preferred_element_type=jnp.float32)
    bada_part = jnp.sum(mod_sum, axis=0)
    grads = (
        lax.psum_scatter(acc_qkv, "dp", scatter_dimension=1, tiled=True),
        lax.psum_scatter(acc_out, "dp", scatter_dimension=1, tiled=True),
        lax.psum_scatter(acc_up, "dp", scatter_dimension=0, tiled=True),
        lax.psum_scatter(acc_bup, "dp", scatter_dimension=1, tiled=True),
        lax.psum_scatter(acc_down, "dp", scatter_dimension=1, tiled=True),
        lax.psum_scatter(bdown_sum, "dp", scatter_dimension=0, tiled=True),
        lax.psum_scatter(gone_sum, "dp", scatter_dimension=0, tiled=True),
        lax.psum_scatter(gtwo_sum, "dp", scatter_dimension=0, tiled=True),
        lax.psum_scatter(ada_part, "dp", scatter_dimension=1, tiled=True),
        lax.psum_scatter(bada_part, "dp", scatter_dimension=0, tiled=True),
    )
    return (
        block_out,
        input_grad,
        cond_grad,
        grads[0],
        grads[1],
        grads[2],
        grads[3],
        grads[4],
        grads[5],
        grads[6],
        grads[7],
        grads[8],
        grads[9],
    )


def solution(mesh):
    return jax.shard_map(
        shards,
        mesh=mesh,
        in_specs=(
            P("dp", "tensor", None),
            P("dp", None),
            P("dp", None),
            P("dp", None),
            P(None, "dp", "tensor"),
            P("tensor", "dp"),
            P("dp", "tensor"),
            P("tensor", "dp"),
            P("tensor", "dp"),
            P("dp"),
            P("dp"),
            P("dp"),
            P(None, "dp"),
            P("dp"),
            P("dp", "tensor", None),
        ),
        out_specs=(
            P("dp", "tensor", None),
            P("dp", "tensor", None),
            P("dp", None),
            P(None, "dp", "tensor"),
            P("tensor", "dp"),
            P("dp", "tensor"),
            P("tensor", "dp"),
            P("tensor", "dp"),
            P("dp"),
            P("dp"),
            P("dp"),
            P(None, "dp"),
            P("dp"),
        ),
        check_vma=False,
    )
```

profile of v0, /device:TPU:0, one launch (start us, length us, event | category | flops | bytes accessed | tf_op | source)
XLA Modules:
  0.0 1710.4 jit_solution(8145431348411284616)
XLA Ops:
  10.7 1382.8 %while.93 = (s32[]{:T(128)}, f32[3,768,192]{1,2,0:T(8,128)}, f32[768,768]{1,0:T(8,128)}, f32[768,768]{1,0:T(8,128)}, f32[1,768]{1,0:T(1,128)}, /*index=5*/f32[76...) while((s32[]{:T(128)}, f32[3,768,192]{1,2,0:T(8,128)}, ...), condition=%wide.region_29.30_spmd.clone, body=%wide.region_0.29_spmd.clone.sunk | while | flops 12401086464 | bytes 355286048 | solution.py:338
  18.7 26.4 %all-reduce.18 = (bf16[4608]{0:T(1024)(128)(2,1)S(1)}, bf16[768]{0:T(1024)(128)(2,1)S(1)}, bf16[768]{0:T(1024)(128)(2,1)S(1)}, bf16[768]{0:T(1024)(128)(2,1)S(1)}, bf16[768]{0:T(1024)(128)(2,1)}) all-reduce(bf16[4608]{0:T(1024)(128)(2,1)S(1)} %dynamic-update-slice.39, ...), channel_id=1, replica_groups=mesh['dp'=8,'tensor'=4] {'dp'}, use_global_device_ids=true, to_apply=%add.1 | all-reduce | flops 7680 | bytes 30720 | tf_op jit(solution)/shard_map/while
  51.1 9.1 all_gather.109
  61.8 12.9 all_gather.108
  78.1 9.5 all-gather.10.cloned.1.call-done
  91.7 15.8 while.94
  112.4 10.6 all-gather.12.cloned.1.call-done
  134.4 12.8 all-gather.16.cloned.1.call-done
  147.2 38.5 %all-gather.14.cloned.1.call-done = bf16[1024,768]{1,0:T(8,128)(2,1)} async-done(((bf16[256,768]{1,0:T(8,128)(2,1)}), bf16[1024,768]{1,0:T(8,128)(2,1)}) %all-gather.14.cloned.1.call-update) | async-done | bytes 1572880 | tf_op jit(solution)/shard_map/while/body/eval_jaxpr/all_gather | solution.py:210
  190.4 19.8 %all-gather.20.cloned.1.call-done = bf16[768,768]{0,1:T(8,128)(2,1)} async-done(((bf16[768,96]{0,1:T(8,128)(2,1)}), bf16[768,768]{0,1:T(8,128)(2,1)}) %all-gather.20.cloned.1.call-update) | async-done | bytes 1179664 | tf_op jit(solution)/shard_map/while/body/eval_jaxpr/all_gather | solution.py:228
  210.2 38.6 %all-gather.18.cloned.1.call-done = bf16[1024,768]{1,0:T(8,128)(2,1)} async-done(((bf16[256,768]{1,0:T(8,128)(2,1)}), bf16[1024,768]{1,0:T(8,128)(2,1)}) %all-gather.18.cloned.1.call-update) | async-done | bytes 1572880 | tf_op jit(solution)/shard_map/while/body/eval_jaxpr/all_gather | solution.py:254
  248.8 6.3 convert_reduce_fusion.5
  259.5 59.4 %reduce-scatter.29.cloned.1.call-done = f32[256,768]{1,0:T(8,128)} async-done(((f32[1024,768]{1,0:T(8,128)}), f32[256,768]{1,0:T(8,128)}) %reduce-scatter.29.cloned.1.call-update) | async-done | bytes 786448 | tf_op jit(solution)/shard_map/while/body/eval_jaxpr/reduce_scatter | solution.py:267
  336.1 5.9 all-to-all-done.1
  345.6 51.6 %while.95 = (s32[]{:T(128)}, f32[1024,3,64]{0,2,1:T(8,128)S(1)}, f32[1024,3,64]{0,2,1:T(8,128)}, f32[2,512,3,64]{1,0,3,2:T(2,128)}, s32[2]{0:T(128)}, /*index=5*...) while((s32[]{:T(128)}, f32[1024,3,64]{0,2,1:T(8,128)S(1)}, ...), condition=%wide.region_14.14_spmd.clone, body=%wide.region_12.13_spmd.clone.sunk | while | flops 1031830016 | bytes 56414492 | solution.py:124
  363.1 8.1 dynamic_update_slice.51
  389.0 8.1 dynamic_update_slice.51
  423.4 41.1 %reduce-scatter.33.cloned.1.call-done = f32[256,768]{1,0:T(8,128)} async-done(((f32[1024,768]{1,0:T(8,128)}), f32[256,768]{1,0:T(8,128)}) %reduce-scatter.33.cloned.1.call-update) | async-done | bytes 786448 | tf_op jit(solution)/shard_map/while/body/eval_jaxpr/reduce_scatter | solution.py:299
  479.8 24.5 %all-reduce.18 = (bf16[4608]{0:T(1024)(128)(2,1)S(1)}, bf16[768]{0:T(1024)(128)(2,1)S(1)}, bf16[768]{0:T(1024)(128)(2,1)S(1)}, bf16[768]{0:T(1024)(128)(2,1)S(1)}, bf16[768]{0:T(1024)(128)(2,1)}) all-reduce(bf16[4608]{0:T(1024)(128)(2,1)S(1)} %dynamic-update-slice.39, ...), channel_id=1, replica_groups=mesh['dp'=8,'tensor'=4] {'dp'}, use_global_device_ids=true, to_apply=%add.1 | all-reduce | flops 7680 | bytes 30720 | tf_op jit(solution)/shard_map/while
  510.3 9.1 all_gather.109
  521.0 13.0 all_gather.108
  537.3 8.6 all-gather.10.cloned.1.call-done
  549.9 15.8 while.94
  570.7 10.6 all-gather.12.cloned.1.call-done
  592.4 13.0 all-gather.16.cloned.1.call-done
  605.4 38.5 %all-gather.14.cloned.1.call-done = bf16[1024,768]{1,0:T(8,128)(2,1)} async-done(((bf16[256,768]{1,0:T(8,128)(2,1)}), bf16[1024,768]{1,0:T(8,128)(2,1)}) %all-gather.14.cloned.1.call-update) | async-done | bytes 1572880 | tf_op jit(solution)/shard_map/while/body/eval_jaxpr/all_gather | solution.py:210
  648.7 19.8 %all-gather.20.cloned.1.call-done = bf16[768,768]{0,1:T(8,128)(2,1)} async-done(((bf16[768,96]{0,1:T(8,128)(2,1)}), bf16[768,768]{0,1:T(8,128)(2,1)}) %all-gather.20.cloned.1.call-update) | async-done | bytes 1179664 | tf_op jit(solution)/shard_map/while/body/eval_jaxpr/all_gather | solution.py:228
  668.4 38.5 %all-gather.18.cloned.1.call-done = bf16[1024,768]{1,0:T(8,128)(2,1)} async-done(((bf16[256,768]{1,0:T(8,128)(2,1)}), bf16[1024,768]{1,0:T(8,128)(2,1)}) %all-gather.18.cloned.1.call-update) | async-done | bytes 1572880 | tf_op jit(solution)/shard_map/while/body/eval_jaxpr/all_gather | solution.py:254
  706.9 6.3 convert_reduce_fusion.5
  717.6 59.4 %reduce-scatter.29.cloned.1.call-done = f32[256,768]{1,0:T(8,128)} async-done(((f32[1024,768]{1,0:T(8,128)}), f32[256,768]{1,0:T(8,128)}) %reduce-scatter.29.cloned.1.call-update) | async-done | bytes 786448 | tf_op jit(solution)/shard_map/while/body/eval_jaxpr/reduce_scatter | solution.py:267
  788.5 5.5 convolution_convert_fusion.5
  794.3 5.8 all-to-all-done.1
  803.7 51.8 %while.95 = (s32[]{:T(128)}, f32[1024,3,64]{0,2,1:T(8,128)S(1)}, f32[1024,3,64]{0,2,1:T(8,128)}, f32[2,512,3,64]{1,0,3,2:T(2,128)}, s32[2]{0:T(128)}, /*index=5*...) while((s32[]{:T(128)}, f32[1024,3,64]{0,2,1:T(8,128)S(1)}, ...), condition=%wide.region_14.14_spmd.clone, body=%wide.region_12.13_spmd.clone.sunk | while | flops 1031830016 | bytes 56414492 | solution.py:124
  821.2 8.1 dynamic_update_slice.51
  847.1 8.1 dynamic_update_slice.51
  864.0 5.7 select_add_fusion.13
  885.8 37.0 %reduce-scatter.33.cloned.1.call-done = f32[256,768]{1,0:T(8,128)} async-done(((f32[1024,768]{1,0:T(8,128)}), f32[256,768]{1,0:T(8,128)}) %reduce-scatter.33.cloned.1.call-update) | async-done | bytes 786448 | tf_op jit(solution)/shard_map/while/body/eval_jaxpr/reduce_scatter | solution.py:299
  937.8 24.5 %all-reduce.18 = (bf16[4608]{0:T(1024)(128)(2,1)S(1)}, bf16[768]{0:T(1024)(128)(2,1)S(1)}, bf16[768]{0:T(1024)(128)(2,1)S(1)}, bf16[768]{0:T(1024)(128)(2,1)S(1)}, bf16[768]{0:T(1024)(128)(2,1)}) all-reduce(bf16[4608]{0:T(1024)(128)(2,1)S(1)} %dynamic-update-slice.39, ...), channel_id=1, replica_groups=mesh['dp'=8,'tensor'=4] {'dp'}, use_global_device_ids=true, to_apply=%add.1 | all-reduce | flops 7680 | bytes 30720 | tf_op jit(solution)/shard_map/while
  968.3 9.1 all_gather.109
  979.0 13.0 all_gather.108
  995.3 8.6 all-gather.10.cloned.1.call-done
  1008.0 15.8 while.94
  1028.7 10.6 all-gather.12.cloned.1.call-done
  1050.5 13.0 all-gather.16.cloned.1.call-done
  1063.5 38.6 %all-gather.14.cloned.1.call-done = bf16[1024,768]{1,0:T(8,128)(2,1)} async-done(((bf16[256,768]{1,0:T(8,128)(2,1)}), bf16[1024,768]{1,0:T(8,128)(2,1)}) %all-gather.14.cloned.1.call-update) | async-done | bytes 1572880 | tf_op jit(solution)/shard_map/while/body/eval_jaxpr/all_gather | solution.py:210
  1106.9 19.8 %all-gather.20.cloned.1.call-done = bf16[768,768]{0,1:T(8,128)(2,1)} async-done(((bf16[768,96]{0,1:T(8,128)(2,1)}), bf16[768,768]{0,1:T(8,128)(2,1)}) %all-gather.20.cloned.1.call-update) | async-done | bytes 1179664 | tf_op jit(solution)/shard_map/while/body/eval_jaxpr/all_gather | solution.py:228
  1126.6 38.5 %all-gather.18.cloned.1.call-done = bf16[1024,768]{1,0:T(8,128)(2,1)} async-done(((bf16[256,768]{1,0:T(8,128)(2,1)}), bf16[1024,768]{1,0:T(8,128)(2,1)}) %all-gather.18.cloned.1.call-update) | async-done | bytes 1572880 | tf_op jit(solution)/shard_map/while/body/eval_jaxpr/all_gather | solution.py:254
  1165.1 6.3 convert_reduce_fusion.5
  1175.8 59.4 %reduce-scatter.29.cloned.1.call-done = f32[256,768]{1,0:T(8,128)} async-done(((f32[1024,768]{1,0:T(8,128)}), f32[256,768]{1,0:T(8,128)}) %reduce-scatter.29.cloned.1.call-update) | async-done | bytes 786448 | tf_op jit(solution)/shard_map/while/body/eval_jaxpr/reduce_scatter | solution.py:267
  1246.7 5.5 convolution_convert_fusion.5
  1252.7 5.6 all-to-all-done.1
  1261.9 51.6 %while.95 = (s32[]{:T(128)}, f32[1024,3,64]{0,2,1:T(8,128)S(1)}, f32[1024,3,64]{0,2,1:T(8,128)}, f32[2,512,3,64]{1,0,3,2:T(2,128)}, s32[2]{0:T(128)}, /*index=5*...) while((s32[]{:T(128)}, f32[1024,3,64]{0,2,1:T(8,128)S(1)}, ...), condition=%wide.region_14.14_spmd.clone, body=%wide.region_12.13_spmd.clone.sunk | while | flops 1031830016 | bytes 56414492 | solution.py:124
  1279.4 8.1 dynamic_update_slice.51
  1305.3 8.1 dynamic_update_slice.51
  1321.9 5.7 select_add_fusion.13
  1343.7 37.0 %reduce-scatter.33.cloned.1.call-done = f32[256,768]{1,0:T(8,128)} async-done(((f32[1024,768]{1,0:T(8,128)}), f32[256,768]{1,0:T(8,128)}) %reduce-scatter.33.cloned.1.call-update) | async-done | bytes 786448 | tf_op jit(solution)/shard_map/while/body/eval_jaxpr/reduce_scatter | solution.py:299
  1395.2 48.7 %reduce-scatter.17.cloned.1.call-done = f32[192,768]{1,0:T(8,128)} async-done(((f32[768,768]{1,0:T(8,128)}), f32[192,768]{1,0:T(8,128)}) %reduce-scatter.17.cloned.1.call-update) | async-done | bytes 589840 | tf_op jit(solution)/shard_map/reduce_scatter | solution.py:344
  1450.1 18.6 %psum.28 = f32[3,4608]{1,0:T(4,128)S(1)} all-reduce(f32[3,4608]{1,0:T(4,128)S(1)} %copy-done.59), channel_id=1, replica_groups=mesh['dp'=8,'tensor'=4] {'tensor'}, use_global_device_ids=true, to_apply=%region_30.31 | all-reduce | flops 13824 | bytes 110592 | tf_op jit(solution)/shard_map/psum | solution.py:345
  1479.8 22.4 %all-reduce.15 = (f32[768]{0:T(1024)S(1)}, f32[768]{0:T(1024)S(1)}, f32[768]{0:T(1024)S(1)}, f32[4608]{0:T(1024)S(1)}) all-reduce(f32[768]{0:T(1024)S(1)} %copy-done.52, f32[768]{0:T(1024)S(1)} %copy-done.49, f32[768]{0:T(1024)S(1)} %copy-done.46, f32[4608]{0:T(1024)S(1)} %reduce_sum.299), channel_id=11, replica_groups=mesh['dp'=8,'tensor'=4] {'dp'}, use_global_device_ids=true, to_apply=%region_38.39.clone | all-reduce | flops 6912 | bytes 55296
  1503.1 9.0 all-reduce.16
  1519.7 44.6 %reduce-scatter.15.cloned.1.call-done = f32[3,96,192]{2,1,0:T(8,128)} async-done(((f32[3,768,192]{2,1,0:T(8,128)}), f32[3,96,192]{2,1,0:T(8,128)}) %reduce-scatter.15.cloned.1.call-update) | async-done | bytes 221200 | tf_op jit(solution)/shard_map/reduce_scatter | solution.py:360
  1564.3 46.2 %reduce-scatter.19.cloned.1.call-done = f32[96,768]{1,0:T(8,128)} async-done(((f32[768,768]{1,0:T(8,128)}), f32[96,768]{1,0:T(8,128)}) %reduce-scatter.19.cloned.1.call-update) | async-done | bytes 294928 | tf_op jit(solution)/shard_map/reduce_scatter | solution.py:362
  1610.5 46.2 %reduce-scatter.23.cloned.1.call-done = f32[128,576]{0,1:T(8,128)} async-done(((f32[128,4608]{0,1:T(8,128)}), f32[128,576]{0,1:T(8,128)}) %reduce-scatter.23.cloned.1.call-update) | async-done | bytes 294928 | tf_op jit(solution)/shard_map/reduce_scatter | solution.py:368
  1656.7 46.0 %reduce-scatter.21.cloned.1.call-done = f32[768,96]{0,1:T(8,128)} async-done(((f32[768,768]{0,1:T(8,128)}), f32[768,96]{0,1:T(8,128)}) %reduce-scatter.21.cloned.1.call-update) | async-done | bytes 294928 | tf_op jit(solution)/shard_map/reduce_scatter | solution.py:364
  (884 shorter events, 447.2 us)
Async XLA Ops:
  11.1 50.7 %copy-start.21 = (bf16[3,96,192]{2,0,1:T(4,128)(2,1)}, bf16[3,96,192]{2,0,1:T(4,128)(2,1)S(1)}, u32[]{:S(2)}) copy-start(bf16[3,96,192]{2,0,1:T(4,128)(2,1)S(1)} %get-tuple-element.1523) | copy-start | bytes 331780 | tf_op jit(solution)/shard_map/while
  11.1 36.4 %all-gather.8.cloned.1.call-start = ((), (), s32[]{:S(2)}) async-start(), calls=%async_computation.19 | async-start | bytes 1327104 | tf_op jit(solution)/shard_map/while/body/eval_jaxpr/all_gather | solution.py:162
  11.8 75.8 %all-gather.10.cloned.1.call-start = ((), (), s32[]{:S(2)}) async-start(), calls=%async_computation.20 | async-start | bytes 1966080 | tf_op jit(solution)/shard_map/while/body/eval_jaxpr/all_gather | solution.py:190
  51.0 72.0 %all-gather.12.cloned.1.call-start = ((), (), s32[]{:S(2)}) async-start(), calls=%async_computation.21 | async-start | bytes 1474560 | tf_op jit(solution)/shard_map/while/body/eval_jaxpr/all_gather | solution.py:205
  61.1 86.1 %all-gather.16.cloned.1.call-start = ((), (), s32[]{:S(2)}) async-start(), calls=%async_computation.23 | async-start | bytes 1327104 | tf_op jit(solution)/shard_map/while/body/eval_jaxpr/all_gather | solution.py:156
  108.9 18.4 %all-to-all-start = ((bf16[4,256,192]{1,2,0:T(8,128)(2,1)}), bf16[4,256,192]{1,2,0:T(8,128)(2,1)S(1)}, u32[]{:S(2)}, u32[]{:S(2)}) async-start(bf16[4,256,192]{1,2,0:T(8,128)(2,1)} %copy.107), calls=%async_computation | async-start | bytes 786432 | tf_op jit(solution)/shard_map/while/body/eval_jaxpr/all_to_all | solution.py:206
  112.3 73.3 %all-gather.14.cloned.1.call-start = ((), (), s32[]{:S(2)}) async-start(), calls=%async_computation.22 | async-start | bytes 1966080 | tf_op jit(solution)/shard_map/while/body/eval_jaxpr/all_gather | solution.py:210
  130.1 188.8 %copy-start.32 = (f32[256]{0:T(256)}, f32[256]{0:T(256)S(1)}, u32[]{:S(2)}) copy-start(f32[256]{0:T(256)S(1)} %broadcast_multiply_fusion.5) | copy-start | bytes 3076 | tf_op jit(solution)/shard_map/while
  130.4 188.5 %copy-start.41 = (f32[256]{0:T(256)}, f32[256]{0:T(256)S(1)}, u32[]{:S(2)}) copy-start(f32[256]{0:T(256)S(1)} %fusion.212) | copy-start | bytes 3076 | tf_op jit(solution)/shard_map/while
  131.4 78.8 %all-gather.20.cloned.1.call-start = ((), (), s32[]{:S(2)}) async-start(), calls=%async_computation.25 | async-start | bytes 1327104 | tf_op jit(solution)/shard_map/while/body/eval_jaxpr/all_gather | solution.py:228
  132.0 116.8 %all-gather.18.cloned.1.call-start = ((), (), s32[]{:S(2)}) async-start(), calls=%async_computation.24 | async-start | bytes 1966080 | tf_op jit(solution)/shard_map/while/body/eval_jaxpr/all_gather | solution.py:254
  133.9 185.0 %reduce-scatter.29.cloned.1.call-start = ((), (), s32[]{:S(2)}) async-start(), calls=%async_computation.26 | async-start | bytes 3932160 | tf_op jit(solution)/shard_map/while/body/eval_jaxpr/reduce_scatter | solution.py:267
  134.4 114.5 %copy-start.56 = (f32[768]{0:T(1024)}, f32[768]{0:T(1024)S(1)}, u32[]{:S(2)}) copy-start(f32[768]{0:T(1024)S(1)} %add.593) | copy-start | bytes 9220 | tf_op jit(solution)/shard_map/while
  190.4 65.9 %copy-start.64 = (bf16[768,768]{1,0:T(8,128)(2,1)S(1)}, bf16[768,768]{1,0:T(8,128)(2,1)}, u32[]{:S(2)}) copy-start(bf16[768,768]{1,0:T(8,128)(2,1)} %all-gather.16.cloned.1.call-done) | copy-start | bytes 3538948 | tf_op jit(solution)/shard_map/while
  259.4 59.5 %copy-start.29 = (f32[768]{0:T(1024)S(1)}, f32[768]{0:T(1024)}, u32[]{:S(2)}) copy-start(f32[768]{0:T(1024)} %copy-done.28) | copy-start | bytes 9220 | tf_op jit(solution)/shard_map/while
  259.5 63.1 %copy-start.3 = (bf16[768,768]{1,0:T(8,128)(2,1)S(1)}, bf16[768,768]{1,0:T(8,128)(2,1)}, u32[]{:S(2)}) copy-start(bf16[768,768]{1,0:T(8,128)(2,1)} %all-gather.12.cloned.1.call-done) | copy-start | bytes 3538948 | tf_op jit(solution)/shard_map/while
  326.8 15.2 all-to-all-start.1
  330.4 83.8 %reduce-scatter.31.cloned.1.call-start = ((), (), s32[]{:S(2)}) async-start(), calls=%async_computation.27 | async-start | bytes 1966080 | tf_op jit(solution)/shard_map/while/body/eval_jaxpr/reduce_scatter | solution.py:215
  335.9 128.6 %reduce-scatter.33.cloned.1.call-start = ((), (), s32[]{:S(2)}) async-start(), calls=%async_computation.28 | async-start | bytes 3932160 | tf_op jit(solution)/shard_map/while/body/eval_jaxpr/reduce_scatter | solution.py:299
  472.2 48.8 %copy-start.21 = (bf16[3,96,192]{2,0,1:T(4,128)(2,1)}, bf16[3,96,192]{2,0,1:T(4,128)(2,1)S(1)}, u32[]{:S(2)}) copy-start(bf16[3,96,192]{2,0,1:T(4,128)(2,1)S(1)} %get-tuple-element.1523) | copy-start | bytes 331780 | tf_op jit(solution)/shard_map/while
  472.2 34.5 %all-gather.8.cloned.1.call-start = ((), (), s32[]{:S(2)}) async-start(), calls=%async_computation.19 | async-start | bytes 1327104 | tf_op jit(solution)/shard_map/while/body/eval_jaxpr/all_gather | solution.py:162
  473.0 72.9 %all-gather.10.cloned.1.call-start = ((), (), s32[]{:S(2)}) async-start(), calls=%async_computation.20 | async-start | bytes 1966080 | tf_op jit(solution)/shard_map/while/body/eval_jaxpr/all_gather | solution.py:190
  510.3 71.0 %all-gather.12.cloned.1.call-start = ((), (), s32[]{:S(2)}) async-start(), calls=%async_computation.21 | async-start | bytes 1474560 | tf_op jit(solution)/shard_map/while/body/eval_jaxpr/all_gather | solution.py:205
  520.3 85.1 %all-gather.16.cloned.1.call-start = ((), (), s32[]{:S(2)}) async-start(), calls=%async_computation.23 | async-start | bytes 1327104 | tf_op jit(solution)/shard_map/while/body/eval_jaxpr/all_gather | solution.py:156
  567.1 18.4 %all-to-all-start = ((bf16[4,256,192]{1,2,0:T(8,128)(2,1)}), bf16[4,256,192]{1,2,0:T(8,128)(2,1)S(1)}, u32[]{:S(2)}, u32[]{:S(2)}) async-start(bf16[4,256,192]{1,2,0:T(8,128)(2,1)} %copy.107), calls=%async_computation | async-start | bytes 786432 | tf_op jit(solution)/shard_map/while/body/eval_jaxpr/all_to_all | solution.py:206
  570.6 73.3 %all-gather.14.cloned.1.call-start = ((), (), s32[]{:S(2)}) async-start(), calls=%async_computation.22 | async-start | bytes 1966080 | tf_op jit(solution)/shard_map/while/body/eval_jaxpr/all_gather | solution.py:210
  588.4 188.6 %copy-start.32 = (f32[256]{0:T(256)}, f32[256]{0:T(256)S(1)}, u32[]{:S(2)}) copy-start(f32[256]{0:T(256)S(1)} %broadcast_multiply_fusion.5) | copy-start | bytes 3076 | tf_op jit(solution)/shard_map/while
  588.6 188.4 %copy-start.41 = (f32[256]{0:T(256)}, f32[256]{0:T(256)S(1)}, u32[]{:S(2)}) copy-start(f32[256]{0:T(256)S(1)} %fusion.212) | copy-start | bytes 3076 | tf_op jit(solution)/shard_map/while
  589.7 78.8 %all-gather.20.cloned.1.call-start = ((), (), s32[]{:S(2)}) async-start(), calls=%async_computation.25 | async-start | bytes 1327104 | tf_op jit(solution)/shard_map/while/body/eval_jaxpr/all_gather | solution.py:228
  590.3 116.7 %all-gather.18.cloned.1.call-start = ((), (), s32[]{:S(2)}) async-start(), calls=%async_computation.24 | async-start | bytes 1966080 | tf_op jit(solution)/shard_map/while/body/eval_jaxpr/all_gather | solution.py:254
  592.1 184.8 %reduce-scatter.29.cloned.1.call-start = ((), (), s32[]{:S(2)}) async-start(), calls=%async_computation.26 | async-start | bytes 3932160 | tf_op jit(solution)/shard_map/while/body/eval_jaxpr/reduce_scatter | solution.py:267
  592.4 114.5 %copy-start.56 = (f32[768]{0:T(1024)}, f32[768]{0:T(1024)S(1)}, u32[]{:S(2)}) copy-start(f32[768]{0:T(1024)S(1)} %add.593) | copy-start | bytes 9220 | tf_op jit(solution)/shard_map/while
  648.7 65.8 %copy-start.64 = (bf16[768,768]{1,0:T(8,128)(2,1)S(1)}, bf16[768,768]{1,0:T(8,128)(2,1)}, u32[]{:S(2)}) copy-start(bf16[768,768]{1,0:T(8,128)(2,1)} %all-gather.16.cloned.1.call-done) | copy-start | bytes 3538948 | tf_op jit(solution)/shard_map/while
  717.5 59.5 %copy-start.29 = (f32[768]{0:T(1024)S(1)}, f32[768]{0:T(1024)}, u32[]{:S(2)}) copy-start(f32[768]{0:T(1024)} %copy-done.28) | copy-start | bytes 9220 | tf_op jit(solution)/shard_map/while
  717.6 63.1 %copy-start.3 = (bf16[768,768]{1,0:T(8,128)(2,1)S(1)}, bf16[768,768]{1,0:T(8,128)(2,1)}, u32[]{:S(2)}) copy-start(bf16[768,768]{1,0:T(8,128)(2,1)} %all-gather.12.cloned.1.call-done) | copy-start | bytes 3538948 | tf_op jit(solution)/shard_map/while
  784.9 15.2 all-to-all-start.1
  788.5 86.5 %reduce-scatter.31.cloned.1.call-start = ((), (), s32[]{:S(2)}) async-start(), calls=%async_computation.27 | async-start | bytes 1966080 | tf_op jit(solution)/shard_map/while/body/eval_jaxpr/reduce_scatter | solution.py:215
  794.0 128.8 %reduce-scatter.33.cloned.1.call-start = ((), (), s32[]{:S(2)}) async-start(), calls=%async_computation.28 | async-start | bytes 3932160 | tf_op jit(solution)/shard_map/while/body/eval_jaxpr/reduce_scatter | solution.py:299
  930.2 48.8 %copy-start.21 = (bf16[3,96,192]{2,0,1:T(4,128)(2,1)}, bf16[3,96,192]{2,0,1:T(4,128)(2,1)S(1)}, u32[]{:S(2)}) copy-start(bf16[3,96,192]{2,0,1:T(4,128)(2,1)S(1)} %get-tuple-element.1523) | copy-start | bytes 331780 | tf_op jit(solution)/shard_map/while
  930.3 34.5 %all-gather.8.cloned.1.call-start = ((), (), s32[]{:S(2)}) async-start(), calls=%async_computation.19 | async-start | bytes 1327104 | tf_op jit(solution)/shard_map/while/body/eval_jaxpr/all_gather | solution.py:162
  931.0 72.9 %all-gather.10.cloned.1.call-start = ((), (), s32[]{:S(2)}) async-start(), calls=%async_computation.20 | async-start | bytes 1966080 | tf_op jit(solution)/shard_map/while/body/eval_jaxpr/all_gather | solution.py:190
  968.3 71.0 %all-gather.12.cloned.1.call-start = ((), (), s32[]{:S(2)}) async-start(), calls=%async_computation.21 | async-start | bytes 1474560 | tf_op jit(solution)/shard_map/while/body/eval_jaxpr/all_gather | solution.py:205
  978.3 85.1 %all-gather.16.cloned.1.call-start = ((), (), s32[]{:S(2)}) async-start(), calls=%async_computation.23 | async-start | bytes 1327104 | tf_op jit(solution)/shard_map/while/body/eval_jaxpr/all_gather | solution.py:156
  1025.2 18.4 %all-to-all-start = ((bf16[4,256,192]{1,2,0:T(8,128)(2,1)}), bf16[4,256,192]{1,2,0:T(8,128)(2,1)S(1)}, u32[]{:S(2)}, u32[]{:S(2)}) async-start(bf16[4,256,192]{1,2,0:T(8,128)(2,1)} %copy.107), calls=%async_computation | async-start | bytes 786432 | tf_op jit(solution)/shard_map/while/body/eval_jaxpr/all_to_all | solution.py:206
  1028.6 73.4 %all-gather.14.cloned.1.call-start = ((), (), s32[]{:S(2)}) async-start(), calls=%async_computation.22 | async-start | bytes 1966080 | tf_op jit(solution)/shard_map/while/body/eval_jaxpr/all_gather | solution.py:210
  1046.4 188.8 %copy-start.32 = (f32[256]{0:T(256)}, f32[256]{0:T(256)S(1)}, u32[]{:S(2)}) copy-start(f32[256]{0:T(256)S(1)} %broadcast_multiply_fusion.5) | copy-start | bytes 3076 | tf_op jit(solution)/shard_map/while
  1046.7 188.5 %copy-start.41 = (f32[256]{0:T(256)}, f32[256]{0:T(256)S(1)}, u32[]{:S(2)}) copy-start(f32[256]{0:T(256)S(1)} %fusion.212) | copy-start | bytes 3076 | tf_op jit(solution)/shard_map/while
  1047.7 78.9 %all-gather.20.cloned.1.call-start = ((), (), s32[]{:S(2)}) async-start(), calls=%async_computation.25 | async-start | bytes 1327104 | tf_op jit(solution)/shard_map/while/body/eval_jaxpr/all_gather | solution.py:228
  1048.3 116.8 %all-gather.18.cloned.1.call-start = ((), (), s32[]{:S(2)}) async-start(), calls=%async_computation.24 | async-start | bytes 1966080 | tf_op jit(solution)/shard_map/while/body/eval_jaxpr/all_gather | solution.py:254
  1050.2 185.0 %reduce-scatter.29.cloned.1.call-start = ((), (), s32[]{:S(2)}) async-start(), calls=%async_computation.26 | async-start | bytes 3932160 | tf_op jit(solution)/shard_map/while/body/eval_jaxpr/reduce_scatter | solution.py:267
  1050.5 114.6 %copy-start.56 = (f32[768]{0:T(1024)}, f32[768]{0:T(1024)S(1)}, u32[]{:S(2)}) copy-start(f32[768]{0:T(1024)S(1)} %add.593) | copy-start | bytes 9220 | tf_op jit(solution)/shard_map/while
  1106.9 65.8 %copy-start.64 = (bf16[768,768]{1,0:T(8,128)(2,1)S(1)}, bf16[768,768]{1,0:T(8,128)(2,1)}, u32[]{:S(2)}) copy-start(bf16[768,768]{1,0:T(8,128)(2,1)} %all-gather.16.cloned.1.call-done) | copy-start | bytes 3538948 | tf_op jit(solution)/shard_map/while
  1175.7 59.5 %copy-start.29 = (f32[768]{0:T(1024)S(1)}, f32[768]{0:T(1024)}, u32[]{:S(2)}) copy-start(f32[768]{0:T(1024)} %copy-done.28) | copy-start | bytes 9220 | tf_op jit(solution)/shard_map/while
  1175.8 63.1 %copy-start.3 = (bf16[768,768]{1,0:T(8,128)(2,1)S(1)}, bf16[768,768]{1,0:T(8,128)(2,1)}, u32[]{:S(2)}) copy-start(bf16[768,768]{1,0:T(8,128)(2,1)} %all-gather.12.cloned.1.call-done) | copy-start | bytes 3538948 | tf_op jit(solution)/shard_map/while
  1243.1 15.2 all-to-all-start.1
  1246.7 86.2 %reduce-scatter.31.cloned.1.call-start = ((), (), s32[]{:S(2)}) async-start(), calls=%async_computation.27 | async-start | bytes 1966080 | tf_op jit(solution)/shard_map/while/body/eval_jaxpr/reduce_scatter | solution.py:215
  1252.2 128.6 %reduce-scatter.33.cloned.1.call-start = ((), (), s32[]{:S(2)}) async-start(), calls=%async_computation.28 | async-start | bytes 3932160 | tf_op jit(solution)/shard_map/while/body/eval_jaxpr/reduce_scatter | solution.py:299
  1393.5 50.4 %reduce-scatter.17.cloned.1.call-start = ((), (), s32[]{:S(2)}) async-start(), calls=%async_computation.13 | async-start | bytes 2949120 | tf_op jit(solution)/shard_map/reduce_scatter | solution.py:344
  1394.1 119.1 %reduce-scatter.27.cloned.1.call-start = ((), (), s32[]{:S(2)}) async-start(), calls=%async_computation.18 | async-start | bytes 442368
  1395.1 122.9 %reduce-scatter.25.cloned.1.call-start = ((), (), s32[]{:S(2)}) async-start(), calls=%async_computation.17 | async-start | bytes 884736
  1446.2 118.1 %reduce-scatter.15.cloned.1.call-start = ((), (), s32[]{:S(2)}) async-start(), calls=%async_computation.12 | async-start | bytes 2654208 | tf_op jit(solution)/shard_map/reduce_scatter | solution.py:360
  1449.2 161.2 %reduce-scatter.19.cloned.1.call-start = ((), (), s32[]{:S(2)}) async-start(), calls=%async_computation.14 | async-start | bytes 2654208 | tf_op jit(solution)/shard_map/reduce_scatter | solution.py:362
  1450.0 206.7 %reduce-scatter.23.cloned.1.call-start = ((), (), s32[]{:S(2)}) async-start(), calls=%async_computation.16 | async-start | bytes 2654208 | tf_op jit(solution)/shard_map/reduce_scatter | solution.py:368
  1474.0 228.7 %reduce-scatter.21.cloned.1.call-start = ((), (), s32[]{:S(2)}) async-start(), calls=%async_computation.15 | async-start | bytes 2654208 | tf_op jit(solution)/shard_map/reduce_scatter | solution.py:364
  (167 other events, 2358.6 us)
Sparse Core Ops, SparseCore 0:
  13.8 26.7 all-gather.7
  51.2 36.4 all-gather.9
  89.7 33.2 all-gather.11
  124.8 22.3 all-gather.15
  148.6 37.0 all-gather.13
  187.4 22.7 all-gather.19
  211.8 37.0 all-gather.17
  259.6 59.2 reduce-scatter.28
  336.0 36.8 reduce-scatter.30
  405.1 59.4 reduce-scatter.32
  474.9 23.8 all-gather.7
  510.4 35.4 all-gather.9
  548.0 33.2 all-gather.11
  583.0 22.3 all-gather.15
  606.8 37.0 all-gather.13
  645.6 22.7 all-gather.19
  669.9 37.0 all-gather.17
  717.7 59.2 reduce-scatter.28
  794.1 36.8 reduce-scatter.30
  863.4 59.3 reduce-scatter.32
  933.0 23.8 all-gather.7
  968.4 35.4 all-gather.9
  1006.0 33.2 all-gather.11
  1041.1 22.3 all-gather.15
  1065.0 37.0 all-gather.13
  1103.8 22.7 all-gather.19
  1128.1 37.0 all-gather.17
  1175.9 59.2 reduce-scatter.28
  1252.3 36.8 reduce-scatter.30
  1321.4 59.3 reduce-scatter.32
Sparse Core Ops, SparseCore 1:
  1396.3 47.6 reduce-scatter.16
  1446.9 33.2 reduce-scatter.26
  1483.2 34.9 reduce-scatter.24
  1522.0 42.2 reduce-scatter.14
  1568.2 42.2 reduce-scatter.18
  1614.4 42.2 reduce-scatter.22
  1660.5 42.2 reduce-scatter.20
where the time goes:
time: 1720 us; the launch traced here: 1710 us
  waiting for transfers between devices  954 us (55%)
  matrix products  237 us (14%)
  blocking collectives  192 us (11%)
  local copies, waits for them, and re-layouts  157 us (9%)
  other arithmetic  94.9 us (6%)
  loops' own time  34.3 us (2%)
  starting transfers between devices  24.2 us (1%)
  between operations  17.3 us (1%)
    reduce_scatter x3, waiting for transfers between devices, micro_step(): lax.psum_scatter(jnp.einsum('lf,df->ld', d_hidden, up_full, preferred_ele...  178 us
    all_gather x3, waiting for transfers between devices, micro_step(): lax.all_gather(d_down.astype(jnp.bfloat16), 'tensor', axis=0, tiled=True)  116 us
    all_gather x3, waiting for transfers between devices, micro_step(): gathered_two = lax.all_gather(normed_two, 'tensor', axis=0, tiled=True)  116 us
    reduce_scatter x3, waiting for transfers between devices, micro_step(): lax.psum_scatter(jnp.einsum('cle,cde->ld', d_projected, qkv_full, preferr...  115 us
    while x3, blocking collectives  75.5 us
    all_gather x3, waiting for transfers between devices, micro_step(): lax.all_gather(w_down, 'dp', axis=1, tiled=True)  59.4 us
    dynamic_update_slice x12, local copies, waits for them, and re-layouts, attend_back(): lax.scan(one_block, (empty, empty), jnp.arange(block_count, dtype=jnp.int...  50.9 us
    reduce_scatter x1, waiting for transfers between devices, shards(): lax.psum_scatter(acc_out, 'tensor', scatter_dimension=0, tiled=True)  48.7 us
  transfers between devices with their start and end apart: 43, of which 36 were waited for; matrix products, arithmetic and copies ran while one was open for 23% of the time, Pallas kernels for 0%

commit v1 on v0

v1 whole, which is shorter than its diff:
```python
from functools import partial

import jax
import jax.numpy as jnp
import numpy as np
from jax import lax
from jax.experimental import pallas as pl
from jax.experimental.pallas import tpu as pltpu
from jax.sharding import PartitionSpec as P

HEAD = 64
PRECISE = lax.Precision.HIGHEST
EPSILON = 1e-05
F32 = jnp.float32
BF16 = jnp.bfloat16
PAIR = 2 * HEAD
BOTH = ("dp", "tensor")
ANY = pl.BlockSpec(memory_space=pl.ANY)
VMEM = pl.BlockSpec(memory_space=pltpu.VMEM)
SMEM = pl.BlockSpec(memory_space=pltpu.SMEM)


def dot_nn(a, b):
    return jnp.dot(a, b, preferred_element_type=F32)


def dot_nt(a, b):
    return lax.dot_general(a, b, (((1,), (1,)), ((), ())), preferred_element_type=F32)


def params(**more):
    return pltpu.CompilerParams(vmem_limit_bytes=58 << 20, **more)


def cost(flops, nbytes, trans=0):
    return pl.CostEstimate(flops=int(flops), bytes_accessed=int(nbytes), transcendentals=int(trans))


def shape(dims, kind):
    return jax.ShapeDtypeStruct(tuple(dims), kind)


def row_at(me_ref, index, rows):
    return pl.multiple_of((me_ref[0] ^ index) * rows, rows)


def qkv_kernel(blocks, me, *refs):
    x_refs, refs = refs[:4], refs[4:]
    (mul, add, cosine, sin_a, sin_b), refs = refs[:5], refs[5:]
    qk_refs, v_refs, refs = refs[:blocks], refs[blocks : 2 * blocks], refs[2 * blocks :]
    (n_t, q_out, k_out, v_out, q_t, k_t, v_t), (w_buf, n_buf, sems) = refs[:7], refs[7:]
    rows = qk_refs[0].shape[1]
    copies = []
    for j in range(blocks):
        at = row_at(me, j, rows)
        copies.append(
            pltpu.make_async_copy(qk_refs[j], w_buf.at[0:2, pl.ds(at, rows), :], sems.at[0, j])
        )
        copies.append(
            pltpu.make_async_copy(v_refs[j].at[0], w_buf.at[2, pl.ds(at, rows), :], sems.at[1, j])
        )
    for copy in copies:
        copy.start()
    part = x_refs[0].shape[0]
    for b, x_ref in enumerate(x_refs):
        x = x_ref[...].astype(F32)
        centred = x - jnp.mean(x, axis=-1, keepdims=True)
        spread = jnp.mean(centred * centred, axis=-1, keepdims=True)
        n_buf[b * part : (b + 1) * part, :] = (
            centred * lax.rsqrt(spread + EPSILON) * mul[...] + add[...]
        ).astype(BF16)
    normed = n_buf[...]
    n_t[...] = normed.T
    for copy in copies:
        copy.wait()
    width = q_out.shape[1]
    for c, (flat, turned, factor) in enumerate(((q_out, q_t, HEAD**-0.5), (k_out, k_t, 1.0))):
        proj = dot_nn(normed, w_buf[c])
        for p in range(width // PAIR):
            lanes = slice(p * PAIR, (p + 1) * PAIR)
            r = proj[:, lanes]
            spun = (
                r * cosine[...]
                + pltpu.roll(r, PAIR - HEAD // 2, 1) * sin_a[...]
                + pltpu.roll(r, HEAD // 2, 1) * sin_b[...]
            )
            spun = spun.astype(BF16) * BF16(factor)
            flat[:, lanes] = spun
            turned[lanes, :] = spun.T
    values = dot_nn(normed, w_buf[2]).astype(BF16)
    v_out[...] = values
    v_t[...] = values.T


def qkv(me, x_parts, mul, add, cosine, sin_a, sin_b, qk_pieces, v_pieces):
    blocks = len(qk_pieces)
    part, width = x_parts[0].shape
    length = 4 * part
    cols = qk_pieces[0].shape[2]
    flat, turned = shape((length, cols), BF16), shape((cols, length), BF16)
    return pl.pallas_call(
        partial(qkv_kernel, blocks),
        out_shape=[shape((width, length), BF16), flat, flat, flat, turned, turned, turned],
        in_specs=[SMEM] + [VMEM] * 9 + [ANY] * (2 * blocks),
        out_specs=[VMEM] * 7,
        scratch_shapes=[
            pltpu.VMEM((3, width, cols), BF16),
            pltpu.VMEM((length, width), BF16),
            pltpu.SemaphoreType.DMA((2, blocks)),
        ],
        compiler_params=params(),
        cost_estimate=cost(6 * length * width * cols, 16e6),
        name="qkv",
    )(me, *x_parts, mul, add, cosine, sin_a, sin_b, *qk_pieces, *v_pieces)


def head_mask(ref, head):
    lane = lax.broadcasted_iota(jnp.int32, (1, PAIR), 1)
    return jnp.where((lane // HEAD) == head, ref[...], jnp.zeros((), BF16))


def same_doc_bias(bias, doc_row, doc_col):
    bias[...] = jnp.where(doc_col[...] == doc_row[...], 0.0, -1e30)


def attend_kernel(q, k, v_t, doc_row, doc_col, mix_t, log_sum, bias):
    @pl.when(pl.program_id(0) == 0)
    def _():
        same_doc_bias(bias, doc_row, doc_col)

    for h in range(2):
        rows = slice(h * HEAD, (h + 1) * HEAD)
        scores = dot_nt(head_mask(k, h), q[...]) + bias[...]
        top = jnp.max(scores, axis=0, keepdims=True)
        weights = jnp.exp(scores - top)
        total = jnp.sum(weights, axis=0, keepdims=True)
        mixed = dot_nn(v_t[rows, :], weights.astype(BF16))
        mix_t[rows, :] = (mixed / total).astype(BF16)
        log_sum[0, h : h + 1, :] = top + jnp.log(total)


def attend(q, k, v_t, doc_row, doc_col):
    length, width = q.shape
    pairs = width // PAIR
    flat = pl.BlockSpec((length, PAIR), lambda i: (0, i))
    turned = pl.BlockSpec((PAIR, length), lambda i: (i, 0))
    return pl.pallas_call(
        attend_kernel,
        grid=(pairs,),
        in_specs=[
            flat,
            flat,
            turned,
            pl.BlockSpec((1, length), lambda i: (0, 0)),
            pl.BlockSpec((length, 1), lambda i: (0, 0)),
        ],
        out_specs=[turned, pl.BlockSpec((1, 2, length), lambda i: (i, 0, 0))],
        out_shape=[shape((width, length), BF16), shape((pairs, 2, length), F32)],
        scratch_shapes=[pltpu.VMEM((length, length), F32)],
        compiler_params=params(),
        cost_estimate=cost(16 * length * length * width, 8e6),
        name="attend",
    )(q, k, v_t, doc_row, doc_col)


def load_out_weight(me, pieces, buf, sems):
    rows = pieces[0].shape[1]
    copies = [
        pltpu.make_async_copy(
            piece.at[1], buf.at[pl.ds(row_at(me, j, rows), rows), :], sems.at[j]
        )
        for j, piece in enumerate(pieces)
    ]
    for copy in copies:
        copy.start()
    return copies


def middle_kernel(blocks, me, *refs):
    x_refs, g_refs, refs = refs[:4], refs[4:8], refs[8:]
    (mix_t, gate_one, mul, add, gate_two), refs = refs[:5], refs[5:]
    pieces, refs = refs[:blocks], refs[blocks:]
    (att, n_two, n_two_t, d_down, d_down_t, d_bias), (w_buf, sems) = refs[:6], refs[6:]
    copies = load_out_weight(me, pieces, w_buf, sems)
    part = x_refs[0].shape[0]
    total = jnp.zeros(gate_two.shape, F32)
    for b, g_ref in enumerate(g_refs):
        scaled = g_ref[...].astype(F32) * gate_two[...]
        total += jnp.sum(scaled, axis=0, keepdims=True)
        d_down[b * part : (b + 1) * part, :] = scaled.astype(BF16)
    d_bias[...] = total
    d_down_t[...] = d_down[...].T
    mixture = mix_t[...].T
    for copy in copies:
        copy.wait()
    for b, x_ref in enumerate(x_refs):
        rows = slice(b * part, (b + 1) * part)
        attention = dot_nt(mixture[rows, :], w_buf[...])
        att[rows, :] = attention
        mid = x_ref[...].astype(F32) + gate_one[...] * attention
        centred = mid - jnp.mean(mid, axis=-1, keepdims=True)
        spread = jnp.mean(centred * centred, axis=-1, keepdims=True)
        n_two[rows, :] = (
            centred * lax.rsqrt(spread + EPSILON) * mul[...] + add[...]
        ).astype(BF16)
    n_two_t[...] = n_two[...].T


def middle(me, x_parts, g_parts, mix_t, gate_one, mul, add, gate_two, pieces):
    blocks = len(pieces)
    part, width = x_parts[0].shape
    length = 4 * part
    inner = mix_t.shape[0]
    flat, turned = shape((length, width), BF16), shape((width, length), BF16)
    return pl.pallas_call(
        partial(middle_kernel, blocks),
        out_shape=[shape((length, width), F32), flat, turned, flat, turned, shape((1, width), F32)],
        in_specs=[SMEM] + [VMEM] * 13 + [ANY] * blocks,
        out_specs=[VMEM] * 6,
        scratch_shapes=[pltpu.VMEM((width, inner), BF16), pltpu.SemaphoreType.DMA((blocks,))],
        compiler_params=params(),
        cost_estimate=cost(2 * length * width * inner, 16e6),
        name="middle",
    )(me, *x_parts, *g_parts, mix_t, gate_one, mul, add, gate_two, *pieces)


def spread_rows(me, value, stage, keep, send):
    blocks, rows = stage.shape[0], stage.shape[1]
    for j in range(blocks):
        stage[j] = value[j * rows : (j + 1) * rows, :].astype(BF16)
    for j in range(blocks):
        block = stage[me[0] ^ j]
        if j % 2 == 0:
            keep[j // 2] = block
        else:
            send[j // 2] = block


C_ROOT = 0.7978845608028654
C_CUBE = 0.044715


def feed_kernel(blocks, steps, first, me, *refs):
    (n_two, n_two_t, d_down, d_down_t, bias), refs = refs[:5], refs[5:]
    if not first:
        (down_in, d_n_in), refs = refs[:2], refs[2:]
    up_refs, down_refs, refs = refs[:blocks], refs[blocks : 2 * blocks], refs[2 * blocks :]
    outs = 5 + 2 * (blocks > 1)
    (down, d_n, d_bias, up_keep, dn_keep), sends = refs[:5], refs[5:outs]
    (w_buf, stage, sems) = refs[outs:]
    step = pl.program_id(0)
    rows = up_refs[0].shape[0]
    chunk = w_buf.shape[3]
    offset = 0 if first else steps * chunk

    def copies(s):
        out = []
        for m, group in enumerate((up_refs, down_refs)):
            for j, piece in enumerate(group):
                out.append(
                    pltpu.make_async_copy(
                        piece.at[:, pl.ds(offset + s * chunk, chunk)],
                        w_buf.at[m, s, pl.ds(row_at(me, j, rows), rows), :],
                        sems.at[m, s, j],
                    )
                )
        return out

    @pl.when(step == 0)
    def _():
        for s in range(steps):
            for copy in copies(s):
                copy.start()
        if first:
            down[...] = jnp.zeros_like(down)
            d_n[...] = jnp.zeros_like(d_n)
        else:
            down[...] = down_in[...]
            d_n[...] = d_n_in[...]

    for s in range(steps):

        @pl.when(step == s)
        def _():
            for copy in copies(s):
                copy.wait()

    w_up = w_buf[0, step]
    w_down_t = w_buf[1, step]
    h = dot_nn(n_two[...], w_up) + bias[0]
    square = h * h
    t = jnp.tanh(C_ROOT * h * (1.0 + C_CUBE * square))
    half = 0.5 + 0.5 * t
    act = (h * half).astype(BF16)
    slope = half + (0.5 * C_ROOT) * h * (1.0 - t * t) * (1.0 + (3.0 * C_CUBE) * square)
    d_h = (dot_nn(d_down[...], w_down_t) * slope).astype(BF16)
    d_bias[0] = jnp.sum(d_h.astype(F32), axis=0, keepdims=True)
    down[...] += dot_nt(act, w_down_t)
    d_n[...] += dot_nt(d_h, w_up)
    up_send, dn_send = sends if sends else (None, None)
    spread_rows(me, dot_nn(n_two_t[...], d_h), stage, up_keep, up_send)
    spread_rows(me, dot_nn(d_down_t[...], act), stage, dn_keep, dn_send)


def feed(me, n_two, n_two_t, d_down, d_down_t, bias, up_pieces, down_pieces, start, before, units):
    blocks = len(up_pieces)
    length, width = n_two.shape
    chunk = 512 if units % 512 == 0 else units
    steps = units // chunk
    first = before is None
    rows = up_pieces[0].shape[0]
    one = pl.Buffered(1)
    flat = pl.BlockSpec((length, width), lambda i: (0, 0), pipeline_mode=one)
    turned = pl.BlockSpec((width, length), lambda i: (0, 0), pipeline_mode=one)
    held = pl.BlockSpec((length, width), lambda i: (0, 0))
    half = max(blocks // 2, 1)
    grad = pl.BlockSpec((half, rows, chunk), lambda i: (0, 0, i))
    grads = 2 if blocks == 1 else 4
    bias_spec = pl.BlockSpec((1, 1, chunk), lambda i: (i + start // chunk, 0, 0))
    return pl.pallas_call(
        partial(feed_kernel, blocks, steps, first),
        grid=(steps,),
        in_specs=[SMEM, flat, turned, flat, turned, bias_spec]
        + ([] if first else [flat, flat])
        + [ANY] * (2 * blocks),
        out_specs=[held, held, pl.BlockSpec((1, 1, chunk), lambda i: (i, 0, 0))] + [grad] * grads,
        out_shape=[shape((length, width), F32)] * 2
        + [shape((steps, 1, chunk), F32)]
        + [shape((half, rows, units), BF16)] * grads,
        scratch_shapes=[
            pltpu.VMEM((2, steps, width, chunk), BF16),
            pltpu.VMEM((blocks, rows, chunk), BF16),
            pltpu.SemaphoreType.DMA((2, steps, blocks)),
        ],
        compiler_params=params(),
        cost_estimate=cost(12 * length * width * units, 20e6),
        name="feed",
    )(
        me,
        n_two,
        n_two_t,
        d_down,
        d_down_t,
        bias.reshape(-1, 1, chunk),
        *(() if first else before),
        *up_pieces,
        *down_pieces,
    )


def turn_kernel(blocks, me, *refs):
    x_refs, g_refs, refs = refs[:4], refs[4:8], refs[8:]
    (att, down, d_n, mix_t, gate_one, mul, gate_two, bias), refs = refs[:8], refs[8:]
    pieces, refs = refs[:blocks], refs[blocks:]
    outs = 9 + (blocks > 1)
    out_refs, (d_mid, d_mix, d_mix_t, sums, keep), sends = refs[:4], refs[4:9], refs[9:outs]
    (w_buf, d_att, stage, sems) = refs[outs:]
    copies = load_out_weight(me, pieces, w_buf, sems)
    part = x_refs[0].shape[0]
    totals = [jnp.zeros(gate_two.shape, F32) for _ in range(4)]
    for b in range(4):
        rows = slice(b * part, (b + 1) * part)
        g = g_refs[b][...].astype(F32)
        attention = att[rows, :]
        mid = x_refs[b][...].astype(F32) + gate_one[...] * attention
        branch = down[rows, :] + bias[...]
        out_refs[b][...] = (mid + gate_two[...] * branch).astype(BF16)
        centred = mid - jnp.mean(mid, axis=-1, keepdims=True)
        inverse = lax.rsqrt(jnp.mean(centred * centred, axis=-1, keepdims=True) + EPSILON)
        unit = centred * inverse
        dn = d_n[rows, :]
        dn_unit = dn * unit
        du = dn * mul[...]
        dm = g + inverse * (
            du
            - jnp.mean(du, axis=-1, keepdims=True)
            - unit * jnp.mean(dn_unit * mul[...], axis=-1, keepdims=True)
        )
        d_mid[rows, :] = dm
        d_att[rows, :] = (dm * gate_one[...]).astype(BF16)
        for n, term in enumerate((g * branch, dn_unit, dn, dm * attention)):
            totals[n] += jnp.sum(term, axis=0, keepdims=True)
    for n in range(4):
        sums[n : n + 1, :] = totals[n]
    for copy in copies:
        copy.wait()
    d_mix[...] = dot_nn(d_att[...], w_buf[...]).astype(BF16)
    d_mix_t[...] = d_mix[...].T
    grad = dot_nt(d_att[...].T, mix_t[...])
    spread_rows(me, grad, stage, keep, sends[0] if sends else None)


def turn(me, x_parts, g_parts, att, down, d_n, mix_t, gate_one, mul, gate_two, bias, pieces):
    blocks = len(pieces)
    part, width = x_parts[0].shape
    length = 4 * part
    inner = mix_t.shape[0]
    rows = pieces[0].shape[1]
    half = max(blocks // 2, 1)
    grads = 1 if blocks == 1 else 2
    return pl.pallas_call(
        partial(turn_kernel, blocks),
        out_shape=[shape((part, width), BF16)] * 4
        + [
            shape((length, width), F32),
            shape((length, inner), BF16),
            shape((inner, length), BF16),
            shape((4, width), F32),
        ]
        + [shape((half, rows, inner), BF16)] * grads,
        in_specs=[SMEM] + [VMEM] * 16 + [ANY] * blocks,
        out_specs=[VMEM] * (8 + grads),
        scratch_shapes=[
            pltpu.VMEM((width, inner), BF16),
            pltpu.VMEM((length, width), BF16),
            pltpu.VMEM((blocks, rows, inner), BF16),
            pltpu.SemaphoreType.DMA((blocks,)),
        ],
        compiler_params=params(),
        cost_estimate=cost(4 * length * width * inner, 24e6),
        name="turn",
    )(
        me, *x_parts, *g_parts, att, down, d_n, mix_t, gate_one, mul, gate_two, bias, *pieces
    )


def attend_back_kernel(
    q, k, v, d_mix, q_t, k_t, d_mix_t, mix_t, log_sum, doc_row, doc_col, cos_t, sin_t,
    dq_t, dk_t, dv_t, bias, dq_acc, dk_acc, dv_acc,
):
    @pl.when(pl.program_id(0) == 0)
    def _():
        same_doc_bias(bias, doc_row, doc_col)

    length = q.shape[0]
    block = 256 if length % 256 == 0 else length
    for h in range(2):
        rows = slice(h * HEAD, (h + 1) * HEAD)
        keys = head_mask(k, h)
        values = head_mask(v, h)
        row_dot = jnp.sum(
            d_mix_t[rows, :].astype(F32) * mix_t[rows, :].astype(F32), axis=0, keepdims=True
        )
        for b in range(length // block):
            c = slice(b * block, (b + 1) * block)
            probs = jnp.exp(dot_nt(keys, q[c, :]) + bias[:, c] - log_sum[0, h : h + 1, c])
            d_scores = (probs * (dot_nt(values, d_mix[c, :]) - row_dot[:, c])).astype(BF16)
            dv_part = dot_nt(d_mix_t[rows, c], probs.astype(BF16))
            dk_part = dot_nt(q_t[rows, c], d_scores)
            if b == 0:
                dv_acc[rows, :] = dv_part
                dk_acc[rows, :] = dk_part
            else:
                dv_acc[rows, :] += dv_part
                dk_acc[rows, :] += dk_part
            dq_acc[rows, c] = dot_nn(k_t[rows, :], d_scores)
    half = HEAD // 2
    for h in range(2):
        one = slice(h * HEAD, h * HEAD + half)
        two = slice(h * HEAD + half, (h + 1) * HEAD)
        for acc, out, factor in ((dq_acc, dq_t, HEAD**-0.5), (dk_acc, dk_t, 1.0)):
            a, b = acc[one, :] * factor, acc[two, :] * factor
            out[one, :] = (a * cos_t[...] + b * sin_t[...]).astype(BF16)
            out[two, :] = (b * cos_t[...] - a * sin_t[...]).astype(BF16)
    dv_t[...] = dv_acc[...].astype(BF16)


def attend_back(q, k, v, d_mix, q_t, k_t, d_mix_t, mix_t, log_sum, doc_row, doc_col, cos_t, sin_t, start, count):
    length, width = q.shape
    flat = pl.BlockSpec((length, PAIR), lambda i: (0, i + start))
    turned = pl.BlockSpec((PAIR, length), lambda i: (i + start, 0))
    out = pl.BlockSpec((PAIR, length), lambda i: (i, 0))
    fixed = lambda a: pl.BlockSpec(a.shape, lambda i: (0, 0))
    return pl.pallas_call(
        attend_back_kernel,
        grid=(count,),
        in_specs=[flat] * 4
        + [turned] * 4
        + [pl.BlockSpec((1, 2, length), lambda i: (i + start, 0, 0))]
        + [fixed(a) for a in (doc_row, doc_col, cos_t, sin_t)],
        out_specs=[out] * 3,
        out_shape=[shape((count * PAIR, length), BF16)] * 3,
        scratch_shapes=[pltpu.VMEM((length, length), F32)] + [pltpu.VMEM((PAIR, length), F32)] * 3,
        compiler_params=params(),
        cost_estimate=cost(28 * length * length * count * PAIR, 14e6 * count * PAIR / width),
        name="attend_back",
    )(q, k, v, d_mix, q_t, k_t, d_mix_t, mix_t, log_sum, doc_row, doc_col, cos_t, sin_t)


def first_kernel(blocks, me, *refs):
    x_refs, refs = refs[:4], refs[4:]
    (d_mid, mul, dq_t, dk_t, dv_t), refs = refs[:5], refs[5:]
    qk_refs, v_refs, refs = refs[:blocks], refs[blocks : 2 * blocks], refs[2 * blocks :]
    out_refs, (sums, w_buf, sems) = refs[:4], refs[4:]
    rows = qk_refs[0].shape[1]
    copies = []
    for j in range(blocks):
        at = row_at(me, j, rows)
        copies.append(
            pltpu.make_async_copy(qk_refs[j], w_buf.at[0:2, pl.ds(at, rows), :], sems.at[0, j])
        )
        copies.append(
            pltpu.make_async_copy(v_refs[j].at[0], w_buf.at[2, pl.ds(at, rows), :], sems.at[1, j])
        )
    for copy in copies:
        copy.start()
    for copy in copies:
        copy.wait()
    d_n_t = (
        dot_nn(w_buf[0], dq_t[...]) + dot_nn(w_buf[1], dk_t[...]) + dot_nn(w_buf[2], dv_t[...])
    )
    part = x_refs[0].shape[0]
    totals = [jnp.zeros(mul.shape, F32) for _ in range(2)]
    for b in range(4):
        r = slice(b * part, (b + 1) * part)
        dn = d_n_t[:, r].T
        x = x_refs[b][...].astype(F32)
        centred = x - jnp.mean(x, axis=-1, keepdims=True)
        inverse = lax.rsqrt(jnp.mean(centred * centred, axis=-1, keepdims=True) + EPSILON)
        unit = centred * inverse
        dn_unit = dn * unit
        du = dn * mul[...]
        out_refs[b][...] = (
            d_mid[r, :]
            + inverse
            * (
                du
                - jnp.mean(du, axis=-1, keepdims=True)
                - unit * jnp.mean(dn_unit * mul[...], axis=-1, keepdims=True)
            )
        ).astype(BF16)
        for n, term in enumerate((dn_unit, dn)):
            totals[n] += jnp.sum(term, axis=0, keepdims=True)
    for n in range(2):
        sums[n : n + 1, :] = totals[n]


def first(me, x_parts, d_mid, mul, dq_t, dk_t, dv_t, qk_pieces, v_pieces):
    blocks = len(qk_pieces)
    part, width = x_parts[0].shape
    length = 4 * part
    cols = dq_t.shape[0]
    return pl.pallas_call(
        partial(first_kernel, blocks),
        out_shape=[shape((part, width), BF16)] * 4 + [shape((2, width), F32)],
        in_specs=[SMEM] + [VMEM] * 9 + [ANY] * (2 * blocks),
        out_specs=[VMEM] * 5,
        scratch_shapes=[pltpu.VMEM((3, width, cols), BF16), pltpu.SemaphoreType.DMA((2, blocks))],
        compiler_params=params(),
        cost_estimate=cost(6 * length * width * cols, 20e6),
        name="first",
    )(me, *x_parts, d_mid, mul, dq_t, dk_t, dv_t, *qk_pieces, *v_pieces)


def qkv_grad_kernel(blocks, me, *refs):
    (n_t, dq_t, dk_t, dv_t), refs = refs[:4], refs[4:]
    outs = 1 + (blocks > 1)
    keep, sends, (stage,) = refs[0], refs[1:outs], refs[outs:]
    rows = stage.shape[1]
    for c, d_t in enumerate((dq_t, dk_t, dv_t)):
        grad = dot_nt(n_t[...], d_t[...])
        for j in range(blocks):
            stage[j] = grad[j * rows : (j + 1) * rows, :].astype(BF16)
        for j in range(blocks):
            block = stage[me[0] ^ j]
            if j % 2 == 0:
                keep[j // 2, c] = block
            else:
                sends[0][j // 2, c] = block


def qkv_grad(me, n_t, dq_t, dk_t, dv_t, blocks):
    width, length = n_t.shape
    cols = dq_t.shape[0]
    rows = width // blocks
    half = max(blocks // 2, 1)
    grads = 1 if blocks == 1 else 2
    return pl.pallas_call(
        partial(qkv_grad_kernel, blocks),
        out_shape=[shape((half, 3, rows, cols), BF16)] * grads,
        in_specs=[SMEM] + [VMEM] * 4,
        out_specs=[VMEM] * grads,
        scratch_shapes=[pltpu.VMEM((blocks, rows, cols), BF16)],
        compiler_params=params(),
        cost_estimate=cost(6 * length * width * cols, 10e6),
        name="qkv_grad",
    )(me, n_t, dq_t, dk_t, dv_t)


class Group:
    def __init__(self, dp_count, tensor_count, per_dp):
        self.dp, self.tensor, self.per_dp = dp_count, tensor_count, per_dp
        self.d, self.r = lax.axis_index("dp"), lax.axis_index("tensor")
        self.paired = dp_count == 8

    def bit(self, v, b):
        return lax.ppermute(v, "dp", [(i, i ^ (1 << b)) for i in range(self.dp)])

    def step(self, v, k):
        return lax.ppermute(v, "dp", [(i, i ^ k) for i in range(self.dp)])

    def z(self, v, k):
        return lax.ppermute(v, "tensor", [(i, i ^ k) for i in range(self.tensor)])

    def owns(self, d, r):
        return 0 <= r - d % 2 < self.per_dp

    def to_owner(self, rows, zero_idle):
        mine = self.r - self.d % 2
        top = self.per_dp - 1
        own = lax.dynamic_index_in_dim(rows, jnp.clip(mine, 0, top), 0, keepdims=False)
        if zero_idle:
            own = jnp.where((mine >= 0) & (mine <= top), own, jnp.zeros_like(own))
        parts = [own]
        for k in range(1, self.tensor):
            want = (self.r ^ k) - self.d % 2
            sent = lax.dynamic_index_in_dim(rows, jnp.clip(want, 0, top), 0, keepdims=False)
            pairs = [
                (d * self.tensor + r, d * self.tensor + (r ^ k))
                for d in range(self.dp)
                for r in range(self.tensor)
                if self.owns(d, r ^ k)
            ]
            parts.append(lax.ppermute(sent, BOTH, pairs))
        return parts

    def from_owner(self, parts):
        came = [parts[0]]
        for k in range(1, self.tensor):
            pairs = [
                (d * self.tensor + r, d * self.tensor + (r ^ k))
                for d in range(self.dp)
                for r in range(self.tensor)
                if self.owns(d, r)
            ]
            came.append(lax.ppermute(parts[k], BOTH, pairs))
        stack = jnp.stack(came)
        return jnp.stack(
            [
                lax.dynamic_index_in_dim(stack, self.r ^ (j + self.d % 2), 0, keepdims=False)
                for j in range(self.per_dp)
            ]
        )

    def z_join(self, v):
        return jnp.concatenate([v] + [self.z(v, k) for k in range(1, self.tensor)], axis=-1)

    def gather(self, v, order):
        if not self.paired:
            return [lax.all_gather(v, "dp", axis=v.ndim - 2, tiled=True)]
        held = {0: v}
        for b in order:
            held |= {j ^ (1 << b): self.bit(p, b) for j, p in held.items()}
        return [held[j] for j in range(self.dp)]

    def reduce(self, keep, *more):
        if not self.paired:
            value = keep[0].astype(F32)
            return lax.psum_scatter(value, "dp", scatter_dimension=value.ndim - 2, tiled=True)
        send, order = more
        got = self.bit(send, 0)
        total = {2 * j: keep[j].astype(F32) + got[j].astype(F32) for j in range(self.dp // 2)}
        for b in order:
            step = 1 << b
            out = {j: p.astype(BF16) for j, p in total.items() if j & step}
            total = {
                j: p + self.bit(out[j ^ step], b).astype(F32)
                for j, p in total.items()
                if not j & step
            }
        return total[0]

    def reduce_two(self, one, two, *sends):
        if not self.paired:
            return self.reduce(one), self.reduce(two)
        return self.reduce(one, sends[0], (1, 2)), self.reduce(two, sends[1], (2, 1))

    def z_reduce(self, v):
        size = v.shape[-1] // self.tensor
        total = v[..., :size]
        for k in range(1, self.tensor):
            out = v[..., k * size : (k + 1) * size].astype(BF16)
            total = total + self.z(out, k).astype(F32)
        return total

    def small_gather(self, v):
        if not self.paired:
            return lax.all_gather(v, "dp", axis=0)
        stack = jnp.stack([v] + [self.step(v, k) for k in range(1, self.dp)])
        return jnp.take(stack, self.d ^ jnp.arange(self.dp), axis=0)

    def small_swap(self, v):
        if not self.paired:
            return lax.all_to_all(v, "dp", split_axis=0, concat_axis=0, tiled=True)
        relative = jnp.take(v, self.d ^ jnp.arange(self.dp), axis=0)
        stack = jnp.stack(
            [relative[0]] + [self.step(relative[k], k) for k in range(1, self.dp)]
        )
        return jnp.take(stack, self.d ^ jnp.arange(self.dp), axis=0)


def silu_slope(c):
    sig = jax.nn.sigmoid(c)
    return sig * (1.0 + c * (1.0 - sig))


def shards(
    inputs, condition, doc_ids, positions, w_qkv, w_out, w_up, bias_up, w_down, bias_down,
    gain_one, gain_two, w_ada, bias_ada, out_grad,
):
    dp_count = lax.axis_size("dp")
    tensor_count = lax.axis_size("tensor")
    per_dp, part, width = inputs.shape
    length = doc_ids.shape[1]
    rows = w_up.shape[0]
    group = Group(dp_count, tensor_count, per_dp)
    blocks = dp_count if group.paired else 1
    d, r = group.d, group.r
    me = jnp.where(group.paired, d, 0).astype(jnp.int32).reshape(1)
    mine = jnp.clip(r - d % 2, 0, per_dp - 1)

    early = jnp.concatenate([w_qkv, w_out.T[None]], axis=0)
    late = jnp.stack([w_up, w_down.T])
    early = group.z_join(early)
    x_parts = group.to_owner(inputs, False)
    late = group.z_join(late)
    g_parts = group.to_owner(out_grad, True)
    qk_pieces = group.gather(early[:2], (1, 2, 0))
    v_pieces = group.gather(early[2:], (2, 1, 0))
    up_pieces = group.gather(late[0], (1, 2, 0))
    down_pieces = group.gather(late[1], (2, 1, 0))

    cond_size = condition.shape[1]
    pad = lambda v: jnp.pad(v, ((0, 0), (0, cond_size - v.shape[1])))
    small = jnp.concatenate(
        [pad(bias_up), pad(bias_down[None]), pad(gain_one[None]), pad(gain_two[None]), condition]
    )
    small = group.small_gather(small)
    whole = lambda i: small[:, i, :rows].reshape(1, width)
    bias_hidden = group.z_join(whole(0)).astype(F32)
    bias_out, gain_1, gain_2 = (whole(i).astype(F32) for i in (1, 2, 3))
    cond_all = small[:, 4:, :].astype(F32)
    act_all = jax.nn.silu(cond_all)
    mod_part = (
        jnp.dot(
            act_all.reshape(-1, cond_size),
            w_ada.astype(F32),
            precision=PRECISE,
            preferred_element_type=F32,
        )
        + bias_ada.astype(F32)
    ).reshape(dp_count, per_dp, -1)
    wanted = jnp.clip(r - jnp.arange(dp_count) % 2, 0, per_dp - 1)
    modulation = group.small_swap(mod_part[jnp.arange(dp_count), wanted])
    shift_1, scale_1, gate_1, shift_2, scale_2, gate_2 = modulation.reshape(6, 1, width)
    mul_1 = gain_1 * (1.0 + scale_1)
    mul_2 = gain_2 * (1.0 + scale_2)

    order = r ^ jnp.arange(tensor_count)
    mixed = lambda v: lax.dynamic_index_in_dim(v, mine, 0, keepdims=False).reshape(
        tensor_count, part
    )[order].reshape(-1)
    docs, places = mixed(doc_ids), mixed(positions)
    doc_row, doc_col = docs[None, :], docs[:, None]
    frequencies = 10000.0 ** (-2.0 * jnp.arange(HEAD // 2, dtype=F32) / HEAD)
    turned = places.astype(F32)[:, None] * frequencies[None, :]
    cosine, sine = jnp.cos(turned), jnp.sin(turned)
    nothing = jnp.zeros_like(sine)
    cos_flat = jnp.concatenate([cosine] * 4, axis=1)
    sin_a = jnp.concatenate([-sine, nothing] * 2, axis=1)
    sin_b = jnp.concatenate([nothing, sine] * 2, axis=1)
    cos_t, sin_t = cosine.T, sine.T

    n_t, q, k, v, q_t, k_t, v_t = qkv(
        me, x_parts, mul_1, shift_1, cos_flat, sin_a, sin_b, qk_pieces, v_pieces
    )
    mix_t, log_sum = attend(q, k, v_t, doc_row, doc_col)
    att, n_two, n_two_t, d_down, d_down_t, d_bias_down = middle(
        me, x_parts, g_parts, mix_t, gate_1, mul_2, shift_2, gate_2, v_pieces
    )
    units = w_up.shape[1] * tensor_count // 2
    feed_args = (me, n_two, n_two_t, d_down, d_down_t, bias_hidden, up_pieces, down_pieces)
    down_a, d_n_a, d_bias_a, *grads_a = feed(*feed_args, 0, None, units)
    down, d_n, d_bias_b, *grads_b = feed(*feed_args, units, (down_a, d_n_a), units)

    up_a, dn_a = group.reduce_two(*grads_a)
    up_b, dn_b = group.reduce_two(*grads_b)

    *out_parts, d_mid, d_mix, d_mix_t, sums = (
        turned_back := turn(
            me, x_parts, g_parts, att, down, d_n, mix_t, gate_1, mul_2, gate_2, bias_out, v_pieces
        )
    )[:8]
    out_sum = group.reduce(*turned_back[8:], (1, 2))
    block_out = group.from_owner(out_parts)

    pairs = q.shape[1] // PAIR
    dq_t, dk_t, dv_t = attend_back(
        q, k, v, d_mix, q_t, k_t, d_mix_t, mix_t, log_sum, doc_row, doc_col, cos_t, sin_t, 0, pairs
    )
    qkv_sum = group.reduce(*qkv_grad(me, n_t, dq_t, dk_t, dv_t, blocks), (2, 1))
    *in_parts, sums_one = first(
        me, x_parts, d_mid, mul_1, dq_t, dk_t, dv_t, qk_pieces, v_pieces
    )
    input_grad = group.from_owner(in_parts)

    grad_qkv = group.z_reduce(qkv_sum)
    grad_out = group.z_reduce(out_sum).T
    grad_up = group.z_reduce(jnp.concatenate([up_a, up_b], axis=-1))
    grad_down = group.z_reduce(jnp.concatenate([dn_a, dn_b], axis=-1)).T

    d_gate_2, norm_2, d_shift_2, d_gate_1 = (sums[n : n + 1] for n in range(4))
    norm_1, d_shift_1 = (sums_one[n : n + 1] for n in range(2))
    d_modulation = jnp.concatenate(
        [d_shift_1, norm_1 * gain_1, d_gate_1, d_shift_2, norm_2 * gain_2, d_gate_2], axis=1
    )
    d_hidden_bias = jnp.concatenate([d_bias_a.reshape(-1), d_bias_b.reshape(-1)])
    sliced = lambda t: t.reshape(dp_count, -1)
    payload = jnp.concatenate(
        [
            sliced(d_modulation),
            sliced(norm_1 * (1.0 + scale_1)),
            sliced(norm_2 * (1.0 + scale_2)),
            sliced(d_bias_down),
            d_hidden_bias.reshape(tensor_count, dp_count, rows)
            .transpose(1, 0, 2)
            .reshape(dp_count, -1),
        ],
        axis=1,
    )
    payload = group.small_swap(payload)
    relative = [payload] + [group.z(payload, k) for k in range(1, tensor_count)]
    mod_width = w_ada.shape[1]
    base = mod_width + 3 * rows
    grad_bias_up = sum(
        jnp.sum(p[:, base + k * rows : base + (k + 1) * rows], axis=0, keepdims=True)
        for k, p in enumerate(relative)
    )
    every = jnp.stack([p[:, :base] for p in relative])[order]
    d_mod_all = every[:, :, :mod_width]
    gains = jnp.sum(every[:, :, mod_width:], axis=(0, 1))
    grad_gain_one, grad_gain_two, grad_bias_down = (
        gains[n * rows : (n + 1) * rows] for n in range(3)
    )
    grad_bias_ada = jnp.sum(d_mod_all, axis=(0, 1))
    grid = np.arange(tensor_count)[:, None] - np.arange(dp_count)[None, :] % 2
    act_used = act_all[np.arange(dp_count)[None, :], np.clip(grid, 0, per_dp - 1)]
    flat_mod = d_mod_all.reshape(tensor_count * dp_count, mod_width)
    grad_ada = lax.dot_general(
        act_used.reshape(tensor_count * dp_count, cond_size),
        flat_mod,
        (((0,), (0,)), ((), ())),
        precision=PRECISE,
        preferred_element_type=F32,
    )
    d_act = lax.dot_general(
        flat_mod,
        w_ada.astype(F32),
        (((1,), (1,)), ((), ())),
        precision=PRECISE,
        preferred_element_type=F32,
    ).reshape(tensor_count, dp_count, cond_size)
    owner = np.arange(per_dp)[None, :] + np.arange(dp_count)[:, None] % 2
    d_act = d_act[owner, np.arange(dp_count)[:, None]]
    d_act = jnp.sum(group.small_swap(d_act), axis=0)
    cond_grad = d_act * silu_slope(condition.astype(F32))
    return (
        block_out,
        input_grad,
        cond_grad,
        grad_qkv,
        grad_out,
        grad_up,
        grad_bias_up,
        grad_down,
        grad_bias_down,
        grad_gain_one,
        grad_gain_two,
        grad_ada,
        grad_bias_ada,
    )


def solution(mesh):
    return jax.shard_map(
        shards,
        mesh=mesh,
        in_specs=(
            P("dp", "tensor", None),
            P("dp", None),
            P("dp", None),
            P("dp", None),
            P(None, "dp", "tensor"),
            P("tensor", "dp"),
            P("dp", "tensor"),
            P("tensor", "dp"),
            P("tensor", "dp"),
            P("dp"),
            P("dp"),
            P("dp"),
            P(None, "dp"),
            P("dp"),
            P("dp", "tensor", None),
        ),
        out_specs=(
            P("dp", "tensor", None),
            P("dp", "tensor", None),
            P("dp", None),
            P(None, "dp", "tensor"),
            P("tensor", "dp"),
            P("dp", "tensor"),
            P("tensor", "dp"),
            P("tensor", "dp"),
            P("dp"),
            P("dp"),
            P("dp"),
            P(None, "dp"),
            P("dp"),
        ),
        check_vma=False,
    )
```

time: 1720 us -> 580 us (0.34)
  waiting for transfers between devices: 954 us -> 187 us
  matrix products: 237 us -> 1.8 us
  blocking collectives: 192 us -> 0 us
  Pallas kernels: 0 us -> 166 us
  local copies, waits for them, and re-layouts: 157 us -> 23.1 us
  starting transfers between devices: 24.2 us -> 157 us
  other arithmetic: 94.9 us -> 37.7 us
  loops' own time: 34.3 us -> 0 us
    reduce_scatter x14 -> x0, waiting for transfers between devices: 525 us -> none  [the longest x3 178 us: micro_step(): lax.psum_scatter(jnp.einsum('lf,df->ld', d_hidden, up_full, preferred_ele...]
    all_gather x21 -> x0, waiting for transfers between devices: 388 us -> none  [the longest x3 116 us: micro_step(): lax.all_gather(d_down.astype(jnp.bfloat16), 'tensor', axis=0, tiled=True)]
    dot_general x80 -> x3, matrix products: 229 us -> 1.8 us  [the longest x1 1.37 us: shards(): lax.dot_general(act_used.reshape(tensor_count * dp_count, cond_size), fla...]
    ppermute x0 -> x116, waiting for transfers between devices: none -> 187 us  [the longest x52 69.3 us: bit(): return lax.ppermute(v, 'dp', [(i, i ^ 1 << b) for i in range(self.dp)])]
    pallas_call x0 -> x9, Pallas kernels: none -> 166 us  [the longest x2 52 us: feed(): pl.pallas_call(partial(feed_kernel, blocks, steps, first), grid=(steps,),...]
    ppermute x0 -> x116, starting transfers between devices: none -> 157 us  [the longest x24 48.4 us: z(): return lax.ppermute(v, 'tensor', [(i, i ^ k) for i in range(self.tensor)])]
    while x3 -> x0, blocking collectives: 75.5 us -> none
    all_gather x6 -> x0, blocking collectives: 66.2 us -> none  [the longest x3 38.9 us: micro_step(): lax.all_gather(w_qkv, 'dp', axis=1, tiled=True)]
  transfers between devices with their start and end apart: 43 -> 116, of which waited for: 36 -> 40; matrix products, arithmetic and copies ran while one was open for 23% -> 9% of each run, Pallas kernels for 0% -> 9%
where the time goes in v1:
time: 580 us; the launch traced here: 575 us
  waiting for transfers between devices  187 us (32%)
  Pallas kernels  166 us (29%)
  starting transfers between devices  157 us (27%)
  other arithmetic  37.7 us (7%)
  local copies, waits for them, and re-layouts  23.1 us (4%)
    ppermute x52, waiting for transfers between devices, bit(): return lax.ppermute(v, 'dp', [(i, i ^ 1 << b) for i in range(self.dp)])  69.3 us
    ppermute x24, waiting for transfers between devices, z(): return lax.ppermute(v, 'tensor', [(i, i ^ k) for i in range(self.tensor)])  54.8 us
    pallas_call x2, Pallas kernels, feed(): pl.pallas_call(partial(feed_kernel, blocks, steps, first), grid=(steps,),...  52 us
    ppermute x24, starting transfers between devices, z(): return lax.ppermute(v, 'tensor', [(i, i ^ k) for i in range(self.tensor)])  48.4 us
    pallas_call x1, Pallas kernels, attend_back(): pl.pallas_call(attend_back_kernel, grid=(count,), in_specs=[flat] * 4 + [...  36 us
    ppermute x52, starting transfers between devices, bit(): return lax.ppermute(v, 'dp', [(i, i ^ 1 << b) for i in range(self.dp)])  31 us
    ppermute x6, starting transfers between devices, to_owner(): parts.append(lax.ppermute(sent, BOTH, pairs))  28.3 us
    ppermute x28, starting transfers between devices, step(): return lax.ppermute(v, 'dp', [(i, i ^ k) for i in range(self.dp)])  24.9 us
  transfers between devices with their start and end apart: 116, of which 40 were waited for; matrix products, arithmetic and copies ran while one was open for 9% of the time, Pallas kernels for 9%

profile of v1, /device:TPU:0, one launch (start us, length us, event | category | flops | bytes accessed | tf_op | source)
XLA Modules:
  0.0 575.2 jit_solution(999241166158614808)
XLA Ops:
  4.6 2.6 collective-permute-start.7
  9.1 2.2 dynamic-slice_bitcast_fusion.3
  11.4 2.7 collective-permute-start.11
  15.9 2.1 collective-permute-done.12
  20.4 2.6 collective-permute-start.38
  29.9 2.2 collective-permute-start.19
  34.9 3.5 collective-permute-start.21
  39.2 3.2 collective-permute-start
  42.4 3.8 collective-permute-done.20
  46.3 1.9 collective-permute-start.22
  48.9 2.4 collective-permute-start.42
  52.1 21.4 %collective-permute-done.22 = bf16[4,96,192]{2,1,0:T(8,128)(2,1)S(1)} collective-permute-done((bf16[4,96,192]{2,1,0:T(8,128)(2,1)}, bf16[4,96,192]{2,1,0:T(8,128)(2,1)S(1)}, u32[]{:S(2)}, u32[]{:S(2)}) %collective-permute-start.22) | collective-permute-done | bytes 147488 | tf_op jit(solution)/shard_map/ppermute | solution.py:603
  73.5 1.9 collective-permute-start.1
  76.7 6.0 %collective-permute-start.3 = (bf16[256,768]{1,0:T(8,128)(2,1)S(1)}, bf16[256,768]{1,0:T(8,128)(2,1)S(1)}, u32[]{:S(2)}, u32[]{:S(2)}) collective-permute-start(bf16[256,768]{1,0:T(8,128)(2,1)S(1)} %get-tuple-element.207), channel_id=1, source_target_pairs={{0,1},{1,0},{3,2},{4,5},{6,7},{7,6},{8,9},{9,8},{11,10},{12,13},{1... | collective-permute-start | bytes 1179656 | tf_op jit(solution)/shard_map/ppermute | solution.py:624
  84.0 14.4 %collective-permute-start.4 = (bf16[256,768]{1,0:T(8,128)(2,1)S(1)}, bf16[256,768]{1,0:T(8,128)(2,1)S(1)}, u32[]{:S(2)}, u32[]{:S(2)}) collective-permute-start(bf16[256,768]{1,0:T(8,128)(2,1)S(1)} %get-tuple-element.209), channel_id=1, source_target_pairs={{0,2},{2,0},{3,1},{4,6},{5,7},{7,5},{8,10},{10,8},{11,9},{12,14},{... | collective-permute-start | bytes 1179656 | tf_op jit(solution)/shard_map/ppermute | solution.py:624
  100.1 16.0 %collective-permute-done.1.refs_2_ = bf16[256,768]{1,0:T(8,128)(2,1)S(1)} collective-permute-done((bf16[256,768]{1,0:T(8,128)(2,1)S(1)}, bf16[256,768]{1,0:T(8,128)(2,1)S(1)}, u32[]{:S(2)}, u32[]{:S(2)}) %collective-permute-start.1) | collective-permute-done | bytes 393248 | tf_op jit(solution)/shard_map/ppermute | solution.py:624
  119.9 8.3 %collective-permute-done.4.refs_6_ = bf16[256,768]{1,0:T(8,128)(2,1)S(1)} collective-permute-done((bf16[256,768]{1,0:T(8,128)(2,1)S(1)}, bf16[256,768]{1,0:T(8,128)(2,1)S(1)}, u32[]{:S(2)}, u32[]{:S(2)}) %collective-permute-start.4) | collective-permute-done | bytes 393248 | tf_op jit(solution)/shard_map/ppermute | solution.py:624
  131.3 1.9 multiply_sine_fusion
  133.2 4.4 collective-permute-done.26.refs_13_
  140.7 1.9 pad_maximum_fusion.8
  144.1 2.7 collective-permute-done.28.refs_15_
  153.1 18.3 %collective-permute-done.53.refs_17_.refs_19_ = bf16[96,3072]{1,0:T(8,128)(2,1)} collective-permute-done((bf16[96,3072]{1,0:T(8,128)(2,1)S(1)}, bf16[96,3072]{1,0:T(8,128)(2,1)}, u32[]{:S(2)}, u32[]{:S(2)}) %collective-permute-start.53) | collective-permute-done | bytes 589856 | tf_op jit(solution)/shard_map/ppermute | solution.py:597
  174.6 12.8 %qkv.1 = (bf16[768,1024]{1,0:T(8,128)(2,1)}, bf16[1024,768]{1,0:T(8,128)(2,1)}, bf16[1024,768]{1,0:T(8,128)(2,1)}, bf16[1024,768]{1,0:T(8,128)(2,1)}, bf16[768,1...) custom-call(s32[1]{0:T(128)} %bitcast.me, bf16[256,768]{1,0:T(8,128)(2,1)} %get-tuple-element.212.refs_0_, ...), custom_call_target="tpu_custom_call" | custom-call | flops 3623878656 | bytes 16000000 | tf_op jit(solution)/shard_map/qkv/pallas_call | solution.py:101
  189.3 22.6 %attend.1 = (bf16[768,1024]{1,0:T(8,128)(2,1)}, f32[6,2,1024]{2,1,0:T(2,128)}) custom-call(bf16[1024,768]{1,0:T(8,128)(2,1)} %get-tuple-element.65.q, bf16[1024,768]{1,0:T(8,128)(2,1)} %get-tuple-element.66.k, bf16[768,1024]{1,0:T(8,128)(2,1)} %get-tuple-element.67.v_t, s32[1,1024]{1,0:T(1,128)} %bitcast.253, s32[1024,1]{1,0:T(8,128)} %bitcast.237), custom_call_target="tpu_custom_call" | custom-call | flops 12884901888 | bytes 8000000 | tf_op jit(solution)/shard_map/attend/pallas_call | solution.py:147
  211.9 9.1 %middle.1 = (f32[1024,768]{1,0:T(8,128)}, bf16[1024,768]{1,0:T(8,128)(2,1)}, bf16[768,1024]{1,0:T(8,128)(2,1)}, bf16[1024,768]{1,0:T(8,128)(2,1)}, bf16[768,1024]{1,0:T(8,128)(2,1)}, /*index=5*/f32[1,768]{1,0:T(1,128)}) custom-call(s32[1]{0:T(128)} %bitcast.me, bf16[256,768]{1,0:T(8,128)(2,1)} %get-tuple-element.212.refs_0_, bf16[256,768]{1,0:T(8,128)(2,1)} %copy-done.2, ...), custom_call_target="tpu_custom_call" | custom-call | flops 1207959552 | bytes 16000000 | tf_op jit(solution)/shard_map/middle/pallas_call | solution.py:215
  223.4 24.9 %feed.2 = (f32[1024,768]{1,0:T(8,128)}, f32[1024,768]{1,0:T(8,128)}, f32[3,1,512]{2,1,0:T(1,128)}, bf16[4,96,1536]{2,1,0:T(8,128)(2,1)}, bf16[4,96,1536]{2,1,0:T...) custom-call(s32[1]{0:T(128)} %bitcast.me, bf16[1024,768]{1,0:T(8,128)(2,1)} %get-tuple-element.70.refs_0_, ...), custom_call_target="tpu_custom_call" | custom-call | flops 14495514624 | bytes 20000000 | tf_op jit(solution)/shard_map/feed/pallas_call | solution.py:320
  248.2 27.1 %feed.3 = (f32[1024,768]{1,0:T(8,128)}, f32[1024,768]{1,0:T(8,128)}, f32[3,1,512]{2,1,0:T(1,128)}, bf16[4,96,1536]{2,1,0:T(8,128)(2,1)}, bf16[4,96,1536]{2,1,0:T...) custom-call(s32[1]{0:T(128)} %bitcast.me, bf16[1024,768]{1,0:T(8,128)(2,1)} %get-tuple-element.70.refs_0_, ...), custom_call_target="tpu_custom_call" | custom-call | flops 14495514624 | bytes 20000000 | tf_op jit(solution)/shard_map/feed/pallas_call | solution.py:320
  276.4 12.9 %turn.1 = (bf16[256,768]{1,0:T(8,128)(2,1)}, bf16[256,768]{1,0:T(8,128)(2,1)}, bf16[256,768]{1,0:T(8,128)(2,1)}, bf16[256,768]{1,0:T(8,128)(2,1)}, f32[1024,768]...) custom-call(s32[1]{0:T(128)} %bitcast.me, ...), custom_call_target="tpu_custom_call" | custom-call | flops 2415919104 | bytes 24000000 | tf_op jit(solution)/shard_map/turn/pallas_call | solution.py:401
  289.2 36.0 %attend_back.1 = (bf16[768,1024]{1,0:T(8,128)(2,1)}, bf16[768,1024]{1,0:T(8,128)(2,1)}, bf16[768,1024]{1,0:T(8,128)(2,1)}) custom-call(bf16[1024,768]{1,0:T(8,128)(2,1)} %get-tuple-element.65.q, bf16[1024,768]{1,0:T(8,128)(2,1)} %get-tuple-element.66.k, bf16[1024,768]{1,0:T(8,128)(2,1)} %get-tuple-element.83.v, bf16[1024,768]{1,0:T(8,128)(2,1)} %get-tuple-element.84.d_mix, ...), custom_call_target="tpu_custom_call" | custom-call | flops 22548578304 | bytes 14000000 | tf_op jit(solution)/shard_map/attend_back/pallas_call | solution.py:474
  325.3 12.3 %first.1 = (bf16[256,768]{1,0:T(8,128)(2,1)}, bf16[256,768]{1,0:T(8,128)(2,1)}, bf16[256,768]{1,0:T(8,128)(2,1)}, bf16[256,768]{1,0:T(8,128)(2,1)}, f32[2,768]{1,0:T(2,128)}) custom-call(s32[1]{0:T(128)} %bitcast.me, bf16[256,768]{1,0:T(8,128)(2,1)} %get-tuple-element.212.refs_0_, bf16[256,768]{1,0:T(8,128)(2,1)} %copy-done.2, bf16[256,768]{1,0:T(8,128)(2,1)} %copy-done.3, ...), custom_call_target="tpu_custom_call" | custom-call | flops 3623878656 | bytes 20000000 | tf_op jit(solution)/shard_map/first/pallas_call | solution.py:543
  347.9 8.7 %qkv_grad.1 = (bf16[4,3,96,768]{3,2,1,0:T(8,128)(2,1)}, bf16[4,3,96,768]{3,2,1,0:T(8,128)(2,1)}) custom-call(s32[1]{0:T(128)} %bitcast.me, bf16[768,1024]{1,0:T(8,128)(2,1)} %get-tuple-element.101.refs_0_, bf16[768,1024]{1,0:T(8,128)(2,1)} %get-tuple-element.89.refs_6_.refs_1_, bf16[768,1024]{1,0:T(8,128)(2,1)} %get-tuple-element.90.refs_7_.refs_2_, ...), custom_call_target="tpu_custom_call" | custom-call | flops 3623878656 | bytes 10000000 | tf_op jit(solution)/shard_map/qkv_grad/pallas_call | solution.py:578
  357.3 7.7 %collective-permute-start.60 = (bf16[256,768]{1,0:T(8,128)(2,1)}, bf16[256,768]{1,0:T(8,128)(2,1)S(1)}, u32[]{:S(2)}, u32[]{:S(2)}) collective-permute-start(bf16[256,768]{1,0:T(8,128)(2,1)} %get-tuple-element.93), channel_id=1, source_target_pairs={{0,1},{1,0},{2,3},{5,4},{6,7},{7,6},{8,9},{9,8},{10,11},{13,12},{1... | collective-permute-start | bytes 1179656 | tf_op jit(solution)/shard_map/ppermute | solution.py:636
  365.1 2.3 collective-permute-start.61
  368.3 7.4 %collective-permute-done.72 = f32[8,1248]{1,0:T(8,128)S(1)} collective-permute-done((f32[8,1248]{1,0:T(8,128)S(1)}, f32[8,1248]{1,0:T(8,128)S(1)}, u32[]{:S(2)}, u32[]{:S(2)}) %collective-permute-start.72) | collective-permute-done | bytes 39968 | tf_op jit(solution)/shard_map/ppermute | solution.py:603
  375.7 7.2 %collective-permute-start.71 = (f32[8,1248]{1,0:T(8,128)S(1)}, f32[8,1248]{1,0:T(8,128)S(1)}, u32[]{:S(2)}, u32[]{:S(2)}) collective-permute-start(f32[8,1248]{1,0:T(8,128)S(1)} %broadcast_select_fusion), channel_id=1, source_target_pairs={{0,2},{1,3},{2,0},{3,1},{4,6},{5,7},{6,4},{7,5},{8,10},{9,11},{10,... | collective-permute-start | bytes 119816 | tf_op jit(solution)/shard_map/ppermute | solution.py:603
  382.9 2.1 collective-permute-done.71
  385.0 3.8 collective-permute-start.70
  388.8 2.0 collective-permute-done.70
  397.4 2.6 collective-permute-done.74
  400.0 3.0 collective-permute-done.75
  404.5 2.1 collective-permute-done.76
  406.6 3.0 collective-permute-done.77
  409.6 2.0 collective-permute-start.78
  411.5 2.5 collective-permute-done.78
  414.1 3.9 collective-permute-done.79
  418.0 3.4 collective-permute-start.62
  422.7 2.4 collective-permute-start.57
  425.1 2.8 collective-permute-start.58
  427.9 5.6 collective-permute-start.59
  437.7 15.8 %collective-permute-done.58 = bf16[256,768]{1,0:T(8,128)(2,1)S(1)} collective-permute-done((bf16[256,768]{1,0:T(8,128)(2,1)}, bf16[256,768]{1,0:T(8,128)(2,1)S(1)}, u32[]{:S(2)}, u32[]{:S(2)}) %collective-permute-start.58) | collective-permute-done | bytes 393248 | tf_op jit(solution)/shard_map/ppermute | solution.py:636
  456.6 2.3 collective-permute-done.88
  460.2 8.6 %collective-permute-start.91 = (bf16[96,192]{1,0:T(8,128)(2,1)S(1)}, bf16[96,192]{1,0:T(8,128)(2,1)S(1)}, u32[]{:S(2)}, u32[]{:S(2)}) collective-permute-start(bf16[96,192]{1,0:T(8,128)(2,1)S(1)} %get-tuple-element.225), channel_id=1, source_target_pairs={{0,1},{1,0},{2,3},{3,2},{4,5},{5,4},{6,7},{7,6},{8,9},{9,8},{10,11... | collective-permute-start | bytes 110600 | tf_op jit(solution)/shard_map/ppermute | solution.py:603
  468.9 2.4 collective-permute-start.93
  485.0 1.9 collective-permute-done.112
  489.1 10.5 %collective-permute-done.107 = bf16[96,1536]{1,0:T(8,128)(2,1)S(1)} collective-permute-done((bf16[96,1536]{1,0:T(8,128)(2,1)S(1)}, bf16[96,1536]{1,0:T(8,128)(2,1)S(1)}, u32[]{:S(2)}, u32[]{:S(2)}) %collective-permute-start.107) | collective-permute-done | bytes 294944 | tf_op jit(solution)/shard_map/ppermute | solution.py:597
  503.9 10.1 %collective-permute-done.96 = bf16[96,1536]{1,0:T(8,128)(2,1)S(1)} collective-permute-done((bf16[96,1536]{1,0:T(8,128)(2,1)S(1)}, bf16[96,1536]{1,0:T(8,128)(2,1)S(1)}, u32[]{:S(2)}, u32[]{:S(2)}) %collective-permute-start.96) | collective-permute-done | bytes 294944 | tf_op jit(solution)/shard_map/ppermute | solution.py:597
  518.5 5.4 collective-permute-done.108
  527.1 6.8 %collective-permute-done.113 = bf16[96,1536]{1,0:T(8,128)(2,1)S(1)} collective-permute-done((bf16[96,1536]{1,0:T(8,128)(2,1)S(1)}, bf16[96,1536]{1,0:T(8,128)(2,1)S(1)}, u32[]{:S(2)}, u32[]{:S(2)}) %collective-permute-start.113) | collective-permute-done | bytes 294944 | tf_op jit(solution)/shard_map/ppermute | solution.py:597
  543.1 3.9 collective-permute-done.82
  548.2 4.0 collective-permute-done.114
  552.8 4.6 collective-permute-start.98
  558.7 3.5 collective-permute-start.85
  563.6 2.7 collective-permute-done.98
  568.4 5.6 collective-permute-done.85
  (462 shorter events, 126.1 us)
Async XLA Ops:
  34.2 12.1 %collective-permute-start.20 = (bf16[4,96,192]{2,1,0:T(8,128)(2,1)}, bf16[4,96,192]{2,1,0:T(8,128)(2,1)}, u32[]{:S(2)}, u32[]{:S(2)}) collective-permute-start(bf16[4,96,192]{2,1,0:T(8,128)(2,1)} %pad_maximum_fusion.10), channel_id=1, source_target_pairs={{0,1},{1,0},{2,3},{3,2},{4,5},{5,4},{6,7},{7,6},{8,9},{9,8},{10,11... | collective-permute-start | bytes 442376 | tf_op jit(solution)/shard_map/ppermute | solution.py:603
  34.9 13.9 %collective-permute-start.21 = (bf16[4,96,192]{2,1,0:T(8,128)(2,1)}, bf16[4,96,192]{2,1,0:T(8,128)(2,1)}, u32[]{:S(2)}, u32[]{:S(2)}) collective-permute-start(bf16[4,96,192]{2,1,0:T(8,128)(2,1)} %pad_maximum_fusion.10), channel_id=1, source_target_pairs={{0,2},{1,3},{2,0},{3,1},{4,6},{5,7},{6,4},{7,5},{8,10},{9,11},{10,... | collective-permute-start | bytes 442376 | tf_op jit(solution)/shard_map/ppermute | solution.py:603
  38.4 37.0 %collective-permute-start.40 = (bf16[2,96,768]{2,1,0:T(8,128)(2,1)}, bf16[2,96,768]{2,1,0:T(8,128)(2,1)}, u32[]{:S(2)}, u32[]{:S(2)}) collective-permute-start(bf16[2,96,768]{2,1,0:T(8,128)(2,1)} %pad_maximum_fusion.9), channel_id=1, source_target_pairs={{0,1},{1,0},{2,3},{3,2},{4,5},{5,4},{6,7},{7,6},{8,9},{9,8},{10,11... | collective-permute-start | bytes 884744 | tf_op jit(solution)/shard_map/ppermute | solution.py:603
  38.5 38.2 %collective-permute-start.41 = (bf16[2,96,768]{2,1,0:T(8,128)(2,1)}, bf16[2,96,768]{2,1,0:T(8,128)(2,1)}, u32[]{:S(2)}, u32[]{:S(2)}) collective-permute-start(bf16[2,96,768]{2,1,0:T(8,128)(2,1)} %pad_maximum_fusion.9), channel_id=1, source_target_pairs={{0,2},{1,3},{2,0},{3,1},{4,6},{5,7},{6,4},{7,5},{8,10},{9,11},{10,... | collective-permute-start | bytes 884744 | tf_op jit(solution)/shard_map/ppermute | solution.py:603
  39.2 59.3 %collective-permute-start = (bf16[256,768]{1,0:T(8,128)(2,1)S(1)}, bf16[256,768]{1,0:T(8,128)(2,1)S(1)}, u32[]{:S(2)}, u32[]{:S(2)}) collective-permute-start(bf16[256,768]{1,0:T(8,128)(2,1)S(1)} %get-tuple-element.211), channel_id=1, source_target_pairs={{0,1},{1,0},{3,2},{4,5},{6,7},{7,6},{8,9},{9,8},{11,10},{12,13},{1... | collective-permute-start | bytes 1179656 | tf_op jit(solution)/shard_map/ppermute | solution.py:624
  46.3 27.2 %collective-permute-start.22 = (bf16[4,96,192]{2,1,0:T(8,128)(2,1)}, bf16[4,96,192]{2,1,0:T(8,128)(2,1)S(1)}, u32[]{:S(2)}, u32[]{:S(2)}) collective-permute-start(bf16[4,96,192]{2,1,0:T(8,128)(2,1)} %pad_maximum_fusion.10), channel_id=1, source_target_pairs={{0,3},{1,2},{2,1},{3,0},{4,7},{5,6},{6,5},{7,4},{8,11},{9,10},{10,... | collective-permute-start | bytes 442376 | tf_op jit(solution)/shard_map/ppermute | solution.py:603
  48.9 35.2 %collective-permute-start.42 = (bf16[2,96,768]{2,1,0:T(8,128)(2,1)}, bf16[2,96,768]{2,1,0:T(8,128)(2,1)S(1)}, u32[]{:S(2)}, u32[]{:S(2)}) collective-permute-start(bf16[2,96,768]{2,1,0:T(8,128)(2,1)} %pad_maximum_fusion.9), channel_id=1, source_target_pairs={{0,3},{1,2},{2,1},{3,0},{4,7},{5,6},{6,5},{7,4},{8,11},{9,10},{10,... | collective-permute-start | bytes 884744 | tf_op jit(solution)/shard_map/ppermute | solution.py:603
  73.5 42.6 %collective-permute-start.1 = (bf16[256,768]{1,0:T(8,128)(2,1)S(1)}, bf16[256,768]{1,0:T(8,128)(2,1)S(1)}, u32[]{:S(2)}, u32[]{:S(2)}) collective-permute-start(bf16[256,768]{1,0:T(8,128)(2,1)S(1)} %get-tuple-element.213), channel_id=1, source_target_pairs={{0,2},{2,0},{3,1},{4,6},{5,7},{7,5},{8,10},{10,8},{11,9},{12,14},{... | collective-permute-start | bytes 1179656 | tf_op jit(solution)/shard_map/ppermute | solution.py:624
  75.4 41.2 %collective-permute-start.2 = (bf16[256,768]{1,0:T(8,128)(2,1)S(1)}, bf16[256,768]{1,0:T(8,128)(2,1)S(1)}, u32[]{:S(2)}, u32[]{:S(2)}) collective-permute-start(bf16[256,768]{1,0:T(8,128)(2,1)S(1)} %get-tuple-element.210), channel_id=1, source_target_pairs={{1,2},{2,1},{3,0},{4,7},{5,6},{6,5},{9,10},{10,9},{11,8},{12,15},{... | collective-permute-start | bytes 1179656 | tf_op jit(solution)/shard_map/ppermute | solution.py:624
  76.7 40.5 %collective-permute-start.3 = (bf16[256,768]{1,0:T(8,128)(2,1)S(1)}, bf16[256,768]{1,0:T(8,128)(2,1)S(1)}, u32[]{:S(2)}, u32[]{:S(2)}) collective-permute-start(bf16[256,768]{1,0:T(8,128)(2,1)S(1)} %get-tuple-element.207), channel_id=1, source_target_pairs={{0,1},{1,0},{3,2},{4,5},{6,7},{7,6},{8,9},{9,8},{11,10},{12,13},{1... | collective-permute-start | bytes 1179656 | tf_op jit(solution)/shard_map/ppermute | solution.py:624
  84.0 44.1 %collective-permute-start.4 = (bf16[256,768]{1,0:T(8,128)(2,1)S(1)}, bf16[256,768]{1,0:T(8,128)(2,1)S(1)}, u32[]{:S(2)}, u32[]{:S(2)}) collective-permute-start(bf16[256,768]{1,0:T(8,128)(2,1)S(1)} %get-tuple-element.209), channel_id=1, source_target_pairs={{0,2},{2,0},{3,1},{4,6},{5,7},{7,5},{8,10},{10,8},{11,9},{12,14},{... | collective-permute-start | bytes 1179656 | tf_op jit(solution)/shard_map/ppermute | solution.py:624
  98.5 29.7 %collective-permute-start.5 = (bf16[256,768]{1,0:T(8,128)(2,1)S(1)}, bf16[256,768]{1,0:T(8,128)(2,1)S(1)}, u32[]{:S(2)}, u32[]{:S(2)}) collective-permute-start(bf16[256,768]{1,0:T(8,128)(2,1)S(1)} %get-tuple-element.206), channel_id=1, source_target_pairs={{1,2},{2,1},{3,0},{4,7},{5,6},{6,5},{9,10},{10,9},{11,8},{12,15},{... | collective-permute-start | bytes 1179656 | tf_op jit(solution)/shard_map/ppermute | solution.py:624
  116.1 12.6 %collective-permute-start.33 = (bf16[2,96,768]{2,1,0:T(8,128)(2,1)S(1)}, bf16[2,96,768]{2,1,0:T(8,128)(2,1)S(1)}, u32[]{:S(2)}, u32[]{:S(2)}) collective-permute-start(bf16[2,96,768]{2,1,0:T(8,128)(2,1)S(1)} %get-tuple-element.214.refs_17_.refs_13_.refs_16_), channel_id=1, source_target_pairs={{0,16},{4,20},{8,24},{12,28},{16,0},{20,4},{24,8},{28,12},{1,17},{... | collective-permute-start | bytes 884744 | tf_op jit(solution)/shard_map/ppermute | solution.py:597
  116.6 12.3 %collective-permute-start.31 = (bf16[2,96,768]{2,1,0:T(8,128)(2,1)S(1)}, bf16[2,96,768]{2,1,0:T(8,128)(2,1)S(1)}, u32[]{:S(2)}, u32[]{:S(2)}) collective-permute-start(bf16[2,96,768]{2,1,0:T(8,128)(2,1)S(1)} %get-tuple-element.214.refs_17_.refs_13_.refs_16_), channel_id=1, source_target_pairs={{0,8},{4,12},{8,0},{12,4},{16,24},{20,28},{24,16},{28,20},{1,9},{5... | collective-permute-start | bytes 884744 | tf_op jit(solution)/shard_map/ppermute | solution.py:597
  117.2 12.3 %collective-permute-start.24 = (bf16[2,96,768]{2,1,0:T(8,128)(2,1)S(1)}, bf16[2,96,768]{2,1,0:T(8,128)(2,1)S(1)}, u32[]{:S(2)}, u32[]{:S(2)}) collective-permute-start(bf16[2,96,768]{2,1,0:T(8,128)(2,1)S(1)} %get-tuple-element.215.refs_9_), channel_id=1, source_target_pairs={{0,8},{4,12},{8,0},{12,4},{16,24},{20,28},{24,16},{28,20},{1,9},{5... | collective-permute-start | bytes 884744 | tf_op jit(solution)/shard_map/ppermute | solution.py:597
  129.8 21.8 %collective-permute-start.44 = (bf16[96,3072]{1,0:T(8,128)(2,1)S(1)}, bf16[96,3072]{1,0:T(8,128)(2,1)}, u32[]{:S(2)}, u32[]{:S(2)}) collective-permute-start(bf16[96,3072]{1,0:T(8,128)(2,1)S(1)} %get-tuple-element.205.refs_5_.refs_7_), channel_id=1, source_target_pairs={{0,8},{4,12},{8,0},{12,4},{16,24},{20,28},{24,16},{28,20},{1,9},{5... | collective-permute-start | bytes 1769480 | tf_op jit(solution)/shard_map/ppermute | solution.py:597
  138.9 12.3 %collective-permute-start.27 = (bf16[2,96,768]{2,1,0:T(8,128)(2,1)S(1)}, bf16[2,96,768]{2,1,0:T(8,128)(2,1)}, u32[]{:S(2)}, u32[]{:S(2)}) collective-permute-start(bf16[2,96,768]{2,1,0:T(8,128)(2,1)S(1)} %collective-permute-done.26.refs_13_), channel_id=1, source_target_pairs={{0,4},{4,0},{8,12},{12,8},{16,20},{20,16},{24,28},{28,24},{1,5},{5... | collective-permute-start | bytes 884744 | tf_op jit(solution)/shard_map/ppermute | solution.py:597
  142.5 28.9 %collective-permute-start.46 = (bf16[96,3072]{1,0:T(8,128)(2,1)S(1)}, bf16[96,3072]{1,0:T(8,128)(2,1)}, u32[]{:S(2)}, u32[]{:S(2)}) collective-permute-start(bf16[96,3072]{1,0:T(8,128)(2,1)S(1)} %get-tuple-element.205.refs_5_.refs_7_), channel_id=1, source_target_pairs={{0,16},{4,20},{8,24},{12,28},{16,0},{20,4},{24,8},{28,12},{1,17},{... | collective-permute-start | bytes 1769480 | tf_op jit(solution)/shard_map/ppermute | solution.py:597
  146.8 24.6 %collective-permute-start.53 = (bf16[96,3072]{1,0:T(8,128)(2,1)S(1)}, bf16[96,3072]{1,0:T(8,128)(2,1)}, u32[]{:S(2)}, u32[]{:S(2)}) collective-permute-start(bf16[96,3072]{1,0:T(8,128)(2,1)S(1)} %get-tuple-element.204.refs_13_.refs_15_), channel_id=1, source_target_pairs={{0,16},{4,20},{8,24},{12,28},{16,0},{20,4},{24,8},{28,12},{1,17},{... | collective-permute-start | bytes 1769480 | tf_op jit(solution)/shard_map/ppermute | solution.py:597
  146.8 25.1 %collective-permute-start.51 = (bf16[96,3072]{1,0:T(8,128)(2,1)S(1)}, bf16[96,3072]{1,0:T(8,128)(2,1)}, u32[]{:S(2)}, u32[]{:S(2)}) collective-permute-start(bf16[96,3072]{1,0:T(8,128)(2,1)S(1)} %get-tuple-element.204.refs_13_.refs_15_), channel_id=1, source_target_pairs={{0,8},{4,12},{8,0},{12,4},{16,24},{20,28},{24,16},{28,20},{1,9},{5... | collective-permute-start | bytes 1769480 | tf_op jit(solution)/shard_map/ppermute | solution.py:597
  151.1 21.6 %collective-permute-start.36 = (bf16[2,96,768]{2,1,0:T(8,128)(2,1)S(1)}, bf16[2,96,768]{2,1,0:T(8,128)(2,1)S(1)}, u32[]{:S(2)}, u32[]{:S(2)}) collective-permute-start(bf16[2,96,768]{2,1,0:T(8,128)(2,1)S(1)} %collective-permute-done.35.refs_23_.refs_19_.refs_22_), channel_id=1, source_target_pairs={{0,4},{4,0},{8,12},{12,8},{16,20},{20,16},{24,28},{28,24},{1,5},{5... | collective-permute-start | bytes 884744 | tf_op jit(solution)/shard_map/ppermute | solution.py:597
  151.6 21.1 %collective-permute-start.29 = (bf16[2,96,768]{2,1,0:T(8,128)(2,1)S(1)}, bf16[2,96,768]{2,1,0:T(8,128)(2,1)S(1)}, u32[]{:S(2)}, u32[]{:S(2)}) collective-permute-start(bf16[2,96,768]{2,1,0:T(8,128)(2,1)S(1)} %collective-permute-done.28.refs_15_), channel_id=1, source_target_pairs={{0,4},{4,0},{8,12},{12,8},{16,20},{20,16},{24,28},{28,24},{1,5},{5... | collective-permute-start | bytes 884744 | tf_op jit(solution)/shard_map/ppermute | solution.py:597
  171.4 15.9 %collective-permute-start.43 = (bf16[96,3072]{1,0:T(8,128)(2,1)S(1)}, bf16[96,3072]{1,0:T(8,128)(2,1)S(1)}, u32[]{:S(2)}, u32[]{:S(2)}) collective-permute-start(bf16[96,3072]{1,0:T(8,128)(2,1)S(1)} %get-tuple-element.205.refs_5_.refs_7_), channel_id=1, source_target_pairs={{0,4},{4,0},{8,12},{12,8},{16,20},{20,16},{24,28},{28,24},{1,5},{5... | collective-permute-start | bytes 1769480 | tf_op jit(solution)/shard_map/ppermute | solution.py:597
  171.5 16.2 %collective-permute-start.50 = (bf16[96,3072]{1,0:T(8,128)(2,1)S(1)}, bf16[96,3072]{1,0:T(8,128)(2,1)S(1)}, u32[]{:S(2)}, u32[]{:S(2)}) collective-permute-start(bf16[96,3072]{1,0:T(8,128)(2,1)S(1)} %get-tuple-element.204.refs_13_.refs_15_), channel_id=1, source_target_pairs={{0,4},{4,0},{8,12},{12,8},{16,20},{20,16},{24,28},{28,24},{1,5},{5... | collective-permute-start | bytes 1769480 | tf_op jit(solution)/shard_map/ppermute | solution.py:597
  172.0 16.0 %collective-permute-start.48 = (bf16[96,3072]{1,0:T(8,128)(2,1)}, bf16[96,3072]{1,0:T(8,128)(2,1)}, u32[]{:S(2)}, u32[]{:S(2)}) collective-permute-start(bf16[96,3072]{1,0:T(8,128)(2,1)} %collective-permute-done.44.refs_7_.refs_9_), channel_id=1, source_target_pairs={{0,16},{4,20},{8,24},{12,28},{16,0},{20,4},{24,8},{28,12},{1,17},{... | collective-permute-start | bytes 1769480 | tf_op jit(solution)/shard_map/ppermute | solution.py:597
  172.7 16.1 %collective-permute-start.45 = (bf16[96,3072]{1,0:T(8,128)(2,1)}, bf16[96,3072]{1,0:T(8,128)(2,1)S(1)}, u32[]{:S(2)}, u32[]{:S(2)}) collective-permute-start(bf16[96,3072]{1,0:T(8,128)(2,1)} %collective-permute-done.44.refs_7_.refs_9_), channel_id=1, source_target_pairs={{0,4},{4,0},{8,12},{12,8},{16,20},{20,16},{24,28},{28,24},{1,5},{5... | collective-permute-start | bytes 1769480 | tf_op jit(solution)/shard_map/ppermute | solution.py:597
  172.7 16.0 %collective-permute-start.55 = (bf16[96,3072]{1,0:T(8,128)(2,1)}, bf16[96,3072]{1,0:T(8,128)(2,1)}, u32[]{:S(2)}, u32[]{:S(2)}) collective-permute-start(bf16[96,3072]{1,0:T(8,128)(2,1)} %collective-permute-done.53.refs_17_.refs_19_), channel_id=1, source_target_pairs={{0,8},{4,12},{8,0},{12,4},{16,24},{20,28},{24,16},{28,20},{1,9},{5... | collective-permute-start | bytes 1769480 | tf_op jit(solution)/shard_map/ppermute | solution.py:597
  187.4 34.4 %collective-permute-start.54 = (bf16[96,3072]{1,0:T(8,128)(2,1)}, bf16[96,3072]{1,0:T(8,128)(2,1)S(1)}, u32[]{:S(2)}, u32[]{:S(2)}) collective-permute-start(bf16[96,3072]{1,0:T(8,128)(2,1)} %collective-permute-done.53.refs_17_.refs_19_), channel_id=1, source_target_pairs={{0,4},{4,0},{8,12},{12,8},{16,20},{20,16},{24,28},{28,24},{1,5},{5... | collective-permute-start | bytes 1769480 | tf_op jit(solution)/shard_map/ppermute | solution.py:597
  187.6 34.2 %collective-permute-start.47 = (bf16[96,3072]{1,0:T(8,128)(2,1)}, bf16[96,3072]{1,0:T(8,128)(2,1)S(1)}, u32[]{:S(2)}, u32[]{:S(2)}) collective-permute-start(bf16[96,3072]{1,0:T(8,128)(2,1)} %collective-permute-done.46.refs_9_.refs_11_), channel_id=1, source_target_pairs={{0,4},{4,0},{8,12},{12,8},{16,20},{20,16},{24,28},{28,24},{1,5},{5... | collective-permute-start | bytes 1769480 | tf_op jit(solution)/shard_map/ppermute | solution.py:597
  188.0 33.8 %collective-permute-start.52 = (bf16[96,3072]{1,0:T(8,128)(2,1)}, bf16[96,3072]{1,0:T(8,128)(2,1)S(1)}, u32[]{:S(2)}, u32[]{:S(2)}) collective-permute-start(bf16[96,3072]{1,0:T(8,128)(2,1)} %collective-permute-done.51.refs_15_.refs_17_), channel_id=1, source_target_pairs={{0,4},{4,0},{8,12},{12,8},{16,20},{20,16},{24,28},{28,24},{1,5},{5... | collective-permute-start | bytes 1769480 | tf_op jit(solution)/shard_map/ppermute | solution.py:597
  188.8 33.1 %collective-permute-start.49 = (bf16[96,3072]{1,0:T(8,128)(2,1)}, bf16[96,3072]{1,0:T(8,128)(2,1)S(1)}, u32[]{:S(2)}, u32[]{:S(2)}) collective-permute-start(bf16[96,3072]{1,0:T(8,128)(2,1)} %collective-permute-done.48.refs_11_.refs_13_), channel_id=1, source_target_pairs={{0,4},{4,0},{8,12},{12,8},{16,20},{20,16},{24,28},{28,24},{1,5},{5... | collective-permute-start | bytes 1769480 | tf_op jit(solution)/shard_map/ppermute | solution.py:597
  188.8 33.1 %collective-permute-start.56 = (bf16[96,3072]{1,0:T(8,128)(2,1)}, bf16[96,3072]{1,0:T(8,128)(2,1)S(1)}, u32[]{:S(2)}, u32[]{:S(2)}) collective-permute-start(bf16[96,3072]{1,0:T(8,128)(2,1)} %collective-permute-done.55.refs_19_.refs_21_), channel_id=1, source_target_pairs={{0,4},{4,0},{8,12},{12,8},{16,20},{20,16},{24,28},{28,24},{1,5},{5... | collective-permute-start | bytes 1769480 | tf_op jit(solution)/shard_map/ppermute | solution.py:597
  342.8 13.8 %collective-permute-start.65 = (f32[1248]{0:T(1024)S(1)}, f32[1248]{0:T(1024)S(1)}, u32[]{:S(2)}, u32[]{:S(2)}) collective-permute-start(f32[1248]{0:T(1024)S(1)} %get-tuple-element.170), channel_id=1, source_target_pairs={{0,12},{4,8},{8,4},{12,0},{16,28},{20,24},{24,20},{28,16},{1,13},{... | collective-permute-start | bytes 14984 | tf_op jit(solution)/shard_map/ppermute | solution.py:600
  343.5 13.7 %collective-permute-start.66 = (f32[1248]{0:T(1024)S(1)}, f32[1248]{0:T(1024)S(1)}, u32[]{:S(2)}, u32[]{:S(2)}) collective-permute-start(f32[1248]{0:T(1024)S(1)} %get-tuple-element.169), channel_id=1, source_target_pairs={{0,16},{4,20},{8,24},{12,28},{16,0},{20,4},{24,8},{28,12},{1,17},{... | collective-permute-start | bytes 14984 | tf_op jit(solution)/shard_map/ppermute | solution.py:600
  344.8 12.5 %collective-permute-start.67 = (f32[1248]{0:T(1024)S(1)}, f32[1248]{0:T(1024)S(1)}, u32[]{:S(2)}, u32[]{:S(2)}) collective-permute-start(f32[1248]{0:T(1024)S(1)} %get-tuple-element.168), channel_id=1, source_target_pairs={{0,20},{4,16},{8,28},{12,24},{16,4},{20,0},{24,12},{28,8},{1,21},{... | collective-permute-start | bytes 14984 | tf_op jit(solution)/shard_map/ppermute | solution.py:600
  345.4 19.7 %collective-permute-start.68 = (f32[1248]{0:T(1024)S(1)}, f32[1248]{0:T(1024)S(1)}, u32[]{:S(2)}, u32[]{:S(2)}) collective-permute-start(f32[1248]{0:T(1024)S(1)} %get-tuple-element.167), channel_id=1, source_target_pairs={{0,24},{4,28},{8,16},{12,20},{16,8},{20,12},{24,0},{28,4},{1,25},{... | collective-permute-start | bytes 14984 | tf_op jit(solution)/shard_map/ppermute | solution.py:600
  347.1 20.3 %collective-permute-start.69 = (f32[1248]{0:T(1024)S(1)}, f32[1248]{0:T(1024)S(1)}, u32[]{:S(2)}, u32[]{:S(2)}) collective-permute-start(f32[1248]{0:T(1024)S(1)} %get-tuple-element.166), channel_id=1, source_target_pairs={{0,28},{4,24},{8,20},{12,16},{16,12},{20,8},{24,4},{28,0},{1,29},{... | collective-permute-start | bytes 14984 | tf_op jit(solution)/shard_map/ppermute | solution.py:600
  356.6 119.0 %collective-permute-start.110 = (bf16[4,96,1536]{2,1,0:T(8,128)(2,1)}, bf16[4,96,1536]{2,1,0:T(8,128)(2,1)}, u32[]{:S(2)}, u32[]{:S(2)}) collective-permute-start(bf16[4,96,1536]{2,1,0:T(8,128)(2,1)} %get-tuple-element.113), channel_id=1, source_target_pairs={{0,4},{4,0},{8,12},{12,8},{16,20},{20,16},{24,28},{28,24},{1,5},{5... | collective-permute-start | bytes 3538952 | tf_op jit(solution)/shard_map/ppermute | solution.py:597
  357.2 76.6 %collective-permute-start.87 = (bf16[4,96,768]{2,1,0:T(8,128)(2,1)S(1)}, bf16[4,96,768]{2,1,0:T(8,128)(2,1)S(1)}, u32[]{:S(2)}, u32[]{:S(2)}) collective-permute-start(bf16[4,96,768]{2,1,0:T(8,128)(2,1)S(1)} %copy-done.44), channel_id=1, source_target_pairs={{0,4},{4,0},{8,12},{12,8},{16,20},{20,16},{24,28},{28,24},{1,5},{5... | collective-permute-start | bytes 1769480 | tf_op jit(solution)/shard_map/ppermute | solution.py:597
  357.3 65.3 %collective-permute-start.60 = (bf16[256,768]{1,0:T(8,128)(2,1)}, bf16[256,768]{1,0:T(8,128)(2,1)S(1)}, u32[]{:S(2)}, u32[]{:S(2)}) collective-permute-start(bf16[256,768]{1,0:T(8,128)(2,1)} %get-tuple-element.93), channel_id=1, source_target_pairs={{0,1},{1,0},{2,3},{5,4},{6,7},{7,6},{8,9},{9,8},{10,11},{13,12},{1... | collective-permute-start | bytes 1179656 | tf_op jit(solution)/shard_map/ppermute | solution.py:636
  365.1 60.0 %collective-permute-start.61 = (bf16[256,768]{1,0:T(8,128)(2,1)}, bf16[256,768]{1,0:T(8,128)(2,1)S(1)}, u32[]{:S(2)}, u32[]{:S(2)}) collective-permute-start(bf16[256,768]{1,0:T(8,128)(2,1)} %get-tuple-element.94), channel_id=1, source_target_pairs={{0,2},{1,3},{2,0},{5,7},{6,4},{7,5},{8,10},{9,11},{10,8},{13,15},{... | collective-permute-start | bytes 1179656 | tf_op jit(solution)/shard_map/ppermute | solution.py:636
  422.7 14.0 %collective-permute-start.57 = (bf16[256,768]{1,0:T(8,128)(2,1)}, bf16[256,768]{1,0:T(8,128)(2,1)S(1)}, u32[]{:S(2)}, u32[]{:S(2)}) collective-permute-start(bf16[256,768]{1,0:T(8,128)(2,1)} %get-tuple-element.79), channel_id=1, source_target_pairs={{0,1},{1,0},{2,3},{5,4},{6,7},{7,6},{8,9},{9,8},{10,11},{13,12},{1... | collective-permute-start | bytes 1179656 | tf_op jit(solution)/shard_map/ppermute | solution.py:636
  425.1 28.4 %collective-permute-start.58 = (bf16[256,768]{1,0:T(8,128)(2,1)}, bf16[256,768]{1,0:T(8,128)(2,1)S(1)}, u32[]{:S(2)}, u32[]{:S(2)}) collective-permute-start(bf16[256,768]{1,0:T(8,128)(2,1)} %get-tuple-element.80), channel_id=1, source_target_pairs={{0,2},{1,3},{2,0},{5,7},{6,4},{7,5},{8,10},{9,11},{10,8},{13,15},{... | collective-permute-start | bytes 1179656 | tf_op jit(solution)/shard_map/ppermute | solution.py:636
  427.9 25.6 %collective-permute-start.59 = (bf16[256,768]{1,0:T(8,128)(2,1)S(1)}, bf16[256,768]{1,0:T(8,128)(2,1)S(1)}, u32[]{:S(2)}, u32[]{:S(2)}) collective-permute-start(bf16[256,768]{1,0:T(8,128)(2,1)S(1)} %copy-done.53), channel_id=1, source_target_pairs={{0,3},{1,2},{2,1},{5,6},{6,5},{7,4},{8,11},{9,10},{10,9},{13,14},{... | collective-permute-start | bytes 1179656 | tf_op jit(solution)/shard_map/ppermute | solution.py:636
  433.8 43.7 %collective-permute-start.105 = (bf16[4,96,1536]{2,1,0:T(8,128)(2,1)}, bf16[4,96,1536]{2,1,0:T(8,128)(2,1)}, u32[]{:S(2)}, u32[]{:S(2)}) collective-permute-start(bf16[4,96,1536]{2,1,0:T(8,128)(2,1)} %get-tuple-element.111), channel_id=1, source_target_pairs={{0,4},{4,0},{8,12},{12,8},{16,20},{20,16},{24,28},{28,24},{1,5},{5... | collective-permute-start | bytes 3538952 | tf_op jit(solution)/shard_map/ppermute | solution.py:597
  436.6 18.1 %collective-permute-start.89 = (bf16[96,768]{1,0:T(8,128)(2,1)S(1)}, bf16[96,768]{1,0:T(8,128)(2,1)S(1)}, u32[]{:S(2)}, u32[]{:S(2)}) collective-permute-start(bf16[96,768]{1,0:T(8,128)(2,1)S(1)} %get-tuple-element.203), channel_id=1, source_target_pairs={{0,8},{4,12},{8,0},{12,4},{16,24},{20,28},{24,16},{28,20},{1,9},{5... | collective-permute-start | bytes 442376 | tf_op jit(solution)/shard_map/ppermute | solution.py:597
  460.2 12.2 %collective-permute-start.91 = (bf16[96,192]{1,0:T(8,128)(2,1)S(1)}, bf16[96,192]{1,0:T(8,128)(2,1)S(1)}, u32[]{:S(2)}, u32[]{:S(2)}) collective-permute-start(bf16[96,192]{1,0:T(8,128)(2,1)S(1)} %get-tuple-element.225), channel_id=1, source_target_pairs={{0,1},{1,0},{2,3},{3,2},{4,5},{5,4},{6,7},{7,6},{8,9},{9,8},{10,11... | collective-permute-start | bytes 110600 | tf_op jit(solution)/shard_map/ppermute | solution.py:603
  474.9 41.3 %collective-permute-start.80 = (bf16[4,3,96,768]{3,2,1,0:T(8,128)(2,1)}, bf16[4,3,96,768]{3,2,1,0:T(8,128)(2,1)S(1)}, u32[]{:S(2)}, u32[]{:S(2)}) collective-permute-start(bf16[4,3,96,768]{3,2,1,0:T(8,128)(2,1)} %get-tuple-element.103), channel_id=1, source_target_pairs={{0,4},{4,0},{8,12},{12,8},{16,20},{20,16},{24,28},{28,24},{1,5},{5... | collective-permute-start | bytes 5308424 | tf_op jit(solution)/shard_map/ppermute | solution.py:597
  477.6 48.0 %collective-permute-start.111 = (bf16[96,1536]{1,0:T(8,128)(2,1)S(1)}, bf16[96,1536]{1,0:T(8,128)(2,1)S(1)}, u32[]{:S(2)}, u32[]{:S(2)}) collective-permute-start(bf16[96,1536]{1,0:T(8,128)(2,1)S(1)} %get-tuple-element.188), channel_id=1, source_target_pairs={{0,16},{4,20},{8,24},{12,28},{16,0},{20,4},{24,8},{28,12},{1,17},{... | collective-permute-start | bytes 884744 | tf_op jit(solution)/shard_map/ppermute | solution.py:597
  480.4 19.2 %collective-permute-start.107 = (bf16[96,1536]{1,0:T(8,128)(2,1)S(1)}, bf16[96,1536]{1,0:T(8,128)(2,1)S(1)}, u32[]{:S(2)}, u32[]{:S(2)}) collective-permute-start(bf16[96,1536]{1,0:T(8,128)(2,1)S(1)} %get-tuple-element.191), channel_id=1, source_target_pairs={{0,16},{4,20},{8,24},{12,28},{16,0},{20,4},{24,8},{28,12},{1,17},{... | collective-permute-start | bytes 884744 | tf_op jit(solution)/shard_map/ppermute | solution.py:597
  482.2 35.3 %collective-permute-start.106 = (bf16[96,1536]{1,0:T(8,128)(2,1)S(1)}, bf16[96,1536]{1,0:T(8,128)(2,1)S(1)}, u32[]{:S(2)}, u32[]{:S(2)}) collective-permute-start(bf16[96,1536]{1,0:T(8,128)(2,1)S(1)} %get-tuple-element.190), channel_id=1, source_target_pairs={{0,16},{4,20},{8,24},{12,28},{16,0},{20,4},{24,8},{28,12},{1,17},{... | collective-permute-start | bytes 884744 | tf_op jit(solution)/shard_map/ppermute | solution.py:597
  487.0 14.7 %collective-permute-start.101 = (bf16[96,1536]{1,0:T(8,128)(2,1)S(1)}, bf16[96,1536]{1,0:T(8,128)(2,1)S(1)}, u32[]{:S(2)}, u32[]{:S(2)}) collective-permute-start(bf16[96,1536]{1,0:T(8,128)(2,1)S(1)} %get-tuple-element.193), channel_id=1, source_target_pairs={{0,8},{4,12},{8,0},{12,4},{16,24},{20,28},{24,16},{28,20},{1,9},{5... | collective-permute-start | bytes 884744 | tf_op jit(solution)/shard_map/ppermute | solution.py:597
  499.6 40.3 %collective-permute-start.100 = (bf16[96,1536]{1,0:T(8,128)(2,1)S(1)}, bf16[96,1536]{1,0:T(8,128)(2,1)S(1)}, u32[]{:S(2)}, u32[]{:S(2)}) collective-permute-start(bf16[96,1536]{1,0:T(8,128)(2,1)S(1)} %get-tuple-element.192), channel_id=1, source_target_pairs={{0,8},{4,12},{8,0},{12,4},{16,24},{20,28},{24,16},{28,20},{1,9},{5... | collective-permute-start | bytes 884744 | tf_op jit(solution)/shard_map/ppermute | solution.py:597
  501.7 12.3 %collective-permute-start.96 = (bf16[96,1536]{1,0:T(8,128)(2,1)S(1)}, bf16[96,1536]{1,0:T(8,128)(2,1)S(1)}, u32[]{:S(2)}, u32[]{:S(2)}) collective-permute-start(bf16[96,1536]{1,0:T(8,128)(2,1)S(1)} %get-tuple-element.195), channel_id=1, source_target_pairs={{0,8},{4,12},{8,0},{12,4},{16,24},{20,28},{24,16},{28,20},{1,9},{5... | collective-permute-start | bytes 884744 | tf_op jit(solution)/shard_map/ppermute | solution.py:597
  516.1 19.5 %collective-permute-start.95 = (bf16[96,1536]{1,0:T(8,128)(2,1)S(1)}, bf16[96,1536]{1,0:T(8,128)(2,1)S(1)}, u32[]{:S(2)}, u32[]{:S(2)}) collective-permute-start(bf16[96,1536]{1,0:T(8,128)(2,1)S(1)} %get-tuple-element.194), channel_id=1, source_target_pairs={{0,8},{4,12},{8,0},{12,4},{16,24},{20,28},{24,16},{28,20},{1,9},{5... | collective-permute-start | bytes 884744 | tf_op jit(solution)/shard_map/ppermute | solution.py:597
  517.5 16.4 %collective-permute-start.113 = (bf16[96,1536]{1,0:T(8,128)(2,1)S(1)}, bf16[96,1536]{1,0:T(8,128)(2,1)S(1)}, u32[]{:S(2)}, u32[]{:S(2)}) collective-permute-start(bf16[96,1536]{1,0:T(8,128)(2,1)S(1)} %fusion.2), channel_id=1, source_target_pairs={{0,8},{4,12},{8,0},{12,4},{16,24},{20,28},{24,16},{28,20},{1,9},{5... | collective-permute-start | bytes 884744 | tf_op jit(solution)/shard_map/ppermute | solution.py:597
  523.9 17.6 %collective-permute-start.102 = (bf16[96,1536]{1,0:T(8,128)(2,1)S(1)}, bf16[96,1536]{1,0:T(8,128)(2,1)S(1)}, u32[]{:S(2)}, u32[]{:S(2)}) collective-permute-start(bf16[96,1536]{1,0:T(8,128)(2,1)S(1)} %fusion.7), channel_id=1, source_target_pairs={{0,16},{4,20},{8,24},{12,28},{16,0},{20,4},{24,8},{28,12},{1,17},{... | collective-permute-start | bytes 884744 | tf_op jit(solution)/shard_map/ppermute | solution.py:597
  525.5 11.7 %collective-permute-start.97 = (bf16[96,1536]{1,0:T(8,128)(2,1)S(1)}, bf16[96,1536]{1,0:T(8,128)(2,1)S(1)}, u32[]{:S(2)}, u32[]{:S(2)}) collective-permute-start(bf16[96,1536]{1,0:T(8,128)(2,1)S(1)} %fusion.10), channel_id=1, source_target_pairs={{0,16},{4,20},{8,24},{12,28},{16,0},{20,4},{24,8},{28,12},{1,17},{... | collective-permute-start | bytes 884744 | tf_op jit(solution)/shard_map/ppermute | solution.py:597
  533.9 13.0 %collective-permute-start.82 = (bf16[3,96,768]{2,1,0:T(8,128)(2,1)S(1)}, bf16[3,96,768]{2,1,0:T(8,128)(2,1)S(1)}, u32[]{:S(2)}, u32[]{:S(2)}) collective-permute-start(bf16[3,96,768]{2,1,0:T(8,128)(2,1)S(1)} %get-tuple-element.187), channel_id=1, source_target_pairs={{0,16},{4,20},{8,24},{12,28},{16,0},{20,4},{24,8},{28,12},{1,17},{... | collective-permute-start | bytes 1327112 | tf_op jit(solution)/shard_map/ppermute | solution.py:597
  535.6 22.6 %collective-permute-start.81 = (bf16[3,96,768]{2,1,0:T(8,128)(2,1)S(1)}, bf16[3,96,768]{2,1,0:T(8,128)(2,1)S(1)}, u32[]{:S(2)}, u32[]{:S(2)}) collective-permute-start(bf16[3,96,768]{2,1,0:T(8,128)(2,1)S(1)} %get-tuple-element.186), channel_id=1, source_target_pairs={{0,16},{4,20},{8,24},{12,28},{16,0},{20,4},{24,8},{28,12},{1,17},{... | collective-permute-start | bytes 1327112 | tf_op jit(solution)/shard_map/ppermute | solution.py:597
  537.2 15.0 %collective-permute-start.114 = (bf16[96,768]{1,0:T(8,128)(2,1)S(1)}, bf16[96,768]{1,0:T(8,128)(2,1)S(1)}, u32[]{:S(2)}, u32[]{:S(2)}) collective-permute-start(bf16[96,768]{1,0:T(8,128)(2,1)S(1)} %get-tuple-element.221), channel_id=1, source_target_pairs={{0,2},{1,3},{2,0},{3,1},{4,6},{5,7},{6,4},{7,5},{8,10},{9,11},{10,... | collective-permute-start | bytes 442376 | tf_op jit(solution)/shard_map/ppermute | solution.py:603
  539.9 12.3 %collective-permute-start.115 = (bf16[96,768]{1,0:T(8,128)(2,1)S(1)}, bf16[96,768]{1,0:T(8,128)(2,1)S(1)}, u32[]{:S(2)}, u32[]{:S(2)}) collective-permute-start(bf16[96,768]{1,0:T(8,128)(2,1)S(1)} %get-tuple-element.222), channel_id=1, source_target_pairs={{0,3},{1,2},{2,1},{3,0},{4,7},{5,6},{6,5},{7,4},{8,11},{9,10},{10,... | collective-permute-start | bytes 442376 | tf_op jit(solution)/shard_map/ppermute | solution.py:603
  552.8 13.5 %collective-permute-start.98 = (bf16[96,768]{1,0:T(8,128)(2,1)S(1)}, bf16[96,768]{1,0:T(8,128)(2,1)S(1)}, u32[]{:S(2)}, u32[]{:S(2)}) collective-permute-start(bf16[96,768]{1,0:T(8,128)(2,1)S(1)} %slice.710), channel_id=1, source_target_pairs={{0,1},{1,0},{2,3},{3,2},{4,5},{5,4},{6,7},{7,6},{8,9},{9,8},{10,11... | collective-permute-start | bytes 442376 | tf_op jit(solution)/shard_map/ppermute | solution.py:603
  558.7 15.2 %collective-permute-start.85 = (bf16[3,96,192]{2,1,0:T(8,128)(2,1)S(1)}, bf16[3,96,192]{2,1,0:T(8,128)(2,1)S(1)}, u32[]{:S(2)}, u32[]{:S(2)}) collective-permute-start(bf16[3,96,192]{2,1,0:T(8,128)(2,1)S(1)} %get-tuple-element.220), channel_id=1, source_target_pairs={{0,2},{1,3},{2,0},{3,1},{4,6},{5,7},{6,4},{7,5},{8,10},{9,11},{10,... | collective-permute-start | bytes 331784 | tf_op jit(solution)/shard_map/ppermute | solution.py:603
  (106 other events, 1273.5 us)

commit v2 on v1

v2 whole, which is shorter than its diff:
```python
from functools import partial

import jax
import jax.numpy as jnp
import numpy as np
from jax import lax
from jax.experimental import pallas as pl
from jax.experimental.pallas import tpu as pltpu
from jax.sharding import PartitionSpec as P

HEAD = 64
PRECISE = lax.Precision.HIGHEST
EPSILON = 1e-05
SHIFT_1, SCALE_1, GATE_1, SHIFT_2, SCALE_2, GATE_2, BIAS_OUT, GAIN_1, GAIN_2 = range(9)
F32 = jnp.float32
BF16 = jnp.bfloat16
PAIR = 2 * HEAD
BOTH = ("dp", "tensor")
ANY = pl.BlockSpec(memory_space=pl.ANY)
VMEM = pl.BlockSpec(memory_space=pltpu.VMEM)
SMEM = pl.BlockSpec(memory_space=pltpu.SMEM)


def dot_nn(a, b):
    return jnp.dot(a, b, preferred_element_type=F32)


def dot_nt(a, b):
    return lax.dot_general(a, b, (((1,), (1,)), ((), ())), preferred_element_type=F32)


def params(**more):
    return pltpu.CompilerParams(vmem_limit_bytes=58 << 20, **more)


def cost(flops, nbytes, trans=0):
    return pl.CostEstimate(flops=int(flops), bytes_accessed=int(nbytes), transcendentals=int(trans))


def shape(dims, kind):
    return jax.ShapeDtypeStruct(tuple(dims), kind)


def row_at(me_ref, index, rows):
    return pl.multiple_of((me_ref[0] ^ index) * rows, rows)


def vec_row(vec, n):
    return vec[n : n + 1, :]


def norm_scale(vec, gain, scale):
    return vec_row(vec, gain) * (1.0 + vec_row(vec, scale))


class Held:
    def __init__(self, parts, rels):
        self.parts, self.rels = parts, rels

    def blocks(self, refs):
        n = 0
        for ref, rel in zip(refs, self.rels):
            for i, j in enumerate(rel):
                yield ref.at[i], j, n
                n += 1

    @property
    def count(self):
        return sum(len(rel) for rel in self.rels)


def qkv_copies(me, qk, vo, refs, w_buf, sems, rows):
    out = []
    parts = len(qk.parts)
    for held, group, planes in ((qk, refs[:parts], (0, 1)), (vo, refs[parts:], (2,))):
        for block, j, n in held.blocks(group):
            for c, plane in enumerate(planes):
                out.append(
                    pltpu.make_async_copy(
                        block.at[pl.ds(c * rows, rows), :],
                        w_buf.at[plane, pl.ds(row_at(me, j, rows), rows), :],
                        sems.at[plane, n],
                    )
                )
    return out


def qkv_kernel(qk, vo, me, *refs):
    x_refs, refs = refs[:4], refs[4:]
    (vec, cosine, sin_a, sin_b), refs = refs[:4], refs[4:]
    mul, add = norm_scale(vec, GAIN_1, SCALE_1), vec_row(vec, SHIFT_1)
    held, refs = refs[: 2 * len(qk.parts)], refs[2 * len(qk.parts) :]
    (n_t, q_out, k_out, v_out, q_t, k_t, v_t), (w_buf, n_buf, sems) = refs[:7], refs[7:]
    copies = qkv_copies(me, qk, vo, held, w_buf, sems, w_buf.shape[1] // qk.count)
    for copy in copies:
        copy.start()
    part = x_refs[0].shape[0]
    for b, x_ref in enumerate(x_refs):
        x = x_ref[...].astype(F32)
        centred = x - jnp.mean(x, axis=-1, keepdims=True)
        spread = jnp.mean(centred * centred, axis=-1, keepdims=True)
        n_buf[b * part : (b + 1) * part, :] = (
            centred * lax.rsqrt(spread + EPSILON) * mul + add
        ).astype(BF16)
    normed = n_buf[...]
    n_t[...] = normed.T
    for copy in copies:
        copy.wait()
    width = q_out.shape[1]
    for c, (flat, turned, factor) in enumerate(((q_out, q_t, HEAD**-0.5), (k_out, k_t, 1.0))):
        proj = dot_nn(normed, w_buf[c])
        for p in range(width // PAIR):
            lanes = slice(p * PAIR, (p + 1) * PAIR)
            r = proj[:, lanes]
            spun = (
                r * cosine[...]
                + pltpu.roll(r, PAIR - HEAD // 2, 1) * sin_a[...]
                + pltpu.roll(r, HEAD // 2, 1) * sin_b[...]
            )
            spun = spun.astype(BF16) * BF16(factor)
            flat[:, lanes] = spun
            turned[lanes, :] = spun.T
    values = dot_nn(normed, w_buf[2]).astype(BF16)
    v_out[...] = values
    v_t[...] = values.T


def qkv(me, x_parts, vec, cosine, sin_a, sin_b, qk, vo):
    part, width = x_parts[0].shape
    length = 4 * part
    cols = qk.parts[0].shape[2]
    flat, turned = shape((length, cols), BF16), shape((cols, length), BF16)
    return pl.pallas_call(
        partial(qkv_kernel, qk, vo),
        out_shape=[shape((width, length), BF16), flat, flat, flat, turned, turned, turned],
        in_specs=[SMEM] + [VMEM] * 8 + [ANY] * (2 * len(qk.parts)),
        out_specs=[VMEM] * 7,
        scratch_shapes=[
            pltpu.VMEM((3, width, cols), BF16),
            pltpu.VMEM((length, width), BF16),
            pltpu.SemaphoreType.DMA((3, qk.count)),
        ],
        compiler_params=params(),
        cost_estimate=cost(6 * length * width * cols, 16e6),
        name="qkv",
    )(me, *x_parts, vec, cosine, sin_a, sin_b, *qk.parts, *vo.parts)


def head_mask(ref, head):
    lane = lax.broadcasted_iota(jnp.int32, (1, PAIR), 1)
    return jnp.where((lane // HEAD) == head, ref[...], jnp.zeros((), BF16))


def same_doc_bias(bias, doc_row, doc_col):
    bias[...] = jnp.where(doc_col[...] == doc_row[...], 0.0, -1e30)


def attend_kernel(q, k, v_t, doc_row, doc_col, mix_t, log_sum, bias):
    @pl.when(pl.program_id(0) == 0)
    def _():
        same_doc_bias(bias, doc_row, doc_col)

    for h in range(2):
        rows = slice(h * HEAD, (h + 1) * HEAD)
        scores = dot_nt(head_mask(k, h), q[...]) + bias[...]
        top = jnp.max(scores, axis=0, keepdims=True)
        weights = jnp.exp(scores - top)
        total = jnp.sum(weights, axis=0, keepdims=True)
        mixed = dot_nn(v_t[rows, :], weights.astype(BF16))
        mix_t[rows, :] = (mixed / total).astype(BF16)
        log_sum[0, h : h + 1, :] = top + jnp.log(total)


def attend(q, k, v_t, doc_row, doc_col):
    length, width = q.shape
    pairs = width // PAIR
    flat = pl.BlockSpec((length, PAIR), lambda i: (0, i))
    turned = pl.BlockSpec((PAIR, length), lambda i: (i, 0))
    return pl.pallas_call(
        attend_kernel,
        grid=(pairs,),
        in_specs=[
            flat,
            flat,
            turned,
            pl.BlockSpec((1, length), lambda i: (0, 0)),
            pl.BlockSpec((length, 1), lambda i: (0, 0)),
        ],
        out_specs=[turned, pl.BlockSpec((1, 2, length), lambda i: (i, 0, 0))],
        out_shape=[shape((width, length), BF16), shape((pairs, 2, length), F32)],
        scratch_shapes=[pltpu.VMEM((length, length), F32)],
        compiler_params=params(),
        cost_estimate=cost(16 * length * length * width, 8e6),
        name="attend",
    )(q, k, v_t, doc_row, doc_col)


def load_out_weight(me, vo, refs, buf, sems):
    rows = buf.shape[0] // vo.count
    copies = [
        pltpu.make_async_copy(
            block.at[pl.ds(rows, rows), :], buf.at[pl.ds(row_at(me, j, rows), rows), :], sems.at[n]
        )
        for block, j, n in vo.blocks(refs)
    ]
    for copy in copies:
        copy.start()
    return copies


def middle_kernel(vo, me, *refs):
    x_refs, g_refs, refs = refs[:4], refs[4:8], refs[8:]
    (mix_t, vec), refs = refs[:2], refs[2:]
    mul, add = norm_scale(vec, GAIN_2, SCALE_2), vec_row(vec, SHIFT_2)
    gate_one, gate_two = vec_row(vec, GATE_1), vec_row(vec, GATE_2)
    pieces, refs = refs[: len(vo.parts)], refs[len(vo.parts) :]
    (att, n_two, n_two_t, d_down, d_down_t, d_bias), (w_buf, sems) = refs[:6], refs[6:]
    copies = load_out_weight(me, vo, pieces, w_buf, sems)
    part = x_refs[0].shape[0]
    total = jnp.zeros(gate_two.shape, F32)
    for b, g_ref in enumerate(g_refs):
        scaled = g_ref[...].astype(F32) * gate_two
        total += jnp.sum(scaled, axis=0, keepdims=True)
        d_down[b * part : (b + 1) * part, :] = scaled.astype(BF16)
    d_bias[...] = total
    d_down_t[...] = d_down[...].T
    mixture = mix_t[...].T
    for copy in copies:
        copy.wait()
    for b, x_ref in enumerate(x_refs):
        rows = slice(b * part, (b + 1) * part)
        attention = dot_nt(mixture[rows, :], w_buf[...])
        att[rows, :] = attention
        mid = x_ref[...].astype(F32) + gate_one * attention
        centred = mid - jnp.mean(mid, axis=-1, keepdims=True)
        spread = jnp.mean(centred * centred, axis=-1, keepdims=True)
        n_two[rows, :] = (
            centred * lax.rsqrt(spread + EPSILON) * mul + add
        ).astype(BF16)
    n_two_t[...] = n_two[...].T


def middle(me, x_parts, g_parts, mix_t, vec, vo):
    part, width = x_parts[0].shape
    length = 4 * part
    inner = mix_t.shape[0]
    flat, turned = shape((length, width), BF16), shape((width, length), BF16)
    return pl.pallas_call(
        partial(middle_kernel, vo),
        out_shape=[shape((length, width), F32), flat, turned, flat, turned, shape((1, width), F32)],
        in_specs=[SMEM] + [VMEM] * 10 + [ANY] * len(vo.parts),
        out_specs=[VMEM] * 6,
        scratch_shapes=[pltpu.VMEM((width, inner), BF16), pltpu.SemaphoreType.DMA((vo.count,))],
        compiler_params=params(),
        cost_estimate=cost(2 * length * width * inner, 16e6),
        name="middle",
    )(me, *x_parts, *g_parts, mix_t, vec, *vo.parts)


def spread_rows(me, value, stage, keep, send=None):
    blocks, rows = stage.shape[0], stage.shape[1]
    for j in range(blocks):
        stage[j] = value[j * rows : (j + 1) * rows, :].astype(BF16)
    for j in range(blocks):
        block = stage[me[0] ^ j]
        if j % 2 == 0:
            keep(j // 2, block)
        else:
            send(j // 2, block)


def writer(ref, *lead):
    def put(slot, block):
        ref[(lead[0], slot, *lead[1:])] = block

    return put


def split_writer(ref, *lead):
    def put(slot, block):
        half = block.shape[-1] // 2
        for s in range(2):
            ref[(s, slot, *lead)] = block[:, s * half : (s + 1) * half]

    return put


C_ROOT = 0.7978845608028654
C_CUBE = 0.044715


def feed_kernel(up, dn, steps, first, me, *refs):
    (n_two, n_two_t, d_down, d_down_t, bias), refs = refs[:5], refs[5:]
    if not first:
        (down_in, d_n_in), refs = refs[:2], refs[2:]
    parts = len(up.parts)
    up_refs, down_refs, refs = refs[:parts], refs[parts : 2 * parts], refs[2 * parts :]
    (down, d_n, d_bias, *grads), (w_buf, stage, sems) = refs[:-3], refs[-3:]
    step = pl.program_id(0)
    rows = up_refs[0].shape[1]
    chunk = w_buf.shape[3]
    offset = 0 if first else steps * chunk

    def copies(s):
        out = []
        for m, (held, group) in enumerate(((up, up_refs), (dn, down_refs))):
            for block, j, n in held.blocks(group):
                out.append(
                    pltpu.make_async_copy(
                        block.at[:, pl.ds(offset + s * chunk, chunk)],
                        w_buf.at[m, s, pl.ds(row_at(me, j, rows), rows), :],
                        sems.at[m, s, n],
                    )
                )
        return out

    @pl.when(step == 0)
    def _():
        for s in range(steps):
            for copy in copies(s):
                copy.start()
        if first:
            down[...] = jnp.zeros_like(down)
            d_n[...] = jnp.zeros_like(d_n)
        else:
            down[...] = down_in[...]
            d_n[...] = d_n_in[...]

    for s in range(steps):

        @pl.when(step == s)
        def _():
            for copy in copies(s):
                copy.wait()

    w_up = w_buf[0, step]
    w_down_t = w_buf[1, step]
    h = dot_nn(n_two[...], w_up) + bias[0]
    square = h * h
    t = jnp.tanh(C_ROOT * h * (1.0 + C_CUBE * square))
    half = 0.5 + 0.5 * t
    act = (h * half).astype(BF16)
    slope = half + (0.5 * C_ROOT) * h * (1.0 - t * t) * (1.0 + (3.0 * C_CUBE) * square)
    d_h = (dot_nn(d_down[...], w_down_t) * slope).astype(BF16)
    d_bias[0] = jnp.sum(d_h.astype(F32), axis=0, keepdims=True)
    down[...] += dot_nt(act, w_down_t)
    d_n[...] += dot_nt(d_h, w_up)
    for m, grad in ((0, dot_nn(n_two_t[...], d_h)), (1, dot_nn(d_down_t[...], act))):
        spread_rows(me, grad, stage, *(writer(ref, m) for ref in grads))


def feed(me, n_two, n_two_t, d_down, d_down_t, bias, up, dn, start, before, units):
    blocks = up.count
    length, width = n_two.shape
    chunk = 512 if units % 512 == 0 else units
    steps = units // chunk
    first = before is None
    rows = width // blocks
    one = pl.Buffered(1)
    flat = pl.BlockSpec((length, width), lambda i: (0, 0), pipeline_mode=one)
    turned = pl.BlockSpec((width, length), lambda i: (0, 0), pipeline_mode=one)
    held = pl.BlockSpec((length, width), lambda i: (0, 0))
    half = max(blocks // 2, 1)
    grad = pl.BlockSpec((2, half, rows, chunk), lambda i: (0, 0, 0, i))
    grads = 1 if blocks == 1 else 2
    bias_spec = pl.BlockSpec((1, 1, chunk), lambda i: (i + start // chunk, 0, 0))
    return pl.pallas_call(
        partial(feed_kernel, up, dn, steps, first),
        grid=(steps,),
        in_specs=[SMEM, flat, turned, flat, turned, bias_spec]
        + ([] if first else [flat, flat])
        + [ANY] * (2 * len(up.parts)),
        out_specs=[held, held, pl.BlockSpec((1, 1, chunk), lambda i: (i, 0, 0))] + [grad] * grads,
        out_shape=[shape((length, width), F32)] * 2
        + [shape((steps, 1, chunk), F32)]
        + [shape((2, half, rows, units), BF16)] * grads,
        scratch_shapes=[
            pltpu.VMEM((2, steps, width, chunk), BF16),
            pltpu.VMEM((blocks, rows, chunk), BF16),
            pltpu.SemaphoreType.DMA((2, steps, blocks)),
        ],
        compiler_params=params(),
        cost_estimate=cost(12 * length * width * units, 20e6),
        name="feed",
    )(
        me,
        n_two,
        n_two_t,
        d_down,
        d_down_t,
        bias.reshape(-1, 1, chunk),
        *(() if first else before),
        *up.parts,
        *dn.parts,
    )


def turn_kernel(vo, me, *refs):
    x_refs, g_refs, refs = refs[:4], refs[4:8], refs[8:]
    (att, down, d_n, mix_t, vec), refs = refs[:5], refs[5:]
    mul, bias = norm_scale(vec, GAIN_2, SCALE_2), vec_row(vec, BIAS_OUT)
    gate_one, gate_two = vec_row(vec, GATE_1), vec_row(vec, GATE_2)
    pieces, refs = refs[: len(vo.parts)], refs[len(vo.parts) :]
    out_refs, (d_mid, d_mix, d_mix_t, sums, d_att_t), (w_buf, d_att, sems) = (
        refs[:4],
        refs[4:9],
        refs[9:],
    )
    copies = load_out_weight(me, vo, pieces, w_buf, sems)
    part = x_refs[0].shape[0]
    totals = [jnp.zeros(gate_two.shape, F32) for _ in range(4)]
    for b in range(4):
        rows = slice(b * part, (b + 1) * part)
        g = g_refs[b][...].astype(F32)
        attention = att[rows, :]
        mid = x_refs[b][...].astype(F32) + gate_one * attention
        branch = down[rows, :] + bias
        out_refs[b][...] = (mid + gate_two * branch).astype(BF16)
        centred = mid - jnp.mean(mid, axis=-1, keepdims=True)
        inverse = lax.rsqrt(jnp.mean(centred * centred, axis=-1, keepdims=True) + EPSILON)
        unit = centred * inverse
        dn = d_n[rows, :]
        dn_unit = dn * unit
        du = dn * mul
        dm = g + inverse * (
            du
            - jnp.mean(du, axis=-1, keepdims=True)
            - unit * jnp.mean(dn_unit * mul, axis=-1, keepdims=True)
        )
        d_mid[rows, :] = dm
        d_att[rows, :] = (dm * gate_one).astype(BF16)
        for n, term in enumerate((g * branch, dn_unit, dn, dm * attention)):
            totals[n] += jnp.sum(term, axis=0, keepdims=True)
    for n in range(4):
        sums[n : n + 1, :] = totals[n]
    for copy in copies:
        copy.wait()
    d_mix[...] = dot_nn(d_att[...], w_buf[...]).astype(BF16)
    d_mix_t[...] = d_mix[...].T
    d_att_t[...] = d_att[...].T


def turn(me, x_parts, g_parts, att, down, d_n, mix_t, vec, vo):
    part, width = x_parts[0].shape
    length = 4 * part
    inner = mix_t.shape[0]
    return pl.pallas_call(
        partial(turn_kernel, vo),
        out_shape=[shape((part, width), BF16)] * 4
        + [
            shape((length, width), F32),
            shape((length, inner), BF16),
            shape((inner, length), BF16),
            shape((4, width), F32),
            shape((width, length), BF16),
        ],
        in_specs=[SMEM] + [VMEM] * 13 + [ANY] * len(vo.parts),
        out_specs=[VMEM] * 9,
        scratch_shapes=[
            pltpu.VMEM((width, inner), BF16),
            pltpu.VMEM((length, width), BF16),
            pltpu.SemaphoreType.DMA((vo.count,)),
        ],
        compiler_params=params(),
        cost_estimate=cost(2 * length * width * inner, 24e6),
        name="turn",
    )(
        me, *x_parts, *g_parts, att, down, d_n, mix_t, vec, *vo.parts
    )


def attend_back_kernel(
    q, k, v, d_mix, q_t, k_t, d_mix_t, mix_t, log_sum, doc_row, doc_col, cos_t, sin_t,
    dq_t, dk_t, dv_t, bias, dq_acc, dk_acc, dv_acc,
):
    @pl.when(pl.program_id(0) == 0)
    def _():
        same_doc_bias(bias, doc_row, doc_col)

    length = q.shape[0]
    block = 256 if length % 256 == 0 else length
    for h in range(2):
        rows = slice(h * HEAD, (h + 1) * HEAD)
        keys = head_mask(k, h)
        values = head_mask(v, h)
        row_dot = jnp.sum(
            d_mix_t[rows, :].astype(F32) * mix_t[rows, :].astype(F32), axis=0, keepdims=True
        )
        for b in range(length // block):
            c = slice(b * block, (b + 1) * block)
            probs = jnp.exp(dot_nt(keys, q[c, :]) + bias[:, c] - log_sum[0, h : h + 1, c])
            d_scores = (probs * (dot_nt(values, d_mix[c, :]) - row_dot[:, c])).astype(BF16)
            dv_part = dot_nt(d_mix_t[rows, c], probs.astype(BF16))
            dk_part = dot_nt(q_t[rows, c], d_scores)
            if b == 0:
                dv_acc[rows, :] = dv_part
                dk_acc[rows, :] = dk_part
            else:
                dv_acc[rows, :] += dv_part
                dk_acc[rows, :] += dk_part
            dq_acc[rows, c] = dot_nn(k_t[rows, :], d_scores)
    half = HEAD // 2
    for h in range(2):
        one = slice(h * HEAD, h * HEAD + half)
        two = slice(h * HEAD + half, (h + 1) * HEAD)
        for acc, out, factor in ((dq_acc, dq_t, HEAD**-0.5), (dk_acc, dk_t, 1.0)):
            a, b = acc[one, :] * factor, acc[two, :] * factor
            out[one, :] = (a * cos_t[...] + b * sin_t[...]).astype(BF16)
            out[two, :] = (b * cos_t[...] - a * sin_t[...]).astype(BF16)
    dv_t[...] = dv_acc[...].astype(BF16)


def attend_back(q, k, v, d_mix, q_t, k_t, d_mix_t, mix_t, log_sum, doc_row, doc_col, cos_t, sin_t, start, count):
    length, width = q.shape
    flat = pl.BlockSpec((length, PAIR), lambda i: (0, i + start))
    turned = pl.BlockSpec((PAIR, length), lambda i: (i + start, 0))
    out = pl.BlockSpec((PAIR, length), lambda i: (i, 0))
    fixed = lambda a: pl.BlockSpec(a.shape, lambda i: (0, 0))
    return pl.pallas_call(
        attend_back_kernel,
        grid=(count,),
        in_specs=[flat] * 4
        + [turned] * 4
        + [pl.BlockSpec((1, 2, length), lambda i: (i + start, 0, 0))]
        + [fixed(a) for a in (doc_row, doc_col, cos_t, sin_t)],
        out_specs=[out] * 3,
        out_shape=[shape((count * PAIR, length), BF16)] * 3,
        scratch_shapes=[pltpu.VMEM((length, length), F32)] + [pltpu.VMEM((PAIR, length), F32)] * 3,
        compiler_params=params(),
        cost_estimate=cost(28 * length * length * count * PAIR, 14e6 * count * PAIR / width),
        name="attend_back",
    )(q, k, v, d_mix, q_t, k_t, d_mix_t, mix_t, log_sum, doc_row, doc_col, cos_t, sin_t)


def first_kernel(qk, vo, me, *refs):
    x_refs, refs = refs[:4], refs[4:]
    (d_mid, vec, dq_t, dk_t, dv_t), refs = refs[:5], refs[5:]
    mul = norm_scale(vec, GAIN_1, SCALE_1)
    held, refs = refs[: 2 * len(qk.parts)], refs[2 * len(qk.parts) :]
    out_refs, (sums, w_buf, sems) = refs[:4], refs[4:]
    copies = qkv_copies(me, qk, vo, held, w_buf, sems, w_buf.shape[1] // qk.count)
    for copy in copies:
        copy.start()
    for copy in copies:
        copy.wait()
    d_n_t = (
        dot_nn(w_buf[0], dq_t[...]) + dot_nn(w_buf[1], dk_t[...]) + dot_nn(w_buf[2], dv_t[...])
    )
    part = x_refs[0].shape[0]
    totals = [jnp.zeros(mul.shape, F32) for _ in range(2)]
    for b in range(4):
        r = slice(b * part, (b + 1) * part)
        dn = d_n_t[:, r].T
        x = x_refs[b][...].astype(F32)
        centred = x - jnp.mean(x, axis=-1, keepdims=True)
        inverse = lax.rsqrt(jnp.mean(centred * centred, axis=-1, keepdims=True) + EPSILON)
        unit = centred * inverse
        dn_unit = dn * unit
        du = dn * mul
        out_refs[b][...] = (
            d_mid[r, :]
            + inverse
            * (
                du
                - jnp.mean(du, axis=-1, keepdims=True)
                - unit * jnp.mean(dn_unit * mul, axis=-1, keepdims=True)
            )
        ).astype(BF16)
        for n, term in enumerate((dn_unit, dn)):
            totals[n] += jnp.sum(term, axis=0, keepdims=True)
    for n in range(2):
        sums[n : n + 1, :] = totals[n]


def first(me, x_parts, d_mid, vec, dq_t, dk_t, dv_t, qk, vo):
    part, width = x_parts[0].shape
    length = 4 * part
    cols = dq_t.shape[0]
    return pl.pallas_call(
        partial(first_kernel, qk, vo),
        out_shape=[shape((part, width), BF16)] * 4 + [shape((2, width), F32)],
        in_specs=[SMEM] + [VMEM] * 9 + [ANY] * (2 * len(qk.parts)),
        out_specs=[VMEM] * 5,
        scratch_shapes=[
            pltpu.VMEM((3, width, cols), BF16),
            pltpu.SemaphoreType.DMA((3, qk.count)),
        ],
        compiler_params=params(),
        cost_estimate=cost(6 * length * width * cols, 20e6),
        name="first",
    )(me, *x_parts, d_mid, vec, dq_t, dk_t, dv_t, *qk.parts, *vo.parts)


def three_terms(v):
    rows = []
    for _ in range(3):
        rows.append(v.astype(BF16).astype(F32))
        v = v - rows[-1]
    rows += [jnp.zeros_like(v)] * 5
    return jnp.concatenate(rows, axis=0).astype(BF16)


def modulate_kernel(qk, vo, zones, me, act, *refs):
    parts = len(qk.parts)
    qk_refs, vo_refs, (vec, bias, ada, small, sems) = refs[:parts], refs[parts:-5], refs[-5:]
    count = qk.count
    rows = ada.shape[0] // count
    cut = rows // 2
    copies = []
    for h, (held, group) in enumerate(((qk, qk_refs), (vo, vo_refs))):
        for block, j, n in held.blocks(group):
            at = row_at(me, j, rows) + h * cut
            copies.append(
                pltpu.make_async_copy(
                    block.at[pl.ds(2 * rows, cut), :], ada.at[pl.ds(at, cut), :], sems.at[h, n]
                )
            )
            if h:
                copies.append(
                    pltpu.make_async_copy(
                        block.at[pl.ds(2 * rows + cut, 16), :],
                        small.at[pl.ds(row_at(me, j, 16), 16), :],
                        sems.at[2, n],
                    )
                )
    for copy in copies:
        copy.start()
    for copy in copies:
        copy.wait()
    kinds = ada.shape[1] // act.shape[1]
    act3 = three_terms(act[...])
    across = vec.shape[1] // rows
    vec[...] = jnp.zeros_like(vec)
    for k in range(kinds):
        lanes = slice(k * act.shape[1], (k + 1) * act.shape[1])
        found = jnp.sum(dot_nt(act3, ada[:, lanes]), axis=0, keepdims=True)
        for d in range(count):
            m = d * kinds + k
            at = (m % across) * rows
            extra = small[d * 16 : (d + 1) * 16, :].astype(F32)
            vec[m // across : m // across + 1, at : at + rows] = (
                found[:, d * rows : (d + 1) * rows] + extra[1:2, k * rows : (k + 1) * rows]
            )
    for d in range(count):
        extra = small[d * 16 : (d + 1) * 16, :].astype(F32)
        here = slice(d * rows, (d + 1) * rows)
        for n in range(3):
            vec[BIAS_OUT + n : BIAS_OUT + n + 1, here] = extra[2:3, n * rows : (n + 1) * rows]
        for n in range(zones):
            far = (n - zones // 2) % zones
            at = n * (extra.shape[1] // zones)
            bias[far : far + 1, here] = extra[0:1, at : at + rows]


def modulate(me, act, qk, vo, zones, rows):
    width = qk.parts[0].shape[2]
    return pl.pallas_call(
        partial(modulate_kernel, qk, vo, zones),
        out_shape=[
            shape((16, width), F32),
            shape((zones, width), F32),
            shape((qk.count * rows, width), BF16),
        ],
        in_specs=[SMEM, VMEM] + [ANY] * (len(qk.parts) + len(vo.parts)),
        out_specs=[VMEM] * 3,
        scratch_shapes=[
            pltpu.VMEM((qk.count * 16, width), BF16),
            pltpu.SemaphoreType.DMA((3, qk.count)),
        ],
        compiler_params=params(),
        cost_estimate=cost(2e7, 4e6),
        name="modulate",
    )(me, act, *qk.parts, *vo.parts)


def gather_up_kernel(count, vec, ada, sums, sums_one, d_bias_down, bias_grad, act, cond, out, spread):
    width = vec.shape[1]
    rows = width // count
    size = act.shape[1]
    kinds = ada.shape[1] // size
    norm_1, norm_2 = sums_one[0:1, :], sums[1:2, :]
    d_mod = (
        sums_one[1:2, :],
        norm_1 * vec_row(vec, GAIN_1),
        sums[3:4, :],
        sums[2:3, :],
        norm_2 * vec_row(vec, GAIN_2),
        sums[0:1, :],
    )
    others = (
        norm_1 * (1.0 + vec_row(vec, SCALE_1)),
        norm_2 * (1.0 + vec_row(vec, SCALE_2)),
        d_bias_down[...],
    )
    out[...] = jnp.zeros_like(out)
    base = (kinds + 3) * rows
    for d in range(count):
        here = slice(d * rows, (d + 1) * rows)
        for k in range(kinds):
            m = d * kinds + k
            at = (m % count) * rows
            piece = d_mod[m // count][:, at : at + rows]
            out[d : d + 1, k * rows : (k + 1) * rows] = piece
            spread[k : k + 1, here] = piece
        for n, value in enumerate(others):
            at = (kinds + n) * rows
            out[d : d + 1, at : at + rows] = value[:, here]
        for n in range(bias_grad.shape[0]):
            at = base + n * rows
            out[d : d + 1, at : at + rows] = bias_grad[n : n + 1, here]
        out[d : d + 1, out.shape[1] - size :] = act[...]
    total = jnp.zeros(act.shape, F32)
    for k in range(kinds):
        three = three_terms(spread[k : k + 1, :])
        total += jnp.sum(dot_nn(three, ada[:, k * size : (k + 1) * size]), axis=0, keepdims=True)
    c = cond[...]
    sig = 1.0 / (1.0 + jnp.exp(-c))
    out[count : count + 1, :size] = total * (sig * (1.0 + c * (1.0 - sig)))


def gather_up(vec, ada, sums, sums_one, d_bias_down, bias_grad, act, cond, count, length):
    return pl.pallas_call(
        partial(gather_up_kernel, count),
        out_shape=shape((2 * count, length), F32),
        in_specs=[VMEM] * 8,
        out_specs=VMEM,
        scratch_shapes=[pltpu.VMEM((8, vec.shape[1]), F32)],
        compiler_params=params(),
        cost_estimate=cost(2e7, 4e6),
        name="gather_up",
    )(vec, ada, sums, sums_one, d_bias_down, bias_grad, act, cond)


def weight_grads_kernel(me, n_t, dq_t, dk_t, dv_t, d_att_t, mix_t, *refs):
    grads, stage = refs[:-1], refs[-1]
    pairs = (n_t, dq_t), (n_t, dk_t), (n_t, dv_t), (d_att_t, mix_t)
    for c, (a, b) in enumerate(pairs):
        grad = dot_nt(a[...], b[...])
        spread_rows(me, grad, stage, *(split_writer(ref, c) for ref in grads))


def weight_grads(me, n_t, dq_t, dk_t, dv_t, d_att_t, mix_t, blocks):
    width, length = n_t.shape
    cols = dq_t.shape[0]
    rows = width // blocks
    half = max(blocks // 2, 1)
    grads = 1 if blocks == 1 else 2
    return pl.pallas_call(
        weight_grads_kernel,
        out_shape=[shape((2, half, 4, rows, cols // 2), BF16)] * grads,
        in_specs=[SMEM] + [VMEM] * 6,
        out_specs=[VMEM] * grads,
        scratch_shapes=[pltpu.VMEM((blocks, rows, cols), BF16)],
        compiler_params=params(),
        cost_estimate=cost(8 * length * width * cols, 14e6),
        name="weight_grads",
    )(me, n_t, dq_t, dk_t, dv_t, d_att_t, mix_t)


class Group:
    def __init__(self, dp_count, tensor_count, per_dp):
        self.dp, self.tensor, self.per_dp = dp_count, tensor_count, per_dp
        self.d, self.r = lax.axis_index("dp"), lax.axis_index("tensor")
        self.paired = dp_count == 8

    def bit(self, v, b):
        return lax.ppermute(v, "dp", [(i, i ^ (1 << b)) for i in range(self.dp)])

    def step(self, v, k):
        return lax.ppermute(v, "dp", [(i, i ^ k) for i in range(self.dp)])

    def z(self, v, k):
        return lax.ppermute(v, "tensor", [(i, i ^ k) for i in range(self.tensor)])

    def owns(self, d, r):
        return 0 <= r - d % 2 < self.per_dp

    def to_owner(self, rows, zero_idle):
        mine = self.r - self.d % 2
        top = self.per_dp - 1
        own = lax.dynamic_index_in_dim(rows, jnp.clip(mine, 0, top), 0, keepdims=False)
        if zero_idle:
            own = jnp.where((mine >= 0) & (mine <= top), own, jnp.zeros_like(own))
        parts = [own]
        for k in range(1, self.tensor):
            want = (self.r ^ k) - self.d % 2
            sent = lax.dynamic_index_in_dim(rows, jnp.clip(want, 0, top), 0, keepdims=False)
            pairs = [
                (d * self.tensor + r, d * self.tensor + (r ^ k))
                for d in range(self.dp)
                for r in range(self.tensor)
                if self.owns(d, r ^ k)
            ]
            parts.append(lax.ppermute(sent, BOTH, pairs))
        return parts

    def to_holder(self, parts):
        came = [parts[0]]
        for k in range(1, self.tensor):
            pairs = [
                (d * self.tensor + r, d * self.tensor + (r ^ k))
                for d in range(self.dp)
                for r in range(self.tensor)
                if self.owns(d, r)
            ]
            came.append(lax.ppermute(parts[k], BOTH, pairs))
        return came

    def held_rows(self, came):
        stack = jnp.stack(came)
        return jnp.stack(
            [
                lax.dynamic_index_in_dim(stack, self.r ^ (j + self.d % 2), 0, keepdims=False)
                for j in range(self.per_dp)
            ]
        )

    def z_pair(self, v, got):
        return jnp.concatenate([v, got], axis=-1)

    def gather_pair(self, v, got, order):
        pair = jnp.stack([v, got])
        return [pair, self.bit(pair, order[1])]

    def gather_cores(self, parts, order):
        one, two = (1 << b for b in order)
        rels = [(0, one), (two, one ^ two)]
        if len(parts) == 1:
            rels = [rels[0] + rels[1]]
        rels += [tuple(j ^ 1 for j in rel) for rel in rels]
        return Held(parts + [self.bit(p, 0) for p in parts], rels)

    def whole(self, v, axis):
        return lax.all_gather(v, "dp", axis=axis, tiled=True)

    def swap(self, v):
        if not self.paired:
            return lax.all_to_all(v, "dp", split_axis=0, concat_axis=0, tiled=True)
        v = jnp.take(v, self.d ^ jnp.arange(self.dp), axis=0)[None]
        for b in range(3):
            v = v.reshape(v.shape[0], v.shape[1] // 2, 2, *v.shape[2:])
            v = jnp.concatenate([v[:, :, 0], self.bit(v[:, :, 1], b)])
        return v[:, 0]


class Flight:
    def __init__(self, value):
        self.value = value


class Sum:
    def __init__(self, group, keep, send=None):
        self.group, self.stage, self.flights = group, 0, []
        if not group.paired:
            value = keep[:, 0].astype(F32)
            value = lax.psum_scatter(value, "dp", scatter_dimension=value.ndim - 2, tiled=True)
            self.total = [value[0], value[1]]
            return
        self.total = [keep[0], keep[1]]
        flight = Flight(group.bit(send, 0))
        self.flights = [(flight, 0), (flight, 1)]

    def settle(self):
        if self.flights:
            self.total = [
                t.astype(F32) + flight.value[at].astype(F32)
                for t, (flight, at) in zip(self.total, self.flights)
            ]
        if self.stage == 2:
            self.total = [t[0] for t in self.total]
        self.flights = []

    def split(self):
        out = []
        for n, order in enumerate(((1, 2), (2, 1))):
            t, b = self.total[n], order[self.stage]
            if self.stage == 0:
                t = t.reshape(2, 2, *t.shape[1:])
                stay, go = (t[:, 0], t[:, 1]) if b == 1 else (t[0], t[1])
            else:
                stay, go = t[:1], t[1:]
            self.total[n] = stay
            out.append((b, go.astype(BF16)))
        self.stage += 1
        self.flights = [None, None]
        return out


def exchange(*sums):
    links = {}
    for t in sums:
        t.settle()
        if t.group.paired:
            for n, (b, go) in enumerate(t.split()):
                links.setdefault(b, []).append((t, n, go))
    for b, items in links.items():
        blocks = [go for _, _, go in items]
        blocks = blocks[0] if len(blocks) == 1 else jnp.concatenate(blocks)
        flight, at = Flight(items[0][0].group.bit(blocks, b)), 0
        for t, n, go in items:
            t.flights[n] = (flight, slice(at, at + go.shape[0]))
            at += go.shape[0]


def tie(value, *sums):
    flights = {id(f): f for t in sums for f, _ in t.flights}
    flights = list(flights.values())
    value, arrived = lax.optimization_barrier((value, [f.value for f in flights]))
    for flight, v in zip(flights, arrived):
        flight.value = v
    return value


def silu_slope(c):
    sig = jax.nn.sigmoid(c)
    return sig * (1.0 + c * (1.0 - sig))


def shards(
    inputs, condition, doc_ids, positions, w_qkv, w_out, w_up, bias_up, w_down, bias_down,
    gain_one, gain_two, w_ada, bias_ada, out_grad,
):
    dp_count = lax.axis_size("dp")
    tensor_count = lax.axis_size("tensor")
    per_dp, part, width = inputs.shape
    length = doc_ids.shape[1]
    rows = w_up.shape[0]
    group = Group(dp_count, tensor_count, per_dp)
    blocks = dp_count if group.paired else 1
    d, r = group.d, group.r
    me = jnp.where(group.paired, d, 0).astype(jnp.int32).reshape(1)
    mine = jnp.clip(r - d % 2, 0, per_dp - 1)
    own_row = lambda v: lax.dynamic_index_in_dim(v, mine, 0, keepdims=False)
    join = lambda parts: jnp.concatenate(parts, axis=-1)

    cols, cond_size, mod_width = w_qkv.shape[2], w_ada.shape[0], w_ada.shape[1]
    ways = (1, 2), (2, 1)
    cond = own_row(condition).astype(F32)[None]
    act = jax.nn.silu(cond)
    early = jnp.concatenate([w_qkv.reshape(-1, cols), w_out.T])
    late = jnp.concatenate([w_up, w_down.T])
    if group.paired:
        early = jnp.concatenate([early, jnp.pad(bias_up, ((0, 15), (0, cols - rows)))])
    if group.paired:
        ada = w_ada.T.reshape(-1, rows, cond_size).transpose(1, 0, 2).reshape(rows, width)
        cut, top = rows // 2, 2 * rows
        wide = lambda v: jnp.pad(v, (0, width - v.shape[0]))[None]
    early = group.z_pair(early, group.z(early, 1))
    early = join([early, group.z(early, 2)])
    late, early = lax.optimization_barrier((late, early))
    late_got = group.z(late, 1)
    if group.paired:
        small = jnp.concatenate(
            [
                early[2 * top : 2 * top + 1],
                wide(bias_ada),
                wide(jnp.concatenate([bias_down, gain_one, gain_two])),
                early[2 * top + 3 :],
            ]
        )
        firsts = (
            jnp.concatenate([early[:top], ada[:cut]]),
            jnp.concatenate([early[top : 2 * top], ada[cut:], small]),
        )
        came = [group.bit(v, way[0]) for v, way in zip(firsts, ways)]
        late_got, came = lax.optimization_barrier((late_got, came))
        late = group.z_pair(late, late_got)
        late_far = group.z(late, 2)
        near = [group.gather_pair(v, got, way) for v, got, way in zip(firsts, came, ways)]
        inputs, late_far, near = lax.optimization_barrier((inputs, late_far, near))
        x_parts = group.to_owner(inputs, False)
        qk, vo = (group.gather_cores([jnp.concatenate(p)], way) for p, way in zip(near, ways))
        late = join([late_far, late])
        late, qk.parts, vo.parts = lax.optimization_barrier((late, qk.parts, vo.parts))
        lates = late[:rows], late[rows:]
        came = [group.bit(v, way[0]) for v, way in zip(lates, ways)]
        vec, bias_hidden, ada_all = modulate(me, act, qk, vo, tensor_count, rows)
        out_grad, x_parts, came = lax.optimization_barrier((out_grad, x_parts, came))
        g_parts = group.to_owner(out_grad, True)
        near = [group.gather_pair(v, got, way) for v, got, way in zip(lates, came, ways)]
    else:
        x_parts = group.to_owner(inputs, False)
        g_parts = group.to_owner(out_grad, True)
        late = group.z_pair(late, late_got)
        late = join([group.z(late, 2), late])
        flat = lambda v: group.whole(v.reshape(2, rows, width), 1).reshape(1, 2 * width, width)
        qk, vo = Held([flat(early[: 2 * rows])], [(0,)]), Held([flat(early[2 * rows :])], [(0,)])
        up, dn = (Held([group.whole(v, 0)[None]], [(0,)]) for v in (late[:rows], late[rows:]))
        w_all = group.whole(w_ada, 1)
        modulation = jnp.dot(
            act, w_all.astype(F32), precision=PRECISE, preferred_element_type=F32
        ) + group.whole(bias_ada, 0).astype(F32)
        small = group.whole(jnp.stack([bias_down, gain_one, gain_two]), 1).astype(F32)
        vec = jnp.concatenate([modulation.reshape(6, width), small, jnp.zeros((7, width), F32)])
        bias_hidden = group.whole(bias_up, 1)
        bias_hidden = jnp.concatenate([group.z(bias_hidden, k) for k in (2, 3, 0, 1)]).astype(F32)

    order = r ^ jnp.arange(tensor_count)
    mixed = lambda v: own_row(v).reshape(tensor_count, part)[order].reshape(-1)
    docs, places = mixed(doc_ids), mixed(positions)
    doc_row, doc_col = docs[None, :], docs[:, None]
    frequencies = 10000.0 ** (-2.0 * jnp.arange(HEAD // 2, dtype=F32) / HEAD)
    turned = places.astype(F32)[:, None] * frequencies[None, :]
    cosine, sine = jnp.cos(turned), jnp.sin(turned)
    nothing = jnp.zeros_like(sine)
    cos_flat = jnp.concatenate([cosine] * 4, axis=1)
    sin_a = jnp.concatenate([-sine, nothing] * 2, axis=1)
    sin_b = jnp.concatenate([nothing, sine] * 2, axis=1)
    cos_t, sin_t = cosine.T, sine.T

    n_t, q, k, v, q_t, k_t, v_t = qkv(me, x_parts, vec, cos_flat, sin_a, sin_b, qk, vo)
    mix_t, log_sum = attend(q, k, v_t, doc_row, doc_col)
    if group.paired:
        mix_t, near, g_parts = lax.optimization_barrier((mix_t, near, g_parts))
        up, dn = (group.gather_cores(p, way) for p, way in zip(near, ways))
    att, n_two, n_two_t, d_down, d_down_t, d_bias_down = middle(
        me, x_parts, g_parts, mix_t, vec, vo
    )
    size = w_up.shape[1]
    feed_args = (me, n_two, n_two_t, d_down, d_down_t, bias_hidden, up, dn)

    down, d_n, d_bias_a, *grads = feed(*feed_args, 0, None, 2 * size)
    sum_a = Sum(group, *grads)
    down, d_n, d_bias_b, *grads = feed(*feed_args, 2 * size, (down, d_n), 2 * size)
    down = tie(down, sum_a)
    exchange(sum_a)
    sum_b = Sum(group, *grads)
    *out_parts, d_mid, d_mix, d_mix_t, sums, d_att_t = turn(
        me, x_parts, g_parts, att, down, d_n, mix_t, vec, vo
    )
    d_mix, out_parts = tie((d_mix, out_parts), sum_a, sum_b)
    came = group.to_holder(out_parts)
    exchange(sum_a, sum_b)
    dq_t, dk_t, dv_t = attend_back(
        q, k, v, d_mix, q_t, k_t, d_mix_t, mix_t, log_sum, doc_row, doc_col, cos_t, sin_t, 0,
        q.shape[1] // PAIR,
    )
    dq_t, came = tie((dq_t, came), sum_a, sum_b)
    block_out = group.held_rows(came)
    sum_a.settle()
    exchange(sum_b)
    far_up = group.z(sum_a.total[0].astype(BF16), 2)
    grads = weight_grads(me, n_t, dq_t, dk_t, dv_t, d_att_t, mix_t, blocks)
    d_mid, grads, far_up, last = tie((d_mid, grads, far_up, sum_a.total[1]), sum_b)
    far_dn = group.z(last.astype(BF16), 2)
    sum_w = Sum(group, *grads)
    *in_parts, sums_one = first(me, x_parts, d_mid, vec, dq_t, dk_t, dv_t, qk, vo)

    in_parts, sums_one, far_dn = tie((in_parts, sums_one, far_dn), sum_w)
    came = group.to_holder(in_parts)
    exchange(sum_w)
    sum_b.settle()
    near = jnp.stack(sum_b.total) + jnp.stack([far_up, far_dn]).astype(F32)
    sums_one, near = tie((sums_one, near), sum_w)
    exchange(sum_w)
    d_bias = jnp.concatenate([d_bias_b.reshape(2, -1), d_bias_a.reshape(2, -1)])
    edge = mod_width + 3 * rows
    if group.paired:
        table = gather_up(
            vec, ada_all, sums, sums_one, d_bias_down, d_bias, act, cond, dp_count,
            edge + tensor_count * rows + 2 * cond_size - (edge + tensor_count * rows) % cond_size,
        )
    else:
        d_gate_2, norm_2, d_shift_2, d_gate_1 = (sums[n : n + 1] for n in range(4))
        norm_1, d_shift_1 = sums_one[:1], sums_one[1:]
        d_mod = [
            d_shift_1, norm_1 * vec[GAIN_1], d_gate_1, d_shift_2, norm_2 * vec[GAIN_2], d_gate_2
        ]
        others = [norm_1 * (1.0 + vec[SCALE_1]), norm_2 * (1.0 + vec[SCALE_2]), d_bias_down]
        sliced = lambda t: t.reshape(dp_count, -1)
        d_mod = jnp.concatenate(d_mod, axis=1)
        d_cond = lax.dot_general(
            d_mod,
            w_all.astype(F32),
            (((1,), (1,)), ((), ())),
            precision=PRECISE,
            preferred_element_type=F32,
        ) * silu_slope(cond)
        table = jnp.concatenate(
            [sliced(d_mod)]
            + [sliced(t) for t in others]
            + [sliced(t) for t in d_bias]
            + [jnp.broadcast_to(act, (dp_count, cond_size))],
            axis=1,
        )
        last = jnp.pad(d_cond, ((0, 0), (0, table.shape[1] - cond_size)))
        table = jnp.concatenate([table, last])
    table, came = tie((table, came), sum_w)
    sum_w.settle()
    input_grad = group.held_rows(came)
    half = near.shape[-1] // 2
    table_got = group.z(table, 1)
    feeds = group.z(near[..., half:].astype(BF16), 1)
    near_w, far_w = sum_w.total
    far_w = group.z(far_w.astype(BF16), 2)
    table_got, far_w, feeds = lax.optimization_barrier((table_got, far_w, feeds))
    grad_up, grad_down = near[..., :half] + feeds.astype(F32)
    near_w = near_w + far_w.astype(F32)
    grad = near_w[..., :cols] + group.z(near_w[..., cols:].astype(BF16), 1).astype(F32)
    grad_qkv, grad_out = grad[:3], grad[3].T
    tables = jnp.stack([table, table_got])
    tables = jnp.concatenate([tables, group.z(tables, 2)]).transpose(1, 0, 2)[:, order]
    arrived = group.swap(tables[:dp_count])
    totals = jnp.sum(arrived[..., :edge], axis=(0, 1))
    biases = arrived[..., edge : edge + tensor_count * rows].reshape(
        dp_count, tensor_count, tensor_count, rows
    )
    wanted = (jnp.arange(tensor_count) == order[:, None])[None, :, :, None]
    grad_bias_up = jnp.sum(jnp.where(wanted, biases, 0.0), axis=(0, 1, 2))
    grad_bias_ada = totals[:mod_width]
    grad_gain_one, grad_gain_two, grad_bias_down = (
        totals[mod_width + n * rows : mod_width + (n + 1) * rows] for n in range(3)
    )
    arrived = arrived.reshape(dp_count * tensor_count, -1)
    grad_ada = lax.dot_general(
        arrived[:, -cond_size:],
        arrived[:, :mod_width],
        (((0,), (0,)), ((), ())),
        precision=PRECISE,
        preferred_element_type=F32,
    )
    cond_grad = jnp.take(
        tables[dp_count, :, :cond_size], jnp.arange(per_dp) + d % 2, axis=0
    )
    return (
        block_out,
        input_grad,
        cond_grad,
        grad_qkv,
        grad_out,
        grad_up,
        grad_bias_up[None],
        grad_down.T,
        grad_bias_down,
        grad_gain_one,
        grad_gain_two,
        grad_ada,
        grad_bias_ada,
    )


def solution(mesh):
    return jax.shard_map(
        shards,
        mesh=mesh,
        in_specs=(
            P("dp", "tensor", None),
            P("dp", None),
            P("dp", None),
            P("dp", None),
            P(None, "dp", "tensor"),
            P("tensor", "dp"),
            P("dp", "tensor"),
            P("tensor", "dp"),
            P("tensor", "dp"),
            P("dp"),
            P("dp"),
            P("dp"),
            P(None, "dp"),
            P("dp"),
            P("dp", "tensor", None),
        ),
        out_specs=(
            P("dp", "tensor", None),
            P("dp", "tensor", None),
            P("dp", None),
            P(None, "dp", "tensor"),
            P("tensor", "dp"),
            P("dp", "tensor"),
            P("tensor", "dp"),
            P("tensor", "dp"),
            P("dp"),
            P("dp"),
            P("dp"),
            P(None, "dp"),
            P("dp"),
        ),
        check_vma=False,
    )
```

time: 580 us -> 421 us (0.73)
  waiting for transfers between devices: 187 us -> 90.3 us
  starting transfers between devices: 157 us -> 79.7 us
  Pallas kernels: 166 us -> 174 us
    ppermute x52 -> x30, waiting for transfers between devices: 69.3 us -> 10.1 us  [bit(): return lax.ppermute(v, 'dp', [(i, i ^ 1 << b) for i in range(self.dp)])]
    ppermute x34 -> x6, waiting for transfers between devices: 38.5 us -> 4.19 us  [to_holder(): came.append(lax.ppermute(parts[k], BOTH, pairs))]
    ppermute x34 -> x6, starting transfers between devices: 49 us -> 19.8 us  [to_holder(): came.append(lax.ppermute(parts[k], BOTH, pairs))]
    ppermute x24 -> x11, starting transfers between devices: 48.4 us -> 21 us  [z(): return lax.ppermute(v, 'tensor', [(i, i ^ k) for i in range(self.tensor)])]
    ppermute x6, waiting for transfers between devices: 24.3 us -> 7.18 us  [to_owner(): parts.append(lax.ppermute(sent, BOTH, pairs))]
    ppermute x6, starting transfers between devices: 28.3 us -> 12.5 us  [to_owner(): parts.append(lax.ppermute(sent, BOTH, pairs))]
    ppermute x24 -> x11, waiting for transfers between devices: 54.8 us -> 68.9 us  [z(): return lax.ppermute(v, 'tensor', [(i, i ^ k) for i in range(self.tensor)])]
    add x5 -> x15, other arithmetic: 4.32 us -> 14.3 us  [the longest x11 13 us: settle(): t.astype(F32) + flight.value[at].astype(F32)]
  transfers between devices with their start and end apart: 116 -> 53, of which waited for: 40 -> 18; matrix products, arithmetic and copies ran while one was open for 9% -> 10% of each run, Pallas kernels for 9% -> 36%
where the time goes in v2:
time: 421 us; the launch traced here: 414 us
  Pallas kernels  174 us (41%)
  waiting for transfers between devices  90.3 us (21%)
  starting transfers between devices  79.7 us (19%)
  other arithmetic  41.4 us (10%)
  local copies, waits for them, and re-layouts  24.7 us (6%)
    ppermute x11, waiting for transfers between devices, z(): return lax.ppermute(v, 'tensor', [(i, i ^ k) for i in range(self.tensor)])  68.9 us
    pallas_call x2, Pallas kernels, feed(): pl.pallas_call(partial(feed_kernel, up, dn, steps, first), grid=(steps,),...  51.6 us
    pallas_call x1, Pallas kernels, attend_back(): pl.pallas_call(attend_back_kernel, grid=(count,), in_specs=[flat] * 4 + [...  36 us
    ppermute x30, starting transfers between devices, bit(): return lax.ppermute(v, 'dp', [(i, i ^ 1 << b) for i in range(self.dp)])  26.3 us
    pallas_call x1, Pallas kernels, attend(): pl.pallas_call(attend_kernel, grid=(pairs,), in_specs=[flat, flat, turned...  23 us
    ppermute x11, starting transfers between devices, z(): return lax.ppermute(v, 'tensor', [(i, i ^ k) for i in range(self.tensor)])  21 us
    ppermute x6, starting transfers between devices, to_holder(): came.append(lax.ppermute(parts[k], BOTH, pairs))  19.8 us
    add x11, other arithmetic, settle(): t.astype(F32) + flight.value[at].astype(F32)  13 us
  transfers between devices with their start and end apart: 53, of which 18 were waited for; matrix products, arithmetic and copies ran while one was open for 10% of the time, Pallas kernels for 36%

profile of v2, /device:TPU:0, one launch (start us, length us, event | category | flops | bytes accessed | tf_op | source)
XLA Modules:
  0.0 413.6 jit_solution(15161859954442983865)
XLA Ops:
  3.3 3.1 collective-permute-start
  7.4 4.1 collective-permute-done
  12.5 2.8 collective-permute-start.1
  15.6 12.9 %collective-permute-done.1 = bf16[400,384]{1,0:T(8,128)(2,1)S(1)} collective-permute-done((bf16[400,384]{1,0:T(8,128)(2,1)S(1)}, bf16[400,384]{1,0:T(8,128)(2,1)S(1)}, u32[]{:S(2)}, u32[]{:S(2)}) %collective-permute-start.1) | collective-permute-done | bytes 307232 | tf_op jit(solution)/shard_map/ppermute | solution.py:773
  29.1 1.5 collective-permute-start.4
  30.6 1.6 collective-permute-start.3
  32.8 6.7 %collective-permute-done.2 = bf16[192,768]{1,0:T(8,128)(2,1)S(1)} collective-permute-done((bf16[192,768]{1,0:T(8,128)(2,1)S(1)}, bf16[192,768]{1,0:T(8,128)(2,1)S(1)}, u32[]{:S(2)}, u32[]{:S(2)}) %collective-permute-start.2) | collective-permute-done | bytes 294944 | tf_op jit(solution)/shard_map/ppermute | solution.py:773
  40.0 1.6 collective-permute-start.7
  42.4 1.9 collective-permute-start.5
  44.3 24.5 %collective-permute-done.5 = bf16[192,1536]{1,0:T(8,128)(2,1)S(1)} collective-permute-done((bf16[192,1536]{1,0:T(8,128)(2,1)S(1)}, bf16[192,1536]{1,0:T(8,128)(2,1)S(1)}, u32[]{:S(2)}, u32[]{:S(2)}) %collective-permute-start.5) | collective-permute-done | bytes 589856 | tf_op jit(solution)/shard_map/ppermute | solution.py:773
  73.7 2.6 dynamic-slice_bitcast_fusion.3
  77.6 3.2 collective-permute-start.8
  80.8 2.7 collective-permute-start.9
  83.7 1.5 slice_bitcast_fusion.9
  85.3 1.5 collective-permute-start.13
  86.7 1.5 collective-permute-start.14
  88.3 1.9 multiply_sine_fusion
  93.7 1.9 pad_maximum_fusion.15
  95.6 3.8 modulate.1
  99.4 7.2 %collective-permute-done.9.refs_2_ = bf16[256,768]{1,0:T(8,128)(2,1)} collective-permute-done((bf16[256,768]{1,0:T(8,128)(2,1)}, bf16[256,768]{1,0:T(8,128)(2,1)}, u32[]{:S(2)}, u32[]{:S(2)}) %collective-permute-start.9) | collective-permute-done | bytes 393248 | tf_op jit(solution)/shard_map/ppermute | solution.py:794
  107.8 1.6 collective-permute-start.16
  109.3 2.2 pad_maximum_fusion.3.refs_5_.refs_7_
  111.5 1.5 collective-permute-start.15
  113.9 1.9 collective-permute-start.17
  115.8 1.9 collective-permute-start.18
  117.7 1.5 collective-permute-start.19
  119.2 11.8 %qkv.1 = (bf16[768,1024]{1,0:T(8,128)(2,1)}, bf16[1024,768]{1,0:T(8,128)(2,1)}, bf16[1024,768]{1,0:T(8,128)(2,1)}, bf16[1024,768]{1,0:T(8,128)(2,1)}, bf16[768,1...) custom-call(s32[1]{0:T(128)} %bitcast.me, bf16[256,768]{1,0:T(8,128)(2,1)} %get-tuple-element.149.refs_0_, ...), custom_call_target="tpu_custom_call" | custom-call | flops 3623878656 | bytes 16000000 | tf_op jit(solution)/shard_map/qkv/pallas_call | solution.py:133
  131.1 23.0 %attend.1 = (bf16[768,1024]{1,0:T(8,128)(2,1)}, f32[6,2,1024]{2,1,0:T(2,128)}) custom-call(bf16[1024,768]{1,0:T(8,128)(2,1)} %get-tuple-element.158.q, bf16[1024,768]{1,0:T(8,128)(2,1)} %get-tuple-element.159.k, bf16[768,1024]{1,0:T(8,128)(2,1)} %get-tuple-element.161.v_t, s32[1,1024]{1,0:T(1,128)} %bitcast.204, s32[1024,1]{1,0:T(8,128)} %bitcast.180), custom_call_target="tpu_custom_call" | custom-call | flops 12884901888 | bytes 8000000 | tf_op jit(solution)/shard_map/attend/pallas_call | solution.py:179
  156.3 8.6 %middle.1 = (f32[1024,768]{1,0:T(8,128)}, bf16[1024,768]{1,0:T(8,128)(2,1)}, bf16[768,1024]{1,0:T(8,128)(2,1)}, bf16[1024,768]{1,0:T(8,128)(2,1)}, bf16[768,1024]{1,0:T(8,128)(2,1)}, /*index=5*/f32[1,768]{1,0:T(1,128)}) custom-call(s32[1]{0:T(128)} %bitcast.me, bf16[256,768]{1,0:T(8,128)(2,1)} %get-tuple-element.149.refs_0_, ...), custom_call_target="tpu_custom_call" | custom-call | flops 1207959552 | bytes 16000000 | tf_op jit(solution)/shard_map/middle/pallas_call | solution.py:248
  165.0 24.8 %feed.2 = (f32[1024,768]{1,0:T(8,128)}, f32[1024,768]{1,0:T(8,128)}, f32[3,1,512]{2,1,0:T(1,128)}, bf16[2,4,96,1536]{3,2,1,0:T(8,128)(2,1)}, bf16[2,4,96,1536]{3,2,1,0:T(8,128)(2,1)}) custom-call(s32[1]{0:T(128)} %bitcast.me, bf16[1024,768]{1,0:T(8,128)(2,1)} %get-tuple-element.172.refs_0_, bf16[768,1024]{1,0:T(8,128)(2,1)} %get-tuple-element.173.refs_1_, ...), custom_call_target="tpu_custom_call" | custom-call | flops 14495514624 | bytes 20000000 | tf_op jit(solution)/shard_map/feed/pallas_call | solution.py:367
  190.3 26.8 %feed.3 = (f32[1024,768]{1,0:T(8,128)}, f32[1024,768]{1,0:T(8,128)}, f32[3,1,512]{2,1,0:T(1,128)}, bf16[2,4,96,1536]{3,2,1,0:T(8,128)(2,1)}, bf16[2,4,96,1536]{3,2,1,0:T(8,128)(2,1)}) custom-call(s32[1]{0:T(128)} %bitcast.me, bf16[1024,768]{1,0:T(8,128)(2,1)} %get-tuple-element.172.refs_0_, bf16[768,1024]{1,0:T(8,128)(2,1)} %get-tuple-element.173.refs_1_, ...), custom_call_target="tpu_custom_call" | custom-call | flops 14495514624 | bytes 20000000 | tf_op jit(solution)/shard_map/feed/pallas_call | solution.py:367
  217.3 1.4 copy-done.14
  218.7 3.0 convert_add_fusion.4
  221.7 1.4 copy-done.2
  226.1 12.5 %turn.1 = (bf16[256,768]{1,0:T(8,128)(2,1)}, bf16[256,768]{1,0:T(8,128)(2,1)}, bf16[256,768]{1,0:T(8,128)(2,1)}, bf16[256,768]{1,0:T(8,128)(2,1)}, f32[1024,768]...) custom-call(s32[1]{0:T(128)} %bitcast.me, ...), custom_call_target="tpu_custom_call" | custom-call | flops 1207959552 | bytes 24000000 | tf_op jit(solution)/shard_map/turn/pallas_call | solution.py:447
  239.8 1.3 fusion.5
  241.7 2.3 convert_add_fusion.2
  249.8 5.6 %collective-permute-start.28 = (bf16[256,768]{1,0:T(8,128)(2,1)}, bf16[256,768]{1,0:T(8,128)(2,1)}, u32[]{:S(2)}, u32[]{:S(2)}) collective-permute-start(bf16[256,768]{1,0:T(8,128)(2,1)} %get-tuple-element.202), channel_id=1, source_target_pairs={{0,1},{1,0},{2,3},{5,4},{6,7},{7,6},{8,9},{9,8},{10,11},{13,12},{1... | collective-permute-start | bytes 1179656 | tf_op jit(solution)/shard_map/ppermute | solution.py:806
  255.4 3.6 collective-permute-start.29
  259.0 2.0 collective-permute-start.30
  261.0 36.0 %attend_back.1 = (bf16[768,1024]{1,0:T(8,128)(2,1)}, bf16[768,1024]{1,0:T(8,128)(2,1)}, bf16[768,1024]{1,0:T(8,128)(2,1)}) custom-call(bf16[1024,768]{1,0:T(8,128)(2,1)} %get-tuple-element.158.q, bf16[1024,768]{1,0:T(8,128)(2,1)} %get-tuple-element.159.k, bf16[1024,768]{1,0:T(8,128)(2,1)} %get-tuple-element.160.v, ...), custom_call_target="tpu_custom_call" | custom-call | flops 22548578304 | bytes 14000000 | tf_op jit(solution)/shard_map/attend_back/pallas_call | solution.py:519
  298.3 1.9 fusion.15
  300.3 1.3 fusion.4
  305.5 11.4 %weight_grads.1 = (bf16[2,4,4,96,384]{4,3,2,1,0:T(8,128)(2,1)}, bf16[2,4,4,96,384]{4,3,2,1,0:T(8,128)(2,1)}) custom-call(s32[1]{0:T(128)} %bitcast.me, bf16[768,1024]{1,0:T(8,128)(2,1)} %get-tuple-element.216.n_t, bf16[768,1024]{1,0:T(8,128)(2,1)} %get-tuple-element.217.dq_t.refs_6_, bf16[768,1024]{1,0:T(8,128)(2,1)} %get-tuple-element.218.dk_t.refs_7_, ...), custom_call_target="tpu_custom_call" | custom-call | flops 4831838208 | bytes 14000000 | tf_op jit(solution)/shard_map/weight_grads/pallas_call | solution.py:748
  319.7 1.8 collective-permute-start.36
  321.5 12.6 %first.1 = (bf16[256,768]{1,0:T(8,128)(2,1)}, bf16[256,768]{1,0:T(8,128)(2,1)}, bf16[256,768]{1,0:T(8,128)(2,1)}, bf16[256,768]{1,0:T(8,128)(2,1)}, f32[2,768]{1,0:T(2,128)}) custom-call(s32[1]{0:T(128)} %bitcast.me, bf16[256,768]{1,0:T(8,128)(2,1)} %get-tuple-element.149.refs_0_, bf16[256,768]{1,0:T(8,128)(2,1)} %collective-permute-done.8.refs_1_, ...), custom_call_target="tpu_custom_call" | custom-call | flops 3623878656 | bytes 20000000 | tf_op jit(solution)/shard_map/first/pallas_call | solution.py:579
  334.1 2.5 collective-permute-done.36
  336.5 2.3 convert_add_fusion
  340.2 1.6 collective-permute-start.39
  341.8 1.9 collective-permute-start.40
  343.8 5.1 %collective-permute-start.41 = (bf16[256,768]{1,0:T(8,128)(2,1)}, bf16[256,768]{1,0:T(8,128)(2,1)S(1)}, u32[]{:S(2)}, u32[]{:S(2)}) collective-permute-start(bf16[256,768]{1,0:T(8,128)(2,1)} %get-tuple-element.246), channel_id=1, source_target_pairs={{0,2},{1,3},{2,0},{5,7},{6,4},{7,5},{8,10},{9,11},{10,8},{13,15},{... | collective-permute-start | bytes 1179656 | tf_op jit(solution)/shard_map/ppermute | solution.py:806
  348.9 1.6 collective-permute-start.42
  351.6 2.4 collective-permute-done.38
  356.9 1.5 collective-permute-start.43
  358.5 1.4 pad_maximum_fusion
  361.2 2.3 gather_up.1
  363.5 4.2 %collective-permute-done.40 = bf16[256,768]{1,0:T(8,128)(2,1)S(1)} collective-permute-done((bf16[256,768]{1,0:T(8,128)(2,1)}, bf16[256,768]{1,0:T(8,128)(2,1)S(1)}, u32[]{:S(2)}, u32[]{:S(2)}) %collective-permute-start.40) | collective-permute-done | bytes 393248 | tf_op jit(solution)/shard_map/ppermute | solution.py:806
  368.8 8.3 %collective-permute-start.46 = (bf16[4,96,384]{2,1,0:T(8,128)(2,1)S(1)}, bf16[4,96,384]{2,1,0:T(8,128)(2,1)S(1)}, u32[]{:S(2)}, u32[]{:S(2)}) collective-permute-start(bf16[4,96,384]{2,1,0:T(8,128)(2,1)S(1)} %fusion.18), channel_id=1, source_target_pairs={{0,2},{1,3},{2,0},{3,1},{4,6},{5,7},{6,4},{7,5},{8,10},{9,11},{10,... | collective-permute-start | bytes 884744 | tf_op jit(solution)/shard_map/ppermute | solution.py:773
  378.6 6.3 %collective-permute-done.45 = f32[16,1408]{1,0:T(8,128)S(1)} collective-permute-done((f32[16,1408]{1,0:T(8,128)}, f32[16,1408]{1,0:T(8,128)S(1)}, u32[]{:S(2)}, u32[]{:S(2)}) %collective-permute-start.45) | collective-permute-done | bytes 90144 | tf_op jit(solution)/shard_map/ppermute | solution.py:773
  384.9 5.0 %collective-permute-done.46 = bf16[4,96,384]{2,1,0:T(8,128)(2,1)S(1)} collective-permute-done((bf16[4,96,384]{2,1,0:T(8,128)(2,1)S(1)}, bf16[4,96,384]{2,1,0:T(8,128)(2,1)S(1)}, u32[]{:S(2)}, u32[]{:S(2)}) %collective-permute-start.46) | collective-permute-done | bytes 294944 | tf_op jit(solution)/shard_map/ppermute | solution.py:773
  392.3 5.6 %collective-permute-done.48 = f32[2,16,1408]{2,1,0:T(8,128)S(1)} collective-permute-done((f32[2,16,1408]{2,1,0:T(8,128)S(1)}, f32[2,16,1408]{2,1,0:T(8,128)S(1)}, u32[]{:S(2)}, u32[]{:S(2)}) %collective-permute-start.48) | collective-permute-done | bytes 180256 | tf_op jit(solution)/shard_map/ppermute | solution.py:773
  403.9 1.7 collective-permute-done.51
  406.9 3.4 collective-permute-done.52
  410.4 1.4 fusion.23
  (276 shorter events, 60.3 us)
Async XLA Ops:
  0.6 27.9 %copy-start.19 = (bf16[3,96,192]{2,1,0:T(8,128)(2,1)S(1)}, bf16[3,96,192]{2,1,0:T(8,128)(2,1)}, u32[]{:S(2)}) copy-start(bf16[3,96,192]{2,1,0:T(8,128)(2,1)} %param.19) | copy-start | bytes 331780
  0.7 14.8 %copy-start.43 = (bf16[96]{0:T(256)(128)(2,1)S(1)}, bf16[96]{0:T(256)(128)(2,1)}, u32[]{:S(2)}) copy-start(bf16[96]{0:T(256)(128)(2,1)} %param.24) | copy-start | bytes 580
  0.7 14.8 %copy-start.42 = (bf16[96]{0:T(256)(128)(2,1)S(1)}, bf16[96]{0:T(256)(128)(2,1)}, u32[]{:S(2)}) copy-start(bf16[96]{0:T(256)(128)(2,1)} %param.25) | copy-start | bytes 580
  0.7 14.9 %copy-start.30 = (bf16[768,96]{0,1:T(8,128)(2,1)S(1)}, bf16[768,96]{0,1:T(8,128)(2,1)}, u32[]{:S(2)}) copy-start(bf16[768,96]{0,1:T(8,128)(2,1)} %param.23) | copy-start | bytes 442372
  0.7 14.9 %copy-start.31 = (bf16[96,768]{1,0:T(8,128)(2,1)S(1)}, bf16[96,768]{1,0:T(8,128)(2,1)}, u32[]{:S(2)}) copy-start(bf16[96,768]{1,0:T(8,128)(2,1)} %param.21) | copy-start | bytes 442372
  3.3 8.2 %collective-permute-start = (bf16[400,192]{1,0:T(8,128)(2,1)S(1)}, bf16[400,192]{1,0:T(8,128)(2,1)S(1)}, u32[]{:S(2)}, u32[]{:S(2)}) collective-permute-start(bf16[400,192]{1,0:T(8,128)(2,1)S(1)} %pad_maximum_fusion.19), channel_id=1, source_target_pairs={{0,1},{1,0},{2,3},{3,2},{4,5},{5,4},{6,7},{7,6},{8,9},{9,8},{10,11... | collective-permute-start | bytes 460808 | tf_op jit(solution)/shard_map/ppermute | solution.py:773
  12.5 16.0 %collective-permute-start.1 = (bf16[400,384]{1,0:T(8,128)(2,1)S(1)}, bf16[400,384]{1,0:T(8,128)(2,1)S(1)}, u32[]{:S(2)}, u32[]{:S(2)}) collective-permute-start(bf16[400,384]{1,0:T(8,128)(2,1)S(1)} %pad_maximum_fusion.17), channel_id=1, source_target_pairs={{0,2},{1,3},{2,0},{3,1},{4,6},{5,7},{6,4},{7,5},{8,10},{9,11},{10,... | collective-permute-start | bytes 921608 | tf_op jit(solution)/shard_map/ppermute | solution.py:773
  15.6 26.7 %copy-start.9 = (bf16[192,768]{1,0:T(8,128)(2,1)}, bf16[192,768]{1,0:T(8,128)(2,1)S(1)}, u32[]{:S(2)}) copy-start(bf16[192,768]{1,0:T(8,128)(2,1)S(1)} %pad_maximum_fusion.18) | copy-start | bytes 884740
  29.1 10.8 %collective-permute-start.4 = (bf16[256,768]{1,0:T(8,128)(2,1)S(1)}, bf16[256,768]{1,0:T(8,128)(2,1)S(1)}, u32[]{:S(2)}, u32[]{:S(2)}) collective-permute-start(bf16[256,768]{1,0:T(8,128)(2,1)S(1)} %concatenate.77), channel_id=1, source_target_pairs={{0,16},{4,20},{8,24},{12,28},{16,0},{20,4},{24,8},{28,12},{1,17},{... | collective-permute-start | bytes 1179656 | tf_op jit(solution)/shard_map/ppermute | solution.py:767
  30.6 9.3 %collective-permute-start.3 = (bf16[240,768]{1,0:T(8,128)(2,1)S(1)}, bf16[240,768]{1,0:T(8,128)(2,1)S(1)}, u32[]{:S(2)}, u32[]{:S(2)}) collective-permute-start(bf16[240,768]{1,0:T(8,128)(2,1)S(1)} %get-tuple-element.333), channel_id=1, source_target_pairs={{0,8},{4,12},{8,0},{12,4},{16,24},{20,28},{24,16},{28,20},{1,9},{5... | collective-permute-start | bytes 1105928 | tf_op jit(solution)/shard_map/ppermute | solution.py:767
  32.2 7.4 %collective-permute-start.2 = (bf16[192,768]{1,0:T(8,128)(2,1)S(1)}, bf16[192,768]{1,0:T(8,128)(2,1)S(1)}, u32[]{:S(2)}, u32[]{:S(2)}) collective-permute-start(bf16[192,768]{1,0:T(8,128)(2,1)S(1)} %pad_maximum_fusion.18), channel_id=1, source_target_pairs={{0,1},{1,0},{2,3},{3,2},{4,5},{5,4},{6,7},{7,6},{8,9},{9,8},{10,11... | collective-permute-start | bytes 884744 | tf_op jit(solution)/shard_map/ppermute | solution.py:773
  40.0 29.7 %collective-permute-start.7 = (bf16[2,256,768]{2,1,0:T(8,128)(2,1)S(1)}, bf16[2,256,768]{2,1,0:T(8,128)(2,1)S(1)}, u32[]{:S(2)}, u32[]{:S(2)}) collective-permute-start(bf16[2,256,768]{2,1,0:T(8,128)(2,1)S(1)} %pad_maximum_fusion.9), channel_id=1, source_target_pairs={{0,8},{4,12},{8,0},{12,4},{16,24},{20,28},{24,16},{28,20},{1,9},{5... | collective-permute-start | bytes 2359304 | tf_op jit(solution)/shard_map/ppermute | solution.py:767
  41.6 27.2 %collective-permute-start.6 = (bf16[2,240,768]{2,1,0:T(8,128)(2,1)S(1)}, bf16[2,240,768]{2,1,0:T(8,128)(2,1)S(1)}, u32[]{:S(2)}, u32[]{:S(2)}) collective-permute-start(bf16[2,240,768]{2,1,0:T(8,128)(2,1)S(1)} %pad_maximum_fusion.10), channel_id=1, source_target_pairs={{0,16},{4,20},{8,24},{12,28},{16,0},{20,4},{24,8},{28,12},{1,17},{... | collective-permute-start | bytes 2211848 | tf_op jit(solution)/shard_map/ppermute | solution.py:767
  42.4 26.4 %collective-permute-start.5 = (bf16[192,1536]{1,0:T(8,128)(2,1)S(1)}, bf16[192,1536]{1,0:T(8,128)(2,1)S(1)}, u32[]{:S(2)}, u32[]{:S(2)}) collective-permute-start(bf16[192,1536]{1,0:T(8,128)(2,1)S(1)} %pad_maximum_fusion.12), channel_id=1, source_target_pairs={{0,2},{1,3},{2,0},{3,1},{4,6},{5,7},{6,4},{7,5},{8,10},{9,11},{10,... | collective-permute-start | bytes 1769480 | tf_op jit(solution)/shard_map/ppermute | solution.py:773
  69.8 13.9 %collective-permute-start.12 = (bf16[4,256,768]{2,1,0:T(8,128)(2,1)S(1)}, bf16[4,256,768]{2,1,0:T(8,128)(2,1)S(1)}, u32[]{:S(2)}, u32[]{:S(2)}) collective-permute-start(bf16[4,256,768]{2,1,0:T(8,128)(2,1)S(1)} %constant_dynamic-update-slice_fusion.2.refs_2_.refs_10_.refs_13_.refs_11_), channel_id=1, source_target_pairs={{0,4},{4,0},{8,12},{12,8},{16,20},{20,16},{24,28},{28,24},{1,5},{5... | collective-permute-start | bytes 4718600 | tf_op jit(solution)/shard_map/ppermute | solution.py:767
  71.8 11.9 %collective-permute-start.11 = (bf16[4,240,768]{2,1,0:T(8,128)(2,1)}, bf16[4,240,768]{2,1,0:T(8,128)(2,1)}, u32[]{:S(2)}, u32[]{:S(2)}) collective-permute-start(bf16[4,240,768]{2,1,0:T(8,128)(2,1)} %constant_dynamic-update-slice_fusion.refs_0_.refs_8_.refs_9_), channel_id=1, source_target_pairs={{0,4},{4,0},{8,12},{12,8},{16,20},{20,16},{24,28},{28,24},{1,5},{5... | collective-permute-start | bytes 4423688 | tf_op jit(solution)/shard_map/ppermute | solution.py:767
  76.3 23.1 %collective-permute-start.10 = (bf16[256,768]{1,0:T(8,128)(2,1)}, bf16[256,768]{1,0:T(8,128)(2,1)S(1)}, u32[]{:S(2)}, u32[]{:S(2)}) collective-permute-start(bf16[256,768]{1,0:T(8,128)(2,1)} %get-tuple-element.322), channel_id=1, source_target_pairs={{1,2},{2,1},{3,0},{4,7},{5,6},{6,5},{9,10},{10,9},{11,8},{12,15},{... | collective-permute-start | bytes 1179656 | tf_op jit(solution)/shard_map/ppermute | solution.py:794
  77.6 21.8 %collective-permute-start.8 = (bf16[256,768]{1,0:T(8,128)(2,1)}, bf16[256,768]{1,0:T(8,128)(2,1)}, u32[]{:S(2)}, u32[]{:S(2)}) collective-permute-start(bf16[256,768]{1,0:T(8,128)(2,1)} %get-tuple-element.324), channel_id=1, source_target_pairs={{0,1},{1,0},{3,2},{4,5},{6,7},{7,6},{8,9},{9,8},{11,10},{12,13},{1... | collective-permute-start | bytes 1179656 | tf_op jit(solution)/shard_map/ppermute | solution.py:794
  80.8 25.8 %collective-permute-start.9 = (bf16[256,768]{1,0:T(8,128)(2,1)}, bf16[256,768]{1,0:T(8,128)(2,1)}, u32[]{:S(2)}, u32[]{:S(2)}) collective-permute-start(bf16[256,768]{1,0:T(8,128)(2,1)} %get-tuple-element.323), channel_id=1, source_target_pairs={{0,2},{2,0},{3,1},{4,6},{5,7},{7,5},{8,10},{10,8},{11,9},{12,14},{... | collective-permute-start | bytes 1179656 | tf_op jit(solution)/shard_map/ppermute | solution.py:794
  85.3 21.3 %collective-permute-start.13 = (bf16[96,3072]{1,0:T(8,128)(2,1)}, bf16[96,3072]{1,0:T(8,128)(2,1)}, u32[]{:S(2)}, u32[]{:S(2)}) collective-permute-start(bf16[96,3072]{1,0:T(8,128)(2,1)} %get-tuple-element.321), channel_id=1, source_target_pairs={{0,8},{4,12},{8,0},{12,4},{16,24},{20,28},{24,16},{28,20},{1,9},{5... | collective-permute-start | bytes 1769480 | tf_op jit(solution)/shard_map/ppermute | solution.py:767
  86.7 19.8 %collective-permute-start.14 = (bf16[96,3072]{1,0:T(8,128)(2,1)}, bf16[96,3072]{1,0:T(8,128)(2,1)}, u32[]{:S(2)}, u32[]{:S(2)}) collective-permute-start(bf16[96,3072]{1,0:T(8,128)(2,1)} %get-tuple-element.320), channel_id=1, source_target_pairs={{0,16},{4,20},{8,24},{12,28},{16,0},{20,4},{24,8},{28,12},{1,17},{... | collective-permute-start | bytes 1769480 | tf_op jit(solution)/shard_map/ppermute | solution.py:767
  107.7 47.4 %copy-start.22 = (bf16[2,96,3072]{2,1,0:T(8,128)(2,1)}, bf16[2,96,3072]{2,1,0:T(8,128)(2,1)S(1)}, u32[]{:S(2)}) copy-start(bf16[2,96,3072]{2,1,0:T(8,128)(2,1)S(1)} %pad_maximum_fusion.4.refs_9_.refs_11_) | copy-start | bytes 3538948
  107.8 46.4 %collective-permute-start.16 = (bf16[2,96,3072]{2,1,0:T(8,128)(2,1)S(1)}, bf16[2,96,3072]{2,1,0:T(8,128)(2,1)}, u32[]{:S(2)}, u32[]{:S(2)}) collective-permute-start(bf16[2,96,3072]{2,1,0:T(8,128)(2,1)S(1)} %pad_maximum_fusion.4.refs_9_.refs_11_), channel_id=1, source_target_pairs={{0,8},{4,12},{8,0},{12,4},{16,24},{20,28},{24,16},{28,20},{1,9},{5... | collective-permute-start | bytes 3538952 | tf_op jit(solution)/shard_map/ppermute | solution.py:767
  111.5 42.7 %collective-permute-start.15 = (bf16[2,96,3072]{2,1,0:T(8,128)(2,1)}, bf16[2,96,3072]{2,1,0:T(8,128)(2,1)}, u32[]{:S(2)}, u32[]{:S(2)}) collective-permute-start(bf16[2,96,3072]{2,1,0:T(8,128)(2,1)} %pad_maximum_fusion.3.refs_5_.refs_7_), channel_id=1, source_target_pairs={{0,16},{4,20},{8,24},{12,28},{16,0},{20,4},{24,8},{28,12},{1,17},{... | collective-permute-start | bytes 3538952 | tf_op jit(solution)/shard_map/ppermute | solution.py:767
  113.9 40.2 %collective-permute-start.17 = (bf16[256,768]{1,0:T(8,128)(2,1)S(1)}, bf16[256,768]{1,0:T(8,128)(2,1)S(1)}, u32[]{:S(2)}, u32[]{:S(2)}) collective-permute-start(bf16[256,768]{1,0:T(8,128)(2,1)S(1)} %get-tuple-element.316), channel_id=1, source_target_pairs={{0,1},{1,0},{3,2},{4,5},{6,7},{7,6},{8,9},{9,8},{11,10},{12,13},{1... | collective-permute-start | bytes 1179656 | tf_op jit(solution)/shard_map/ppermute | solution.py:794
  115.8 38.3 %collective-permute-start.18 = (bf16[256,768]{1,0:T(8,128)(2,1)S(1)}, bf16[256,768]{1,0:T(8,128)(2,1)S(1)}, u32[]{:S(2)}, u32[]{:S(2)}) collective-permute-start(bf16[256,768]{1,0:T(8,128)(2,1)S(1)} %get-tuple-element.315), channel_id=1, source_target_pairs={{0,2},{2,0},{3,1},{4,6},{5,7},{7,5},{8,10},{10,8},{11,9},{12,14},{... | collective-permute-start | bytes 1179656 | tf_op jit(solution)/shard_map/ppermute | solution.py:794
  117.7 36.4 %collective-permute-start.19 = (bf16[256,768]{1,0:T(8,128)(2,1)S(1)}, bf16[256,768]{1,0:T(8,128)(2,1)S(1)}, u32[]{:S(2)}, u32[]{:S(2)}) collective-permute-start(bf16[256,768]{1,0:T(8,128)(2,1)S(1)} %get-tuple-element.314), channel_id=1, source_target_pairs={{1,2},{2,1},{3,0},{4,7},{5,6},{6,5},{9,10},{10,9},{11,8},{12,15},{... | collective-permute-start | bytes 1179656 | tf_op jit(solution)/shard_map/ppermute | solution.py:794
  131.1 24.6 %copy-start.33 = (f32[4,768]{1,0:T(4,128)S(1)}, f32[4,768]{1,0:T(4,128)}, u32[]{:S(2)}) copy-start(f32[4,768]{1,0:T(4,128)} %get-tuple-element.176) | copy-start | bytes 36868
  154.2 10.8 %collective-permute-start.20 = (bf16[2,96,3072]{2,1,0:T(8,128)(2,1)}, bf16[2,96,3072]{2,1,0:T(8,128)(2,1)}, u32[]{:S(2)}, u32[]{:S(2)}) collective-permute-start(bf16[2,96,3072]{2,1,0:T(8,128)(2,1)} %pad_maximum_fusion.3.refs_5_.refs_7_), channel_id=1, source_target_pairs={{0,4},{4,0},{8,12},{12,8},{16,20},{20,16},{24,28},{28,24},{1,5},{5... | collective-permute-start | bytes 3538952 | tf_op jit(solution)/shard_map/ppermute | solution.py:767
  155.1 9.9 %collective-permute-start.21 = (bf16[2,96,3072]{2,1,0:T(8,128)(2,1)}, bf16[2,96,3072]{2,1,0:T(8,128)(2,1)}, u32[]{:S(2)}, u32[]{:S(2)}) collective-permute-start(bf16[2,96,3072]{2,1,0:T(8,128)(2,1)} %collective-permute-done.15.refs_6_.refs_8_), channel_id=1, source_target_pairs={{0,4},{4,0},{8,12},{12,8},{16,20},{20,16},{24,28},{28,24},{1,5},{5... | collective-permute-start | bytes 3538952 | tf_op jit(solution)/shard_map/ppermute | solution.py:767
  155.2 9.8 %collective-permute-start.22 = (bf16[2,96,3072]{2,1,0:T(8,128)(2,1)S(1)}, bf16[2,96,3072]{2,1,0:T(8,128)(2,1)}, u32[]{:S(2)}, u32[]{:S(2)}) collective-permute-start(bf16[2,96,3072]{2,1,0:T(8,128)(2,1)S(1)} %pad_maximum_fusion.4.refs_9_.refs_11_), channel_id=1, source_target_pairs={{0,4},{4,0},{8,12},{12,8},{16,20},{20,16},{24,28},{28,24},{1,5},{5... | collective-permute-start | bytes 3538952 | tf_op jit(solution)/shard_map/ppermute | solution.py:767
  155.6 9.4 %collective-permute-start.23 = (bf16[2,96,3072]{2,1,0:T(8,128)(2,1)}, bf16[2,96,3072]{2,1,0:T(8,128)(2,1)}, u32[]{:S(2)}, u32[]{:S(2)}) collective-permute-start(bf16[2,96,3072]{2,1,0:T(8,128)(2,1)} %collective-permute-done.16.refs_10_.refs_12_), channel_id=1, source_target_pairs={{0,4},{4,0},{8,12},{12,8},{16,20},{20,16},{24,28},{28,24},{1,5},{5... | collective-permute-start | bytes 3538952 | tf_op jit(solution)/shard_map/ppermute | solution.py:767
  189.8 27.5 %collective-permute-start.24 = (bf16[2,4,96,1536]{3,2,1,0:T(8,128)(2,1)}, bf16[2,4,96,1536]{3,2,1,0:T(8,128)(2,1)S(1)}, u32[]{:S(2)}, u32[]{:S(2)}) collective-permute-start(bf16[2,4,96,1536]{3,2,1,0:T(8,128)(2,1)} %get-tuple-element.184), channel_id=1, source_target_pairs={{0,4},{4,0},{8,12},{12,8},{16,20},{20,16},{24,28},{28,24},{1,5},{5... | collective-permute-start | bytes 7077896 | tf_op jit(solution)/shard_map/ppermute | solution.py:767
  217.1 21.5 %collective-permute-start.27 = (bf16[2,4,96,1536]{3,2,1,0:T(8,128)(2,1)}, bf16[2,4,96,1536]{3,2,1,0:T(8,128)(2,1)S(1)}, u32[]{:S(2)}, u32[]{:S(2)}) collective-permute-start(bf16[2,4,96,1536]{3,2,1,0:T(8,128)(2,1)} %get-tuple-element.194), channel_id=1, source_target_pairs={{0,4},{4,0},{8,12},{12,8},{16,20},{20,16},{24,28},{28,24},{1,5},{5... | collective-permute-start | bytes 7077896 | tf_op jit(solution)/shard_map/ppermute | solution.py:767
  223.2 15.8 %collective-permute-start.25 = (bf16[2,96,1536]{2,1,0:T(8,128)(2,1)S(1)}, bf16[2,96,1536]{2,1,0:T(8,128)(2,1)}, u32[]{:S(2)}, u32[]{:S(2)}) collective-permute-start(bf16[2,96,1536]{2,1,0:T(8,128)(2,1)S(1)} %fusion.9), channel_id=1, source_target_pairs={{0,8},{4,12},{8,0},{12,4},{16,24},{20,28},{24,16},{28,20},{1,9},{5... | collective-permute-start | bytes 1769480 | tf_op jit(solution)/shard_map/ppermute | solution.py:767
  224.3 15.5 %collective-permute-start.26 = (bf16[2,96,1536]{2,1,0:T(8,128)(2,1)S(1)}, bf16[2,96,1536]{2,1,0:T(8,128)(2,1)}, u32[]{:S(2)}, u32[]{:S(2)}) collective-permute-start(bf16[2,96,1536]{2,1,0:T(8,128)(2,1)S(1)} %fusion.6), channel_id=1, source_target_pairs={{0,16},{4,20},{8,24},{12,28},{16,0},{20,4},{24,8},{28,12},{1,17},{... | collective-permute-start | bytes 1769480 | tf_op jit(solution)/shard_map/ppermute | solution.py:767
  245.1 52.0 %collective-permute-start.32 = (bf16[3,96,1536]{2,1,0:T(8,128)(2,1)}, bf16[3,96,1536]{2,1,0:T(8,128)(2,1)}, u32[]{:S(2)}, u32[]{:S(2)}) collective-permute-start(bf16[3,96,1536]{2,1,0:T(8,128)(2,1)} %pad_maximum_fusion.8), channel_id=1, source_target_pairs={{0,8},{4,12},{8,0},{12,4},{16,24},{20,28},{24,16},{28,20},{1,9},{5... | collective-permute-start | bytes 2654216 | tf_op jit(solution)/shard_map/ppermute | solution.py:767
  248.6 48.5 %collective-permute-start.31 = (bf16[3,96,1536]{2,1,0:T(8,128)(2,1)}, bf16[3,96,1536]{2,1,0:T(8,128)(2,1)}, u32[]{:S(2)}, u32[]{:S(2)}) collective-permute-start(bf16[3,96,1536]{2,1,0:T(8,128)(2,1)} %pad_maximum_fusion.7), channel_id=1, source_target_pairs={{0,16},{4,20},{8,24},{12,28},{16,0},{20,4},{24,8},{28,12},{1,17},{... | collective-permute-start | bytes 2654216 | tf_op jit(solution)/shard_map/ppermute | solution.py:767
  249.8 47.3 %collective-permute-start.28 = (bf16[256,768]{1,0:T(8,128)(2,1)}, bf16[256,768]{1,0:T(8,128)(2,1)}, u32[]{:S(2)}, u32[]{:S(2)}) collective-permute-start(bf16[256,768]{1,0:T(8,128)(2,1)} %get-tuple-element.202), channel_id=1, source_target_pairs={{0,1},{1,0},{2,3},{5,4},{6,7},{7,6},{8,9},{9,8},{10,11},{13,12},{1... | collective-permute-start | bytes 1179656 | tf_op jit(solution)/shard_map/ppermute | solution.py:806
  255.4 41.7 %collective-permute-start.29 = (bf16[256,768]{1,0:T(8,128)(2,1)}, bf16[256,768]{1,0:T(8,128)(2,1)}, u32[]{:S(2)}, u32[]{:S(2)}) collective-permute-start(bf16[256,768]{1,0:T(8,128)(2,1)} %get-tuple-element.203), channel_id=1, source_target_pairs={{0,2},{1,3},{2,0},{5,7},{6,4},{7,5},{8,10},{9,11},{10,8},{13,15},{... | collective-permute-start | bytes 1179656 | tf_op jit(solution)/shard_map/ppermute | solution.py:806
  259.0 38.1 %collective-permute-start.30 = (bf16[256,768]{1,0:T(8,128)(2,1)}, bf16[256,768]{1,0:T(8,128)(2,1)}, u32[]{:S(2)}, u32[]{:S(2)}) collective-permute-start(bf16[256,768]{1,0:T(8,128)(2,1)} %get-tuple-element.204), channel_id=1, source_target_pairs={{0,3},{1,2},{2,1},{5,6},{6,5},{7,4},{8,11},{9,10},{10,9},{13,14},{... | collective-permute-start | bytes 1179656 | tf_op jit(solution)/shard_map/ppermute | solution.py:806
  302.8 14.1 %collective-permute-start.35 = (bf16[1,96,1536]{2,1,0:T(8,128)(2,1)S(1)}, bf16[1,96,1536]{2,1,0:T(8,128)(2,1)S(1)}, u32[]{:S(2)}, u32[]{:S(2)}) collective-permute-start(bf16[1,96,1536]{2,1,0:T(8,128)(2,1)S(1)} %slice.465), channel_id=1, source_target_pairs={{0,8},{4,12},{8,0},{12,4},{16,24},{20,28},{24,16},{28,20},{1,9},{5... | collective-permute-start | bytes 884744 | tf_op jit(solution)/shard_map/ppermute | solution.py:767
  303.8 13.1 %collective-permute-start.34 = (bf16[1,96,1536]{2,1,0:T(8,128)(2,1)S(1)}, bf16[1,96,1536]{2,1,0:T(8,128)(2,1)S(1)}, u32[]{:S(2)}, u32[]{:S(2)}) collective-permute-start(bf16[1,96,1536]{2,1,0:T(8,128)(2,1)S(1)} %slice.466), channel_id=1, source_target_pairs={{0,16},{4,20},{8,24},{12,28},{16,0},{20,4},{24,8},{28,12},{1,17},{... | collective-permute-start | bytes 884744 | tf_op jit(solution)/shard_map/ppermute | solution.py:767
  304.4 13.3 %collective-permute-start.33 = (bf16[96,1536]{1,0:T(8,128)(2,1)S(1)}, bf16[96,1536]{1,0:T(8,128)(2,1)}, u32[]{:S(2)}, u32[]{:S(2)}) collective-permute-start(bf16[96,1536]{1,0:T(8,128)(2,1)S(1)} %fusion.17), channel_id=1, source_target_pairs={{0,2},{1,3},{2,0},{3,1},{4,6},{5,7},{6,4},{7,5},{8,10},{9,11},{10,... | collective-permute-start | bytes 884744 | tf_op jit(solution)/shard_map/ppermute | solution.py:773
  305.5 15.9 %copy-start.7 = (f32[2,96,1536]{2,1,0:T(8,128)S(1)}, f32[2,96,1536]{2,1,0:T(8,128)}, u32[]{:S(2)}) copy-start(f32[2,96,1536]{2,1,0:T(8,128)} %copy-done.6) | copy-start | bytes 3538948
  317.6 18.9 %collective-permute-start.37 = (bf16[2,4,4,96,384]{4,3,2,1,0:T(8,128)(2,1)}, bf16[2,4,4,96,384]{4,3,2,1,0:T(8,128)(2,1)}, u32[]{:S(2)}, u32[]{:S(2)}) collective-permute-start(bf16[2,4,4,96,384]{4,3,2,1,0:T(8,128)(2,1)} %get-tuple-element.232), channel_id=1, source_target_pairs={{0,4},{4,0},{8,12},{12,8},{16,20},{20,16},{24,28},{28,24},{1,5},{5... | collective-permute-start | bytes 7077896 | tf_op jit(solution)/shard_map/ppermute | solution.py:767
  319.7 16.8 %collective-permute-start.36 = (bf16[96,1536]{1,0:T(8,128)(2,1)}, bf16[96,1536]{1,0:T(8,128)(2,1)S(1)}, u32[]{:S(2)}, u32[]{:S(2)}) collective-permute-start(bf16[96,1536]{1,0:T(8,128)(2,1)} %fusion.15), channel_id=1, source_target_pairs={{0,2},{1,3},{2,0},{3,1},{4,6},{5,7},{6,4},{7,5},{8,10},{9,11},{10,... | collective-permute-start | bytes 884744 | tf_op jit(solution)/shard_map/ppermute | solution.py:773
  321.5 15.0 %copy-start.11 = (bf16[2,4,4,96,384]{4,3,2,1,0:T(8,128)(2,1)S(1)}, bf16[2,4,4,96,384]{4,3,2,1,0:T(8,128)(2,1)}, u32[]{:S(2)}) copy-start(bf16[2,4,4,96,384]{4,3,2,1,0:T(8,128)(2,1)} %get-tuple-element.238) | copy-start | bytes 7077892
  338.9 15.0 %collective-permute-start.38 = (bf16[2,4,96,384]{3,2,1,0:T(8,128)(2,1)S(1)}, bf16[2,4,96,384]{3,2,1,0:T(8,128)(2,1)S(1)}, u32[]{:S(2)}, u32[]{:S(2)}) collective-permute-start(bf16[2,4,96,384]{3,2,1,0:T(8,128)(2,1)S(1)} %fusion.11), channel_id=1, source_target_pairs={{0,8},{4,12},{8,0},{12,4},{16,24},{20,28},{24,16},{28,20},{1,9},{5... | collective-permute-start | bytes 1769480 | tf_op jit(solution)/shard_map/ppermute | solution.py:767
  340.2 14.8 %collective-permute-start.39 = (bf16[2,4,96,384]{3,2,1,0:T(8,128)(2,1)S(1)}, bf16[2,4,96,384]{3,2,1,0:T(8,128)(2,1)S(1)}, u32[]{:S(2)}, u32[]{:S(2)}) collective-permute-start(bf16[2,4,96,384]{3,2,1,0:T(8,128)(2,1)S(1)} %fusion.8), channel_id=1, source_target_pairs={{0,16},{4,20},{8,24},{12,28},{16,0},{20,4},{24,8},{28,12},{1,17},{... | collective-permute-start | bytes 1769480 | tf_op jit(solution)/shard_map/ppermute | solution.py:767
  341.8 25.9 %collective-permute-start.40 = (bf16[256,768]{1,0:T(8,128)(2,1)}, bf16[256,768]{1,0:T(8,128)(2,1)S(1)}, u32[]{:S(2)}, u32[]{:S(2)}) collective-permute-start(bf16[256,768]{1,0:T(8,128)(2,1)} %get-tuple-element.245), channel_id=1, source_target_pairs={{0,1},{1,0},{2,3},{5,4},{6,7},{7,6},{8,9},{9,8},{10,11},{13,12},{1... | collective-permute-start | bytes 1179656 | tf_op jit(solution)/shard_map/ppermute | solution.py:806
  343.8 23.9 %collective-permute-start.41 = (bf16[256,768]{1,0:T(8,128)(2,1)}, bf16[256,768]{1,0:T(8,128)(2,1)S(1)}, u32[]{:S(2)}, u32[]{:S(2)}) collective-permute-start(bf16[256,768]{1,0:T(8,128)(2,1)} %get-tuple-element.246), channel_id=1, source_target_pairs={{0,2},{1,3},{2,0},{5,7},{6,4},{7,5},{8,10},{9,11},{10,8},{13,15},{... | collective-permute-start | bytes 1179656 | tf_op jit(solution)/shard_map/ppermute | solution.py:806
  348.9 18.8 %collective-permute-start.42 = (bf16[256,768]{1,0:T(8,128)(2,1)}, bf16[256,768]{1,0:T(8,128)(2,1)S(1)}, u32[]{:S(2)}, u32[]{:S(2)}) collective-permute-start(bf16[256,768]{1,0:T(8,128)(2,1)} %get-tuple-element.247), channel_id=1, source_target_pairs={{0,3},{1,2},{2,1},{5,6},{6,5},{7,4},{8,11},{9,10},{10,9},{13,14},{... | collective-permute-start | bytes 1179656 | tf_op jit(solution)/shard_map/ppermute | solution.py:806
  355.1 12.6 %collective-permute-start.44 = (bf16[1,4,96,384]{3,2,1,0:T(8,128)(2,1)S(1)}, bf16[1,4,96,384]{3,2,1,0:T(8,128)(2,1)}, u32[]{:S(2)}, u32[]{:S(2)}) collective-permute-start(bf16[1,4,96,384]{3,2,1,0:T(8,128)(2,1)S(1)} %slice.463), channel_id=1, source_target_pairs={{0,8},{4,12},{8,0},{12,4},{16,24},{20,28},{24,16},{28,20},{1,9},{5... | collective-permute-start | bytes 884744 | tf_op jit(solution)/shard_map/ppermute | solution.py:767
  356.9 10.8 %collective-permute-start.43 = (bf16[1,4,96,384]{3,2,1,0:T(8,128)(2,1)}, bf16[1,4,96,384]{3,2,1,0:T(8,128)(2,1)S(1)}, u32[]{:S(2)}, u32[]{:S(2)}) collective-permute-start(bf16[1,4,96,384]{3,2,1,0:T(8,128)(2,1)} %slice.464), channel_id=1, source_target_pairs={{0,16},{4,20},{8,24},{12,28},{16,0},{20,4},{24,8},{28,12},{1,17},{... | collective-permute-start | bytes 884744 | tf_op jit(solution)/shard_map/ppermute | solution.py:767
  361.1 16.0 %copy-start.27 = (bf16[256,768]{1,0:T(8,128)(2,1)S(1)}, bf16[256,768]{1,0:T(8,128)(2,1)}, u32[]{:S(2)}) copy-start(bf16[256,768]{1,0:T(8,128)(2,1)} %get-tuple-element.250) | copy-start | bytes 1179652
  367.7 10.9 %collective-permute-start.47 = (bf16[2,96,768]{2,1,0:T(8,128)(2,1)S(1)}, bf16[2,96,768]{2,1,0:T(8,128)(2,1)S(1)}, u32[]{:S(2)}, u32[]{:S(2)}) collective-permute-start(bf16[2,96,768]{2,1,0:T(8,128)(2,1)S(1)} %slice.462), channel_id=1, source_target_pairs={{0,1},{1,0},{2,3},{3,2},{4,5},{5,4},{6,7},{7,6},{8,9},{9,8},{10,11... | collective-permute-start | bytes 884744 | tf_op jit(solution)/shard_map/ppermute | solution.py:773
  368.8 21.1 %collective-permute-start.46 = (bf16[4,96,384]{2,1,0:T(8,128)(2,1)S(1)}, bf16[4,96,384]{2,1,0:T(8,128)(2,1)S(1)}, u32[]{:S(2)}, u32[]{:S(2)}) collective-permute-start(bf16[4,96,384]{2,1,0:T(8,128)(2,1)S(1)} %fusion.18), channel_id=1, source_target_pairs={{0,2},{1,3},{2,0},{3,1},{4,6},{5,7},{6,4},{7,5},{8,10},{9,11},{10,... | collective-permute-start | bytes 884744 | tf_op jit(solution)/shard_map/ppermute | solution.py:773
  377.1 7.8 %collective-permute-start.45 = (f32[16,1408]{1,0:T(8,128)}, f32[16,1408]{1,0:T(8,128)S(1)}, u32[]{:S(2)}, u32[]{:S(2)}) collective-permute-start(f32[16,1408]{1,0:T(8,128)} %gather_up.1), channel_id=1, source_target_pairs={{0,1},{1,0},{2,3},{3,2},{4,5},{5,4},{6,7},{7,6},{8,9},{9,8},{10,11... | collective-permute-start | bytes 270344 | tf_op jit(solution)/shard_map/ppermute | solution.py:773
  389.9 8.0 %collective-permute-start.48 = (f32[2,16,1408]{2,1,0:T(8,128)S(1)}, f32[2,16,1408]{2,1,0:T(8,128)S(1)}, u32[]{:S(2)}, u32[]{:S(2)}) collective-permute-start(f32[2,16,1408]{2,1,0:T(8,128)S(1)} %pad_maximum_fusion.20), channel_id=1, source_target_pairs={{0,2},{1,3},{2,0},{3,1},{4,6},{5,7},{6,4},{7,5},{8,10},{9,11},{10,... | collective-permute-start | bytes 540680 | tf_op jit(solution)/shard_map/ppermute | solution.py:773
  390.3 10.5 %collective-permute-start.49 = (bf16[4,96,192]{2,1,0:T(8,128)(2,1)S(1)}, bf16[4,96,192]{2,1,0:T(8,128)(2,1)S(1)}, u32[]{:S(2)}, u32[]{:S(2)}) collective-permute-start(bf16[4,96,192]{2,1,0:T(8,128)(2,1)S(1)} %slice.469), channel_id=1, source_target_pairs={{0,1},{1,0},{2,3},{3,2},{4,5},{5,4},{6,7},{7,6},{8,9},{9,8},{10,11... | collective-permute-start | bytes 442376 | tf_op jit(solution)/shard_map/ppermute | solution.py:773
  399.4 1.4 collective-permute-start.50
  400.9 4.7 %collective-permute-start.51 = (f32[2,2,4,1408]{3,2,1,0:T(4,128)S(1)}, f32[2,2,4,1408]{3,2,1,0:T(4,128)S(1)}, u32[]{:S(2)}, u32[]{:S(2)}) collective-permute-start(f32[2,2,4,1408]{3,2,1,0:T(4,128)S(1)} %get-tuple-element.341), channel_id=1, source_target_pairs={{0,8},{4,12},{8,0},{12,4},{16,24},{20,28},{24,16},{28,20},{1,9},{5... | collective-permute-start | bytes 270344 | tf_op jit(solution)/shard_map/ppermute | solution.py:767
  405.7 4.6 %collective-permute-start.52 = (f32[4,1,4,1408]{3,2,0,1:T(4,128)S(1)}, f32[4,1,4,1408]{3,2,0,1:T(4,128)S(1)}, u32[]{:S(2)}, u32[]{:S(2)}) collective-permute-start(f32[4,1,4,1408]{3,2,0,1:T(4,128)S(1)} %get-tuple-element.339), channel_id=1, source_target_pairs={{0,16},{4,20},{8,24},{12,28},{16,0},{20,4},{24,8},{28,12},{1,17},{... | collective-permute-start | bytes 270344 | tf_op jit(solution)/shard_map/ppermute | solution.py:767
  (35 other events, 205.1 us)

commit v3 on v2

v3 whole, which is shorter than its diff:
```python
from functools import partial

import jax
import jax.numpy as jnp
import numpy as np
from jax import lax
from jax.experimental import pallas as pl
from jax.experimental.pallas import tpu as pltpu
from jax.sharding import PartitionSpec as P

HEAD = 64
PRECISE = lax.Precision.HIGHEST
EPSILON = 1e-05
SHIFT_1, SCALE_1, GATE_1, SHIFT_2, SCALE_2, GATE_2, BIAS_OUT, GAIN_1, GAIN_2 = range(9)
F32 = jnp.float32
BF16 = jnp.bfloat16
PAIR = 2 * HEAD
BOTH = ("dp", "tensor")
ANY = pl.BlockSpec(memory_space=pl.ANY)
VMEM = pl.BlockSpec(memory_space=pltpu.VMEM)
SMEM = pl.BlockSpec(memory_space=pltpu.SMEM)


def dot_nn(a, b):
    return jnp.dot(a, b, preferred_element_type=F32)


def dot_nt(a, b):
    return lax.dot_general(a, b, (((1,), (1,)), ((), ())), preferred_element_type=F32)


def params(**more):
    return pltpu.CompilerParams(vmem_limit_bytes=58 << 20, **more)


def cost(flops, nbytes, trans=0):
    return pl.CostEstimate(flops=int(flops), bytes_accessed=int(nbytes), transcendentals=int(trans))


def shape(dims, kind):
    return jax.ShapeDtypeStruct(tuple(dims), kind)


def row_at(me_ref, index, rows):
    return pl.multiple_of((me_ref[0] ^ index) * rows, rows)


def at_step(n, act):
    pl.when(pl.program_id(0) == n)(act)


def pick(refs, out, each=1):
    rows = refs[0].shape[0]
    for n, ref in enumerate(refs):
        at = pl.ds(n % each * rows, rows)
        at_step(n // each, lambda ref=ref, at=at: out.__setitem__((at, slice(None)), ref[...]))
    return out[...].astype(F32)


def put(refs, value):
    for n, ref in enumerate(refs):
        at_step(n, lambda ref=ref: ref.__setitem__(..., value))


def add_row(ref, n, value):
    at_step(0, lambda: ref.__setitem__((slice(n, n + 1), slice(None)), jnp.zeros_like(value)))
    ref[n : n + 1, :] += value


def start_all(copies):
    def act():
        for copy in copies:
            copy.start()

    at_step(0, act)


def wait_all(copies):
    def act():
        for copy in copies:
            copy.wait()

    at_step(0, act)


def row_block(rows, cols):
    return pl.BlockSpec((rows, cols), lambda i: (i, 0))


def col_block(rows, cols):
    return pl.BlockSpec((rows, cols), lambda i: (0, i))


def vec_row(vec, n):
    return vec[n : n + 1, :]


def norm_scale(vec, gain, scale):
    return vec_row(vec, gain) * (1.0 + vec_row(vec, scale))


def rotary_kernel(places, frequencies, cos_flat, sin_a, sin_b, cos_t, sin_t):
    angle = frequencies[...] * places[...]
    cosine, sine = jnp.cos(angle), jnp.sin(angle)
    cos_t[...], sin_t[...] = cosine, sine
    nothing = jnp.zeros_like(sine)
    cos_flat[...] = jnp.concatenate([cosine] * 4, axis=0).T
    sin_a[...] = jnp.concatenate([-sine, nothing] * 2, axis=0).T
    sin_b[...] = jnp.concatenate([nothing, sine] * 2, axis=0).T


def rotary(places, frequencies):
    length, half = places.shape[1], frequencies.shape[0]
    return pl.pallas_call(
        rotary_kernel,
        out_shape=[shape((length, 4 * half), F32)] * 3 + [shape((half, length), F32)] * 2,
        in_specs=[VMEM] * 2,
        out_specs=[VMEM] * 5,
        compiler_params=params(),
        cost_estimate=cost(6e6, 2e6),
        name="rotary",
    )(places, frequencies)


class Held:
    def __init__(self, parts, rels, offset=0):
        self.parts, self.rels, self.offset = parts, rels, offset

    def blocks(self, refs):
        n = 0
        for ref, rel in zip(refs, self.rels):
            for i, j in enumerate(rel):
                yield ref.at[i + self.offset], j, n
                n += 1

    @property
    def count(self):
        return sum(len(rel) for rel in self.rels)


def qkv_copies(me, qk, vo, refs, w_buf, sems, rows):
    out = []
    parts = len(qk.parts)
    for held, group, planes in ((qk, refs[:parts], (0, 1)), (vo, refs[parts:], (2,))):
        for block, j, n in held.blocks(group):
            for c, plane in enumerate(planes):
                out.append(
                    pltpu.make_async_copy(
                        block.at[pl.ds(c * rows, rows), :],
                        w_buf.at[plane, pl.ds(row_at(me, j, rows), rows), :],
                        sems.at[plane, n],
                    )
                )
    return out


def qkv_kernel(qk, vo, me, *refs):
    x_refs, refs = refs[:4], refs[4:]
    (vec, cosine, sin_a, sin_b), refs = refs[:4], refs[4:]
    mul, add = norm_scale(vec, GAIN_1, SCALE_1), vec_row(vec, SHIFT_1)
    held, refs = refs[: 2 * len(qk.parts)], refs[2 * len(qk.parts) :]
    (n_t, k_out, v_out, q_t, k_t, v_t), (w_buf, x_buf, sems) = refs[:6], refs[6:]
    copies = qkv_copies(me, qk, vo, held, w_buf, sems, w_buf.shape[1] // qk.count)
    start_all(copies)
    x = pick(x_refs, x_buf, 2)
    centred = x - jnp.mean(x, axis=-1, keepdims=True)
    spread = jnp.mean(centred * centred, axis=-1, keepdims=True)
    normed = (centred * lax.rsqrt(spread + EPSILON) * mul + add).astype(BF16)
    n_t[...] = normed.T
    wait_all(copies)
    width = k_out.shape[1]
    for c, (flat, turned, factor) in enumerate(((None, q_t, HEAD**-0.5), (k_out, k_t, 1.0))):
        proj = dot_nn(normed, w_buf[c])
        for p in range(width // PAIR):
            lanes = slice(p * PAIR, (p + 1) * PAIR)
            r = proj[:, lanes]
            spun = (
                r * cosine[...]
                + pltpu.roll(r, PAIR - HEAD // 2, 1) * sin_a[...]
                + pltpu.roll(r, HEAD // 2, 1) * sin_b[...]
            )
            spun = spun.astype(BF16) * BF16(factor)
            if flat is not None:
                flat[:, lanes] = spun
            turned[lanes, :] = spun.T
    values = dot_nn(normed, w_buf[2]).astype(BF16)
    v_out[...] = values
    v_t[...] = values.T


def qkv(me, x_parts, vec, cosine, sin_a, sin_b, qk, vo):
    part, width = x_parts[0].shape
    length = 4 * part
    cols = qk.parts[0].shape[2]
    flat, turned = shape((length, cols), BF16), shape((cols, length), BF16)
    return pl.pallas_call(
        partial(qkv_kernel, qk, vo),
        grid=(2,),
        out_shape=[shape((width, length), BF16), flat, flat, turned, turned, turned],
        in_specs=[SMEM]
        + [VMEM] * 5
        + [row_block(2 * part, PAIR)] * 3
        + [ANY] * (2 * len(qk.parts)),
        out_specs=[col_block(width, 2 * part)]
        + [row_block(2 * part, cols)] * 2
        + [col_block(cols, 2 * part)] * 3,
        scratch_shapes=[
            pltpu.VMEM((3, width, cols), BF16),
            pltpu.VMEM((2 * part, width), BF16),
            pltpu.SemaphoreType.DMA((3, qk.count)),
        ],
        compiler_params=params(),
        cost_estimate=cost(6 * length * width * cols, 16e6),
        name="qkv",
    )(me, *x_parts, vec, cosine, sin_a, sin_b, *qk.parts, *vo.parts)


def three_terms(v):
    rows = []
    for _ in range(3):
        rows.append(v.astype(BF16).astype(F32))
        v = v - rows[-1]
    rows += [jnp.zeros_like(v)] * 5
    return jnp.concatenate(rows, axis=0).astype(BF16)


DOCS, TERMS = 8, 16


def added_lanes(out, doc_col):
    lane = lax.broadcasted_iota(jnp.int32, out.shape, 1) % HEAD
    other = jnp.where(lane == doc_col[...], 0.0, -1e30)
    ones = jnp.where((lane >= TERMS) & (lane < TERMS + 3), 1.0, 0.0)
    out[...] = jnp.where(lane < DOCS, other, ones).astype(BF16)


def document_rows(doc_row):
    row = lax.broadcasted_iota(jnp.int32, (TERMS, doc_row.shape[1]), 0)
    return jnp.where(row == doc_row[...], 1.0, 0.0).astype(BF16)


def with_lanes(ref, added, head):
    lane = lax.broadcasted_iota(jnp.int32, (1, PAIR), 1)
    return jnp.where((lane // HEAD) == head, ref[...], added[...])


def with_rows(out, ref, head, rows):
    own, other = head * HEAD, (1 - head) * HEAD
    out[own : own + HEAD, :] = ref[own : own + HEAD, :]
    out[other : other + HEAD, :] = jnp.zeros((HEAD, out.shape[1]), BF16)
    for n, value in enumerate(rows):
        if value is not None:
            at = other + n * TERMS
            out[at : at + value.shape[0], :] = value


def attend_kernel(q_t, k, v_t, doc_row, doc_col, mix_t, log_sum, added, ahead):
    @pl.when(pl.program_id(0) == 0)
    def _():
        added_lanes(added, doc_col)

    docs = document_rows(doc_row)
    for h in range(2):
        with_rows(ahead.at[h], q_t, h, [docs])

    for h in range(2):
        rows = slice(h * HEAD, (h + 1) * HEAD)
        scores = dot_nn(with_lanes(k, added, h), ahead[h])
        top = jnp.max(scores, axis=0, keepdims=True)
        weights = jnp.exp(scores - top)
        total = jnp.sum(weights, axis=0, keepdims=True)
        mixed = dot_nn(v_t[rows, :], weights.astype(BF16))
        mix_t[rows, :] = (mixed / total).astype(BF16)
        log_sum[0, h] = top + jnp.log(total)


def attend(q_t, k, v_t, doc_row, doc_col):
    length, width = k.shape
    pairs = width // PAIR
    flat = pl.BlockSpec((length, PAIR), lambda i: (0, i))
    turned = pl.BlockSpec((PAIR, length), lambda i: (i, 0))
    return pl.pallas_call(
        attend_kernel,
        grid=(pairs,),
        in_specs=[
            turned,
            flat,
            turned,
            pl.BlockSpec((1, length), lambda i: (0, 0)),
            pl.BlockSpec((length, 1), lambda i: (0, 0)),
        ],
        out_specs=[turned, pl.BlockSpec((1, 2, 1, length), lambda i: (i, 0, 0, 0))],
        out_shape=[shape((width, length), BF16), shape((pairs, 2, 1, length), F32)],
        scratch_shapes=[pltpu.VMEM((length, PAIR), BF16), pltpu.VMEM((2, PAIR, length), BF16)],
        compiler_params=params(),
        cost_estimate=cost(16 * length * length * width, 8e6),
        name="attend",
    )(q_t, k, v_t, doc_row, doc_col)


def load_out_weight(me, vo, refs, buf, sems):
    rows = buf.shape[0] // vo.count
    copies = [
        pltpu.make_async_copy(
            block.at[pl.ds(rows, rows), :], buf.at[pl.ds(row_at(me, j, rows), rows), :], sems.at[n]
        )
        for block, j, n in vo.blocks(refs)
    ]
    start_all(copies)
    return copies


def middle_kernel(vo, me, *refs):
    x_refs, g_refs, refs = refs[:4], refs[4:8], refs[8:]
    (mix_t, vec), refs = refs[:2], refs[2:]
    mul, add = norm_scale(vec, GAIN_2, SCALE_2), vec_row(vec, SHIFT_2)
    gate_one, gate_two = vec_row(vec, GATE_1), vec_row(vec, GATE_2)
    pieces, refs = refs[: len(vo.parts)], refs[len(vo.parts) :]
    (att, n_two, n_two_t, d_down, d_down_t, d_bias, mix), (w_buf, x_buf, sems) = refs[:7], refs[7:]
    copies = load_out_weight(me, vo, pieces, w_buf, sems)
    scaled = pick(g_refs, x_buf) * gate_two
    add_row(d_bias, 0, jnp.sum(scaled, axis=0, keepdims=True))
    scaled = scaled.astype(BF16)
    d_down[...] = scaled
    d_down_t[...] = scaled.T
    wait_all(copies)
    mixture = mix_t[...].T
    mix[...] = mixture
    attention = dot_nt(mixture, w_buf[...])
    att[...] = attention
    mid = pick(x_refs, x_buf) + gate_one * attention
    centred = mid - jnp.mean(mid, axis=-1, keepdims=True)
    spread = jnp.mean(centred * centred, axis=-1, keepdims=True)
    normed = (centred * lax.rsqrt(spread + EPSILON) * mul + add).astype(BF16)
    n_two[...] = normed
    n_two_t[...] = normed.T


def middle(me, x_parts, g_parts, mix_t, vec, vo):
    part, width = x_parts[0].shape
    length = 4 * part
    inner = mix_t.shape[0]
    flat, turned = shape((length, width), BF16), shape((width, length), BF16)
    return pl.pallas_call(
        partial(middle_kernel, vo),
        grid=(4,),
        out_shape=[shape((length, width), F32), flat, turned, flat, turned]
        + [shape((1, width), F32), shape((length, inner), BF16)],
        in_specs=[SMEM]
        + [VMEM] * 8
        + [col_block(inner, part), VMEM]
        + [ANY] * len(vo.parts),
        out_specs=[
            row_block(part, width),
            row_block(part, width),
            col_block(width, part),
            row_block(part, width),
            col_block(width, part),
            VMEM,
            row_block(part, inner),
        ],
        scratch_shapes=[
            pltpu.VMEM((width, inner), BF16),
            pltpu.VMEM((part, width), BF16),
            pltpu.SemaphoreType.DMA((vo.count,)),
        ],
        compiler_params=params(),
        cost_estimate=cost(2 * length * width * inner, 16e6),
        name="middle",
    )(me, *x_parts, *g_parts, mix_t, vec, *vo.parts)


def spread_rows(me, value, stage, keep, send=None):
    blocks, rows = stage.shape[0], stage.shape[1]
    for j in range(blocks):
        stage[j] = value[j * rows : (j + 1) * rows, :].astype(BF16)
    for j in range(blocks):
        block = stage[me[0] ^ j]
        if j % 2 == 0:
            keep(j // 2, block)
        else:
            send(j // 2, block)


def writer(ref, *lead):
    def put(slot, block):
        ref[(lead[0], slot, *lead[1:])] = block

    return put


def split_writer(ref, *lead):
    def put(slot, block):
        half = block.shape[-1] // 2
        for s in range(2):
            ref[(s, slot, *lead)] = block[:, s * half : (s + 1) * half]

    return put


C_ROOT = 0.7978845608028654
C_CUBE = 0.044715


def feed_kernel(up, dn, steps, first, me, *refs):
    (n_two, n_two_t, d_down, d_down_t, bias), refs = refs[:5], refs[5:]
    if not first:
        (down_in, d_n_in), refs = refs[:2], refs[2:]
    parts = len(up.parts)
    up_refs, down_refs, refs = refs[:parts], refs[parts : 2 * parts], refs[2 * parts :]
    (down, d_n, d_bias, *grads), (w_buf, stage, sems) = refs[:-3], refs[-3:]
    step = pl.program_id(0)
    rows = up_refs[0].shape[1]
    chunk = w_buf.shape[3]
    offset = 0 if first else steps * chunk

    def copies(s):
        out = []
        for m, (held, group) in enumerate(((up, up_refs), (dn, down_refs))):
            for block, j, n in held.blocks(group):
                out.append(
                    pltpu.make_async_copy(
                        block.at[:, pl.ds(offset + s * chunk, chunk)],
                        w_buf.at[m, s, pl.ds(row_at(me, j, rows), rows), :],
                        sems.at[m, s, n],
                    )
                )
        return out

    @pl.when(step == 0)
    def _():
        for s in range(steps):
            for copy in copies(s):
                copy.start()
        if first:
            down[...] = jnp.zeros_like(down)
            d_n[...] = jnp.zeros_like(d_n)
        else:
            down[...] = down_in[...]
            d_n[...] = d_n_in[...]

    for s in range(steps):

        @pl.when(step == s)
        def _():
            for copy in copies(s):
                copy.wait()

    w_up = w_buf[0, step]
    w_down_t = w_buf[1, step]
    h = dot_nn(n_two[...], w_up) + bias[0]
    square = h * h
    t = jnp.tanh(C_ROOT * h * (1.0 + C_CUBE * square))
    half = 0.5 + 0.5 * t
    act = (h * half).astype(BF16)
    slope = half + (0.5 * C_ROOT) * h * (1.0 - t * t) * (1.0 + (3.0 * C_CUBE) * square)
    d_h = (dot_nn(d_down[...], w_down_t) * slope).astype(BF16)
    d_bias[0] = jnp.sum(d_h.astype(F32), axis=0, keepdims=True)
    down[...] += dot_nt(act, w_down_t)
    d_n[...] += dot_nt(d_h, w_up)
    for m, grad in ((0, dot_nn(n_two_t[...], d_h)), (1, dot_nn(d_down_t[...], act))):
        spread_rows(me, grad, stage, *(writer(ref, m) for ref in grads))


def feed(me, n_two, n_two_t, d_down, d_down_t, bias, up, dn, start, before, units):
    blocks = up.count
    length, width = n_two.shape
    chunk = 512 if units % 512 == 0 else units
    steps = units // chunk
    first = before is None
    rows = width // blocks
    one = pl.Buffered(1)
    flat = pl.BlockSpec((length, width), lambda i: (0, 0), pipeline_mode=one)
    turned = pl.BlockSpec((width, length), lambda i: (0, 0), pipeline_mode=one)
    held = pl.BlockSpec((length, width), lambda i: (0, 0))
    half = max(blocks // 2, 1)
    grad = pl.BlockSpec((2, half, rows, chunk), lambda i: (0, 0, 0, i))
    grads = 1 if blocks == 1 else 2
    bias_spec = pl.BlockSpec((1, 1, chunk), lambda i: (i + start // chunk, 0, 0))
    return pl.pallas_call(
        partial(feed_kernel, up, dn, steps, first),
        grid=(steps,),
        in_specs=[SMEM, flat, turned, flat, turned, bias_spec]
        + ([] if first else [flat, flat])
        + [ANY] * (2 * len(up.parts)),
        out_specs=[held, held, pl.BlockSpec((1, 1, chunk), lambda i: (i, 0, 0))] + [grad] * grads,
        out_shape=[shape((length, width), F32)] * 2
        + [shape((steps, 1, chunk), F32)]
        + [shape((2, half, rows, units), BF16)] * grads,
        scratch_shapes=[
            pltpu.VMEM((2, steps, width, chunk), BF16),
            pltpu.VMEM((blocks, rows, chunk), BF16),
            pltpu.SemaphoreType.DMA((2, steps, blocks)),
        ],
        compiler_params=params(),
        cost_estimate=cost(12 * length * width * units, 20e6),
        name="feed",
    )(
        me,
        n_two,
        n_two_t,
        d_down,
        d_down_t,
        bias.reshape(-1, 1, chunk),
        *(() if first else before),
        *up.parts,
        *dn.parts,
    )


def turn_kernel(vo, me, *refs):
    x_refs, g_refs, refs = refs[:4], refs[4:8], refs[8:]
    (att, down, d_n, vec), refs = refs[:4], refs[4:]
    mul, bias = norm_scale(vec, GAIN_2, SCALE_2), vec_row(vec, BIAS_OUT)
    gate_one, gate_two = vec_row(vec, GATE_1), vec_row(vec, GATE_2)
    pieces, refs = refs[: len(vo.parts)], refs[len(vo.parts) :]
    out_refs, (d_mid, d_mix_t, sums, d_att_t), (w_buf, x_buf, sems) = (
        refs[:4],
        refs[4:8],
        refs[8:],
    )
    copies = load_out_weight(me, vo, pieces, w_buf, sems)
    g = pick(g_refs, x_buf)
    attention = att[...]
    mid = pick(x_refs, x_buf) + gate_one * attention
    branch = down[...] + bias
    put(out_refs, (mid + gate_two * branch).astype(BF16))
    centred = mid - jnp.mean(mid, axis=-1, keepdims=True)
    inverse = lax.rsqrt(jnp.mean(centred * centred, axis=-1, keepdims=True) + EPSILON)
    unit = centred * inverse
    dn = d_n[...]
    dn_unit = dn * unit
    du = dn * mul
    dm = g + inverse * (
        du
        - jnp.mean(du, axis=-1, keepdims=True)
        - unit * jnp.mean(dn_unit * mul, axis=-1, keepdims=True)
    )
    d_mid[...] = dm
    for n, term in enumerate((g * branch, dn_unit, dn, dm * attention)):
        add_row(sums, n, jnp.sum(term, axis=0, keepdims=True))
    d_att = (dm * gate_one).astype(BF16)
    d_att_t[...] = d_att.T
    wait_all(copies)
    d_mix_t[...] = dot_nn(d_att, w_buf[...]).astype(BF16).T


def turn(me, x_parts, g_parts, att, down, d_n, vec, vo):
    part, width = x_parts[0].shape
    length = 4 * part
    inner = vo.parts[0].shape[2]
    return pl.pallas_call(
        partial(turn_kernel, vo),
        grid=(4,),
        out_shape=[shape((part, width), BF16)] * 4
        + [
            shape((length, width), F32),
            shape((inner, length), BF16),
            shape((4, width), F32),
            shape((width, length), BF16),
        ],
        in_specs=[SMEM]
        + [VMEM] * 8
        + [row_block(part, width)] * 3
        + [VMEM]
        + [ANY] * len(vo.parts),
        out_specs=[VMEM] * 4
        + [
            row_block(part, width),
            col_block(inner, part),
            VMEM,
            col_block(width, part),
        ],
        scratch_shapes=[
            pltpu.VMEM((width, inner), BF16),
            pltpu.VMEM((part, width), BF16),
            pltpu.SemaphoreType.DMA((vo.count,)),
        ],
        compiler_params=params(),
        cost_estimate=cost(2 * length * width * inner, 24e6),
        name="turn",
    )(
        me, *x_parts, *g_parts, att, down, d_n, vec, *vo.parts
    )


def attend_back_kernel(
    k, v, q_t, k_t, d_mix_t, mix_t, log_sum, doc_row, doc_col, cos_t, sin_t,
    dq, dk, dv, added, ahead, dq_acc, dk_acc, dv_acc,
):
    @pl.when(pl.program_id(0) == 0)
    def _():
        added_lanes(added, doc_col)

    length = k.shape[0]
    block = 256 if length % 256 == 0 else length
    docs = document_rows(doc_row)
    for h in range(2):
        rows = slice(h * HEAD, (h + 1) * HEAD)
        row_dot = jnp.sum(
            d_mix_t[rows, :].astype(F32) * mix_t[rows, :].astype(F32), axis=0, keepdims=True
        )
        with_rows(ahead.at[h, 0], q_t, h, [docs, three_terms(-log_sum[0, h])])
        with_rows(ahead.at[h, 1], d_mix_t, h, [None, three_terms(-row_dot)])

    for h in range(2):
        rows = slice(h * HEAD, (h + 1) * HEAD)
        keys, values = with_lanes(k, added, h), with_lanes(v, added, h)
        for b in range(length // block):
            c = slice(b * block, (b + 1) * block)
            probs = jnp.exp(dot_nn(keys, ahead[h, 0, :, c]))
            d_scores = (probs * dot_nn(values, ahead[h, 1, :, c])).astype(BF16)
            dv_part = dot_nt(d_mix_t[rows, c], probs.astype(BF16))
            dk_part = dot_nt(q_t[rows, c], d_scores)
            if b == 0:
                dv_acc[rows, :] = dv_part
                dk_acc[rows, :] = dk_part
            else:
                dv_acc[rows, :] += dv_part
                dk_acc[rows, :] += dk_part
            dq_acc[rows, c] = dot_nn(k_t[rows, :], d_scores)

    half = HEAD // 2
    for acc, out, factor in ((dq_acc, dq, HEAD**-0.5), (dk_acc, dk, 1.0)):
        turned = []
        for h in range(2):
            a = acc[h * HEAD : h * HEAD + half, :] * factor
            b = acc[h * HEAD + half : (h + 1) * HEAD, :] * factor
            turned.append(a * cos_t[...] + b * sin_t[...])
            turned.append(b * cos_t[...] - a * sin_t[...])
        out[...] = jnp.concatenate(turned, axis=0).astype(BF16).T
    dv[...] = dv_acc[...].astype(BF16).T


def attend_back(k, v, q_t, k_t, d_mix_t, mix_t, log_sum, doc_row, doc_col, cos_t, sin_t):
    length, width = k.shape
    count = width // PAIR
    flat = pl.BlockSpec((length, PAIR), lambda i: (0, i))
    turned = pl.BlockSpec((PAIR, length), lambda i: (i, 0))
    fixed = lambda a: pl.BlockSpec(a.shape, lambda i: (0, 0))
    return pl.pallas_call(
        attend_back_kernel,
        grid=(count,),
        in_specs=[flat] * 2
        + [turned] * 4
        + [pl.BlockSpec((1, 2, 1, length), lambda i: (i, 0, 0, 0))]
        + [fixed(a) for a in (doc_row, doc_col, cos_t, sin_t)],
        out_specs=[flat] * 3,
        out_shape=[shape((length, width), BF16)] * 3,
        scratch_shapes=[
            pltpu.VMEM((length, PAIR), BF16),
            pltpu.VMEM((2, 2, PAIR, length), BF16),
        ]
        + [pltpu.VMEM((PAIR, length), F32)] * 3,
        compiler_params=params(),
        cost_estimate=cost(28 * length * length * width, 14e6),
        name="attend_back",
    )(k, v, q_t, k_t, d_mix_t, mix_t, log_sum, doc_row, doc_col, cos_t, sin_t)


def first_kernel(qk, vo, me, *refs):
    x_refs, refs = refs[:4], refs[4:]
    (d_mid, vec, dq, dk, dv), refs = refs[:5], refs[5:]
    mul = norm_scale(vec, GAIN_1, SCALE_1)
    held, refs = refs[: 2 * len(qk.parts)], refs[2 * len(qk.parts) :]
    out_refs, (sums, w_buf, x_buf, sems) = refs[:4], refs[4:]
    copies = qkv_copies(me, qk, vo, held, w_buf, sems, w_buf.shape[1] // qk.count)
    start_all(copies)
    x = pick(x_refs, x_buf)
    centred = x - jnp.mean(x, axis=-1, keepdims=True)
    inverse = lax.rsqrt(jnp.mean(centred * centred, axis=-1, keepdims=True) + EPSILON)
    unit = centred * inverse
    wait_all(copies)
    dn = dot_nt(dq[...], w_buf[0]) + dot_nt(dk[...], w_buf[1]) + dot_nt(dv[...], w_buf[2])
    dn_unit = dn * unit
    du = dn * mul
    put(
        out_refs,
        (
            d_mid[...]
            + inverse
            * (
                du
                - jnp.mean(du, axis=-1, keepdims=True)
                - unit * jnp.mean(dn_unit * mul, axis=-1, keepdims=True)
            )
        ).astype(BF16),
    )
    for n, term in enumerate((dn_unit, dn)):
        add_row(sums, n, jnp.sum(term, axis=0, keepdims=True))


def first(me, x_parts, d_mid, vec, dq, dk, dv, qk, vo):
    part, width = x_parts[0].shape
    length = 4 * part
    cols = dq.shape[1]
    return pl.pallas_call(
        partial(first_kernel, qk, vo),
        grid=(4,),
        out_shape=[shape((part, width), BF16)] * 4 + [shape((2, width), F32)],
        in_specs=[SMEM]
        + [VMEM] * 4
        + [row_block(part, width), VMEM]
        + [row_block(part, cols)] * 3
        + [ANY] * (2 * len(qk.parts)),
        out_specs=[VMEM] * 5,
        scratch_shapes=[
            pltpu.VMEM((3, width, cols), BF16),
            pltpu.VMEM((part, width), BF16),
            pltpu.SemaphoreType.DMA((3, qk.count)),
        ],
        compiler_params=params(),
        cost_estimate=cost(6 * length * width * cols, 20e6),
        name="first",
    )(me, *x_parts, d_mid, vec, dq, dk, dv, *qk.parts, *vo.parts)


def modulate_kernel(qk, vo, zones, me, act, *refs):
    parts = len(qk.parts)
    qk_refs, vo_refs, (vec, bias, ada, small, sems) = refs[:parts], refs[parts:-5], refs[-5:]
    count = qk.count
    rows = ada.shape[0] // count
    cut = rows // 2
    copies = []
    for h, (held, group) in enumerate(((qk, qk_refs), (vo, vo_refs))):
        for block, j, n in held.blocks(group):
            at = row_at(me, j, rows) + h * cut
            copies.append(
                pltpu.make_async_copy(
                    block.at[pl.ds(2 * rows, cut), :], ada.at[pl.ds(at, cut), :], sems.at[h, n]
                )
            )
            if h:
                copies.append(
                    pltpu.make_async_copy(
                        block.at[pl.ds(2 * rows + cut, 16), :],
                        small.at[pl.ds(row_at(me, j, 16), 16), :],
                        sems.at[2, n],
                    )
                )
    for copy in copies:
        copy.start()
    for copy in copies:
        copy.wait()
    kinds = ada.shape[1] // act.shape[1]
    act3 = three_terms(act[...])
    across = vec.shape[1] // rows
    vec[...] = jnp.zeros_like(vec)
    for k in range(kinds):
        lanes = slice(k * act.shape[1], (k + 1) * act.shape[1])
        found = jnp.sum(dot_nt(act3, ada[:, lanes]), axis=0, keepdims=True)
        for d in range(count):
            m = d * kinds + k
            at = (m % across) * rows
            extra = small[d * 16 : (d + 1) * 16, :].astype(F32)
            vec[m // across : m // across + 1, at : at + rows] = (
                found[:, d * rows : (d + 1) * rows] + extra[1:2, k * rows : (k + 1) * rows]
            )
    for d in range(count):
        extra = small[d * 16 : (d + 1) * 16, :].astype(F32)
        here = slice(d * rows, (d + 1) * rows)
        for n in range(3):
            vec[BIAS_OUT + n : BIAS_OUT + n + 1, here] = extra[2:3, n * rows : (n + 1) * rows]
        for n in range(zones):
            far = (n - zones // 2) % zones
            at = n * (extra.shape[1] // zones)
            bias[far : far + 1, here] = extra[0:1, at : at + rows]


def modulate(me, act, qk, vo, zones, rows):
    width = qk.parts[0].shape[2]
    return pl.pallas_call(
        partial(modulate_kernel, qk, vo, zones),
        out_shape=[
            shape((16, width), F32),
            shape((zones, width), F32),
            shape((qk.count * rows, width), BF16),
        ],
        in_specs=[SMEM, VMEM] + [ANY] * (len(qk.parts) + len(vo.parts)),
        out_specs=[VMEM] * 3,
        scratch_shapes=[
            pltpu.VMEM((qk.count * 16, width), BF16),
            pltpu.SemaphoreType.DMA((3, qk.count)),
        ],
        compiler_params=params(),
        cost_estimate=cost(2e7, 4e6),
        name="modulate",
    )(me, act, *qk.parts, *vo.parts)


def gather_up_kernel(
    count, me, vec, ada, sums, sums_one, d_bias_down, bias_grad, act, cond, keep, send, d_cond, out, spread
):
    width = vec.shape[1]
    rows = width // count
    size = act.shape[1]
    kinds = ada.shape[1] // size
    norm_1, norm_2 = sums_one[0:1, :], sums[1:2, :]
    d_mod = (
        sums_one[1:2, :],
        norm_1 * vec_row(vec, GAIN_1),
        sums[3:4, :],
        sums[2:3, :],
        norm_2 * vec_row(vec, GAIN_2),
        sums[0:1, :],
    )
    others = (
        norm_1 * (1.0 + vec_row(vec, SCALE_1)),
        norm_2 * (1.0 + vec_row(vec, SCALE_2)),
        d_bias_down[...],
    )
    out[...] = jnp.zeros_like(out)
    base = (kinds + 3) * rows
    for d in range(count):
        here = slice(d * rows, (d + 1) * rows)
        for k in range(kinds):
            m = d * kinds + k
            at = (m % count) * rows
            piece = d_mod[m // count][:, at : at + rows]
            out[d, :, k * rows : (k + 1) * rows] = piece
            spread[k : k + 1, here] = piece
        for n, value in enumerate(others):
            at = (kinds + n) * rows
            out[d, :, at : at + rows] = value[:, here]
        for n in range(bias_grad.shape[0]):
            at = base + n * rows
            out[d, :, at : at + rows] = bias_grad[n : n + 1, here]
        out[d, :, out.shape[2] - size :] = act[...]
    total = jnp.zeros(act.shape, F32)
    for k in range(kinds):
        three = three_terms(spread[k : k + 1, :])
        total += jnp.sum(dot_nn(three, ada[:, k * size : (k + 1) * size]), axis=0, keepdims=True)
    c = cond[...]
    sig = 1.0 / (1.0 + jnp.exp(-c))
    d_cond[...] = total * (sig * (1.0 + c * (1.0 - sig)))

    for j in range(count // 2):
        keep[j] = out[me[0] ^ (2 * j)]
        send[j] = out[me[0] ^ (2 * j + 1)]


def gather_up(me, vec, ada, sums, sums_one, d_bias_down, bias_grad, act, cond, count, length):
    return pl.pallas_call(
        partial(gather_up_kernel, count),
        out_shape=[shape((count // 2, 1, length), F32)] * 2 + [shape(act.shape, F32)],
        in_specs=[SMEM] + [VMEM] * 8,
        out_specs=[VMEM] * 3,
        scratch_shapes=[
            pltpu.VMEM((count, 1, length), F32),
            pltpu.VMEM((8, vec.shape[1]), F32),
        ],
        compiler_params=params(),
        cost_estimate=cost(2e7, 4e6),
        name="gather_up",
    )(me, vec, ada, sums, sums_one, d_bias_down, bias_grad, act, cond)


def weight_grads_kernel(me, n_t, d_att_t, dq, dk, dv, mix_t, *refs):
    *grads, left, right, stage, sems = refs
    copies = [
        pltpu.make_async_copy(ref, held, sems.at[n])
        for n, (ref, held) in enumerate(
            (
                (n_t, left.at[0]),
                (dq, right.at[0]),
                (dk, right.at[1]),
                (dv, right.at[2]),
                (d_att_t, left.at[1]),
                (mix_t, right.at[3]),
            )
        )
    ]
    start_all(copies)
    wait_all(copies[:2])
    at_step(1, copies[2].wait)
    at_step(2, copies[3].wait)

    def last():
        copies[4].wait()
        copies[5].wait()

    at_step(3, last)
    step = pl.program_id(0)
    grad = dot_nn(left[jnp.where(step == 3, 1, 0)], right[step])
    spread_rows(me, grad, stage, *(split_writer(ref, 0) for ref in grads))


def weight_grads(me, n_t, d_att_t, dq, dk, dv, mix, blocks):
    width, length = n_t.shape
    cols = dq.shape[1]
    rows = width // blocks
    half = max(blocks // 2, 1)
    grads = 1 if blocks == 1 else 2
    return pl.pallas_call(
        weight_grads_kernel,
        grid=(4,),
        out_shape=[shape((2, half, 4, rows, cols // 2), BF16)] * grads,
        in_specs=[SMEM] + [ANY] * 6,
        out_specs=[
            pl.BlockSpec((2, half, 1, rows, cols // 2), lambda i: (0, 0, i, 0, 0))
        ]
        * grads,
        scratch_shapes=[
            pltpu.VMEM((2, width, length), BF16),
            pltpu.VMEM((4, length, cols), BF16),
            pltpu.VMEM((blocks, rows, cols), BF16),
            pltpu.SemaphoreType.DMA((6,)),
        ],
        compiler_params=params(),
        cost_estimate=cost(8 * length * width * cols, 14e6),
        name="weight_grads",
    )(me, n_t, d_att_t, dq, dk, dv, mix)


class Group:
    def __init__(self, dp_count, tensor_count, per_dp):
        self.dp, self.tensor, self.per_dp = dp_count, tensor_count, per_dp
        self.d, self.r = lax.axis_index("dp"), lax.axis_index("tensor")
        self.paired = dp_count == 8

    def bit(self, v, b):
        return lax.ppermute(v, "dp", [(i, i ^ (1 << b)) for i in range(self.dp)])

    def step(self, v, k):
        return lax.ppermute(v, "dp", [(i, i ^ k) for i in range(self.dp)])

    def z(self, v, k):
        return lax.ppermute(v, "tensor", [(i, i ^ k) for i in range(self.tensor)])

    def owns(self, d, r):
        return 0 <= r - d % 2 < self.per_dp

    def for_owner(self, rows, zero_idle):
        mine = self.r - self.d % 2
        top = self.per_dp - 1
        own = lax.dynamic_index_in_dim(rows, jnp.clip(mine, 0, top), 0, keepdims=False)
        if zero_idle:
            own = jnp.where((mine >= 0) & (mine <= top), own, jnp.zeros_like(own))
        parts = [own]
        for k in range(1, self.tensor):
            want = (self.r ^ k) - self.d % 2
            parts.append(
                lax.dynamic_index_in_dim(rows, jnp.clip(want, 0, top), 0, keepdims=False)
            )
        return parts

    def ship(self, v, k, to_owner):
        pairs = [
            (d * self.tensor + r, d * self.tensor + (r ^ k))
            for d in range(self.dp)
            for r in range(self.tensor)
            if self.owns(d, r ^ k if to_owner else r)
        ]
        return lax.ppermute(v, BOTH, pairs)

    def held_rows(self, came):
        stack = jnp.stack(came)
        return jnp.stack(
            [
                lax.dynamic_index_in_dim(stack, self.r ^ (j + self.d % 2), 0, keepdims=False)
                for j in range(self.per_dp)
            ]
        )

    def z_pair(self, v, got):
        return jnp.concatenate([v, got], axis=-1)

    def gather_pair(self, v, got, order):
        pair = jnp.stack([v, got])
        return [pair, self.bit(pair, order[1])]

    def gather_cores(self, parts, order):
        one, two = (1 << b for b in order)
        rels = [(0, one), (two, one ^ two)]
        rels += [tuple(j ^ 1 for j in rel) for rel in rels]
        return Held(parts + [self.bit(p, 0) for p in parts], rels)

    def gather_cores_joined(self, pairs, orders):
        near = jnp.concatenate([p for pair in pairs for p in pair])
        far = self.bit(near, 0)
        held = []
        for n, order in enumerate(orders):
            one, two = (1 << b for b in order)
            rel = (0, one, two, one ^ two)
            held.append(Held([near, far], [rel, tuple(j ^ 1 for j in rel)], 4 * n))
        return held

    def whole(self, v, axis):
        return lax.all_gather(v, "dp", axis=axis, tiled=True)


class Flight:
    def __init__(self, value):
        self.value = value


class Sum:
    def __init__(self, group, keep, send=None):
        self.group, self.stage, self.flights, self.terms = group, 0, [], []
        if not group.paired:
            value = keep[:, 0].astype(F32)
            value = lax.psum_scatter(value, "dp", scatter_dimension=value.ndim - 2, tiled=True)
            self.total = [value[0], value[1]]
            return
        self.terms = [[keep], [keep]]
        flight = Flight(group.bit(send, 0))
        self.flights = [(flight, 0), (flight, 1)]

    def settle(self):
        for terms, (flight, at) in zip(self.terms, self.flights):
            terms.append(flight.value if self.stage == 0 else flight.value[at])
        if self.flights and self.stage == 2:
            self.total = [sum(t[0].astype(F32) for t in terms) for terms in self.terms]
        self.flights = []

    def split(self):
        out = []
        for n, order in enumerate(((1, 2), (2, 1))):
            b = order[self.stage]
            if self.stage:
                stay, go = [t[:1] for t in self.terms[n]], [t[1:] for t in self.terms[n]]
            else:
                sides = [t.reshape(2, 2, 2, *t.shape[2:]) for t in self.terms[n]]
                if b == 1:
                    stay, go = [t[n, :, 0] for t in sides], [t[n, :, 1] for t in sides]
                else:
                    stay, go = [t[n, 0] for t in sides], [t[n, 1] for t in sides]
            self.terms[n] = stay
            out.append((b, sum(t.astype(F32) for t in go).astype(BF16)))
        self.stage += 1
        self.flights = [None, None]
        return out


def exchange(*sums):
    links = {}
    for t in sums:
        t.settle()
        if t.group.paired:
            for n, (b, go) in enumerate(t.split()):
                links.setdefault(b, []).append((t, n, go))
    for b, items in links.items():
        blocks = [go for _, _, go in items]
        blocks = blocks[0] if len(blocks) == 1 else jnp.concatenate(blocks)
        flight, at = Flight(items[0][0].group.bit(blocks, b)), 0
        for t, n, go in items:
            t.flights[n] = (flight, slice(at, at + go.shape[0]))
            at += go.shape[0]


def tie(value, *sums):
    flights = {id(f): f for t in sums for f, _ in t.flights}
    flights = list(flights.values())
    value, arrived = lax.optimization_barrier((value, [f.value for f in flights]))
    for flight, v in zip(flights, arrived):
        flight.value = v
    return value


def silu_slope(c):
    sig = jax.nn.sigmoid(c)
    return sig * (1.0 + c * (1.0 - sig))


def shards(
    inputs, condition, doc_ids, positions, w_qkv, w_out, w_up, bias_up, w_down, bias_down,
    gain_one, gain_two, w_ada, bias_ada, out_grad,
):
    dp_count = lax.axis_size("dp")
    tensor_count = lax.axis_size("tensor")
    per_dp, part, width = inputs.shape
    length = doc_ids.shape[1]
    rows = w_up.shape[0]
    group = Group(dp_count, tensor_count, per_dp)
    blocks = dp_count if group.paired else 1
    d, r = group.d, group.r
    me = jnp.where(group.paired, d, 0).astype(jnp.int32).reshape(1)
    mine = jnp.clip(r - d % 2, 0, per_dp - 1)
    own_row = lambda v: lax.dynamic_index_in_dim(v, mine, 0, keepdims=False)
    join = lambda parts: jnp.concatenate(parts, axis=-1)

    order = r ^ jnp.arange(tensor_count)
    mixed = lambda v: own_row(v).reshape(tensor_count, part)[order].reshape(-1)
    docs, places = mixed(doc_ids), mixed(positions)
    doc_row, doc_col = docs[None, :], docs[:, None]
    frequencies = 10000.0 ** (-2.0 * jnp.arange(HEAD // 2, dtype=F32) / HEAD)
    cos_flat, sin_a, sin_b, cos_t, sin_t = rotary(
        places.astype(F32)[None, :], frequencies[:, None]
    )

    cols, cond_size, mod_width = w_qkv.shape[2], w_ada.shape[0], w_ada.shape[1]
    ways = (1, 2), (2, 1)
    cond = own_row(condition).astype(F32)[None]
    act = jax.nn.silu(cond)
    early = jnp.concatenate([w_qkv.reshape(-1, cols), w_out.T])
    late = jnp.concatenate([w_up, w_down.T])
    if group.paired:
        early = jnp.concatenate([early, jnp.pad(bias_up, ((0, 15), (0, cols - rows)))])
    if group.paired:
        ada = w_ada.T.reshape(-1, rows, cond_size).transpose(1, 0, 2).reshape(rows, width)
        cut, top = rows // 2, 2 * rows
        wide = lambda v: jnp.pad(v, (0, width - v.shape[0]))[None]
    x_parts, g_parts = group.for_owner(inputs, False), group.for_owner(out_grad, True)
    early = group.z_pair(early, group.z(early, 2))
    early = join([early, group.z(early, 1)])
    turns = cos_flat, sin_a, sin_b, cos_t, sin_t, doc_row, doc_col
    late, early, x_parts, g_parts = lax.optimization_barrier((late, early, x_parts, g_parts))
    late_got = group.z(late, 2)
    if group.paired:
        small = jnp.concatenate(
            [
                early[2 * top : 2 * top + 1],
                wide(bias_ada),
                wide(jnp.concatenate([bias_down, gain_one, gain_two])),
                early[2 * top + 3 :],
            ]
        )
        firsts = (
            jnp.concatenate([early[:top], ada[:cut], jnp.zeros_like(small)]),
            jnp.concatenate([early[top : 2 * top], ada[cut:], small]),
        )
        came = [group.bit(v, way[0]) for v, way in zip(firsts, ways)]
        late_got, came = lax.optimization_barrier((late_got, came))
        late = group.z_pair(late, late_got)
        late_far = group.z(late, 1)
        near = [group.gather_pair(v, got, way) for v, got, way in zip(firsts, came, ways)]
        x_parts[2] = group.ship(x_parts[2], 2, True)
        late_far, near, x_parts, turns = lax.optimization_barrier((late_far, near, x_parts, turns))
        cos_flat, sin_a, sin_b, cos_t, sin_t, doc_row, doc_col = turns
        for n in (3, 1):
            x_parts[n] = group.ship(x_parts[n], n, True)
        late = join([late_far, late])
        qk, vo = group.gather_cores_joined(near, ways)
        lates = late[:rows], late[rows:]
        came = [group.bit(v, way[0]) for v, way in zip(lates, ways)]
        vec, bias_hidden, ada_all = modulate(me, act, qk, vo, tensor_count, rows)
        x_parts, g_parts, came, vec = lax.optimization_barrier((x_parts, g_parts, came, vec))
        for n in range(1, tensor_count):
            g_parts[n] = group.ship(g_parts[n], n, True)
        near = [group.gather_pair(v, got, way) for v, got, way in zip(lates, came, ways)]
    else:
        for n in range(1, tensor_count):
            x_parts[n] = group.ship(x_parts[n], n, True)
            g_parts[n] = group.ship(g_parts[n], n, True)
        late = group.z_pair(late, late_got)
        late = join([group.z(late, 1), late])
        flat = lambda v: group.whole(v.reshape(2, rows, width), 1).reshape(1, 2 * width, width)
        qk, vo = Held([flat(early[: 2 * rows])], [(0,)]), Held([flat(early[2 * rows :])], [(0,)])
        up, dn = (Held([group.whole(v, 0)[None]], [(0,)]) for v in (late[:rows], late[rows:]))
        w_all = group.whole(w_ada, 1)
        modulation = jnp.dot(
            act, w_all.astype(F32), precision=PRECISE, preferred_element_type=F32
        ) + group.whole(bias_ada, 0).astype(F32)
        small = group.whole(jnp.stack([bias_down, gain_one, gain_two]), 1).astype(F32)
        vec = jnp.concatenate([modulation.reshape(6, width), small, jnp.zeros((7, width), F32)])
        bias_hidden = group.whole(bias_up, 1)
        bias_hidden = jnp.concatenate([group.z(bias_hidden, k) for k in (1, 3, 0, 2)]).astype(F32)

    n_t, k, v, q_t, k_t, v_t = qkv(me, x_parts, vec, cos_flat, sin_a, sin_b, qk, vo)
    mix_t, log_sum = attend(q_t, k, v_t, doc_row, doc_col)
    if group.paired:
        mix_t, near, g_parts = lax.optimization_barrier((mix_t, near, g_parts))
        up, dn = (group.gather_cores(p, way) for p, way in zip(near, ways))
    att, n_two, n_two_t, d_down, d_down_t, d_bias_down, mix = middle(
        me, x_parts, g_parts, mix_t, vec, vo
    )
    size = w_up.shape[1]
    feed_args = (me, n_two, n_two_t, d_down, d_down_t, bias_hidden, up, dn)

    down, d_n, d_bias_a, *grads = feed(*feed_args, 0, None, 2 * size)
    sum_a = Sum(group, *grads)
    down, d_n, d_bias_b, *grads = feed(*feed_args, 2 * size, (down, d_n), 2 * size)
    down = tie(down, sum_a)
    exchange(sum_a)
    sum_b = Sum(group, *grads)
    *out_parts, d_mid, d_mix_t, sums, d_att_t = turn(
        me, x_parts, g_parts, att, down, d_n, vec, vo
    )
    d_mix_t, out_parts = tie((d_mix_t, out_parts), sum_a, sum_b)
    came = out_parts[:1] + [group.ship(out_parts[n], n, False) for n in range(1, tensor_count)]
    exchange(sum_a, sum_b)
    dq, dk, dv = attend_back(
        k, v, q_t, k_t, d_mix_t, mix_t, log_sum, doc_row, doc_col, cos_t, sin_t
    )
    dq, came = tie((dq, came), sum_a, sum_b)
    block_out = group.held_rows(came)
    sum_a.settle()
    exchange(sum_b)
    far_up = group.z(sum_a.total[0].astype(BF16), 1)
    grads = weight_grads(me, n_t, d_att_t, dq, dk, dv, mix, blocks)
    d_mid, grads, far_up, last = tie((d_mid, grads, far_up, sum_a.total[1]), sum_b)
    far_dn = group.z(last.astype(BF16), 1)
    sum_w = Sum(group, *grads)
    *in_parts, sums_one = first(me, x_parts, d_mid, vec, dq, dk, dv, qk, vo)

    in_parts, far_dn = tie((in_parts, far_dn), sum_w)
    exchange(sum_w)
    came = in_parts[:1] + [group.ship(in_parts[n], n, False) for n in range(1, tensor_count)]
    sum_b.settle()
    near = jnp.stack(sum_b.total) + jnp.stack([far_up, far_dn]).astype(F32)
    sums_one, near = tie((sums_one, near), sum_w)
    exchange(sum_w)
    d_bias = jnp.concatenate([d_bias_b.reshape(2, -1), d_bias_a.reshape(2, -1)])
    edge = mod_width + 3 * rows
    if group.paired:
        length = edge + tensor_count * rows + 2 * cond_size
        keep, send, d_cond = gather_up(
            me, vec, ada_all, sums, sums_one, d_bias_down, d_bias, act, cond, dp_count,
            length - length % cond_size,
        )
    else:
        d_gate_2, norm_2, d_shift_2, d_gate_1 = (sums[n : n + 1] for n in range(4))
        norm_1, d_shift_1 = sums_one[:1], sums_one[1:]
        d_mod = [
            d_shift_1, norm_1 * vec[GAIN_1], d_gate_1, d_shift_2, norm_2 * vec[GAIN_2], d_gate_2
        ]
        others = [norm_1 * (1.0 + vec[SCALE_1]), norm_2 * (1.0 + vec[SCALE_2]), d_bias_down]
        sliced = lambda t: t.reshape(dp_count, -1)
        d_mod = jnp.concatenate(d_mod, axis=1)
        d_cond = lax.dot_general(
            d_mod,
            w_all.astype(F32),
            (((1,), (1,)), ((), ())),
            precision=PRECISE,
            preferred_element_type=F32,
        ) * silu_slope(cond)
        table = jnp.concatenate(
            [sliced(d_mod)]
            + [sliced(t) for t in others]
            + [sliced(t) for t in d_bias]
            + [jnp.broadcast_to(act, (dp_count, cond_size))],
            axis=1,
        )
    half = near.shape[-1] // 2
    if group.paired:
        step = [keep, group.bit(send, 0)]
        step, came, near = tie((step, came, near), sum_w)
        sum_w.settle()
        step = jnp.concatenate(step, axis=1)
        step = [step[0]] + [group.step(step[n], 2 * n) for n in range(1, dp_count // 2)]
    else:
        step = [lax.all_to_all(table, "dp", split_axis=0, concat_axis=0, tiled=True)]
    feeds = group.z(near[..., half:].astype(BF16), 2)
    near_w, far_w = sum_w.total
    far_w = group.z(far_w.astype(BF16), 1)
    step, far_w, feeds, came = lax.optimization_barrier((step, far_w, feeds, came))
    near_w = near_w + far_w.astype(F32)
    grad = group.z(near_w[..., cols:].astype(BF16), 2)
    length = step[0].shape[-1]
    d_cond = jnp.pad(d_cond, ((0, 0), (0, length - cond_size)))
    arrived = jnp.concatenate([t.reshape(-1, length) for t in step] + [d_cond])
    arrived = jnp.stack([arrived] + [group.z(arrived, k) for k in range(1, tensor_count)])
    grad = near_w[..., :cols] + grad.astype(F32)
    grad_qkv, grad_out = grad[:3], grad[3].T
    grad_up, grad_down = near[..., :half] + feeds.astype(F32)
    input_grad = group.held_rows(came)
    place = jnp.asarray([0, 2, 1, 3])[order]
    arrived = arrived[order]
    conds = arrived[:, dp_count, :cond_size]
    arrived = arrived[:, :dp_count]
    totals = jnp.sum(arrived[..., :edge], axis=(0, 1))
    biases = arrived[..., edge : edge + tensor_count * rows].reshape(
        tensor_count, dp_count, tensor_count, rows
    )
    wanted = (jnp.arange(tensor_count) == place[:, None])[:, None, :, None]
    grad_bias_up = jnp.sum(jnp.where(wanted, biases, 0.0), axis=(0, 1, 2))
    grad_bias_ada = totals[:mod_width]
    grad_gain_one, grad_gain_two, grad_bias_down = (
        totals[mod_width + n * rows : mod_width + (n + 1) * rows] for n in range(3)
    )
    arrived = arrived.reshape(dp_count * tensor_count, -1)
    grad_ada = lax.dot_general(
        arrived[:, -cond_size:],
        arrived[:, :mod_width],
        (((0,), (0,)), ((), ())),
        precision=PRECISE,
        preferred_element_type=F32,
    )
    cond_grad = jnp.take(conds, jnp.arange(per_dp) + d % 2, axis=0)
    return (
        block_out,
        input_grad,
        cond_grad,
        grad_qkv,
        grad_out,
        grad_up,
        grad_bias_up[None],
        grad_down.T,
        grad_bias_down,
        grad_gain_one,
        grad_gain_two,
        grad_ada,
        grad_bias_ada,
    )


def solution(mesh):
    return jax.shard_map(
        shards,
        mesh=mesh,
        in_specs=(
            P("dp", "tensor", None),
            P("dp", None),
            P("dp", None),
            P("dp", None),
            P(None, "dp", "tensor"),
            P("tensor", "dp"),
            P("dp", "tensor"),
            P("tensor", "dp"),
            P("tensor", "dp"),
            P("dp"),
            P("dp"),
            P("dp"),
            P(None, "dp"),
            P("dp"),
            P("dp", "tensor", None),
        ),
        out_specs=(
            P("dp", "tensor", None),
            P("dp", "tensor", None),
            P("dp", None),
            P(None, "dp", "tensor"),
            P("tensor", "dp"),
            P("dp", "tensor"),
            P("tensor", "dp"),
            P("tensor", "dp"),
            P("dp"),
            P("dp"),
            P("dp"),
            P(None, "dp"),
            P("dp"),
        ),
        check_vma=False,
    )
```

time: 421 us -> 403 us (0.957)
  waiting for transfers between devices: 90.3 us -> 61.3 us
  starting transfers between devices: 79.7 us -> 91 us
    ppermute x11 -> x12, waiting for transfers between devices: 68.9 us -> 33.6 us  [z(): return lax.ppermute(v, 'tensor', [(i, i ^ k) for i in range(self.tensor)])]
    convert_element_type x2 -> x11, other arithmetic: 2.04 us -> 14.2 us  [the longest x9 11.6 us: split(): out.append((b, sum((t.astype(F32) for t in go)).astype(BF16)))]
    ppermute x12 -> x15, starting transfers between devices: 32.4 us -> 42.9 us  [the longest x12 39.3 us: ship(): return lax.ppermute(v, BOTH, pairs)]
    add x12 -> x3, other arithmetic: 13 us -> 3.51 us  [the longest x2 3.47 us: settle(): sum((t[0].astype(F32) for t in terms))]
    ppermute x12 -> x15, waiting for transfers between devices: 11.4 us -> 20.1 us  [the longest x12 18.4 us: ship(): return lax.ppermute(v, BOTH, pairs)]
    ppermute x11 -> x12, starting transfers between devices: 21 us -> 25.7 us  [z(): return lax.ppermute(v, 'tensor', [(i, i ^ k) for i in range(self.tensor)])]
    ppermute x30 -> x27, starting transfers between devices: 26.3 us -> 22.4 us  [bit(): return lax.ppermute(v, 'dp', [(i, i ^ 1 << b) for i in range(self.dp)])]
    ppermute x30 -> x27, waiting for transfers between devices: 10.1 us -> 7.58 us  [bit(): return lax.ppermute(v, 'dp', [(i, i ^ 1 << b) for i in range(self.dp)])]
  transfers between devices with their start and end apart: 53 -> 54, of which waited for: 18 -> 16; matrix products, arithmetic and copies ran while one was open for 10% -> 11% of each run, Pallas kernels for 36% -> 37%
where the time goes in v3:
time: 403 us; the launch traced here: 397 us
  Pallas kernels  173 us (43%)
  starting transfers between devices  91 us (23%)
  waiting for transfers between devices  61.3 us (15%)
  other arithmetic  40.9 us (10%)
  local copies, waits for them, and re-layouts  27.7 us (7%)
    pallas_call x2, Pallas kernels, feed(): pl.pallas_call(partial(feed_kernel, up, dn, steps, first), grid=(steps,),...  52 us
    ppermute x12, starting transfers between devices, ship(): return lax.ppermute(v, BOTH, pairs)  39.3 us
    pallas_call x1, Pallas kernels, attend_back(): pl.pallas_call(attend_back_kernel, grid=(count,), in_specs=[flat] * 2 + [...  35.7 us
    ppermute x12, waiting for transfers between devices, z(): return lax.ppermute(v, 'tensor', [(i, i ^ k) for i in range(self.tensor)])  33.6 us
    ppermute x12, starting transfers between devices, z(): return lax.ppermute(v, 'tensor', [(i, i ^ k) for i in range(self.tensor)])  25.7 us
    ppermute x27, starting transfers between devices, bit(): return lax.ppermute(v, 'dp', [(i, i ^ 1 << b) for i in range(self.dp)])  22.4 us
    pallas_call x1, Pallas kernels, attend(): pl.pallas_call(attend_kernel, grid=(pairs,), in_specs=[turned, flat, turn...  20.2 us
    ppermute x12, waiting for transfers between devices, ship(): return lax.ppermute(v, BOTH, pairs)  18.4 us
  transfers between devices with their start and end apart: 54, of which 16 were waited for; matrix products, arithmetic and copies ran while one was open for 11% of the time, Pallas kernels for 37%

profile of v3, /device:TPU:0, one launch (start us, length us, event | category | flops | bytes accessed | tf_op | source)
XLA Modules:
  0.0 397.1 jit_solution(15580874574123209760)
XLA Ops:
  3.3 4.1 %collective-permute-start = (bf16[400,192]{1,0:T(8,128)(2,1)S(1)}, bf16[400,192]{1,0:T(8,128)(2,1)S(1)}, u32[]{:S(2)}, u32[]{:S(2)}) collective-permute-start(bf16[400,192]{1,0:T(8,128)(2,1)S(1)} %pad_maximum_fusion.15), channel_id=1, source_target_pairs={{0,2},{1,3},{2,0},{3,1},{4,6},{5,7},{6,4},{7,5},{8,10},{9,11},{10,... | collective-permute-start | bytes 460808 | tf_op jit(solution)/shard_map/ppermute | solution.py:928
  10.1 6.8 %collective-permute-done = bf16[400,192]{1,0:T(8,128)(2,1)S(1)} collective-permute-done((bf16[400,192]{1,0:T(8,128)(2,1)S(1)}, bf16[400,192]{1,0:T(8,128)(2,1)S(1)}, u32[]{:S(2)}, u32[]{:S(2)}) %collective-permute-start) | collective-permute-done | bytes 153632 | tf_op jit(solution)/shard_map/ppermute | solution.py:928
  18.9 1.7 dynamic-slice_bitcast_fusion
  20.6 4.9 %collective-permute-done.1 = bf16[400,384]{1,0:T(8,128)(2,1)S(1)} collective-permute-done((bf16[400,384]{1,0:T(8,128)(2,1)S(1)}, bf16[400,384]{1,0:T(8,128)(2,1)S(1)}, u32[]{:S(2)}, u32[]{:S(2)}) %collective-permute-start.1) | collective-permute-done | bytes 307232 | tf_op jit(solution)/shard_map/ppermute | solution.py:928
  26.1 1.4 collective-permute-start.4
  27.6 1.6 collective-permute-start.3
  29.2 3.3 collective-permute-start.2
  32.5 12.4 %collective-permute-done.2 = bf16[192,768]{1,0:T(8,128)(2,1)S(1)} collective-permute-done((bf16[192,768]{1,0:T(8,128)(2,1)S(1)}, bf16[192,768]{1,0:T(8,128)(2,1)S(1)}, u32[]{:S(2)}, u32[]{:S(2)}) %collective-permute-start.2) | collective-permute-done | bytes 294944 | tf_op jit(solution)/shard_map/ppermute | solution.py:928
  47.9 5.3 %collective-permute-start.8 = (bf16[256,768]{1,0:T(8,128)(2,1)S(1)}, bf16[256,768]{1,0:T(8,128)(2,1)S(1)}, u32[]{:S(2)}, u32[]{:S(2)}) collective-permute-start(bf16[256,768]{1,0:T(8,128)(2,1)S(1)} %copy-done.39), channel_id=1, source_target_pairs={{0,2},{2,0},{3,1},{4,6},{5,7},{7,5},{8,10},{10,8},{11,9},{12,14},{... | collective-permute-start | bytes 1179656 | tf_op jit(solution)/shard_map/ppermute | solution.py:954
  56.9 2.5 rotary.1
  59.4 9.2 %collective-permute-done.8.refs_2_ = bf16[256,768]{1,0:T(8,128)(2,1)S(1)} collective-permute-done((bf16[256,768]{1,0:T(8,128)(2,1)S(1)}, bf16[256,768]{1,0:T(8,128)(2,1)S(1)}, u32[]{:S(2)}, u32[]{:S(2)}) %collective-permute-start.8) | collective-permute-done | bytes 393248 | tf_op jit(solution)/shard_map/ppermute | solution.py:954
  72.5 1.8 constant_dynamic-update-slice_fusion.2
  74.4 1.6 slice_bitcast_fusion.6
  76.0 1.5 collective-permute-start.11
  77.5 1.5 collective-permute-start.12
  80.3 6.7 %collective-permute-start.9 = (bf16[256,768]{1,0:T(8,128)(2,1)}, bf16[256,768]{1,0:T(8,128)(2,1)}, u32[]{:S(2)}, u32[]{:S(2)}) collective-permute-start(bf16[256,768]{1,0:T(8,128)(2,1)} %get-tuple-element.184), channel_id=1, source_target_pairs={{0,1},{1,0},{3,2},{4,5},{6,7},{7,6},{8,9},{9,8},{11,10},{12,13},{1... | collective-permute-start | bytes 1179656 | tf_op jit(solution)/shard_map/ppermute | solution.py:954
  88.6 3.8 modulate.1
  92.5 3.9 collective-permute-done.9.refs_1_
  100.1 5.4 %collective-permute-start.16 = (bf16[256,768]{1,0:T(8,128)(2,1)S(1)}, bf16[256,768]{1,0:T(8,128)(2,1)S(1)}, u32[]{:S(2)}, u32[]{:S(2)}) collective-permute-start(bf16[256,768]{1,0:T(8,128)(2,1)S(1)} %copy-done.37), channel_id=1, source_target_pairs={{0,1},{1,0},{3,2},{4,5},{6,7},{7,6},{8,9},{9,8},{11,10},{12,13},{1... | collective-permute-start | bytes 1179656 | tf_op jit(solution)/shard_map/ppermute | solution.py:954
  105.5 1.9 collective-permute-start.17
  107.4 1.5 collective-permute-start.18
  108.9 12.5 %qkv.1 = (bf16[768,1024]{1,0:T(8,128)(2,1)}, bf16[1024,768]{1,0:T(8,128)(2,1)}, bf16[1024,768]{1,0:T(8,128)(2,1)}, bf16[768,1024]{1,0:T(8,128)(2,1)}, bf16[768,1...) custom-call(s32[1]{0:T(128)} %bitcast.me, bf16[256,768]{1,0:T(8,128)(2,1)} %get-tuple-element.197.refs_0_, ...), custom_call_target="tpu_custom_call" | custom-call | flops 3623878656 | bytes 16000000 | tf_op jit(solution)/shard_map/qkv/pallas_call | solution.py:196
  121.4 20.2 %attend.1 = (bf16[768,1024]{1,0:T(8,128)(2,1)}, f32[6,2,1,1024]{3,2,1,0:T(1,128)}) custom-call(bf16[768,1024]{1,0:T(8,128)(2,1)} %get-tuple-element.207.q_t, bf16[1024,768]{1,0:T(8,128)(2,1)} %get-tuple-element.205.k, bf16[768,1024]{1,0:T(8,128)(2,1)} %get-tuple-element.209.v_t, s32[1,1024]{1,0:T(1,128)} %bitcast.234, s32[1024,1]{1,0:T(8,128)} %copy.70.doc_col), custom_call_target="tpu_custom_call" | custom-call | flops 12884901888 | bytes 8000000 | tf_op jit(solution)/shard_map/attend/pallas_call | solution.py:282
  141.8 1.6 collective-permute-start.19
  144.6 9.3 %middle.1 = (f32[1024,768]{1,0:T(8,128)}, bf16[1024,768]{1,0:T(8,128)(2,1)}, bf16[768,1024]{1,0:T(8,128)(2,1)}, bf16[1024,768]{1,0:T(8,128)(2,1)}, bf16[768,1024...) custom-call(s32[1]{0:T(128)} %bitcast.me, bf16[256,768]{1,0:T(8,128)(2,1)} %get-tuple-element.197.refs_0_, ...), custom_call_target="tpu_custom_call" | custom-call | flops 1207959552 | bytes 16000000 | tf_op jit(solution)/shard_map/middle/pallas_call | solution.py:344
  154.0 25.2 %feed.2 = (f32[1024,768]{1,0:T(8,128)}, f32[1024,768]{1,0:T(8,128)}, f32[3,1,512]{2,1,0:T(1,128)}, bf16[2,4,96,1536]{3,2,1,0:T(8,128)(2,1)}, bf16[2,4,96,1536]{3,2,1,0:T(8,128)(2,1)}) custom-call(s32[1]{0:T(128)} %bitcast.me, bf16[1024,768]{1,0:T(8,128)(2,1)} %get-tuple-element.225.refs_0_, bf16[768,1024]{1,0:T(8,128)(2,1)} %get-tuple-element.226.refs_1_, ...), custom_call_target="tpu_custom_call" | custom-call | flops 14495514624 | bytes 20000000 | tf_op jit(solution)/shard_map/feed/pallas_call | solution.py:480
  179.7 26.8 %feed.3 = (f32[1024,768]{1,0:T(8,128)}, f32[1024,768]{1,0:T(8,128)}, f32[3,1,512]{2,1,0:T(1,128)}, bf16[2,4,96,1536]{3,2,1,0:T(8,128)(2,1)}, bf16[2,4,96,1536]{3,2,1,0:T(8,128)(2,1)}) custom-call(s32[1]{0:T(128)} %bitcast.me, bf16[1024,768]{1,0:T(8,128)(2,1)} %get-tuple-element.225.refs_0_, bf16[768,1024]{1,0:T(8,128)(2,1)} %get-tuple-element.226.refs_1_, ...), custom_call_target="tpu_custom_call" | custom-call | flops 14495514624 | bytes 20000000 | tf_op jit(solution)/shard_map/feed/pallas_call | solution.py:480
  206.7 2.0 fusion.1
  208.7 2.0 fusion
  210.7 1.5 collective-permute-start.25
  213.3 12.8 %turn.1 = (bf16[256,768]{1,0:T(8,128)(2,1)}, bf16[256,768]{1,0:T(8,128)(2,1)}, bf16[256,768]{1,0:T(8,128)(2,1)}, bf16[256,768]{1,0:T(8,128)(2,1)}, f32[1024,768]...) custom-call(s32[1]{0:T(128)} %bitcast.me, ...), custom_call_target="tpu_custom_call" | custom-call | flops 1207959552 | bytes 24000000 | tf_op jit(solution)/shard_map/turn/pallas_call | solution.py:552
  228.7 1.4 fusion.15
  233.7 4.8 %collective-permute-start.27 = (bf16[256,768]{1,0:T(8,128)(2,1)}, bf16[256,768]{1,0:T(8,128)(2,1)}, u32[]{:S(2)}, u32[]{:S(2)}) collective-permute-start(bf16[256,768]{1,0:T(8,128)(2,1)} %get-tuple-element.254), channel_id=1, source_target_pairs={{0,1},{1,0},{2,3},{5,4},{6,7},{7,6},{8,9},{9,8},{10,11},{13,12},{1... | collective-permute-start | bytes 1179656 | tf_op jit(solution)/shard_map/ppermute | solution.py:954
  238.5 3.6 collective-permute-start.28
  242.1 2.0 collective-permute-start.29
  244.1 35.7 %attend_back.1 = (bf16[1024,768]{1,0:T(8,128)(2,1)}, bf16[1024,768]{1,0:T(8,128)(2,1)}, bf16[1024,768]{1,0:T(8,128)(2,1)}) custom-call(bf16[1024,768]{1,0:T(8,128)(2,1)} %get-tuple-element.205.k, bf16[1024,768]{1,0:T(8,128)(2,1)} %get-tuple-element.206.v, bf16[768,1024]{1,0:T(8,128)(2,1)} %get-tuple-element.207.q_t, ...), custom_call_target="tpu_custom_call" | custom-call | flops 22548578304 | bytes 14000000 | tf_op jit(solution)/shard_map/attend_back/pallas_call | solution.py:641
  279.9 2.1 convert_add_fusion.4
  282.0 1.9 fusion.13
  285.1 1.6 collective-permute-start.33
  287.4 1.7 collective-permute-start.32
  289.1 9.0 %weight_grads.1 = (bf16[2,4,4,96,384]{4,3,2,1,0:T(8,128)(2,1)}, bf16[2,4,4,96,384]{4,3,2,1,0:T(8,128)(2,1)}) custom-call(s32[1]{0:T(128)} %bitcast.me, bf16[768,1024]{1,0:T(8,128)(2,1)} %get-tuple-element.268.n_t, bf16[768,1024]{1,0:T(8,128)(2,1)} %get-tuple-element.269.d_att_t, bf16[1024,768]{1,0:T(8,128)(2,1)} %get-tuple-element.270.dq.refs_6_, ...), custom_call_target="tpu_custom_call" | custom-call | flops 4831838208 | bytes 14000000 | tf_op jit(solution)/shard_map/weight_grads/pallas_call | solution.py:894
  304.8 12.7 %first.1 = (bf16[256,768]{1,0:T(8,128)(2,1)}, bf16[256,768]{1,0:T(8,128)(2,1)}, bf16[256,768]{1,0:T(8,128)(2,1)}, bf16[256,768]{1,0:T(8,128)(2,1)}, f32[2,768]{1,0:T(2,128)}) custom-call(s32[1]{0:T(128)} %bitcast.me, bf16[256,768]{1,0:T(8,128)(2,1)} %get-tuple-element.197.refs_0_, bf16[256,768]{1,0:T(8,128)(2,1)} %collective-permute-done.9.refs_1_, ...), custom_call_target="tpu_custom_call" | custom-call | flops 3623878656 | bytes 20000000 | tf_op jit(solution)/shard_map/first/pallas_call | solution.py:697
  322.6 1.4 fusion.12
  324.1 3.5 collective-permute-start.40
  327.5 1.9 collective-permute-start.41
  329.4 1.5 collective-permute-start.42
  331.1 5.2 %collective-permute-done.38 = bf16[2,4,96,384]{3,2,1,0:T(8,128)(2,1)S(1)} collective-permute-done((bf16[2,4,96,384]{3,2,1,0:T(8,128)(2,1)S(1)}, bf16[2,4,96,384]{3,2,1,0:T(8,128)(2,1)S(1)}, u32[]{:S(2)}, u32[]{:S(2)}) %collective-permute-start.38) | collective-permute-done | bytes 589856 | tf_op jit(solution)/shard_map/ppermute | solution.py:922
  336.6 1.5 fusion.9
  338.0 1.6 collective-permute-start.43
  339.6 1.4 collective-permute-start.44
  341.0 1.4 pad_maximum_fusion
  342.4 2.3 gather_up.1
  344.7 4.3 %collective-permute-done.40 = bf16[256,768]{1,0:T(8,128)(2,1)S(1)} collective-permute-done((bf16[256,768]{1,0:T(8,128)(2,1)}, bf16[256,768]{1,0:T(8,128)(2,1)S(1)}, u32[]{:S(2)}, u32[]{:S(2)}) %collective-permute-start.40) | collective-permute-done | bytes 393248 | tf_op jit(solution)/shard_map/ppermute | solution.py:954
  351.7 6.3 %collective-permute-start.48 = (bf16[4,96,384]{2,1,0:T(8,128)(2,1)S(1)}, bf16[4,96,384]{2,1,0:T(8,128)(2,1)S(1)}, u32[]{:S(2)}, u32[]{:S(2)}) collective-permute-start(bf16[4,96,384]{2,1,0:T(8,128)(2,1)S(1)} %fusion.7), channel_id=1, source_target_pairs={{0,1},{1,0},{2,3},{3,2},{4,5},{5,4},{6,7},{7,6},{8,9},{9,8},{10,11... | collective-permute-start | bytes 884744 | tf_op jit(solution)/shard_map/ppermute | solution.py:928
  360.2 1.5 collective-permute-start.46
  364.7 1.6 collective-permute-done.47
  366.3 4.8 %collective-permute-done.48 = bf16[4,96,384]{2,1,0:T(8,128)(2,1)S(1)} collective-permute-done((bf16[4,96,384]{2,1,0:T(8,128)(2,1)S(1)}, bf16[4,96,384]{2,1,0:T(8,128)(2,1)S(1)}, u32[]{:S(2)}, u32[]{:S(2)}) %collective-permute-start.48) | collective-permute-done | bytes 294944 | tf_op jit(solution)/shard_map/ppermute | solution.py:928
  372.5 1.5 concatenate.61
  374.0 2.8 collective-permute-start.50
  376.8 2.8 collective-permute-start.51
  382.8 1.6 collective-permute-start.53
  385.9 2.3 collective-permute-done.51
  389.0 1.4 fusion.17
  393.0 2.4 collective-permute-done.53
  (282 shorter events, 66.8 us)
Async XLA Ops:
  0.7 18.2 %copy-start.16 = (bf16[3,256,768]{2,1,0:T(8,128)(2,1)S(1)}, bf16[3,256,768]{2,1,0:T(8,128)(2,1)}, u32[]{:S(2)}) copy-start(bf16[3,256,768]{2,1,0:T(8,128)(2,1)} %param.16) | copy-start | bytes 3538948
  3.3 13.6 %collective-permute-start = (bf16[400,192]{1,0:T(8,128)(2,1)S(1)}, bf16[400,192]{1,0:T(8,128)(2,1)S(1)}, u32[]{:S(2)}, u32[]{:S(2)}) collective-permute-start(bf16[400,192]{1,0:T(8,128)(2,1)S(1)} %pad_maximum_fusion.15), channel_id=1, source_target_pairs={{0,2},{1,3},{2,0},{3,1},{4,6},{5,7},{6,4},{7,5},{8,10},{9,11},{10,... | collective-permute-start | bytes 460808 | tf_op jit(solution)/shard_map/ppermute | solution.py:928
  17.1 8.5 %collective-permute-start.1 = (bf16[400,384]{1,0:T(8,128)(2,1)S(1)}, bf16[400,384]{1,0:T(8,128)(2,1)S(1)}, u32[]{:S(2)}, u32[]{:S(2)}) collective-permute-start(bf16[400,384]{1,0:T(8,128)(2,1)S(1)} %pad_maximum_fusion.13), channel_id=1, source_target_pairs={{0,1},{1,0},{2,3},{3,2},{4,5},{5,4},{6,7},{7,6},{8,9},{9,8},{10,11... | collective-permute-start | bytes 921608 | tf_op jit(solution)/shard_map/ppermute | solution.py:928
  18.9 27.4 %copy-start.7 = (bf16[192,768]{1,0:T(8,128)(2,1)}, bf16[192,768]{1,0:T(8,128)(2,1)S(1)}, u32[]{:S(2)}) copy-start(bf16[192,768]{1,0:T(8,128)(2,1)S(1)} %pad_maximum_fusion.14) | copy-start | bytes 884740
  26.1 18.8 %collective-permute-start.4 = (bf16[256,768]{1,0:T(8,128)(2,1)S(1)}, bf16[256,768]{1,0:T(8,128)(2,1)S(1)}, u32[]{:S(2)}, u32[]{:S(2)}) collective-permute-start(bf16[256,768]{1,0:T(8,128)(2,1)S(1)} %concatenate.53), channel_id=1, source_target_pairs={{0,16},{4,20},{8,24},{12,28},{16,0},{20,4},{24,8},{28,12},{1,17},{... | collective-permute-start | bytes 1179656 | tf_op jit(solution)/shard_map/ppermute | solution.py:922
  27.6 17.3 %collective-permute-start.3 = (bf16[256,768]{1,0:T(8,128)(2,1)S(1)}, bf16[256,768]{1,0:T(8,128)(2,1)S(1)}, u32[]{:S(2)}, u32[]{:S(2)}) collective-permute-start(bf16[256,768]{1,0:T(8,128)(2,1)S(1)} %get-tuple-element.410), channel_id=1, source_target_pairs={{0,8},{4,12},{8,0},{12,4},{16,24},{20,28},{24,16},{28,20},{1,9},{5... | collective-permute-start | bytes 1179656 | tf_op jit(solution)/shard_map/ppermute | solution.py:922
  29.2 15.7 %collective-permute-start.2 = (bf16[192,768]{1,0:T(8,128)(2,1)S(1)}, bf16[192,768]{1,0:T(8,128)(2,1)S(1)}, u32[]{:S(2)}, u32[]{:S(2)}) collective-permute-start(bf16[192,768]{1,0:T(8,128)(2,1)S(1)} %pad_maximum_fusion.14), channel_id=1, source_target_pairs={{0,2},{1,3},{2,0},{3,1},{4,6},{5,7},{6,4},{7,5},{8,10},{9,11},{10,... | collective-permute-start | bytes 884744 | tf_op jit(solution)/shard_map/ppermute | solution.py:928
  45.0 23.7 %copy-start.4 = (bf16[2,256,768]{2,1,0:T(8,128)(2,1)}, bf16[2,256,768]{2,1,0:T(8,128)(2,1)S(1)}, u32[]{:S(2)}) copy-start(bf16[2,256,768]{2,1,0:T(8,128)(2,1)S(1)} %pad_maximum_fusion.9) | copy-start | bytes 2359300
  45.0 23.7 %collective-permute-start.7 = (bf16[2,256,768]{2,1,0:T(8,128)(2,1)S(1)}, bf16[2,256,768]{2,1,0:T(8,128)(2,1)S(1)}, u32[]{:S(2)}, u32[]{:S(2)}) collective-permute-start(bf16[2,256,768]{2,1,0:T(8,128)(2,1)S(1)} %pad_maximum_fusion.9), channel_id=1, source_target_pairs={{0,8},{4,12},{8,0},{12,4},{16,24},{20,28},{24,16},{28,20},{1,9},{5... | collective-permute-start | bytes 2359304 | tf_op jit(solution)/shard_map/ppermute | solution.py:922
  45.7 23.0 %copy-start.6 = (bf16[2,256,768]{2,1,0:T(8,128)(2,1)}, bf16[2,256,768]{2,1,0:T(8,128)(2,1)S(1)}, u32[]{:S(2)}) copy-start(bf16[2,256,768]{2,1,0:T(8,128)(2,1)S(1)} %pad_maximum_fusion.8) | copy-start | bytes 2359300
  45.7 23.0 %collective-permute-start.6 = (bf16[2,256,768]{2,1,0:T(8,128)(2,1)S(1)}, bf16[2,256,768]{2,1,0:T(8,128)(2,1)}, u32[]{:S(2)}, u32[]{:S(2)}) collective-permute-start(bf16[2,256,768]{2,1,0:T(8,128)(2,1)S(1)} %pad_maximum_fusion.8), channel_id=1, source_target_pairs={{0,16},{4,20},{8,24},{12,28},{16,0},{20,4},{24,8},{28,12},{1,17},{... | collective-permute-start | bytes 2359304 | tf_op jit(solution)/shard_map/ppermute | solution.py:922
  47.1 21.6 %collective-permute-start.5 = (bf16[192,1536]{1,0:T(8,128)(2,1)}, bf16[192,1536]{1,0:T(8,128)(2,1)}, u32[]{:S(2)}, u32[]{:S(2)}) collective-permute-start(bf16[192,1536]{1,0:T(8,128)(2,1)} %pad_maximum_fusion.11), channel_id=1, source_target_pairs={{0,1},{1,0},{2,3},{3,2},{4,5},{5,4},{6,7},{7,6},{8,9},{9,8},{10,11... | collective-permute-start | bytes 1769480 | tf_op jit(solution)/shard_map/ppermute | solution.py:928
  47.9 20.8 %collective-permute-start.8 = (bf16[256,768]{1,0:T(8,128)(2,1)S(1)}, bf16[256,768]{1,0:T(8,128)(2,1)S(1)}, u32[]{:S(2)}, u32[]{:S(2)}) collective-permute-start(bf16[256,768]{1,0:T(8,128)(2,1)S(1)} %copy-done.39), channel_id=1, source_target_pairs={{0,2},{2,0},{3,1},{4,6},{5,7},{7,5},{8,10},{10,8},{11,9},{12,14},{... | collective-permute-start | bytes 1179656 | tf_op jit(solution)/shard_map/ppermute | solution.py:954
  56.3 31.2 %copy-start.50 = (s32[1,1,4,256]{3,1,2,0:T(1,128)}, s32[1,1,4,256]{3,1,2,0:T(1,128)S(1)}, u32[]{:S(2)}) copy-start(s32[1,1,4,256]{3,1,2,0:T(1,128)S(1)} %copy.80) | copy-start | bytes 12292
  72.4 16.2 %collective-permute-start.13 = (bf16[8,256,768]{2,1,0:T(8,128)(2,1)S(1)}, bf16[8,256,768]{2,1,0:T(8,128)(2,1)}, u32[]{:S(2)}, u32[]{:S(2)}) collective-permute-start(bf16[8,256,768]{2,1,0:T(8,128)(2,1)S(1)} %constant_dynamic-update-slice_fusion.3.refs_0_.refs_2_.refs_8_.refs_10_.refs_12_.refs_9_.refs_11_), channel_id=1, source_target_pairs={{0,4},{4,0},{8,12},{12,8},{16,20},{20,16},{24,28},{28,24},{1,5},{5... | collective-permute-start | bytes 9437192 | tf_op jit(solution)/shard_map/ppermute | solution.py:922
  76.0 20.3 %collective-permute-start.11 = (bf16[96,3072]{1,0:T(8,128)(2,1)}, bf16[96,3072]{1,0:T(8,128)(2,1)}, u32[]{:S(2)}, u32[]{:S(2)}) collective-permute-start(bf16[96,3072]{1,0:T(8,128)(2,1)} %get-tuple-element.396), channel_id=1, source_target_pairs={{0,8},{4,12},{8,0},{12,4},{16,24},{20,28},{24,16},{28,20},{1,9},{5... | collective-permute-start | bytes 1769480 | tf_op jit(solution)/shard_map/ppermute | solution.py:922
  77.5 18.8 %collective-permute-start.12 = (bf16[96,3072]{1,0:T(8,128)(2,1)}, bf16[96,3072]{1,0:T(8,128)(2,1)}, u32[]{:S(2)}, u32[]{:S(2)}) collective-permute-start(bf16[96,3072]{1,0:T(8,128)(2,1)} %get-tuple-element.395), channel_id=1, source_target_pairs={{0,16},{4,20},{8,24},{12,28},{16,0},{20,4},{24,8},{28,12},{1,17},{... | collective-permute-start | bytes 1769480 | tf_op jit(solution)/shard_map/ppermute | solution.py:922
  79.0 13.4 %collective-permute-start.10 = (bf16[256,768]{1,0:T(8,128)(2,1)}, bf16[256,768]{1,0:T(8,128)(2,1)S(1)}, u32[]{:S(2)}, u32[]{:S(2)}) collective-permute-start(bf16[256,768]{1,0:T(8,128)(2,1)} %get-tuple-element.186), channel_id=1, source_target_pairs={{1,2},{2,1},{3,0},{4,7},{5,6},{6,5},{9,10},{10,9},{11,8},{12,15},{... | collective-permute-start | bytes 1179656 | tf_op jit(solution)/shard_map/ppermute | solution.py:954
  80.3 16.0 %collective-permute-start.9 = (bf16[256,768]{1,0:T(8,128)(2,1)}, bf16[256,768]{1,0:T(8,128)(2,1)}, u32[]{:S(2)}, u32[]{:S(2)}) collective-permute-start(bf16[256,768]{1,0:T(8,128)(2,1)} %get-tuple-element.184), channel_id=1, source_target_pairs={{0,1},{1,0},{3,2},{4,5},{6,7},{7,6},{8,9},{9,8},{11,10},{12,13},{1... | collective-permute-start | bytes 1179656 | tf_op jit(solution)/shard_map/ppermute | solution.py:954
  97.5 45.9 %copy-start.21 = (bf16[2,96,3072]{2,1,0:T(8,128)(2,1)}, bf16[2,96,3072]{2,1,0:T(8,128)(2,1)S(1)}, u32[]{:S(2)}) copy-start(bf16[2,96,3072]{2,1,0:T(8,128)(2,1)S(1)} %pad_maximum_fusion.3.refs_9_.refs_11_) | copy-start | bytes 3538948
  97.6 44.2 %collective-permute-start.15 = (bf16[2,96,3072]{2,1,0:T(8,128)(2,1)S(1)}, bf16[2,96,3072]{2,1,0:T(8,128)(2,1)}, u32[]{:S(2)}, u32[]{:S(2)}) collective-permute-start(bf16[2,96,3072]{2,1,0:T(8,128)(2,1)S(1)} %pad_maximum_fusion.3.refs_9_.refs_11_), channel_id=1, source_target_pairs={{0,8},{4,12},{8,0},{12,4},{16,24},{20,28},{24,16},{28,20},{1,9},{5... | collective-permute-start | bytes 3538952 | tf_op jit(solution)/shard_map/ppermute | solution.py:922
  99.5 42.2 %copy-start.22 = (bf16[2,96,3072]{2,1,0:T(8,128)(2,1)}, bf16[2,96,3072]{2,1,0:T(8,128)(2,1)S(1)}, u32[]{:S(2)}) copy-start(bf16[2,96,3072]{2,1,0:T(8,128)(2,1)S(1)} %pad_maximum_fusion.2.refs_5_.refs_7_) | copy-start | bytes 3538948
  99.5 42.2 %collective-permute-start.14 = (bf16[2,96,3072]{2,1,0:T(8,128)(2,1)S(1)}, bf16[2,96,3072]{2,1,0:T(8,128)(2,1)}, u32[]{:S(2)}, u32[]{:S(2)}) collective-permute-start(bf16[2,96,3072]{2,1,0:T(8,128)(2,1)S(1)} %pad_maximum_fusion.2.refs_5_.refs_7_), channel_id=1, source_target_pairs={{0,16},{4,20},{8,24},{12,28},{16,0},{20,4},{24,8},{28,12},{1,17},{... | collective-permute-start | bytes 3538952 | tf_op jit(solution)/shard_map/ppermute | solution.py:922
  100.1 41.6 %collective-permute-start.16 = (bf16[256,768]{1,0:T(8,128)(2,1)S(1)}, bf16[256,768]{1,0:T(8,128)(2,1)S(1)}, u32[]{:S(2)}, u32[]{:S(2)}) collective-permute-start(bf16[256,768]{1,0:T(8,128)(2,1)S(1)} %copy-done.37), channel_id=1, source_target_pairs={{0,1},{1,0},{3,2},{4,5},{6,7},{7,6},{8,9},{9,8},{11,10},{12,13},{1... | collective-permute-start | bytes 1179656 | tf_op jit(solution)/shard_map/ppermute | solution.py:954
  105.5 36.2 %collective-permute-start.17 = (bf16[256,768]{1,0:T(8,128)(2,1)S(1)}, bf16[256,768]{1,0:T(8,128)(2,1)S(1)}, u32[]{:S(2)}, u32[]{:S(2)}) collective-permute-start(bf16[256,768]{1,0:T(8,128)(2,1)S(1)} %copy-done.36), channel_id=1, source_target_pairs={{0,2},{2,0},{3,1},{4,6},{5,7},{7,5},{8,10},{10,8},{11,9},{12,14},{... | collective-permute-start | bytes 1179656 | tf_op jit(solution)/shard_map/ppermute | solution.py:954
  107.4 34.3 %collective-permute-start.18 = (bf16[256,768]{1,0:T(8,128)(2,1)S(1)}, bf16[256,768]{1,0:T(8,128)(2,1)S(1)}, u32[]{:S(2)}, u32[]{:S(2)}) collective-permute-start(bf16[256,768]{1,0:T(8,128)(2,1)S(1)} %copy-done.35), channel_id=1, source_target_pairs={{1,2},{2,1},{3,0},{4,7},{5,6},{6,5},{9,10},{10,9},{11,8},{12,15},{... | collective-permute-start | bytes 1179656 | tf_op jit(solution)/shard_map/ppermute | solution.py:954
  121.4 22.5 %copy-start.51 = (f32[4,768]{1,0:T(4,128)S(1)}, f32[4,768]{1,0:T(4,128)}, u32[]{:S(2)}) copy-start(f32[4,768]{1,0:T(4,128)} %get-tuple-element.229) | copy-start | bytes 36868
  141.8 12.2 %collective-permute-start.19 = (bf16[2,96,3072]{2,1,0:T(8,128)(2,1)S(1)}, bf16[2,96,3072]{2,1,0:T(8,128)(2,1)}, u32[]{:S(2)}, u32[]{:S(2)}) collective-permute-start(bf16[2,96,3072]{2,1,0:T(8,128)(2,1)S(1)} %pad_maximum_fusion.2.refs_5_.refs_7_), channel_id=1, source_target_pairs={{0,4},{4,0},{8,12},{12,8},{16,20},{20,16},{24,28},{28,24},{1,5},{5... | collective-permute-start | bytes 3538952 | tf_op jit(solution)/shard_map/ppermute | solution.py:922
  143.4 10.6 %collective-permute-start.20 = (bf16[2,96,3072]{2,1,0:T(8,128)(2,1)}, bf16[2,96,3072]{2,1,0:T(8,128)(2,1)}, u32[]{:S(2)}, u32[]{:S(2)}) collective-permute-start(bf16[2,96,3072]{2,1,0:T(8,128)(2,1)} %collective-permute-done.14.refs_6_.refs_8_), channel_id=1, source_target_pairs={{0,4},{4,0},{8,12},{12,8},{16,20},{20,16},{24,28},{28,24},{1,5},{5... | collective-permute-start | bytes 3538952 | tf_op jit(solution)/shard_map/ppermute | solution.py:922
  143.5 10.5 %collective-permute-start.21 = (bf16[2,96,3072]{2,1,0:T(8,128)(2,1)S(1)}, bf16[2,96,3072]{2,1,0:T(8,128)(2,1)}, u32[]{:S(2)}, u32[]{:S(2)}) collective-permute-start(bf16[2,96,3072]{2,1,0:T(8,128)(2,1)S(1)} %pad_maximum_fusion.3.refs_9_.refs_11_), channel_id=1, source_target_pairs={{0,4},{4,0},{8,12},{12,8},{16,20},{20,16},{24,28},{28,24},{1,5},{5... | collective-permute-start | bytes 3538952 | tf_op jit(solution)/shard_map/ppermute | solution.py:922
  143.9 10.1 %collective-permute-start.22 = (bf16[2,96,3072]{2,1,0:T(8,128)(2,1)}, bf16[2,96,3072]{2,1,0:T(8,128)(2,1)}, u32[]{:S(2)}, u32[]{:S(2)}) collective-permute-start(bf16[2,96,3072]{2,1,0:T(8,128)(2,1)} %collective-permute-done.15.refs_10_.refs_12_), channel_id=1, source_target_pairs={{0,4},{4,0},{8,12},{12,8},{16,20},{20,16},{24,28},{28,24},{1,5},{5... | collective-permute-start | bytes 3538952 | tf_op jit(solution)/shard_map/ppermute | solution.py:922
  179.2 27.4 %collective-permute-start.23 = (bf16[2,4,96,1536]{3,2,1,0:T(8,128)(2,1)}, bf16[2,4,96,1536]{3,2,1,0:T(8,128)(2,1)}, u32[]{:S(2)}, u32[]{:S(2)}) collective-permute-start(bf16[2,4,96,1536]{3,2,1,0:T(8,128)(2,1)} %get-tuple-element.237), channel_id=1, source_target_pairs={{0,4},{4,0},{8,12},{12,8},{16,20},{20,16},{24,28},{28,24},{1,5},{5... | collective-permute-start | bytes 7077896 | tf_op jit(solution)/shard_map/ppermute | solution.py:922
  179.7 26.9 %copy-start.12 = (bf16[2,4,96,1536]{3,2,1,0:T(8,128)(2,1)S(1)}, bf16[2,4,96,1536]{3,2,1,0:T(8,128)(2,1)}, u32[]{:S(2)}) copy-start(bf16[2,4,96,1536]{3,2,1,0:T(8,128)(2,1)} %get-tuple-element.245) | copy-start | bytes 7077892
  206.5 19.5 %collective-permute-start.26 = (bf16[2,4,96,1536]{3,2,1,0:T(8,128)(2,1)}, bf16[2,4,96,1536]{3,2,1,0:T(8,128)(2,1)S(1)}, u32[]{:S(2)}, u32[]{:S(2)}) collective-permute-start(bf16[2,4,96,1536]{3,2,1,0:T(8,128)(2,1)} %get-tuple-element.247), channel_id=1, source_target_pairs={{0,4},{4,0},{8,12},{12,8},{16,20},{20,16},{24,28},{28,24},{1,5},{5... | collective-permute-start | bytes 7077896 | tf_op jit(solution)/shard_map/ppermute | solution.py:922
  210.7 15.9 %collective-permute-start.25 = (bf16[2,96,1536]{2,1,0:T(8,128)(2,1)}, bf16[2,96,1536]{2,1,0:T(8,128)(2,1)S(1)}, u32[]{:S(2)}, u32[]{:S(2)}) collective-permute-start(bf16[2,96,1536]{2,1,0:T(8,128)(2,1)} %fusion.1), channel_id=1, source_target_pairs={{0,16},{4,20},{8,24},{12,28},{16,0},{20,4},{24,8},{28,12},{1,17},{... | collective-permute-start | bytes 1769480 | tf_op jit(solution)/shard_map/ppermute | solution.py:922
  212.2 15.6 %collective-permute-start.24 = (bf16[2,96,1536]{2,1,0:T(8,128)(2,1)}, bf16[2,96,1536]{2,1,0:T(8,128)(2,1)S(1)}, u32[]{:S(2)}, u32[]{:S(2)}) collective-permute-start(bf16[2,96,1536]{2,1,0:T(8,128)(2,1)} %fusion), channel_id=1, source_target_pairs={{0,8},{4,12},{8,0},{12,4},{16,24},{20,28},{24,16},{28,20},{1,9},{5... | collective-permute-start | bytes 1769480 | tf_op jit(solution)/shard_map/ppermute | solution.py:922
  226.1 55.9 %copy-start.10 = (bf16[2,4,96,1536]{3,2,1,0:T(8,128)(2,1)}, bf16[2,4,96,1536]{3,2,1,0:T(8,128)(2,1)S(1)}, u32[]{:S(2)}) copy-start(bf16[2,4,96,1536]{3,2,1,0:T(8,128)(2,1)S(1)} %collective-permute-done.26) | copy-start | bytes 7077892
  231.1 48.7 %collective-permute-start.31 = (bf16[3,96,1536]{2,1,0:T(8,128)(2,1)}, bf16[3,96,1536]{2,1,0:T(8,128)(2,1)S(1)}, u32[]{:S(2)}, u32[]{:S(2)}) collective-permute-start(bf16[3,96,1536]{2,1,0:T(8,128)(2,1)} %pad_maximum_fusion.7), channel_id=1, source_target_pairs={{0,8},{4,12},{8,0},{12,4},{16,24},{20,28},{24,16},{28,20},{1,9},{5... | collective-permute-start | bytes 2654216 | tf_op jit(solution)/shard_map/ppermute | solution.py:922
  233.2 46.7 %collective-permute-start.30 = (bf16[3,96,1536]{2,1,0:T(8,128)(2,1)}, bf16[3,96,1536]{2,1,0:T(8,128)(2,1)}, u32[]{:S(2)}, u32[]{:S(2)}) collective-permute-start(bf16[3,96,1536]{2,1,0:T(8,128)(2,1)} %pad_maximum_fusion.6), channel_id=1, source_target_pairs={{0,16},{4,20},{8,24},{12,28},{16,0},{20,4},{24,8},{28,12},{1,17},{... | collective-permute-start | bytes 2654216 | tf_op jit(solution)/shard_map/ppermute | solution.py:922
  233.7 46.2 %collective-permute-start.27 = (bf16[256,768]{1,0:T(8,128)(2,1)}, bf16[256,768]{1,0:T(8,128)(2,1)}, u32[]{:S(2)}, u32[]{:S(2)}) collective-permute-start(bf16[256,768]{1,0:T(8,128)(2,1)} %get-tuple-element.254), channel_id=1, source_target_pairs={{0,1},{1,0},{2,3},{5,4},{6,7},{7,6},{8,9},{9,8},{10,11},{13,12},{1... | collective-permute-start | bytes 1179656 | tf_op jit(solution)/shard_map/ppermute | solution.py:954
  238.5 41.3 %collective-permute-start.28 = (bf16[256,768]{1,0:T(8,128)(2,1)}, bf16[256,768]{1,0:T(8,128)(2,1)}, u32[]{:S(2)}, u32[]{:S(2)}) collective-permute-start(bf16[256,768]{1,0:T(8,128)(2,1)} %get-tuple-element.255), channel_id=1, source_target_pairs={{0,2},{1,3},{2,0},{5,7},{6,4},{7,5},{8,10},{9,11},{10,8},{13,15},{... | collective-permute-start | bytes 1179656 | tf_op jit(solution)/shard_map/ppermute | solution.py:954
  242.1 37.8 %collective-permute-start.29 = (bf16[256,768]{1,0:T(8,128)(2,1)}, bf16[256,768]{1,0:T(8,128)(2,1)}, u32[]{:S(2)}, u32[]{:S(2)}) collective-permute-start(bf16[256,768]{1,0:T(8,128)(2,1)} %get-tuple-element.256), channel_id=1, source_target_pairs={{0,3},{1,2},{2,1},{5,6},{6,5},{7,4},{8,11},{9,10},{10,9},{13,14},{... | collective-permute-start | bytes 1179656 | tf_op jit(solution)/shard_map/ppermute | solution.py:954
  285.1 13.0 %collective-permute-start.33 = (bf16[1,96,1536]{2,1,0:T(8,128)(2,1)}, bf16[1,96,1536]{2,1,0:T(8,128)(2,1)S(1)}, u32[]{:S(2)}, u32[]{:S(2)}) collective-permute-start(bf16[1,96,1536]{2,1,0:T(8,128)(2,1)} %get-tuple-element.384), channel_id=1, source_target_pairs={{0,16},{4,20},{8,24},{12,28},{16,0},{20,4},{24,8},{28,12},{1,17},{... | collective-permute-start | bytes 884744 | tf_op jit(solution)/shard_map/ppermute | solution.py:922
  286.7 11.4 %collective-permute-start.34 = (bf16[1,96,1536]{2,1,0:T(8,128)(2,1)S(1)}, bf16[1,96,1536]{2,1,0:T(8,128)(2,1)S(1)}, u32[]{:S(2)}, u32[]{:S(2)}) collective-permute-start(bf16[1,96,1536]{2,1,0:T(8,128)(2,1)S(1)} %get-tuple-element.383), channel_id=1, source_target_pairs={{0,8},{4,12},{8,0},{12,4},{16,24},{20,28},{24,16},{28,20},{1,9},{5... | collective-permute-start | bytes 884744 | tf_op jit(solution)/shard_map/ppermute | solution.py:922
  287.4 10.8 %collective-permute-start.32 = (bf16[96,1536]{1,0:T(8,128)(2,1)S(1)}, bf16[96,1536]{1,0:T(8,128)(2,1)S(1)}, u32[]{:S(2)}, u32[]{:S(2)}) collective-permute-start(bf16[96,1536]{1,0:T(8,128)(2,1)S(1)} %fusion.8), channel_id=1, source_target_pairs={{0,1},{1,0},{2,3},{3,2},{4,5},{5,4},{6,7},{7,6},{8,9},{9,8},{10,11... | collective-permute-start | bytes 884744 | tf_op jit(solution)/shard_map/ppermute | solution.py:928
  299.0 18.6 %collective-permute-start.36 = (bf16[2,4,4,96,384]{4,3,2,1,0:T(8,128)(2,1)}, bf16[2,4,4,96,384]{4,3,2,1,0:T(8,128)(2,1)}, u32[]{:S(2)}, u32[]{:S(2)}) collective-permute-start(bf16[2,4,4,96,384]{4,3,2,1,0:T(8,128)(2,1)} %get-tuple-element.288), channel_id=1, source_target_pairs={{0,4},{4,0},{8,12},{12,8},{16,20},{20,16},{24,28},{28,24},{1,5},{5... | collective-permute-start | bytes 7077896 | tf_op jit(solution)/shard_map/ppermute | solution.py:922
  304.5 13.0 %collective-permute-start.35 = (bf16[96,1536]{1,0:T(8,128)(2,1)}, bf16[96,1536]{1,0:T(8,128)(2,1)S(1)}, u32[]{:S(2)}, u32[]{:S(2)}) collective-permute-start(bf16[96,1536]{1,0:T(8,128)(2,1)} %convert_add_fusion.4), channel_id=1, source_target_pairs={{0,1},{1,0},{2,3},{3,2},{4,5},{5,4},{6,7},{7,6},{8,9},{9,8},{10,11... | collective-permute-start | bytes 884744 | tf_op jit(solution)/shard_map/ppermute | solution.py:928
  320.7 15.6 %collective-permute-start.38 = (bf16[2,4,96,384]{3,2,1,0:T(8,128)(2,1)S(1)}, bf16[2,4,96,384]{3,2,1,0:T(8,128)(2,1)S(1)}, u32[]{:S(2)}, u32[]{:S(2)}) collective-permute-start(bf16[2,4,96,384]{3,2,1,0:T(8,128)(2,1)S(1)} %fusion.5), channel_id=1, source_target_pairs={{0,16},{4,20},{8,24},{12,28},{16,0},{20,4},{24,8},{28,12},{1,17},{... | collective-permute-start | bytes 1769480 | tf_op jit(solution)/shard_map/ppermute | solution.py:922
  321.3 15.2 %collective-permute-start.37 = (bf16[2,4,96,384]{3,2,1,0:T(8,128)(2,1)S(1)}, bf16[2,4,96,384]{3,2,1,0:T(8,128)(2,1)S(1)}, u32[]{:S(2)}, u32[]{:S(2)}) collective-permute-start(bf16[2,4,96,384]{3,2,1,0:T(8,128)(2,1)S(1)} %fusion.4), channel_id=1, source_target_pairs={{0,8},{4,12},{8,0},{12,4},{16,24},{20,28},{24,16},{28,20},{1,9},{5... | collective-permute-start | bytes 1769480 | tf_op jit(solution)/shard_map/ppermute | solution.py:922
  324.1 25.0 %collective-permute-start.40 = (bf16[256,768]{1,0:T(8,128)(2,1)}, bf16[256,768]{1,0:T(8,128)(2,1)S(1)}, u32[]{:S(2)}, u32[]{:S(2)}) collective-permute-start(bf16[256,768]{1,0:T(8,128)(2,1)} %get-tuple-element.299), channel_id=1, source_target_pairs={{0,1},{1,0},{2,3},{5,4},{6,7},{7,6},{8,9},{9,8},{10,11},{13,12},{1... | collective-permute-start | bytes 1179656 | tf_op jit(solution)/shard_map/ppermute | solution.py:954
  327.5 22.6 %collective-permute-start.41 = (bf16[256,768]{1,0:T(8,128)(2,1)}, bf16[256,768]{1,0:T(8,128)(2,1)S(1)}, u32[]{:S(2)}, u32[]{:S(2)}) collective-permute-start(bf16[256,768]{1,0:T(8,128)(2,1)} %get-tuple-element.300), channel_id=1, source_target_pairs={{0,2},{1,3},{2,0},{5,7},{6,4},{7,5},{8,10},{9,11},{10,8},{13,15},{... | collective-permute-start | bytes 1179656 | tf_op jit(solution)/shard_map/ppermute | solution.py:954
  329.4 20.7 %collective-permute-start.42 = (bf16[256,768]{1,0:T(8,128)(2,1)}, bf16[256,768]{1,0:T(8,128)(2,1)S(1)}, u32[]{:S(2)}, u32[]{:S(2)}) collective-permute-start(bf16[256,768]{1,0:T(8,128)(2,1)} %get-tuple-element.301), channel_id=1, source_target_pairs={{0,3},{1,2},{2,1},{5,6},{6,5},{7,4},{8,11},{9,10},{10,9},{13,14},{... | collective-permute-start | bytes 1179656 | tf_op jit(solution)/shard_map/ppermute | solution.py:954
  338.0 12.4 %collective-permute-start.43 = (bf16[1,4,96,384]{3,2,1,0:T(8,128)(2,1)S(1)}, bf16[1,4,96,384]{3,2,1,0:T(8,128)(2,1)S(1)}, u32[]{:S(2)}, u32[]{:S(2)}) collective-permute-start(bf16[1,4,96,384]{3,2,1,0:T(8,128)(2,1)S(1)} %get-tuple-element.380), channel_id=1, source_target_pairs={{0,16},{4,20},{8,24},{12,28},{16,0},{20,4},{24,8},{28,12},{1,17},{... | collective-permute-start | bytes 884744 | tf_op jit(solution)/shard_map/ppermute | solution.py:922
  339.6 10.8 %collective-permute-start.44 = (bf16[1,4,96,384]{3,2,1,0:T(8,128)(2,1)S(1)}, bf16[1,4,96,384]{3,2,1,0:T(8,128)(2,1)}, u32[]{:S(2)}, u32[]{:S(2)}) collective-permute-start(bf16[1,4,96,384]{3,2,1,0:T(8,128)(2,1)S(1)} %get-tuple-element.379), channel_id=1, source_target_pairs={{0,8},{4,12},{8,0},{12,4},{16,24},{20,28},{24,16},{28,20},{1,9},{5... | collective-permute-start | bytes 884744 | tf_op jit(solution)/shard_map/ppermute | solution.py:922
  349.0 1.4 collective-permute-start.39
  351.7 19.3 %collective-permute-start.48 = (bf16[4,96,384]{2,1,0:T(8,128)(2,1)S(1)}, bf16[4,96,384]{2,1,0:T(8,128)(2,1)S(1)}, u32[]{:S(2)}, u32[]{:S(2)}) collective-permute-start(bf16[4,96,384]{2,1,0:T(8,128)(2,1)S(1)} %fusion.7), channel_id=1, source_target_pairs={{0,1},{1,0},{2,3},{3,2},{4,5},{5,4},{6,7},{7,6},{8,9},{9,8},{10,11... | collective-permute-start | bytes 884744 | tf_op jit(solution)/shard_map/ppermute | solution.py:928
  358.0 13.0 %collective-permute-start.49 = (bf16[2,96,768]{2,1,0:T(8,128)(2,1)S(1)}, bf16[2,96,768]{2,1,0:T(8,128)(2,1)S(1)}, u32[]{:S(2)}, u32[]{:S(2)}) collective-permute-start(bf16[2,96,768]{2,1,0:T(8,128)(2,1)S(1)} %slice.557), channel_id=1, source_target_pairs={{0,2},{1,3},{2,0},{3,1},{4,6},{5,7},{6,4},{7,5},{8,10},{9,11},{10,... | collective-permute-start | bytes 884744 | tf_op jit(solution)/shard_map/ppermute | solution.py:928
  359.3 5.3 %collective-permute-start.45 = (f32[2,1408]{1,0:T(2,128)S(1)}, f32[2,1408]{1,0:T(2,128)S(1)}, u32[]{:S(2)}, u32[]{:S(2)}) collective-permute-start(f32[2,1408]{1,0:T(2,128)S(1)} %get-tuple-element.415), channel_id=1, source_target_pairs={{0,8},{4,12},{8,0},{12,4},{16,24},{20,28},{24,16},{28,20},{1,9},{5... | collective-permute-start | bytes 33800 | tf_op jit(solution)/shard_map/ppermute | solution.py:925
  360.2 4.5 %collective-permute-start.46 = (f32[2,1408]{1,0:T(2,128)S(1)}, f32[2,1408]{1,0:T(2,128)S(1)}, u32[]{:S(2)}, u32[]{:S(2)}) collective-permute-start(f32[2,1408]{1,0:T(2,128)S(1)} %get-tuple-element.416), channel_id=1, source_target_pairs={{0,16},{4,20},{8,24},{12,28},{16,0},{20,4},{24,8},{28,12},{1,17},{... | collective-permute-start | bytes 33800 | tf_op jit(solution)/shard_map/ppermute | solution.py:925
  361.7 4.6 %collective-permute-start.47 = (f32[2,1408]{1,0:T(2,128)S(1)}, f32[2,1408]{1,0:T(2,128)S(1)}, u32[]{:S(2)}, u32[]{:S(2)}) collective-permute-start(f32[2,1408]{1,0:T(2,128)S(1)} %get-tuple-element.413), channel_id=1, source_target_pairs={{0,24},{4,28},{8,16},{12,20},{16,8},{20,12},{24,0},{28,4},{1,25},{... | collective-permute-start | bytes 33800 | tf_op jit(solution)/shard_map/ppermute | solution.py:925
  374.0 11.9 %collective-permute-start.50 = (f32[9,1408]{1,0:T(8,128)S(1)}, f32[9,1408]{1,0:T(8,128)S(1)}, u32[]{:S(2)}, u32[]{:S(2)}) collective-permute-start(f32[9,1408]{1,0:T(8,128)S(1)} %concatenate.61), channel_id=1, source_target_pairs={{0,1},{1,0},{2,3},{3,2},{4,5},{5,4},{6,7},{7,6},{8,9},{9,8},{10,11... | collective-permute-start | bytes 152072 | tf_op jit(solution)/shard_map/ppermute | solution.py:928
  376.8 11.4 %collective-permute-start.51 = (f32[9,1408]{1,0:T(8,128)S(1)}, f32[9,1408]{1,0:T(8,128)S(1)}, u32[]{:S(2)}, u32[]{:S(2)}) collective-permute-start(f32[9,1408]{1,0:T(8,128)S(1)} %concatenate.61), channel_id=1, source_target_pairs={{0,2},{1,3},{2,0},{3,1},{4,6},{5,7},{6,4},{7,5},{8,10},{9,11},{10,... | collective-permute-start | bytes 152072 | tf_op jit(solution)/shard_map/ppermute | solution.py:928
  379.6 8.6 %collective-permute-start.52 = (f32[9,1408]{1,0:T(8,128)S(1)}, f32[9,1408]{1,0:T(8,128)S(1)}, u32[]{:S(2)}, u32[]{:S(2)}) collective-permute-start(f32[9,1408]{1,0:T(8,128)S(1)} %concatenate.61), channel_id=1, source_target_pairs={{0,3},{1,2},{2,1},{3,0},{4,7},{5,6},{6,5},{7,4},{8,11},{9,10},{10,... | collective-permute-start | bytes 152072 | tf_op jit(solution)/shard_map/ppermute | solution.py:928
  382.8 12.6 %collective-permute-start.53 = (bf16[4,96,192]{2,1,0:T(8,128)(2,1)S(1)}, bf16[4,96,192]{2,1,0:T(8,128)(2,1)S(1)}, u32[]{:S(2)}, u32[]{:S(2)}) collective-permute-start(bf16[4,96,192]{2,1,0:T(8,128)(2,1)S(1)} %slice.558), channel_id=1, source_target_pairs={{0,2},{1,3},{2,0},{3,1},{4,6},{5,7},{6,4},{7,5},{8,10},{9,11},{10,... | collective-permute-start | bytes 442376 | tf_op jit(solution)/shard_map/ppermute | solution.py:928
  (50 other events, 313.0 us)

commit v4 on v3

--- a/solution.py
+++ b/solution.py
@@ -29,8 +29,11 @@
     return lax.dot_general(a, b, (((1,), (1,)), ((), ())), preferred_element_type=F32)
 
 
-def params(**more):
-    return pltpu.CompilerParams(vmem_limit_bytes=58 << 20, **more)
+VMEM_MIB = {'feed': 48, 'turn': 48, 'attend_back': 48, 'weight_grads': 48}
+
+
+def params(name):
+    return pltpu.CompilerParams(vmem_limit_bytes=VMEM_MIB.get(name, 58) << 20)
 
 
 def cost(flops, nbytes, trans=0):
@@ -116,7 +119,7 @@
         out_shape=[shape((length, 4 * half), F32)] * 3 + [shape((half, length), F32)] * 2,
         in_specs=[VMEM] * 2,
         out_specs=[VMEM] * 5,
-        compiler_params=params(),
+        compiler_params=params("rotary"),
         cost_estimate=cost(6e6, 2e6),
         name="rotary",
     )(places, frequencies)
@@ -209,7 +212,7 @@
             pltpu.VMEM((2 * part, width), BF16),
             pltpu.SemaphoreType.DMA((3, qk.count)),
         ],
-        compiler_params=params(),
+        compiler_params=params("qkv"),
         cost_estimate=cost(6 * length * width * cols, 16e6),
         name="qkv",
     )(me, *x_parts, vec, cosine, sin_a, sin_b, *qk.parts, *vo.parts)
@@ -292,7 +295,7 @@
         out_specs=[turned, pl.BlockSpec((1, 2, 1, length), lambda i: (i, 0, 0, 0))],
         out_shape=[shape((width, length), BF16), shape((pairs, 2, 1, length), F32)],
         scratch_shapes=[pltpu.VMEM((length, PAIR), BF16), pltpu.VMEM((2, PAIR, length), BF16)],
-        compiler_params=params(),
+        compiler_params=params("attend"),
         cost_estimate=cost(16 * length * length * width, 8e6),
         name="attend",
     )(q_t, k, v_t, doc_row, doc_col)
@@ -364,7 +367,7 @@
             pltpu.VMEM((part, width), BF16),
             pltpu.SemaphoreType.DMA((vo.count,)),
         ],
-        compiler_params=params(),
+        compiler_params=params("middle"),
         cost_estimate=cost(2 * length * width * inner, 16e6),
         name="middle",
     )(me, *x_parts, *g_parts, mix_t, vec, *vo.parts)
@@ -382,9 +385,15 @@
             send(j // 2, block)
 
 
-def writer(ref, *lead):
+def slot_of(stream, slot, count):
+    if stream == 0 and count == 4:
+        slot = (0, 2, 1, 3)[slot]
+    return slot
+
+
+def writer(ref, stream):
     def put(slot, block):
-        ref[(lead[0], slot, *lead[1:])] = block
+        ref[stream, slot_of(stream, slot, ref.shape[1])] = block
 
     return put
 
@@ -393,7 +402,7 @@
     def put(slot, block):
         half = block.shape[-1] // 2
         for s in range(2):
-            ref[(s, slot, *lead)] = block[:, s * half : (s + 1) * half]
+            ref[(s, slot_of(s, slot, ref.shape[1]), *lead)] = block[:, s * half : (s + 1) * half]
 
     return put
 
@@ -492,7 +501,7 @@
             pltpu.VMEM((blocks, rows, chunk), BF16),
             pltpu.SemaphoreType.DMA((2, steps, blocks)),
         ],
-        compiler_params=params(),
+        compiler_params=params("feed"),
         cost_estimate=cost(12 * length * width * units, 20e6),
         name="feed",
     )(
@@ -576,7 +585,7 @@
             pltpu.VMEM((part, width), BF16),
             pltpu.SemaphoreType.DMA((vo.count,)),
         ],
-        compiler_params=params(),
+        compiler_params=params("turn"),
         cost_estimate=cost(2 * length * width * inner, 24e6),
         name="turn",
     )(
@@ -608,17 +617,15 @@
         keys, values = with_lanes(k, added, h), with_lanes(v, added, h)
         for b in range(length // block):
             c = slice(b * block, (b + 1) * block)
-            probs = jnp.exp(dot_nn(keys, ahead[h, 0, :, c]))
-            d_scores = (probs * dot_nn(values, ahead[h, 1, :, c])).astype(BF16)
-            dv_part = dot_nt(d_mix_t[rows, c], probs.astype(BF16))
-            dk_part = dot_nt(q_t[rows, c], d_scores)
+            probs = jnp.exp(dot_nn(keys[c], ahead[h, 0]))
+            d_scores = (probs * dot_nn(values[c], ahead[h, 1])).astype(BF16)
+            dv_acc[rows, c] = dot_nt(d_mix_t[rows, :], probs.astype(BF16))
+            dk_acc[rows, c] = dot_nt(q_t[rows, :], d_scores)
+            dq_part = dot_nn(k_t[rows, c], d_scores)
             if b == 0:
-                dv_acc[rows, :] = dv_part
-                dk_acc[rows, :] = dk_part
+                dq_acc[rows, :] = dq_part
             else:
-                dv_acc[rows, :] += dv_part
-                dk_acc[rows, :] += dk_part
-            dq_acc[rows, c] = dot_nn(k_t[rows, :], d_scores)
+                dq_acc[rows, :] += dq_part
 
     half = HEAD // 2
     for acc, out, factor in ((dq_acc, dq, HEAD**-0.5), (dk_acc, dk, 1.0)):
@@ -652,7 +659,7 @@
             pltpu.VMEM((2, 2, PAIR, length), BF16),
         ]
         + [pltpu.VMEM((PAIR, length), F32)] * 3,
-        compiler_params=params(),
+        compiler_params=params("attend_back"),
         cost_estimate=cost(28 * length * length * width, 14e6),
         name="attend_back",
     )(k, v, q_t, k_t, d_mix_t, mix_t, log_sum, doc_row, doc_col, cos_t, sin_t)
@@ -709,7 +716,7 @@
             pltpu.VMEM((part, width), BF16),
             pltpu.SemaphoreType.DMA((3, qk.count)),
         ],
-        compiler_params=params(),
+        compiler_params=params("first"),
         cost_estimate=cost(6 * length * width * cols, 20e6),
         name="first",
     )(me, *x_parts, d_mid, vec, dq, dk, dv, *qk.parts, *vo.parts)
@@ -782,14 +789,15 @@
             pltpu.VMEM((qk.count * 16, width), BF16),
             pltpu.SemaphoreType.DMA((3, qk.count)),
         ],
-        compiler_params=params(),
+        compiler_params=params("modulate"),
         cost_estimate=cost(2e7, 4e6),
         name="modulate",
     )(me, act, *qk.parts, *vo.parts)
 
 
 def gather_up_kernel(
-    count, me, vec, ada, sums, sums_one, d_bias_down, bias_grad, act, cond, keep, send, d_cond, out, spread
+    count, me, vec, ada, sums, sums_one, d_bias_down, d_bias_b, d_bias_a, act, cond,
+    keep, send, d_cond, out, spread, bias_grad
 ):
     width = vec.shape[1]
     rows = width // count
@@ -810,6 +818,17 @@
         d_bias_down[...],
     )
     out[...] = jnp.zeros_like(out)
+    chunk = d_bias_a.shape[2]
+    for n, ref in enumerate((d_bias_b, d_bias_a)):
+        for c in range(ref.shape[0]):
+            at = c * chunk
+            while at < (c + 1) * chunk:
+                zone = at // width
+                to = min((c + 1) * chunk, (zone + 1) * width)
+                bias_grad[2 * n + zone : 2 * n + zone + 1, at - zone * width : to - zone * width] = (
+                    ref[c][:, at - c * chunk : to - c * chunk]
+                )
+                at = to
     base = (kinds + 3) * rows
     for d in range(count):
         here = slice(d * rows, (d + 1) * rows)
@@ -839,20 +858,21 @@
         send[j] = out[me[0] ^ (2 * j + 1)]
 
 
-def gather_up(me, vec, ada, sums, sums_one, d_bias_down, bias_grad, act, cond, count, length):
+def gather_up(me, vec, ada, sums, sums_one, d_bias_down, d_bias_b, d_bias_a, act, cond, count, length):
     return pl.pallas_call(
         partial(gather_up_kernel, count),
         out_shape=[shape((count // 2, 1, length), F32)] * 2 + [shape(act.shape, F32)],
-        in_specs=[SMEM] + [VMEM] * 8,
+        in_specs=[SMEM] + [VMEM] * 9,
         out_specs=[VMEM] * 3,
         scratch_shapes=[
             pltpu.VMEM((count, 1, length), F32),
             pltpu.VMEM((8, vec.shape[1]), F32),
+            pltpu.VMEM((4, vec.shape[1]), F32),
         ],
-        compiler_params=params(),
+        compiler_params=params("gather_up"),
         cost_estimate=cost(2e7, 4e6),
         name="gather_up",
-    )(me, vec, ada, sums, sums_one, d_bias_down, bias_grad, act, cond)
+    )(me, vec, ada, sums, sums_one, d_bias_down, d_bias_b, d_bias_a, act, cond)
 
 
 def weight_grads_kernel(me, n_t, d_att_t, dq, dk, dv, mix_t, *refs):
@@ -906,7 +926,7 @@
             pltpu.VMEM((blocks, rows, cols), BF16),
             pltpu.SemaphoreType.DMA((6,)),
         ],
-        compiler_params=params(),
+        compiler_params=params("weight_grads"),
         cost_estimate=cost(8 * length * width * cols, 14e6),
         name="weight_grads",
     )(me, n_t, d_att_t, dq, dk, dv, mix)
@@ -1020,11 +1040,7 @@
             if self.stage:
                 stay, go = [t[:1] for t in self.terms[n]], [t[1:] for t in self.terms[n]]
             else:
-                sides = [t.reshape(2, 2, 2, *t.shape[2:]) for t in self.terms[n]]
-                if b == 1:
-                    stay, go = [t[n, :, 0] for t in sides], [t[n, :, 1] for t in sides]
-                else:
-                    stay, go = [t[n, 0] for t in sides], [t[n, 1] for t in sides]
+                stay, go = [t[n, :2] for t in self.terms[n]], [t[n, 2:] for t in self.terms[n]]
             self.terms[n] = stay
             out.append((b, sum(t.astype(F32) for t in go).astype(BF16)))
         self.stage += 1
@@ -1129,9 +1145,8 @@
         cos_flat, sin_a, sin_b, cos_t, sin_t, doc_row, doc_col = turns
         for n in (3, 1):
             x_parts[n] = group.ship(x_parts[n], n, True)
-        late = join([late_far, late])
         qk, vo = group.gather_cores_joined(near, ways)
-        lates = late[:rows], late[rows:]
+        lates = join([late_far[:rows], late[:rows]]), join([late_far[rows:], late[rows:]])
         came = [group.bit(v, way[0]) for v, way in zip(lates, ways)]
         vec, bias_hidden, ada_all = modulate(me, act, qk, vo, tensor_count, rows)
         x_parts, g_parts, came, vec = lax.optimization_barrier((x_parts, g_parts, came, vec))
@@ -1200,12 +1215,11 @@
     near = jnp.stack(sum_b.total) + jnp.stack([far_up, far_dn]).astype(F32)
     sums_one, near = tie((sums_one, near), sum_w)
     exchange(sum_w)
-    d_bias = jnp.concatenate([d_bias_b.reshape(2, -1), d_bias_a.reshape(2, -1)])
     edge = mod_width + 3 * rows
     if group.paired:
         length = edge + tensor_count * rows + 2 * cond_size
         keep, send, d_cond = gather_up(
-            me, vec, ada_all, sums, sums_one, d_bias_down, d_bias, act, cond, dp_count,
+            me, vec, ada_all, sums, sums_one, d_bias_down, d_bias_b, d_bias_a, act, cond, dp_count,
             length - length % cond_size,
         )
     else:
@@ -1227,7 +1241,7 @@
         table = jnp.concatenate(
             [sliced(d_mod)]
             + [sliced(t) for t in others]
-            + [sliced(t) for t in d_bias]
+            + [sliced(t) for half in (d_bias_b, d_bias_a) for t in half.reshape(2, -1)]
             + [jnp.broadcast_to(act, (dp_count, cond_size))],
             axis=1,
         )

time: 403 us -> 379 us (0.940)
  other arithmetic: 40.9 us -> 30.8 us
  Pallas kernels: 173 us -> 164 us
  local copies, waits for them, and re-layouts: 27.7 us -> 21 us
    convert_element_type x9 -> x6, other arithmetic: 11.6 us -> 4.6 us  [split(): out.append((b, sum((t.astype(F32) for t in go)).astype(BF16)))]
    unnamed x131 -> x118, local copies, waits for them, and re-layouts: 11.4 us -> 8.48 us
  transfers between devices with their start and end apart: 54 -> 54, of which waited for: 16 -> 17; matrix products, arithmetic and copies ran while one was open for 11% -> 9% of each run, Pallas kernels for 37% -> 38%
where the time goes in v4:
time: 379 us; the launch traced here: 373 us
  Pallas kernels  164 us (43%)
  starting transfers between devices  93.3 us (25%)
  waiting for transfers between devices  60.6 us (16%)
  other arithmetic  30.8 us (8%)
  local copies, waits for them, and re-layouts  21 us (6%)
    pallas_call x2, Pallas kernels, feed(): pl.pallas_call(partial(feed_kernel, up, dn, steps, first), grid=(steps,),...  48.6 us
    ppermute x12, starting transfers between devices, ship(): return lax.ppermute(v, BOTH, pairs)  40.1 us
    ppermute x12, waiting for transfers between devices, z(): return lax.ppermute(v, 'tensor', [(i, i ^ k) for i in range(self.tensor)])  33.9 us
    pallas_call x1, Pallas kernels, attend_back(): pl.pallas_call(attend_back_kernel, grid=(count,), in_specs=[flat] * 2 + [...  32.6 us
    ppermute x12, starting transfers between devices, z(): return lax.ppermute(v, 'tensor', [(i, i ^ k) for i in range(self.tensor)])  26.6 us
    ppermute x27, starting transfers between devices, bit(): return lax.ppermute(v, 'dp', [(i, i ^ 1 << b) for i in range(self.dp)])  23 us
    pallas_call x1, Pallas kernels, attend(): pl.pallas_call(attend_kernel, grid=(pairs,), in_specs=[turned, flat, turn...  20.2 us
    ppermute x12, waiting for transfers between devices, ship(): return lax.ppermute(v, BOTH, pairs)  19.7 us
  transfers between devices with their start and end apart: 54, of which 17 were waited for; matrix products, arithmetic and copies ran while one was open for 9% of the time, Pallas kernels for 38%

profile of v4, /device:TPU:0, one launch (start us, length us, event | category | flops | bytes accessed | tf_op | source)
XLA Modules:
  0.0 372.9 jit_solution(13790852601101660833)
XLA Ops:
  3.3 4.1 %collective-permute-start = (bf16[400,192]{1,0:T(8,128)(2,1)S(1)}, bf16[400,192]{1,0:T(8,128)(2,1)S(1)}, u32[]{:S(2)}, u32[]{:S(2)}) collective-permute-start(bf16[400,192]{1,0:T(8,128)(2,1)S(1)} %pad_maximum_fusion.16), channel_id=1, source_target_pairs={{0,2},{1,3},{2,0},{3,1},{4,6},{5,7},{6,4},{7,5},{8,10},{9,11},{10,... | collective-permute-start | bytes 460808 | tf_op jit(solution)/shard_map/ppermute | solution.py:948
  10.1 6.8 %collective-permute-done = bf16[400,192]{1,0:T(8,128)(2,1)S(1)} collective-permute-done((bf16[400,192]{1,0:T(8,128)(2,1)S(1)}, bf16[400,192]{1,0:T(8,128)(2,1)S(1)}, u32[]{:S(2)}, u32[]{:S(2)}) %collective-permute-start) | collective-permute-done | bytes 153632 | tf_op jit(solution)/shard_map/ppermute | solution.py:948
  18.9 1.7 dynamic-slice_bitcast_fusion
  20.6 5.0 %collective-permute-done.1 = bf16[400,384]{1,0:T(8,128)(2,1)S(1)} collective-permute-done((bf16[400,384]{1,0:T(8,128)(2,1)S(1)}, bf16[400,384]{1,0:T(8,128)(2,1)S(1)}, u32[]{:S(2)}, u32[]{:S(2)}) %collective-permute-start.1) | collective-permute-done | bytes 307232 | tf_op jit(solution)/shard_map/ppermute | solution.py:948
  26.1 1.4 collective-permute-start.4
  27.6 1.6 collective-permute-start.3
  29.2 3.3 collective-permute-start.2
  32.6 12.3 %collective-permute-done.2 = bf16[192,768]{1,0:T(8,128)(2,1)S(1)} collective-permute-done((bf16[192,768]{1,0:T(8,128)(2,1)S(1)}, bf16[192,768]{1,0:T(8,128)(2,1)S(1)}, u32[]{:S(2)}, u32[]{:S(2)}) %collective-permute-start.2) | collective-permute-done | bytes 294944 | tf_op jit(solution)/shard_map/ppermute | solution.py:948
  47.1 5.3 %collective-permute-start.8 = (bf16[256,768]{1,0:T(8,128)(2,1)}, bf16[256,768]{1,0:T(8,128)(2,1)S(1)}, u32[]{:S(2)}, u32[]{:S(2)}) collective-permute-start(bf16[256,768]{1,0:T(8,128)(2,1)} %get-tuple-element.176), channel_id=1, source_target_pairs={{0,2},{2,0},{3,1},{4,6},{5,7},{7,5},{8,10},{10,8},{11,9},{12,14},{... | collective-permute-start | bytes 1179656 | tf_op jit(solution)/shard_map/ppermute | solution.py:974
  55.5 2.5 rotary.1
  58.1 9.7 %collective-permute-done.8.refs_2_ = bf16[256,768]{1,0:T(8,128)(2,1)S(1)} collective-permute-done((bf16[256,768]{1,0:T(8,128)(2,1)}, bf16[256,768]{1,0:T(8,128)(2,1)S(1)}, u32[]{:S(2)}, u32[]{:S(2)}) %collective-permute-start.8) | collective-permute-done | bytes 393248 | tf_op jit(solution)/shard_map/ppermute | solution.py:974
  68.8 2.1 constant_dynamic-update-slice_fusion.4
  74.1 1.6 collective-permute-start.12
  75.8 1.6 collective-permute-start.11
  78.7 6.6 %collective-permute-start.9 = (bf16[256,768]{1,0:T(8,128)(2,1)S(1)}, bf16[256,768]{1,0:T(8,128)(2,1)S(1)}, u32[]{:S(2)}, u32[]{:S(2)}) collective-permute-start(bf16[256,768]{1,0:T(8,128)(2,1)S(1)} %copy-done.48), channel_id=1, source_target_pairs={{0,1},{1,0},{3,2},{4,5},{6,7},{7,6},{8,9},{9,8},{11,10},{12,13},{1... | collective-permute-start | bytes 1179656 | tf_op jit(solution)/shard_map/ppermute | solution.py:974
  86.8 3.8 %modulate.1 = (f32[16,768]{1,0:T(8,128)}, f32[4,768]{1,0:T(4,128)}, bf16[768,768]{1,0:T(8,128)(2,1)}) custom-call(s32[1]{0:T(128)} %bitcast.me, f32[1,128]{1,0:T(1,128)} %get-tuple-element.364.act, bf16[8,256,768]{2,1,0:T(8,128)(2,1)} %constant_dynamic-update-slice_fusion.2.refs_0_.refs_2_.refs_8_.refs_10_.refs_12_.refs_9_.refs_11_, ...), custom_call_target="tpu_custom_call" | custom-call | flops 20000000 | bytes 4000000 | tf_op jit(solution)/shard_map/modulate/pallas_call | solution.py:779
  90.6 4.1 %collective-permute-done.9.refs_1_ = bf16[256,768]{1,0:T(8,128)(2,1)S(1)} collective-permute-done((bf16[256,768]{1,0:T(8,128)(2,1)S(1)}, bf16[256,768]{1,0:T(8,128)(2,1)S(1)}, u32[]{:S(2)}, u32[]{:S(2)}) %collective-permute-start.9) | collective-permute-done | bytes 393248 | tf_op jit(solution)/shard_map/ppermute | solution.py:974
  94.7 2.3 pad_maximum_fusion.3.refs_9_.refs_11_
  97.6 2.2 pad_maximum_fusion.2.refs_5_.refs_7_
  100.3 5.4 %collective-permute-start.16 = (bf16[256,768]{1,0:T(8,128)(2,1)S(1)}, bf16[256,768]{1,0:T(8,128)(2,1)S(1)}, u32[]{:S(2)}, u32[]{:S(2)}) collective-permute-start(bf16[256,768]{1,0:T(8,128)(2,1)S(1)} %copy-done.44), channel_id=1, source_target_pairs={{0,1},{1,0},{3,2},{4,5},{6,7},{7,6},{8,9},{9,8},{11,10},{12,13},{1... | collective-permute-start | bytes 1179656 | tf_op jit(solution)/shard_map/ppermute | solution.py:974
  105.7 1.9 collective-permute-start.17
  107.6 1.5 collective-permute-start.18
  109.1 12.6 %qkv.1 = (bf16[768,1024]{1,0:T(8,128)(2,1)}, bf16[1024,768]{1,0:T(8,128)(2,1)}, bf16[1024,768]{1,0:T(8,128)(2,1)}, bf16[768,1024]{1,0:T(8,128)(2,1)}, bf16[768,1...) custom-call(s32[1]{0:T(128)} %bitcast.me, bf16[256,768]{1,0:T(8,128)(2,1)} %get-tuple-element.197.refs_0_, ...), custom_call_target="tpu_custom_call" | custom-call | flops 3623878656 | bytes 16000000 | tf_op jit(solution)/shard_map/qkv/pallas_call | solution.py:199
  121.7 20.2 %attend.1 = (bf16[768,1024]{1,0:T(8,128)(2,1)}, f32[6,2,1,1024]{3,2,1,0:T(1,128)}) custom-call(bf16[768,1024]{1,0:T(8,128)(2,1)} %get-tuple-element.207.q_t, bf16[1024,768]{1,0:T(8,128)(2,1)} %get-tuple-element.205.k, bf16[768,1024]{1,0:T(8,128)(2,1)} %get-tuple-element.209.v_t, s32[1,1024]{1,0:T(1,128)} %bitcast.175, s32[1024,1]{1,0:T(8,128)} %copy.39.doc_col), custom_call_target="tpu_custom_call" | custom-call | flops 12884901888 | bytes 8000000 | tf_op jit(solution)/shard_map/attend/pallas_call | solution.py:285
  142.0 1.4 collective-permute-start.19
  144.1 9.4 %middle.1 = (f32[1024,768]{1,0:T(8,128)}, bf16[1024,768]{1,0:T(8,128)(2,1)}, bf16[768,1024]{1,0:T(8,128)(2,1)}, bf16[1024,768]{1,0:T(8,128)(2,1)}, bf16[768,1024...) custom-call(s32[1]{0:T(128)} %bitcast.me, bf16[256,768]{1,0:T(8,128)(2,1)} %get-tuple-element.197.refs_0_, ...), custom_call_target="tpu_custom_call" | custom-call | flops 1207959552 | bytes 16000000 | tf_op jit(solution)/shard_map/middle/pallas_call | solution.py:347
  153.5 23.4 %feed.2 = (f32[1024,768]{1,0:T(8,128)}, f32[1024,768]{1,0:T(8,128)}, f32[3,1,512]{2,1,0:T(1,128)S(1)}, bf16[2,4,96,1536]{3,2,1,0:T(8,128)(2,1)}, bf16[2,4,96,1536]{3,2,1,0:T(8,128)(2,1)}) custom-call(s32[1]{0:T(128)} %bitcast.me, bf16[1024,768]{1,0:T(8,128)(2,1)} %get-tuple-element.225.refs_0_, bf16[768,1024]{1,0:T(8,128)(2,1)} %get-tuple-element.226.refs_1_, ...), custom_call_target="tpu_custom_call" | custom-call | flops 14495514624 | bytes 20000000 | tf_op jit(solution)/shard_map/feed/pallas_call | solution.py:489
  177.5 25.2 %feed.3 = (f32[1024,768]{1,0:T(8,128)}, f32[1024,768]{1,0:T(8,128)}, f32[3,1,512]{2,1,0:T(1,128)S(1)}, bf16[2,4,96,1536]{3,2,1,0:T(8,128)(2,1)}, bf16[2,4,96,1536]{3,2,1,0:T(8,128)(2,1)}) custom-call(s32[1]{0:T(128)} %bitcast.me, bf16[1024,768]{1,0:T(8,128)(2,1)} %get-tuple-element.225.refs_0_, bf16[768,1024]{1,0:T(8,128)(2,1)} %get-tuple-element.226.refs_1_, ...), custom_call_target="tpu_custom_call" | custom-call | flops 14495514624 | bytes 20000000 | tf_op jit(solution)/shard_map/feed/pallas_call | solution.py:489
  203.3 1.4 collective-permute-start.24
  204.7 1.5 collective-permute-start.25
  206.3 11.6 %turn.1 = (bf16[256,768]{1,0:T(8,128)(2,1)S(1)}, bf16[256,768]{1,0:T(8,128)(2,1)S(1)}, bf16[256,768]{1,0:T(8,128)(2,1)S(1)}, bf16[256,768]{1,0:T(8,128)(2,1)S(1)...) custom-call(s32[1]{0:T(128)} %bitcast.me, ...), custom_call_target="tpu_custom_call" | custom-call | flops 1207959552 | bytes 24000000 | tf_op jit(solution)/shard_map/turn/pallas_call | solution.py:561
  221.8 1.6 collective-permute-start.30
  223.4 5.1 %collective-permute-start.27 = (bf16[256,768]{1,0:T(8,128)(2,1)S(1)}, bf16[256,768]{1,0:T(8,128)(2,1)S(1)}, u32[]{:S(2)}, u32[]{:S(2)}) collective-permute-start(bf16[256,768]{1,0:T(8,128)(2,1)S(1)} %get-tuple-element.254), channel_id=1, source_target_pairs={{0,1},{1,0},{2,3},{5,4},{6,7},{7,6},{8,9},{9,8},{10,11},{13,12},{1... | collective-permute-start | bytes 1179656 | tf_op jit(solution)/shard_map/ppermute | solution.py:974
  228.5 2.9 collective-permute-start.28
  231.4 2.0 collective-permute-start.29
  233.4 32.6 %attend_back.1 = (bf16[1024,768]{1,0:T(8,128)(2,1)S(1)}, bf16[1024,768]{1,0:T(8,128)(2,1)S(1)}, bf16[1024,768]{1,0:T(8,128)(2,1)S(1)}) custom-call(bf16[1024,768]{1,0:T(8,128)(2,1)} %get-tuple-element.205.k, bf16[1024,768]{1,0:T(8,128)(2,1)} %get-tuple-element.206.v, bf16[768,1024]{1,0:T(8,128)(2,1)} %get-tuple-element.207.q_t, ...), custom_call_target="tpu_custom_call" | custom-call | flops 22548578304 | bytes 14000000 | tf_op jit(solution)/shard_map/attend_back/pallas_call | solution.py:648
  267.3 1.7 convert_add_fusion.4
  269.5 1.4 fusion.8
  271.4 1.5 collective-permute-start.34
  273.0 2.4 collective-permute-start.32
  275.4 7.5 %weight_grads.1 = (bf16[2,4,4,96,384]{4,3,2,1,0:T(8,128)(2,1)}, bf16[2,4,4,96,384]{4,3,2,1,0:T(8,128)(2,1)}) custom-call(s32[1]{0:T(128)} %bitcast.me, bf16[768,1024]{1,0:T(8,128)(2,1)S(1)} %copy-done.24, bf16[768,1024]{1,0:T(8,128)(2,1)S(1)} %copy-done.25, bf16[1024,768]{1,0:T(8,128)(2,1)S(1)} %get-tuple-element.270.dq.refs_6_, ...), custom_call_target="tpu_custom_call" | custom-call | flops 4831838208 | bytes 14000000 | tf_op jit(solution)/shard_map/weight_grads/pallas_call | solution.py:914
  284.1 12.7 %first.1 = (bf16[256,768]{1,0:T(8,128)(2,1)}, bf16[256,768]{1,0:T(8,128)(2,1)}, bf16[256,768]{1,0:T(8,128)(2,1)}, bf16[256,768]{1,0:T(8,128)(2,1)}, f32[2,768]{1,0:T(2,128)}) custom-call(s32[1]{0:T(128)} %bitcast.me, bf16[256,768]{1,0:T(8,128)(2,1)} %get-tuple-element.197.refs_0_, bf16[256,768]{1,0:T(8,128)(2,1)} %copy-done.5, bf16[256,768]{1,0:T(8,128)(2,1)} %copy-done.1, ...), custom_call_target="tpu_custom_call" | custom-call | flops 3623878656 | bytes 20000000 | tf_op jit(solution)/shard_map/first/pallas_call | solution.py:704
  296.8 1.5 fusion.5
  298.9 1.5 collective-permute-start.38
  300.4 1.7 fusion.12
  302.1 3.7 collective-permute-start.40
  305.8 2.3 collective-permute-start.41
  308.1 2.2 collective-permute-start.42
  311.5 2.6 collective-permute-done.37
  314.3 2.1 fusion.9
  316.4 1.5 collective-permute-start.43
  320.3 2.2 gather_up.1
  322.6 4.6 %collective-permute-done.40 = bf16[256,768]{1,0:T(8,128)(2,1)} collective-permute-done((bf16[256,768]{1,0:T(8,128)(2,1)}, bf16[256,768]{1,0:T(8,128)(2,1)}, u32[]{:S(2)}, u32[]{:S(2)}) %collective-permute-start.40) | collective-permute-done | bytes 393248 | tf_op jit(solution)/shard_map/ppermute | solution.py:974
  329.9 6.4 %collective-permute-start.48 = (bf16[4,96,384]{2,1,0:T(8,128)(2,1)S(1)}, bf16[4,96,384]{2,1,0:T(8,128)(2,1)S(1)}, u32[]{:S(2)}, u32[]{:S(2)}) collective-permute-start(bf16[4,96,384]{2,1,0:T(8,128)(2,1)S(1)} %fusion.7), channel_id=1, source_target_pairs={{0,1},{1,0},{2,3},{3,2},{4,5},{5,4},{6,7},{7,6},{8,9},{9,8},{10,11... | collective-permute-start | bytes 884744 | tf_op jit(solution)/shard_map/ppermute | solution.py:948
  339.4 1.4 collective-permute-start.47
  342.1 1.8 collective-permute-done.47
  343.9 5.1 %collective-permute-done.48 = bf16[4,96,384]{2,1,0:T(8,128)(2,1)S(1)} collective-permute-done((bf16[4,96,384]{2,1,0:T(8,128)(2,1)S(1)}, bf16[4,96,384]{2,1,0:T(8,128)(2,1)S(1)}, u32[]{:S(2)}, u32[]{:S(2)}) %collective-permute-start.48) | collective-permute-done | bytes 294944 | tf_op jit(solution)/shard_map/ppermute | solution.py:948
  349.1 3.4 collective-permute-start.50
  352.6 2.8 collective-permute-start.51
  356.3 1.3 fusion.6
  357.7 1.6 collective-permute-start.53
  359.3 1.4 pad_maximum_fusion.1
  362.0 4.0 %collective-permute-done.51 = f32[9,1408]{1,0:T(8,128)S(1)} collective-permute-done((f32[9,1408]{1,0:T(8,128)S(1)}, f32[9,1408]{1,0:T(8,128)S(1)}, u32[]{:S(2)}, u32[]{:S(2)}) %collective-permute-start.51) | collective-permute-done | bytes 50720 | tf_op jit(solution)/shard_map/ppermute | solution.py:948
  366.7 1.4 fusion.17
  (263 shorter events, 48.9 us)
Async XLA Ops:
  0.6 16.3 %copy-start.37 = (bf16[3,96,192]{2,1,0:T(8,128)(2,1)S(1)}, bf16[3,96,192]{2,1,0:T(8,128)(2,1)}, u32[]{:S(2)}) copy-start(bf16[3,96,192]{2,1,0:T(8,128)(2,1)} %param.20) | copy-start | bytes 331780
  0.7 18.2 %copy-start.36 = (bf16[3,256,768]{2,1,0:T(8,128)(2,1)S(1)}, bf16[3,256,768]{2,1,0:T(8,128)(2,1)}, u32[]{:S(2)}) copy-start(bf16[3,256,768]{2,1,0:T(8,128)(2,1)} %param.16) | copy-start | bytes 3538948
  0.7 18.2 %copy-start.35 = (bf16[3,256,768]{2,1,0:T(8,128)(2,1)S(1)}, bf16[3,256,768]{2,1,0:T(8,128)(2,1)}, u32[]{:S(2)}) copy-start(bf16[3,256,768]{2,1,0:T(8,128)(2,1)} %param.30) | copy-start | bytes 3538948
  3.3 13.6 %collective-permute-start = (bf16[400,192]{1,0:T(8,128)(2,1)S(1)}, bf16[400,192]{1,0:T(8,128)(2,1)S(1)}, u32[]{:S(2)}, u32[]{:S(2)}) collective-permute-start(bf16[400,192]{1,0:T(8,128)(2,1)S(1)} %pad_maximum_fusion.16), channel_id=1, source_target_pairs={{0,2},{1,3},{2,0},{3,1},{4,6},{5,7},{6,4},{7,5},{8,10},{9,11},{10,... | collective-permute-start | bytes 460808 | tf_op jit(solution)/shard_map/ppermute | solution.py:948
  17.1 8.5 %collective-permute-start.1 = (bf16[400,384]{1,0:T(8,128)(2,1)S(1)}, bf16[400,384]{1,0:T(8,128)(2,1)S(1)}, u32[]{:S(2)}, u32[]{:S(2)}) collective-permute-start(bf16[400,384]{1,0:T(8,128)(2,1)S(1)} %pad_maximum_fusion.14), channel_id=1, source_target_pairs={{0,1},{1,0},{2,3},{3,2},{4,5},{5,4},{6,7},{7,6},{8,9},{9,8},{10,11... | collective-permute-start | bytes 921608 | tf_op jit(solution)/shard_map/ppermute | solution.py:948
  26.1 18.8 %collective-permute-start.4 = (bf16[256,768]{1,0:T(8,128)(2,1)S(1)}, bf16[256,768]{1,0:T(8,128)(2,1)S(1)}, u32[]{:S(2)}, u32[]{:S(2)}) collective-permute-start(bf16[256,768]{1,0:T(8,128)(2,1)S(1)} %concatenate.52), channel_id=1, source_target_pairs={{0,16},{4,20},{8,24},{12,28},{16,0},{20,4},{24,8},{28,12},{1,17},{... | collective-permute-start | bytes 1179656 | tf_op jit(solution)/shard_map/ppermute | solution.py:942
  27.6 17.3 %collective-permute-start.3 = (bf16[256,768]{1,0:T(8,128)(2,1)S(1)}, bf16[256,768]{1,0:T(8,128)(2,1)S(1)}, u32[]{:S(2)}, u32[]{:S(2)}) collective-permute-start(bf16[256,768]{1,0:T(8,128)(2,1)S(1)} %get-tuple-element.407), channel_id=1, source_target_pairs={{0,8},{4,12},{8,0},{12,4},{16,24},{20,28},{24,16},{28,20},{1,9},{5... | collective-permute-start | bytes 1179656 | tf_op jit(solution)/shard_map/ppermute | solution.py:942
  29.2 15.7 %collective-permute-start.2 = (bf16[192,768]{1,0:T(8,128)(2,1)S(1)}, bf16[192,768]{1,0:T(8,128)(2,1)S(1)}, u32[]{:S(2)}, u32[]{:S(2)}) collective-permute-start(bf16[192,768]{1,0:T(8,128)(2,1)S(1)} %pad_maximum_fusion.15), channel_id=1, source_target_pairs={{0,2},{1,3},{2,0},{3,1},{4,6},{5,7},{6,4},{7,5},{8,10},{9,11},{10,... | collective-permute-start | bytes 884744 | tf_op jit(solution)/shard_map/ppermute | solution.py:948
  45.0 22.8 %collective-permute-start.7 = (bf16[2,256,768]{2,1,0:T(8,128)(2,1)S(1)}, bf16[2,256,768]{2,1,0:T(8,128)(2,1)S(1)}, u32[]{:S(2)}, u32[]{:S(2)}) collective-permute-start(bf16[2,256,768]{2,1,0:T(8,128)(2,1)S(1)} %pad_maximum_fusion.9), channel_id=1, source_target_pairs={{0,8},{4,12},{8,0},{12,4},{16,24},{20,28},{24,16},{28,20},{1,9},{5... | collective-permute-start | bytes 2359304 | tf_op jit(solution)/shard_map/ppermute | solution.py:942
  45.7 22.1 %collective-permute-start.6 = (bf16[2,256,768]{2,1,0:T(8,128)(2,1)S(1)}, bf16[2,256,768]{2,1,0:T(8,128)(2,1)}, u32[]{:S(2)}, u32[]{:S(2)}) collective-permute-start(bf16[2,256,768]{2,1,0:T(8,128)(2,1)S(1)} %pad_maximum_fusion.8), channel_id=1, source_target_pairs={{0,16},{4,20},{8,24},{12,28},{16,0},{20,4},{24,8},{28,12},{1,17},{... | collective-permute-start | bytes 2359304 | tf_op jit(solution)/shard_map/ppermute | solution.py:942
  46.3 21.5 %collective-permute-start.5 = (bf16[192,1536]{1,0:T(8,128)(2,1)S(1)}, bf16[192,1536]{1,0:T(8,128)(2,1)}, u32[]{:S(2)}, u32[]{:S(2)}) collective-permute-start(bf16[192,1536]{1,0:T(8,128)(2,1)S(1)} %constant_dynamic-update-slice_fusion), channel_id=1, source_target_pairs={{0,1},{1,0},{2,3},{3,2},{4,5},{5,4},{6,7},{7,6},{8,9},{9,8},{10,11... | collective-permute-start | bytes 1769480 | tf_op jit(solution)/shard_map/ppermute | solution.py:948
  47.1 20.7 %collective-permute-start.8 = (bf16[256,768]{1,0:T(8,128)(2,1)}, bf16[256,768]{1,0:T(8,128)(2,1)S(1)}, u32[]{:S(2)}, u32[]{:S(2)}) collective-permute-start(bf16[256,768]{1,0:T(8,128)(2,1)} %get-tuple-element.176), channel_id=1, source_target_pairs={{0,2},{2,0},{3,1},{4,6},{5,7},{7,5},{8,10},{10,8},{11,9},{12,14},{... | collective-permute-start | bytes 1179656 | tf_op jit(solution)/shard_map/ppermute | solution.py:974
  54.9 30.9 %copy-start.19 = (s32[1,1,4,256]{3,1,2,0:T(1,128)}, s32[1,1,4,256]{3,1,2,0:T(1,128)S(1)}, u32[]{:S(2)}) copy-start(s32[1,1,4,256]{3,1,2,0:T(1,128)S(1)} %copy.45) | copy-start | bytes 12292
  72.8 14.0 %collective-permute-start.13 = (bf16[8,256,768]{2,1,0:T(8,128)(2,1)}, bf16[8,256,768]{2,1,0:T(8,128)(2,1)}, u32[]{:S(2)}, u32[]{:S(2)}) collective-permute-start(bf16[8,256,768]{2,1,0:T(8,128)(2,1)} %constant_dynamic-update-slice_fusion.2.refs_0_.refs_2_.refs_8_.refs_10_.refs_12_.refs_9_.refs_11_), channel_id=1, source_target_pairs={{0,4},{4,0},{8,12},{12,8},{16,20},{20,16},{24,28},{28,24},{1,5},{5... | collective-permute-start | bytes 9437192 | tf_op jit(solution)/shard_map/ppermute | solution.py:942
  74.1 20.6 %collective-permute-start.12 = (bf16[96,3072]{1,0:T(8,128)(2,1)S(1)}, bf16[96,3072]{1,0:T(8,128)(2,1)}, u32[]{:S(2)}, u32[]{:S(2)}) collective-permute-start(bf16[96,3072]{1,0:T(8,128)(2,1)S(1)} %get-tuple-element.399), channel_id=1, source_target_pairs={{0,16},{4,20},{8,24},{12,28},{16,0},{20,4},{24,8},{28,12},{1,17},{... | collective-permute-start | bytes 1769480 | tf_op jit(solution)/shard_map/ppermute | solution.py:942
  75.8 18.9 %collective-permute-start.11 = (bf16[96,3072]{1,0:T(8,128)(2,1)S(1)}, bf16[96,3072]{1,0:T(8,128)(2,1)}, u32[]{:S(2)}, u32[]{:S(2)}) collective-permute-start(bf16[96,3072]{1,0:T(8,128)(2,1)S(1)} %get-tuple-element.401), channel_id=1, source_target_pairs={{0,8},{4,12},{8,0},{12,4},{16,24},{20,28},{24,16},{28,20},{1,9},{5... | collective-permute-start | bytes 1769480 | tf_op jit(solution)/shard_map/ppermute | solution.py:942
  77.4 13.2 %collective-permute-start.10 = (bf16[256,768]{1,0:T(8,128)(2,1)}, bf16[256,768]{1,0:T(8,128)(2,1)S(1)}, u32[]{:S(2)}, u32[]{:S(2)}) collective-permute-start(bf16[256,768]{1,0:T(8,128)(2,1)} %get-tuple-element.186), channel_id=1, source_target_pairs={{1,2},{2,1},{3,0},{4,7},{5,6},{6,5},{9,10},{10,9},{11,8},{12,15},{... | collective-permute-start | bytes 1179656 | tf_op jit(solution)/shard_map/ppermute | solution.py:974
  78.7 16.0 %collective-permute-start.9 = (bf16[256,768]{1,0:T(8,128)(2,1)S(1)}, bf16[256,768]{1,0:T(8,128)(2,1)S(1)}, u32[]{:S(2)}, u32[]{:S(2)}) collective-permute-start(bf16[256,768]{1,0:T(8,128)(2,1)S(1)} %copy-done.48), channel_id=1, source_target_pairs={{0,1},{1,0},{3,2},{4,5},{6,7},{7,6},{8,9},{9,8},{11,10},{12,13},{1... | collective-permute-start | bytes 1179656 | tf_op jit(solution)/shard_map/ppermute | solution.py:974
  97.1 45.0 %collective-permute-start.15 = (bf16[2,96,3072]{2,1,0:T(8,128)(2,1)}, bf16[2,96,3072]{2,1,0:T(8,128)(2,1)}, u32[]{:S(2)}, u32[]{:S(2)}) collective-permute-start(bf16[2,96,3072]{2,1,0:T(8,128)(2,1)} %pad_maximum_fusion.3.refs_9_.refs_11_), channel_id=1, source_target_pairs={{0,8},{4,12},{8,0},{12,4},{16,24},{20,28},{24,16},{28,20},{1,9},{5... | collective-permute-start | bytes 3538952 | tf_op jit(solution)/shard_map/ppermute | solution.py:942
  99.8 42.2 %collective-permute-start.14 = (bf16[2,96,3072]{2,1,0:T(8,128)(2,1)}, bf16[2,96,3072]{2,1,0:T(8,128)(2,1)}, u32[]{:S(2)}, u32[]{:S(2)}) collective-permute-start(bf16[2,96,3072]{2,1,0:T(8,128)(2,1)} %pad_maximum_fusion.2.refs_5_.refs_7_), channel_id=1, source_target_pairs={{0,16},{4,20},{8,24},{12,28},{16,0},{20,4},{24,8},{28,12},{1,17},{... | collective-permute-start | bytes 3538952 | tf_op jit(solution)/shard_map/ppermute | solution.py:942
  100.3 41.7 %collective-permute-start.16 = (bf16[256,768]{1,0:T(8,128)(2,1)S(1)}, bf16[256,768]{1,0:T(8,128)(2,1)S(1)}, u32[]{:S(2)}, u32[]{:S(2)}) collective-permute-start(bf16[256,768]{1,0:T(8,128)(2,1)S(1)} %copy-done.44), channel_id=1, source_target_pairs={{0,1},{1,0},{3,2},{4,5},{6,7},{7,6},{8,9},{9,8},{11,10},{12,13},{1... | collective-permute-start | bytes 1179656 | tf_op jit(solution)/shard_map/ppermute | solution.py:974
  105.7 36.3 %collective-permute-start.17 = (bf16[256,768]{1,0:T(8,128)(2,1)S(1)}, bf16[256,768]{1,0:T(8,128)(2,1)S(1)}, u32[]{:S(2)}, u32[]{:S(2)}) collective-permute-start(bf16[256,768]{1,0:T(8,128)(2,1)S(1)} %copy-done.43), channel_id=1, source_target_pairs={{0,2},{2,0},{3,1},{4,6},{5,7},{7,5},{8,10},{10,8},{11,9},{12,14},{... | collective-permute-start | bytes 1179656 | tf_op jit(solution)/shard_map/ppermute | solution.py:974
  107.6 34.4 %collective-permute-start.18 = (bf16[256,768]{1,0:T(8,128)(2,1)S(1)}, bf16[256,768]{1,0:T(8,128)(2,1)S(1)}, u32[]{:S(2)}, u32[]{:S(2)}) collective-permute-start(bf16[256,768]{1,0:T(8,128)(2,1)S(1)} %copy-done.42), channel_id=1, source_target_pairs={{1,2},{2,1},{3,0},{4,7},{5,6},{6,5},{9,10},{10,9},{11,8},{12,15},{... | collective-permute-start | bytes 1179656 | tf_op jit(solution)/shard_map/ppermute | solution.py:974
  121.7 22.3 %copy-start.50 = (f32[4,768]{1,0:T(4,128)S(1)}, f32[4,768]{1,0:T(4,128)}, u32[]{:S(2)}) copy-start(f32[4,768]{1,0:T(4,128)} %get-tuple-element.229) | copy-start | bytes 36868
  142.0 11.5 %collective-permute-start.19 = (bf16[2,96,3072]{2,1,0:T(8,128)(2,1)}, bf16[2,96,3072]{2,1,0:T(8,128)(2,1)S(1)}, u32[]{:S(2)}, u32[]{:S(2)}) collective-permute-start(bf16[2,96,3072]{2,1,0:T(8,128)(2,1)} %pad_maximum_fusion.2.refs_5_.refs_7_), channel_id=1, source_target_pairs={{0,4},{4,0},{8,12},{12,8},{16,20},{20,16},{24,28},{28,24},{1,5},{5... | collective-permute-start | bytes 3538952 | tf_op jit(solution)/shard_map/ppermute | solution.py:942
  143.5 10.0 %collective-permute-start.20 = (bf16[2,96,3072]{2,1,0:T(8,128)(2,1)}, bf16[2,96,3072]{2,1,0:T(8,128)(2,1)}, u32[]{:S(2)}, u32[]{:S(2)}) collective-permute-start(bf16[2,96,3072]{2,1,0:T(8,128)(2,1)} %collective-permute-done.14.refs_6_.refs_8_), channel_id=1, source_target_pairs={{0,4},{4,0},{8,12},{12,8},{16,20},{20,16},{24,28},{28,24},{1,5},{5... | collective-permute-start | bytes 3538952 | tf_op jit(solution)/shard_map/ppermute | solution.py:942
  143.5 10.0 %collective-permute-start.21 = (bf16[2,96,3072]{2,1,0:T(8,128)(2,1)}, bf16[2,96,3072]{2,1,0:T(8,128)(2,1)}, u32[]{:S(2)}, u32[]{:S(2)}) collective-permute-start(bf16[2,96,3072]{2,1,0:T(8,128)(2,1)} %pad_maximum_fusion.3.refs_9_.refs_11_), channel_id=1, source_target_pairs={{0,4},{4,0},{8,12},{12,8},{16,20},{20,16},{24,28},{28,24},{1,5},{5... | collective-permute-start | bytes 3538952 | tf_op jit(solution)/shard_map/ppermute | solution.py:942
  144.0 9.5 %collective-permute-start.22 = (bf16[2,96,3072]{2,1,0:T(8,128)(2,1)}, bf16[2,96,3072]{2,1,0:T(8,128)(2,1)}, u32[]{:S(2)}, u32[]{:S(2)}) collective-permute-start(bf16[2,96,3072]{2,1,0:T(8,128)(2,1)} %collective-permute-done.15.refs_10_.refs_12_), channel_id=1, source_target_pairs={{0,4},{4,0},{8,12},{12,8},{16,20},{20,16},{24,28},{28,24},{1,5},{5... | collective-permute-start | bytes 3538952 | tf_op jit(solution)/shard_map/ppermute | solution.py:942
  177.0 25.7 %copy-start.22 = (f32[3,1,512]{2,1,0:T(1,128)}, f32[3,1,512]{2,1,0:T(1,128)S(1)}, u32[]{:S(2)}) copy-start(f32[3,1,512]{2,1,0:T(1,128)S(1)} %get-tuple-element.295.d_bias_a) | copy-start | bytes 18436
  177.0 25.9 %collective-permute-start.23 = (bf16[2,4,96,1536]{3,2,1,0:T(8,128)(2,1)}, bf16[2,4,96,1536]{3,2,1,0:T(8,128)(2,1)S(1)}, u32[]{:S(2)}, u32[]{:S(2)}) collective-permute-start(bf16[2,4,96,1536]{3,2,1,0:T(8,128)(2,1)} %get-tuple-element.237), channel_id=1, source_target_pairs={{0,4},{4,0},{8,12},{12,8},{16,20},{20,16},{24,28},{28,24},{1,5},{5... | collective-permute-start | bytes 7077896 | tf_op jit(solution)/shard_map/ppermute | solution.py:942
  177.5 25.4 %copy-start.33 = (bf16[2,4,96,1536]{3,2,1,0:T(8,128)(2,1)S(1)}, bf16[2,4,96,1536]{3,2,1,0:T(8,128)(2,1)}, u32[]{:S(2)}) copy-start(bf16[2,4,96,1536]{3,2,1,0:T(8,128)(2,1)} %get-tuple-element.245) | copy-start | bytes 7077892
  202.7 15.3 %collective-permute-start.26 = (bf16[2,4,96,1536]{3,2,1,0:T(8,128)(2,1)}, bf16[2,4,96,1536]{3,2,1,0:T(8,128)(2,1)S(1)}, u32[]{:S(2)}, u32[]{:S(2)}) collective-permute-start(bf16[2,4,96,1536]{3,2,1,0:T(8,128)(2,1)} %get-tuple-element.247), channel_id=1, source_target_pairs={{0,4},{4,0},{8,12},{12,8},{16,20},{20,16},{24,28},{28,24},{1,5},{5... | collective-permute-start | bytes 7077896 | tf_op jit(solution)/shard_map/ppermute | solution.py:942
  202.9 17.2 %copy-start.34 = (bf16[2,4,96,1536]{3,2,1,0:T(8,128)(2,1)}, bf16[2,4,96,1536]{3,2,1,0:T(8,128)(2,1)S(1)}, u32[]{:S(2)}) copy-start(bf16[2,4,96,1536]{3,2,1,0:T(8,128)(2,1)S(1)} %collective-permute-done.23) | copy-start | bytes 7077892
  203.3 15.7 %collective-permute-start.24 = (bf16[2,96,1536]{2,1,0:T(8,128)(2,1)S(1)}, bf16[2,96,1536]{2,1,0:T(8,128)(2,1)S(1)}, u32[]{:S(2)}, u32[]{:S(2)}) collective-permute-start(bf16[2,96,1536]{2,1,0:T(8,128)(2,1)S(1)} %get-tuple-element.379), channel_id=1, source_target_pairs={{0,8},{4,12},{8,0},{12,4},{16,24},{20,28},{24,16},{28,20},{1,9},{5... | collective-permute-start | bytes 1769480 | tf_op jit(solution)/shard_map/ppermute | solution.py:942
  204.7 15.3 %collective-permute-start.25 = (bf16[2,96,1536]{2,1,0:T(8,128)(2,1)S(1)}, bf16[2,96,1536]{2,1,0:T(8,128)(2,1)S(1)}, u32[]{:S(2)}, u32[]{:S(2)}) collective-permute-start(bf16[2,96,1536]{2,1,0:T(8,128)(2,1)S(1)} %get-tuple-element.378), channel_id=1, source_target_pairs={{0,16},{4,20},{8,24},{12,28},{16,0},{20,4},{24,8},{28,12},{1,17},{... | collective-permute-start | bytes 1769480 | tf_op jit(solution)/shard_map/ppermute | solution.py:942
  218.0 51.1 %copy-start.31 = (bf16[2,4,96,1536]{3,2,1,0:T(8,128)(2,1)}, bf16[2,4,96,1536]{3,2,1,0:T(8,128)(2,1)S(1)}, u32[]{:S(2)}) copy-start(bf16[2,4,96,1536]{3,2,1,0:T(8,128)(2,1)S(1)} %collective-permute-done.26) | copy-start | bytes 7077892
  221.1 46.1 %collective-permute-start.31 = (bf16[3,96,1536]{2,1,0:T(8,128)(2,1)S(1)}, bf16[3,96,1536]{2,1,0:T(8,128)(2,1)S(1)}, u32[]{:S(2)}, u32[]{:S(2)}) collective-permute-start(bf16[3,96,1536]{2,1,0:T(8,128)(2,1)S(1)} %pad_maximum_fusion.7), channel_id=1, source_target_pairs={{0,8},{4,12},{8,0},{12,4},{16,24},{20,28},{24,16},{28,20},{1,9},{5... | collective-permute-start | bytes 2654216 | tf_op jit(solution)/shard_map/ppermute | solution.py:942
  221.8 45.5 %collective-permute-start.30 = (bf16[3,96,1536]{2,1,0:T(8,128)(2,1)S(1)}, bf16[3,96,1536]{2,1,0:T(8,128)(2,1)S(1)}, u32[]{:S(2)}, u32[]{:S(2)}) collective-permute-start(bf16[3,96,1536]{2,1,0:T(8,128)(2,1)S(1)} %pad_maximum_fusion.6), channel_id=1, source_target_pairs={{0,16},{4,20},{8,24},{12,28},{16,0},{20,4},{24,8},{28,12},{1,17},{... | collective-permute-start | bytes 2654216 | tf_op jit(solution)/shard_map/ppermute | solution.py:942
  223.4 43.9 %collective-permute-start.27 = (bf16[256,768]{1,0:T(8,128)(2,1)S(1)}, bf16[256,768]{1,0:T(8,128)(2,1)S(1)}, u32[]{:S(2)}, u32[]{:S(2)}) collective-permute-start(bf16[256,768]{1,0:T(8,128)(2,1)S(1)} %get-tuple-element.254), channel_id=1, source_target_pairs={{0,1},{1,0},{2,3},{5,4},{6,7},{7,6},{8,9},{9,8},{10,11},{13,12},{1... | collective-permute-start | bytes 1179656 | tf_op jit(solution)/shard_map/ppermute | solution.py:974
  228.5 38.8 %collective-permute-start.28 = (bf16[256,768]{1,0:T(8,128)(2,1)S(1)}, bf16[256,768]{1,0:T(8,128)(2,1)}, u32[]{:S(2)}, u32[]{:S(2)}) collective-permute-start(bf16[256,768]{1,0:T(8,128)(2,1)S(1)} %get-tuple-element.255), channel_id=1, source_target_pairs={{0,2},{1,3},{2,0},{5,7},{6,4},{7,5},{8,10},{9,11},{10,8},{13,15},{... | collective-permute-start | bytes 1179656 | tf_op jit(solution)/shard_map/ppermute | solution.py:974
  231.4 35.9 %collective-permute-start.29 = (bf16[256,768]{1,0:T(8,128)(2,1)S(1)}, bf16[256,768]{1,0:T(8,128)(2,1)}, u32[]{:S(2)}, u32[]{:S(2)}) collective-permute-start(bf16[256,768]{1,0:T(8,128)(2,1)S(1)} %get-tuple-element.256), channel_id=1, source_target_pairs={{0,3},{1,2},{2,1},{5,6},{6,5},{7,4},{8,11},{9,10},{10,9},{13,14},{... | collective-permute-start | bytes 1179656 | tf_op jit(solution)/shard_map/ppermute | solution.py:974
  233.4 33.9 %copy-start.41 = (bf16[2,96,1536]{2,1,0:T(8,128)(2,1)S(1)}, bf16[2,96,1536]{2,1,0:T(8,128)(2,1)}, u32[]{:S(2)}) copy-start(bf16[2,96,1536]{2,1,0:T(8,128)(2,1)} %copy-done.40) | copy-start | bytes 1769476
  270.9 12.1 %collective-permute-start.33 = (bf16[1,96,1536]{2,1,0:T(8,128)(2,1)S(1)}, bf16[1,96,1536]{2,1,0:T(8,128)(2,1)}, u32[]{:S(2)}, u32[]{:S(2)}) collective-permute-start(bf16[1,96,1536]{2,1,0:T(8,128)(2,1)S(1)} %get-tuple-element.373), channel_id=1, source_target_pairs={{0,16},{4,20},{8,24},{12,28},{16,0},{20,4},{24,8},{28,12},{1,17},{... | collective-permute-start | bytes 884744 | tf_op jit(solution)/shard_map/ppermute | solution.py:942
  271.4 11.5 %collective-permute-start.34 = (bf16[1,96,1536]{2,1,0:T(8,128)(2,1)S(1)}, bf16[1,96,1536]{2,1,0:T(8,128)(2,1)}, u32[]{:S(2)}, u32[]{:S(2)}) collective-permute-start(bf16[1,96,1536]{2,1,0:T(8,128)(2,1)S(1)} %get-tuple-element.372), channel_id=1, source_target_pairs={{0,8},{4,12},{8,0},{12,4},{16,24},{20,28},{24,16},{28,20},{1,9},{5... | collective-permute-start | bytes 884744 | tf_op jit(solution)/shard_map/ppermute | solution.py:942
  273.0 10.0 %collective-permute-start.32 = (bf16[96,1536]{1,0:T(8,128)(2,1)S(1)}, bf16[96,1536]{1,0:T(8,128)(2,1)}, u32[]{:S(2)}, u32[]{:S(2)}) collective-permute-start(bf16[96,1536]{1,0:T(8,128)(2,1)S(1)} %fusion.8), channel_id=1, source_target_pairs={{0,1},{1,0},{2,3},{3,2},{4,5},{5,4},{6,7},{7,6},{8,9},{9,8},{10,11... | collective-permute-start | bytes 884744 | tf_op jit(solution)/shard_map/ppermute | solution.py:948
  283.0 13.8 %collective-permute-start.36 = (bf16[2,4,4,96,384]{4,3,2,1,0:T(8,128)(2,1)}, bf16[2,4,4,96,384]{4,3,2,1,0:T(8,128)(2,1)}, u32[]{:S(2)}, u32[]{:S(2)}) collective-permute-start(bf16[2,4,4,96,384]{4,3,2,1,0:T(8,128)(2,1)} %get-tuple-element.288), channel_id=1, source_target_pairs={{0,4},{4,0},{8,12},{12,8},{16,20},{20,16},{24,28},{28,24},{1,5},{5... | collective-permute-start | bytes 7077896 | tf_op jit(solution)/shard_map/ppermute | solution.py:942
  284.0 12.8 %collective-permute-start.35 = (bf16[96,1536]{1,0:T(8,128)(2,1)S(1)}, bf16[96,1536]{1,0:T(8,128)(2,1)S(1)}, u32[]{:S(2)}, u32[]{:S(2)}) collective-permute-start(bf16[96,1536]{1,0:T(8,128)(2,1)S(1)} %convert_add_fusion.4), channel_id=1, source_target_pairs={{0,1},{1,0},{2,3},{3,2},{4,5},{5,4},{6,7},{7,6},{8,9},{9,8},{10,11... | collective-permute-start | bytes 884744 | tf_op jit(solution)/shard_map/ppermute | solution.py:948
  298.3 15.8 %collective-permute-start.37 = (bf16[2,4,96,384]{3,2,1,0:T(8,128)(2,1)S(1)}, bf16[2,4,96,384]{3,2,1,0:T(8,128)(2,1)S(1)}, u32[]{:S(2)}, u32[]{:S(2)}) collective-permute-start(bf16[2,4,96,384]{3,2,1,0:T(8,128)(2,1)S(1)} %get-tuple-element.369), channel_id=1, source_target_pairs={{0,8},{4,12},{8,0},{12,4},{16,24},{20,28},{24,16},{28,20},{1,9},{5... | collective-permute-start | bytes 1769480 | tf_op jit(solution)/shard_map/ppermute | solution.py:942
  298.9 15.4 %collective-permute-start.38 = (bf16[2,4,96,384]{3,2,1,0:T(8,128)(2,1)S(1)}, bf16[2,4,96,384]{3,2,1,0:T(8,128)(2,1)S(1)}, u32[]{:S(2)}, u32[]{:S(2)}) collective-permute-start(bf16[2,4,96,384]{3,2,1,0:T(8,128)(2,1)S(1)} %get-tuple-element.368), channel_id=1, source_target_pairs={{0,16},{4,20},{8,24},{12,28},{16,0},{20,4},{24,8},{28,12},{1,17},{... | collective-permute-start | bytes 1769480 | tf_op jit(solution)/shard_map/ppermute | solution.py:942
  302.1 25.1 %collective-permute-start.40 = (bf16[256,768]{1,0:T(8,128)(2,1)}, bf16[256,768]{1,0:T(8,128)(2,1)}, u32[]{:S(2)}, u32[]{:S(2)}) collective-permute-start(bf16[256,768]{1,0:T(8,128)(2,1)} %get-tuple-element.299), channel_id=1, source_target_pairs={{0,1},{1,0},{2,3},{5,4},{6,7},{7,6},{8,9},{9,8},{10,11},{13,12},{1... | collective-permute-start | bytes 1179656 | tf_op jit(solution)/shard_map/ppermute | solution.py:974
  305.8 22.7 %collective-permute-start.41 = (bf16[256,768]{1,0:T(8,128)(2,1)}, bf16[256,768]{1,0:T(8,128)(2,1)}, u32[]{:S(2)}, u32[]{:S(2)}) collective-permute-start(bf16[256,768]{1,0:T(8,128)(2,1)} %get-tuple-element.300), channel_id=1, source_target_pairs={{0,2},{1,3},{2,0},{5,7},{6,4},{7,5},{8,10},{9,11},{10,8},{13,15},{... | collective-permute-start | bytes 1179656 | tf_op jit(solution)/shard_map/ppermute | solution.py:974
  308.1 20.4 %collective-permute-start.42 = (bf16[256,768]{1,0:T(8,128)(2,1)}, bf16[256,768]{1,0:T(8,128)(2,1)}, u32[]{:S(2)}, u32[]{:S(2)}) collective-permute-start(bf16[256,768]{1,0:T(8,128)(2,1)} %get-tuple-element.301), channel_id=1, source_target_pairs={{0,3},{1,2},{2,1},{5,6},{6,5},{7,4},{8,11},{9,10},{10,9},{13,14},{... | collective-permute-start | bytes 1179656 | tf_op jit(solution)/shard_map/ppermute | solution.py:974
  316.4 12.2 %collective-permute-start.43 = (bf16[1,4,96,384]{3,2,1,0:T(8,128)(2,1)}, bf16[1,4,96,384]{3,2,1,0:T(8,128)(2,1)}, u32[]{:S(2)}, u32[]{:S(2)}) collective-permute-start(bf16[1,4,96,384]{3,2,1,0:T(8,128)(2,1)} %get-tuple-element.367), channel_id=1, source_target_pairs={{0,16},{4,20},{8,24},{12,28},{16,0},{20,4},{24,8},{28,12},{1,17},{... | collective-permute-start | bytes 884744 | tf_op jit(solution)/shard_map/ppermute | solution.py:942
  317.9 10.7 %collective-permute-start.44 = (bf16[1,4,96,384]{3,2,1,0:T(8,128)(2,1)}, bf16[1,4,96,384]{3,2,1,0:T(8,128)(2,1)}, u32[]{:S(2)}, u32[]{:S(2)}) collective-permute-start(bf16[1,4,96,384]{3,2,1,0:T(8,128)(2,1)} %get-tuple-element.366), channel_id=1, source_target_pairs={{0,8},{4,12},{8,0},{12,4},{16,24},{20,28},{24,16},{28,20},{1,9},{5... | collective-permute-start | bytes 884744 | tf_op jit(solution)/shard_map/ppermute | solution.py:942
  327.2 1.4 collective-permute-start.39
  329.9 19.2 %collective-permute-start.48 = (bf16[4,96,384]{2,1,0:T(8,128)(2,1)S(1)}, bf16[4,96,384]{2,1,0:T(8,128)(2,1)S(1)}, u32[]{:S(2)}, u32[]{:S(2)}) collective-permute-start(bf16[4,96,384]{2,1,0:T(8,128)(2,1)S(1)} %fusion.7), channel_id=1, source_target_pairs={{0,1},{1,0},{2,3},{3,2},{4,5},{5,4},{6,7},{7,6},{8,9},{9,8},{10,11... | collective-permute-start | bytes 884744 | tf_op jit(solution)/shard_map/ppermute | solution.py:948
  336.3 12.7 %collective-permute-start.49 = (bf16[2,96,768]{2,1,0:T(8,128)(2,1)S(1)}, bf16[2,96,768]{2,1,0:T(8,128)(2,1)S(1)}, u32[]{:S(2)}, u32[]{:S(2)}) collective-permute-start(bf16[2,96,768]{2,1,0:T(8,128)(2,1)S(1)} %slice.523), channel_id=1, source_target_pairs={{0,2},{1,3},{2,0},{3,1},{4,6},{5,7},{6,4},{7,5},{8,10},{9,11},{10,... | collective-permute-start | bytes 884744 | tf_op jit(solution)/shard_map/ppermute | solution.py:948
  337.2 4.7 %collective-permute-start.45 = (f32[2,1408]{1,0:T(2,128)S(1)}, f32[2,1408]{1,0:T(2,128)S(1)}, u32[]{:S(2)}, u32[]{:S(2)}) collective-permute-start(f32[2,1408]{1,0:T(2,128)S(1)} %get-tuple-element.412), channel_id=1, source_target_pairs={{0,8},{4,12},{8,0},{12,4},{16,24},{20,28},{24,16},{28,20},{1,9},{5... | collective-permute-start | bytes 33800 | tf_op jit(solution)/shard_map/ppermute | solution.py:945
  338.4 3.7 collective-permute-start.46
  339.4 4.6 %collective-permute-start.47 = (f32[2,1408]{1,0:T(2,128)S(1)}, f32[2,1408]{1,0:T(2,128)S(1)}, u32[]{:S(2)}, u32[]{:S(2)}) collective-permute-start(f32[2,1408]{1,0:T(2,128)S(1)} %get-tuple-element.410), channel_id=1, source_target_pairs={{0,24},{4,28},{8,16},{12,20},{16,8},{20,12},{24,0},{28,4},{1,25},{... | collective-permute-start | bytes 33800 | tf_op jit(solution)/shard_map/ppermute | solution.py:945
  349.1 12.9 %collective-permute-start.50 = (f32[9,1408]{1,0:T(8,128)S(1)}, f32[9,1408]{1,0:T(8,128)S(1)}, u32[]{:S(2)}, u32[]{:S(2)}) collective-permute-start(f32[9,1408]{1,0:T(8,128)S(1)} %concatenate.60), channel_id=1, source_target_pairs={{0,1},{1,0},{2,3},{3,2},{4,5},{5,4},{6,7},{7,6},{8,9},{9,8},{10,11... | collective-permute-start | bytes 152072 | tf_op jit(solution)/shard_map/ppermute | solution.py:948
  352.6 13.5 %collective-permute-start.51 = (f32[9,1408]{1,0:T(8,128)S(1)}, f32[9,1408]{1,0:T(8,128)S(1)}, u32[]{:S(2)}, u32[]{:S(2)}) collective-permute-start(f32[9,1408]{1,0:T(8,128)S(1)} %concatenate.60), channel_id=1, source_target_pairs={{0,2},{1,3},{2,0},{3,1},{4,6},{5,7},{6,4},{7,5},{8,10},{9,11},{10,... | collective-permute-start | bytes 152072 | tf_op jit(solution)/shard_map/ppermute | solution.py:948
  355.4 10.7 %collective-permute-start.52 = (f32[9,1408]{1,0:T(8,128)S(1)}, f32[9,1408]{1,0:T(8,128)S(1)}, u32[]{:S(2)}, u32[]{:S(2)}) collective-permute-start(f32[9,1408]{1,0:T(8,128)S(1)} %concatenate.60), channel_id=1, source_target_pairs={{0,3},{1,2},{2,1},{3,0},{4,7},{5,6},{6,5},{7,4},{8,11},{9,10},{10,... | collective-permute-start | bytes 152072 | tf_op jit(solution)/shard_map/ppermute | solution.py:948
  357.7 13.5 %collective-permute-start.53 = (bf16[4,96,192]{2,1,0:T(8,128)(2,1)S(1)}, bf16[4,96,192]{2,1,0:T(8,128)(2,1)S(1)}, u32[]{:S(2)}, u32[]{:S(2)}) collective-permute-start(bf16[4,96,192]{2,1,0:T(8,128)(2,1)S(1)} %slice.524), channel_id=1, source_target_pairs={{0,2},{1,3},{2,0},{3,1},{4,6},{5,7},{6,4},{7,5},{8,10},{9,11},{10,... | collective-permute-start | bytes 442376 | tf_op jit(solution)/shard_map/ppermute | solution.py:948
  (44 other events, 251.6 us)

commit v5 on v4

--- a/solution.py
+++ b/solution.py
@@ -57,16 +57,35 @@
     for n, ref in enumerate(refs):
         at = pl.ds(n % each * rows, rows)
         at_step(n // each, lambda ref=ref, at=at: out.__setitem__((at, slice(None)), ref[...]))
-    return out[...].astype(F32)
-
-
-def put(refs, value):
+
+
+def copy_out(refs, source):
     for n, ref in enumerate(refs):
-        at_step(n, lambda ref=ref: ref.__setitem__(..., value))
+        at_step(n, lambda ref=ref: ref.__setitem__(..., source[...]))
+
+
+STEP = 256
+
+
+def over_rows(count, act):
+    size = min(STEP, count)
+
+    @pl.loop(0, count // size)
+    def _(i):
+        act(pl.ds(pl.multiple_of(i * size, size), size))
+
+
+def normed(x):
+    centred = x - jnp.mean(x, axis=-1, keepdims=True)
+    inverse = lax.rsqrt(jnp.mean(centred * centred, axis=-1, keepdims=True) + EPSILON)
+    return centred * inverse, inverse
+
+
+def clear_rows(ref):
+    at_step(0, lambda: ref.__setitem__(..., jnp.zeros(ref.shape, ref.dtype)))
 
 
 def add_row(ref, n, value):
-    at_step(0, lambda: ref.__setitem__((slice(n, n + 1), slice(None)), jnp.zeros_like(value)))
     ref[n : n + 1, :] += value
 
 
@@ -165,15 +184,19 @@
     (n_t, k_out, v_out, q_t, k_t, v_t), (w_buf, x_buf, sems) = refs[:6], refs[6:]
     copies = qkv_copies(me, qk, vo, held, w_buf, sems, w_buf.shape[1] // qk.count)
     start_all(copies)
-    x = pick(x_refs, x_buf, 2)
-    centred = x - jnp.mean(x, axis=-1, keepdims=True)
-    spread = jnp.mean(centred * centred, axis=-1, keepdims=True)
-    normed = (centred * lax.rsqrt(spread + EPSILON) * mul + add).astype(BF16)
-    n_t[...] = normed.T
+    pick(x_refs, x_buf, 2)
+
+    def norm(rows):
+        unit, _ = normed(x_buf[rows, :].astype(F32))
+        x_buf[rows, :] = (unit * mul + add).astype(BF16)
+
+    over_rows(x_buf.shape[0], norm)
+    tokens = x_buf[...]
+    n_t[...] = tokens.T
     wait_all(copies)
     width = k_out.shape[1]
     for c, (flat, turned, factor) in enumerate(((None, q_t, HEAD**-0.5), (k_out, k_t, 1.0))):
-        proj = dot_nn(normed, w_buf[c])
+        proj = dot_nn(tokens, w_buf[c])
         for p in range(width // PAIR):
             lanes = slice(p * PAIR, (p + 1) * PAIR)
             r = proj[:, lanes]
@@ -186,7 +209,7 @@
             if flat is not None:
                 flat[:, lanes] = spun
             turned[lanes, :] = spun.T
-    values = dot_nn(normed, w_buf[2]).astype(BF16)
+    values = dot_nn(tokens, w_buf[2]).astype(BF16)
     v_out[...] = values
     v_t[...] = values.T
 
@@ -321,22 +344,27 @@
     pieces, refs = refs[: len(vo.parts)], refs[len(vo.parts) :]
     (att, n_two, n_two_t, d_down, d_down_t, d_bias, mix), (w_buf, x_buf, sems) = refs[:7], refs[7:]
     copies = load_out_weight(me, vo, pieces, w_buf, sems)
-    scaled = pick(g_refs, x_buf) * gate_two
-    add_row(d_bias, 0, jnp.sum(scaled, axis=0, keepdims=True))
-    scaled = scaled.astype(BF16)
-    d_down[...] = scaled
-    d_down_t[...] = scaled.T
+    pick(g_refs, x_buf)
+
+    def scale(rows):
+        scaled = x_buf[rows, :].astype(F32) * gate_two
+        add_row(d_bias, 0, jnp.sum(scaled, axis=0, keepdims=True))
+        d_down[rows, :] = scaled.astype(BF16)
+
+    clear_rows(d_bias)
+    over_rows(x_buf.shape[0], scale)
+    d_down_t[...] = d_down[...].T
+    pick(x_refs, x_buf)
     wait_all(copies)
-    mixture = mix_t[...].T
-    mix[...] = mixture
-    attention = dot_nt(mixture, w_buf[...])
-    att[...] = attention
-    mid = pick(x_refs, x_buf) + gate_one * attention
-    centred = mid - jnp.mean(mid, axis=-1, keepdims=True)
-    spread = jnp.mean(centred * centred, axis=-1, keepdims=True)
-    normed = (centred * lax.rsqrt(spread + EPSILON) * mul + add).astype(BF16)
-    n_two[...] = normed
-    n_two_t[...] = normed.T
+    mix[...] = mix_t[...].T
+    att[...] = dot_nt(mix[...], w_buf[...])
+
+    def norm(rows):
+        unit, _ = normed(x_buf[rows, :].astype(F32) + gate_one * att[rows, :])
+        n_two[rows, :] = (unit * mul + add).astype(BF16)
+
+    over_rows(x_buf.shape[0], norm)
+    n_two_t[...] = n_two[...].T
 
 
 def middle(me, x_parts, g_parts, mix_t, vec, vo):
@@ -523,35 +551,43 @@
     mul, bias = norm_scale(vec, GAIN_2, SCALE_2), vec_row(vec, BIAS_OUT)
     gate_one, gate_two = vec_row(vec, GATE_1), vec_row(vec, GATE_2)
     pieces, refs = refs[: len(vo.parts)], refs[len(vo.parts) :]
-    out_refs, (d_mid, d_mix_t, sums, d_att_t), (w_buf, x_buf, sems) = (
+    out_refs, (d_mid, d_mix_t, sums, d_att_t), (w_buf, x_buf, g_buf, d_att, sems) = (
         refs[:4],
         refs[4:8],
         refs[8:],
     )
     copies = load_out_weight(me, vo, pieces, w_buf, sems)
-    g = pick(g_refs, x_buf)
-    attention = att[...]
-    mid = pick(x_refs, x_buf) + gate_one * attention
-    branch = down[...] + bias
-    put(out_refs, (mid + gate_two * branch).astype(BF16))
-    centred = mid - jnp.mean(mid, axis=-1, keepdims=True)
-    inverse = lax.rsqrt(jnp.mean(centred * centred, axis=-1, keepdims=True) + EPSILON)
-    unit = centred * inverse
-    dn = d_n[...]
-    dn_unit = dn * unit
-    du = dn * mul
-    dm = g + inverse * (
-        du
-        - jnp.mean(du, axis=-1, keepdims=True)
-        - unit * jnp.mean(dn_unit * mul, axis=-1, keepdims=True)
-    )
-    d_mid[...] = dm
-    for n, term in enumerate((g * branch, dn_unit, dn, dm * attention)):
-        add_row(sums, n, jnp.sum(term, axis=0, keepdims=True))
-    d_att = (dm * gate_one).astype(BF16)
-    d_att_t[...] = d_att.T
+    pick(g_refs, g_buf)
+    pick(x_refs, x_buf)
+    clear_rows(sums)
+
+    def back(rows):
+        g = g_buf[rows, :].astype(F32)
+        attention = att[rows, :]
+        mid = x_buf[rows, :].astype(F32) + gate_one * attention
+        branch = down[rows, :] + bias
+        x_buf[rows, :] = (mid + gate_two * branch).astype(BF16)
+        add_row(sums, 0, jnp.sum(g * branch, axis=0, keepdims=True))
+        unit, inverse = normed(mid)
+        dn = d_n[rows, :]
+        dn_unit = dn * unit
+        add_row(sums, 1, jnp.sum(dn_unit, axis=0, keepdims=True))
+        add_row(sums, 2, jnp.sum(dn, axis=0, keepdims=True))
+        du = dn * mul
+        dm = g + inverse * (
+            du
+            - jnp.mean(du, axis=-1, keepdims=True)
+            - unit * jnp.mean(dn_unit * mul, axis=-1, keepdims=True)
+        )
+        d_mid[rows, :] = dm
+        add_row(sums, 3, jnp.sum(dm * attention, axis=0, keepdims=True))
+        d_att[rows, :] = (dm * gate_one).astype(BF16)
+
+    over_rows(x_buf.shape[0], back)
+    copy_out(out_refs, x_buf)
+    d_att_t[...] = d_att[...].T
     wait_all(copies)
-    d_mix_t[...] = dot_nn(d_att, w_buf[...]).astype(BF16).T
+    d_mix_t[...] = dot_nn(d_att[...], w_buf[...]).astype(BF16).T
 
 
 def turn(me, x_parts, g_parts, att, down, d_n, vec, vo):
@@ -583,6 +619,8 @@
         scratch_shapes=[
             pltpu.VMEM((width, inner), BF16),
             pltpu.VMEM((part, width), BF16),
+            pltpu.VMEM((part, width), BF16),
+            pltpu.VMEM((part, width), BF16),
             pltpu.SemaphoreType.DMA((vo.count,)),
         ],
         compiler_params=params("turn"),
@@ -670,31 +708,33 @@
     (d_mid, vec, dq, dk, dv), refs = refs[:5], refs[5:]
     mul = norm_scale(vec, GAIN_1, SCALE_1)
     held, refs = refs[: 2 * len(qk.parts)], refs[2 * len(qk.parts) :]
-    out_refs, (sums, w_buf, x_buf, sems) = refs[:4], refs[4:]
+    out_refs, (sums, w_buf, x_buf, d_n, sems) = refs[:4], refs[4:]
     copies = qkv_copies(me, qk, vo, held, w_buf, sems, w_buf.shape[1] // qk.count)
     start_all(copies)
-    x = pick(x_refs, x_buf)
-    centred = x - jnp.mean(x, axis=-1, keepdims=True)
-    inverse = lax.rsqrt(jnp.mean(centred * centred, axis=-1, keepdims=True) + EPSILON)
-    unit = centred * inverse
+    pick(x_refs, x_buf)
+    clear_rows(sums)
     wait_all(copies)
-    dn = dot_nt(dq[...], w_buf[0]) + dot_nt(dk[...], w_buf[1]) + dot_nt(dv[...], w_buf[2])
-    dn_unit = dn * unit
-    du = dn * mul
-    put(
-        out_refs,
-        (
-            d_mid[...]
+    d_n[...] = dot_nt(dq[...], w_buf[0]) + dot_nt(dk[...], w_buf[1]) + dot_nt(dv[...], w_buf[2])
+
+    def back(rows):
+        unit, inverse = normed(x_buf[rows, :].astype(F32))
+        dn = d_n[rows, :]
+        dn_unit = dn * unit
+        du = dn * mul
+        x_buf[rows, :] = (
+            d_mid[rows, :]
             + inverse
             * (
                 du
                 - jnp.mean(du, axis=-1, keepdims=True)
                 - unit * jnp.mean(dn_unit * mul, axis=-1, keepdims=True)
             )
-        ).astype(BF16),
-    )
-    for n, term in enumerate((dn_unit, dn)):
-        add_row(sums, n, jnp.sum(term, axis=0, keepdims=True))
+        ).astype(BF16)
+        add_row(sums, 0, jnp.sum(dn_unit, axis=0, keepdims=True))
+        add_row(sums, 1, jnp.sum(dn, axis=0, keepdims=True))
+
+    over_rows(x_buf.shape[0], back)
+    copy_out(out_refs, x_buf)
 
 
 def first(me, x_parts, d_mid, vec, dq, dk, dv, qk, vo):
@@ -714,6 +754,7 @@
         scratch_shapes=[
             pltpu.VMEM((3, width, cols), BF16),
             pltpu.VMEM((part, width), BF16),
+            pltpu.VMEM((part, width), F32),
             pltpu.SemaphoreType.DMA((3, qk.count)),
         ],
         compiler_params=params("first"),

time: 379 us -> 378 us (level)
  transfers between devices with their start and end apart: 54 -> 54, of which waited for: 17 -> 17; matrix products, arithmetic and copies ran while one was open for 9% -> 9% of each run, Pallas kernels for 38% -> 37%
where the time goes in v5:
time: 378 us; the launch traced here: 372 us
  Pallas kernels  162 us (43%)
  starting transfers between devices  93.7 us (25%)
  waiting for transfers between devices  61.2 us (16%)
  other arithmetic  30.8 us (8%)
  local copies, waits for them, and re-layouts  20.8 us (6%)
    pallas_call x2, Pallas kernels, feed(): pl.pallas_call(partial(feed_kernel, up, dn, steps, first), grid=(steps,),...  48.6 us
    ppermute x12, starting transfers between devices, ship(): return lax.ppermute(v, BOTH, pairs)  40.1 us
    ppermute x12, waiting for transfers between devices, z(): return lax.ppermute(v, 'tensor', [(i, i ^ k) for i in range(self.tensor)])  34 us
    pallas_call x1, Pallas kernels, attend_back(): pl.pallas_call(attend_back_kernel, grid=(count,), in_specs=[flat] * 2 + [...  32.6 us
    ppermute x12, starting transfers between devices, z(): return lax.ppermute(v, 'tensor', [(i, i ^ k) for i in range(self.tensor)])  26.6 us
    ppermute x27, starting transfers between devices, bit(): return lax.ppermute(v, 'dp', [(i, i ^ 1 << b) for i in range(self.dp)])  23.5 us
    pallas_call x1, Pallas kernels, attend(): pl.pallas_call(attend_kernel, grid=(pairs,), in_specs=[turned, flat, turn...  20.2 us
    ppermute x12, waiting for transfers between devices, ship(): return lax.ppermute(v, BOTH, pairs)  19.3 us
  transfers between devices with their start and end apart: 54, of which 17 were waited for; matrix products, arithmetic and copies ran while one was open for 9% of the time, Pallas kernels for 37%

profile of v5, /device:TPU:0, one launch (start us, length us, event | category | flops | bytes accessed | tf_op | source)
XLA Modules:
  0.0 371.9 jit_solution(321511971587658575)
XLA Ops:
  3.3 4.1 %collective-permute-start = (bf16[400,192]{1,0:T(8,128)(2,1)S(1)}, bf16[400,192]{1,0:T(8,128)(2,1)S(1)}, u32[]{:S(2)}, u32[]{:S(2)}) collective-permute-start(bf16[400,192]{1,0:T(8,128)(2,1)S(1)} %pad_maximum_fusion.16), channel_id=1, source_target_pairs={{0,2},{1,3},{2,0},{3,1},{4,6},{5,7},{6,4},{7,5},{8,10},{9,11},{10,... | collective-permute-start | bytes 460808 | tf_op jit(solution)/shard_map/ppermute | solution.py:989
  10.1 6.8 %collective-permute-done = bf16[400,192]{1,0:T(8,128)(2,1)S(1)} collective-permute-done((bf16[400,192]{1,0:T(8,128)(2,1)S(1)}, bf16[400,192]{1,0:T(8,128)(2,1)S(1)}, u32[]{:S(2)}, u32[]{:S(2)}) %collective-permute-start) | collective-permute-done | bytes 153632 | tf_op jit(solution)/shard_map/ppermute | solution.py:989
  18.9 1.7 dynamic-slice_bitcast_fusion
  20.6 5.0 %collective-permute-done.1 = bf16[400,384]{1,0:T(8,128)(2,1)S(1)} collective-permute-done((bf16[400,384]{1,0:T(8,128)(2,1)S(1)}, bf16[400,384]{1,0:T(8,128)(2,1)S(1)}, u32[]{:S(2)}, u32[]{:S(2)}) %collective-permute-start.1) | collective-permute-done | bytes 307232 | tf_op jit(solution)/shard_map/ppermute | solution.py:989
  27.6 1.6 collective-permute-start.3
  29.2 3.3 collective-permute-start.2
  32.6 12.3 %collective-permute-done.2 = bf16[192,768]{1,0:T(8,128)(2,1)S(1)} collective-permute-done((bf16[192,768]{1,0:T(8,128)(2,1)S(1)}, bf16[192,768]{1,0:T(8,128)(2,1)S(1)}, u32[]{:S(2)}, u32[]{:S(2)}) %collective-permute-start.2) | collective-permute-done | bytes 294944 | tf_op jit(solution)/shard_map/ppermute | solution.py:989
  47.1 5.3 %collective-permute-start.8 = (bf16[256,768]{1,0:T(8,128)(2,1)}, bf16[256,768]{1,0:T(8,128)(2,1)S(1)}, u32[]{:S(2)}, u32[]{:S(2)}) collective-permute-start(bf16[256,768]{1,0:T(8,128)(2,1)} %get-tuple-element.176), channel_id=1, source_target_pairs={{0,2},{2,0},{3,1},{4,6},{5,7},{7,5},{8,10},{10,8},{11,9},{12,14},{... | collective-permute-start | bytes 1179656 | tf_op jit(solution)/shard_map/ppermute | solution.py:1015
  55.5 2.5 rotary.1
  58.1 9.7 %collective-permute-done.8.refs_2_ = bf16[256,768]{1,0:T(8,128)(2,1)S(1)} collective-permute-done((bf16[256,768]{1,0:T(8,128)(2,1)}, bf16[256,768]{1,0:T(8,128)(2,1)S(1)}, u32[]{:S(2)}, u32[]{:S(2)}) %collective-permute-start.8) | collective-permute-done | bytes 393248 | tf_op jit(solution)/shard_map/ppermute | solution.py:1015
  68.8 2.1 constant_dynamic-update-slice_fusion.4
  74.1 1.6 collective-permute-start.12
  75.8 1.6 collective-permute-start.11
  78.7 6.6 %collective-permute-start.9 = (bf16[256,768]{1,0:T(8,128)(2,1)S(1)}, bf16[256,768]{1,0:T(8,128)(2,1)S(1)}, u32[]{:S(2)}, u32[]{:S(2)}) collective-permute-start(bf16[256,768]{1,0:T(8,128)(2,1)S(1)} %copy-done.48), channel_id=1, source_target_pairs={{0,1},{1,0},{3,2},{4,5},{6,7},{7,6},{8,9},{9,8},{11,10},{12,13},{1... | collective-permute-start | bytes 1179656 | tf_op jit(solution)/shard_map/ppermute | solution.py:1015
  86.8 3.8 %modulate.1 = (f32[16,768]{1,0:T(8,128)}, f32[4,768]{1,0:T(4,128)}, bf16[768,768]{1,0:T(8,128)(2,1)}) custom-call(s32[1]{0:T(128)} %bitcast.me, f32[1,128]{1,0:T(1,128)} %get-tuple-element.364.act, bf16[8,256,768]{2,1,0:T(8,128)(2,1)} %constant_dynamic-update-slice_fusion.2.refs_0_.refs_2_.refs_8_.refs_10_.refs_12_.refs_9_.refs_11_, ...), custom_call_target="tpu_custom_call" | custom-call | flops 20000000 | bytes 4000000 | tf_op jit(solution)/shard_map/modulate/pallas_call | solution.py:820
  90.6 4.1 %collective-permute-done.9.refs_1_ = bf16[256,768]{1,0:T(8,128)(2,1)S(1)} collective-permute-done((bf16[256,768]{1,0:T(8,128)(2,1)S(1)}, bf16[256,768]{1,0:T(8,128)(2,1)S(1)}, u32[]{:S(2)}, u32[]{:S(2)}) %collective-permute-start.9) | collective-permute-done | bytes 393248 | tf_op jit(solution)/shard_map/ppermute | solution.py:1015
  94.7 2.3 pad_maximum_fusion.3.refs_9_.refs_11_
  97.6 2.2 pad_maximum_fusion.2.refs_5_.refs_7_
  100.3 5.4 %collective-permute-start.16 = (bf16[256,768]{1,0:T(8,128)(2,1)S(1)}, bf16[256,768]{1,0:T(8,128)(2,1)S(1)}, u32[]{:S(2)}, u32[]{:S(2)}) collective-permute-start(bf16[256,768]{1,0:T(8,128)(2,1)S(1)} %copy-done.44), channel_id=1, source_target_pairs={{0,1},{1,0},{3,2},{4,5},{6,7},{7,6},{8,9},{9,8},{11,10},{12,13},{1... | collective-permute-start | bytes 1179656 | tf_op jit(solution)/shard_map/ppermute | solution.py:1015
  105.7 1.9 collective-permute-start.17
  107.6 1.5 collective-permute-start.18
  109.1 12.9 %qkv.1 = (bf16[768,1024]{1,0:T(8,128)(2,1)}, bf16[1024,768]{1,0:T(8,128)(2,1)}, bf16[1024,768]{1,0:T(8,128)(2,1)}, bf16[768,1024]{1,0:T(8,128)(2,1)}, bf16[768,1...) custom-call(s32[1]{0:T(128)} %bitcast.me, bf16[256,768]{1,0:T(8,128)(2,1)} %get-tuple-element.197.refs_0_, ...), custom_call_target="tpu_custom_call" | custom-call | flops 3623878656 | bytes 16000000 | tf_op jit(solution)/shard_map/qkv/pallas_call | solution.py:222
  122.0 20.2 %attend.1 = (bf16[768,1024]{1,0:T(8,128)(2,1)}, f32[6,2,1,1024]{3,2,1,0:T(1,128)}) custom-call(bf16[768,1024]{1,0:T(8,128)(2,1)} %get-tuple-element.207.q_t, bf16[1024,768]{1,0:T(8,128)(2,1)} %get-tuple-element.205.k, bf16[768,1024]{1,0:T(8,128)(2,1)} %get-tuple-element.209.v_t, s32[1,1024]{1,0:T(1,128)} %bitcast.175, s32[1024,1]{1,0:T(8,128)} %copy.39.doc_col), custom_call_target="tpu_custom_call" | custom-call | flops 12884901888 | bytes 8000000 | tf_op jit(solution)/shard_map/attend/pallas_call | solution.py:308
  142.3 1.4 collective-permute-start.19
  144.4 9.7 %middle.1 = (f32[1024,768]{1,0:T(8,128)}, bf16[1024,768]{1,0:T(8,128)(2,1)}, bf16[768,1024]{1,0:T(8,128)(2,1)}, bf16[1024,768]{1,0:T(8,128)(2,1)}, bf16[768,1024...) custom-call(s32[1]{0:T(128)} %bitcast.me, bf16[256,768]{1,0:T(8,128)(2,1)} %get-tuple-element.197.refs_0_, ...), custom_call_target="tpu_custom_call" | custom-call | flops 1207959552 | bytes 16000000 | tf_op jit(solution)/shard_map/middle/pallas_call | solution.py:375
  154.1 23.4 %feed.2 = (f32[1024,768]{1,0:T(8,128)}, f32[1024,768]{1,0:T(8,128)}, f32[3,1,512]{2,1,0:T(1,128)S(1)}, bf16[2,4,96,1536]{3,2,1,0:T(8,128)(2,1)}, bf16[2,4,96,1536]{3,2,1,0:T(8,128)(2,1)}) custom-call(s32[1]{0:T(128)} %bitcast.me, bf16[1024,768]{1,0:T(8,128)(2,1)} %get-tuple-element.225.refs_0_, bf16[768,1024]{1,0:T(8,128)(2,1)} %get-tuple-element.226.refs_1_, ...), custom_call_target="tpu_custom_call" | custom-call | flops 14495514624 | bytes 20000000 | tf_op jit(solution)/shard_map/feed/pallas_call | solution.py:517
  178.0 25.2 %feed.3 = (f32[1024,768]{1,0:T(8,128)}, f32[1024,768]{1,0:T(8,128)}, f32[3,1,512]{2,1,0:T(1,128)S(1)}, bf16[2,4,96,1536]{3,2,1,0:T(8,128)(2,1)}, bf16[2,4,96,1536]{3,2,1,0:T(8,128)(2,1)}) custom-call(s32[1]{0:T(128)} %bitcast.me, bf16[1024,768]{1,0:T(8,128)(2,1)} %get-tuple-element.225.refs_0_, bf16[768,1024]{1,0:T(8,128)(2,1)} %get-tuple-element.226.refs_1_, ...), custom_call_target="tpu_custom_call" | custom-call | flops 14495514624 | bytes 20000000 | tf_op jit(solution)/shard_map/feed/pallas_call | solution.py:517
  203.8 1.4 collective-permute-start.24
  205.2 1.5 collective-permute-start.25
  206.8 10.3 %turn.1 = (bf16[256,768]{1,0:T(8,128)(2,1)S(1)}, bf16[256,768]{1,0:T(8,128)(2,1)S(1)}, bf16[256,768]{1,0:T(8,128)(2,1)S(1)}, bf16[256,768]{1,0:T(8,128)(2,1)S(1)...) custom-call(s32[1]{0:T(128)} %bitcast.me, ...), custom_call_target="tpu_custom_call" | custom-call | flops 1207959552 | bytes 24000000 | tf_op jit(solution)/shard_map/turn/pallas_call | solution.py:597
  217.2 2.3 collective-permute-done.24
  222.3 1.6 collective-permute-start.30
  223.9 4.8 %collective-permute-start.27 = (bf16[256,768]{1,0:T(8,128)(2,1)S(1)}, bf16[256,768]{1,0:T(8,128)(2,1)S(1)}, u32[]{:S(2)}, u32[]{:S(2)}) collective-permute-start(bf16[256,768]{1,0:T(8,128)(2,1)S(1)} %get-tuple-element.254), channel_id=1, source_target_pairs={{0,1},{1,0},{2,3},{5,4},{6,7},{7,6},{8,9},{9,8},{10,11},{13,12},{1... | collective-permute-start | bytes 1179656 | tf_op jit(solution)/shard_map/ppermute | solution.py:1015
  228.7 2.9 collective-permute-start.28
  231.5 2.0 collective-permute-start.29
  233.6 32.6 %attend_back.1 = (bf16[1024,768]{1,0:T(8,128)(2,1)S(1)}, bf16[1024,768]{1,0:T(8,128)(2,1)S(1)}, bf16[1024,768]{1,0:T(8,128)(2,1)S(1)}) custom-call(bf16[1024,768]{1,0:T(8,128)(2,1)} %get-tuple-element.205.k, bf16[1024,768]{1,0:T(8,128)(2,1)} %get-tuple-element.206.v, bf16[768,1024]{1,0:T(8,128)(2,1)} %get-tuple-element.207.q_t, ...), custom_call_target="tpu_custom_call" | custom-call | flops 22548578304 | bytes 14000000 | tf_op jit(solution)/shard_map/attend_back/pallas_call | solution.py:686
  267.5 1.7 convert_add_fusion.4
  269.6 1.4 fusion.8
  271.6 1.5 collective-permute-start.34
  273.1 2.4 collective-permute-start.32
  275.6 7.5 %weight_grads.1 = (bf16[2,4,4,96,384]{4,3,2,1,0:T(8,128)(2,1)}, bf16[2,4,4,96,384]{4,3,2,1,0:T(8,128)(2,1)}) custom-call(s32[1]{0:T(128)} %bitcast.me, bf16[768,1024]{1,0:T(8,128)(2,1)S(1)} %copy-done.24, bf16[768,1024]{1,0:T(8,128)(2,1)S(1)} %copy-done.25, bf16[1024,768]{1,0:T(8,128)(2,1)S(1)} %get-tuple-element.270.dq.refs_6_, ...), custom_call_target="tpu_custom_call" | custom-call | flops 4831838208 | bytes 14000000 | tf_op jit(solution)/shard_map/weight_grads/pallas_call | solution.py:955
  284.2 11.6 %first.1 = (bf16[256,768]{1,0:T(8,128)(2,1)}, bf16[256,768]{1,0:T(8,128)(2,1)}, bf16[256,768]{1,0:T(8,128)(2,1)}, bf16[256,768]{1,0:T(8,128)(2,1)}, f32[2,768]{1,0:T(2,128)}) custom-call(s32[1]{0:T(128)} %bitcast.me, bf16[256,768]{1,0:T(8,128)(2,1)} %get-tuple-element.197.refs_0_, bf16[256,768]{1,0:T(8,128)(2,1)} %copy-done.5, bf16[256,768]{1,0:T(8,128)(2,1)} %copy-done.1, ...), custom_call_target="tpu_custom_call" | custom-call | flops 3623878656 | bytes 20000000 | tf_op jit(solution)/shard_map/first/pallas_call | solution.py:744
  295.8 1.5 fusion.5
  297.9 1.5 collective-permute-start.38
  299.4 1.7 fusion.12
  301.1 3.7 %collective-permute-start.40 = (bf16[256,768]{1,0:T(8,128)(2,1)}, bf16[256,768]{1,0:T(8,128)(2,1)}, u32[]{:S(2)}, u32[]{:S(2)}) collective-permute-start(bf16[256,768]{1,0:T(8,128)(2,1)} %get-tuple-element.299), channel_id=1, source_target_pairs={{0,1},{1,0},{2,3},{5,4},{6,7},{7,6},{8,9},{9,8},{10,11},{13,12},{1... | collective-permute-start | bytes 1179656 | tf_op jit(solution)/shard_map/ppermute | solution.py:1015
  304.9 2.3 collective-permute-start.41
  307.2 2.5 collective-permute-start.42
  310.8 2.3 collective-permute-done.37
  313.3 2.1 fusion.9
  315.4 1.5 collective-permute-start.43
  316.9 1.5 collective-permute-start.44
  319.7 2.2 gather_up.1
  322.0 4.2 %collective-permute-done.40 = bf16[256,768]{1,0:T(8,128)(2,1)} collective-permute-done((bf16[256,768]{1,0:T(8,128)(2,1)}, bf16[256,768]{1,0:T(8,128)(2,1)}, u32[]{:S(2)}, u32[]{:S(2)}) %collective-permute-start.40) | collective-permute-done | bytes 393248 | tf_op jit(solution)/shard_map/ppermute | solution.py:1015
  329.0 6.4 %collective-permute-start.48 = (bf16[4,96,384]{2,1,0:T(8,128)(2,1)S(1)}, bf16[4,96,384]{2,1,0:T(8,128)(2,1)S(1)}, u32[]{:S(2)}, u32[]{:S(2)}) collective-permute-start(bf16[4,96,384]{2,1,0:T(8,128)(2,1)S(1)} %fusion.7), channel_id=1, source_target_pairs={{0,1},{1,0},{2,3},{3,2},{4,5},{5,4},{6,7},{7,6},{8,9},{9,8},{10,11... | collective-permute-start | bytes 884744 | tf_op jit(solution)/shard_map/ppermute | solution.py:989
  336.3 1.5 collective-permute-start.45
  338.3 1.5 collective-permute-start.47
  341.5 1.4 collective-permute-done.47
  342.9 5.2 %collective-permute-done.48 = bf16[4,96,384]{2,1,0:T(8,128)(2,1)S(1)} collective-permute-done((bf16[4,96,384]{2,1,0:T(8,128)(2,1)S(1)}, bf16[4,96,384]{2,1,0:T(8,128)(2,1)S(1)}, u32[]{:S(2)}, u32[]{:S(2)}) %collective-permute-start.48) | collective-permute-done | bytes 294944 | tf_op jit(solution)/shard_map/ppermute | solution.py:989
  348.2 3.4 collective-permute-start.50
  351.6 2.8 collective-permute-start.51
  356.8 1.6 collective-permute-start.53
  358.4 1.4 pad_maximum_fusion.1
  361.1 4.0 %collective-permute-done.51 = f32[9,1408]{1,0:T(8,128)S(1)} collective-permute-done((f32[9,1408]{1,0:T(8,128)S(1)}, f32[9,1408]{1,0:T(8,128)S(1)}, u32[]{:S(2)}, u32[]{:S(2)}) %collective-permute-start.51) | collective-permute-done | bytes 50720 | tf_op jit(solution)/shard_map/ppermute | solution.py:989
  (263 shorter events, 49.8 us)
Async XLA Ops:
  0.6 16.3 %copy-start.37 = (bf16[3,96,192]{2,1,0:T(8,128)(2,1)S(1)}, bf16[3,96,192]{2,1,0:T(8,128)(2,1)}, u32[]{:S(2)}) copy-start(bf16[3,96,192]{2,1,0:T(8,128)(2,1)} %param.20) | copy-start | bytes 331780
  0.7 18.2 %copy-start.36 = (bf16[3,256,768]{2,1,0:T(8,128)(2,1)S(1)}, bf16[3,256,768]{2,1,0:T(8,128)(2,1)}, u32[]{:S(2)}) copy-start(bf16[3,256,768]{2,1,0:T(8,128)(2,1)} %param.16) | copy-start | bytes 3538948
  0.7 18.2 %copy-start.35 = (bf16[3,256,768]{2,1,0:T(8,128)(2,1)S(1)}, bf16[3,256,768]{2,1,0:T(8,128)(2,1)}, u32[]{:S(2)}) copy-start(bf16[3,256,768]{2,1,0:T(8,128)(2,1)} %param.30) | copy-start | bytes 3538948
  3.3 13.6 %collective-permute-start = (bf16[400,192]{1,0:T(8,128)(2,1)S(1)}, bf16[400,192]{1,0:T(8,128)(2,1)S(1)}, u32[]{:S(2)}, u32[]{:S(2)}) collective-permute-start(bf16[400,192]{1,0:T(8,128)(2,1)S(1)} %pad_maximum_fusion.16), channel_id=1, source_target_pairs={{0,2},{1,3},{2,0},{3,1},{4,6},{5,7},{6,4},{7,5},{8,10},{9,11},{10,... | collective-permute-start | bytes 460808 | tf_op jit(solution)/shard_map/ppermute | solution.py:989
  17.1 8.5 %collective-permute-start.1 = (bf16[400,384]{1,0:T(8,128)(2,1)S(1)}, bf16[400,384]{1,0:T(8,128)(2,1)S(1)}, u32[]{:S(2)}, u32[]{:S(2)}) collective-permute-start(bf16[400,384]{1,0:T(8,128)(2,1)S(1)} %pad_maximum_fusion.14), channel_id=1, source_target_pairs={{0,1},{1,0},{2,3},{3,2},{4,5},{5,4},{6,7},{7,6},{8,9},{9,8},{10,11... | collective-permute-start | bytes 921608 | tf_op jit(solution)/shard_map/ppermute | solution.py:989
  26.1 18.8 %collective-permute-start.4 = (bf16[256,768]{1,0:T(8,128)(2,1)S(1)}, bf16[256,768]{1,0:T(8,128)(2,1)S(1)}, u32[]{:S(2)}, u32[]{:S(2)}) collective-permute-start(bf16[256,768]{1,0:T(8,128)(2,1)S(1)} %concatenate.52), channel_id=1, source_target_pairs={{0,16},{4,20},{8,24},{12,28},{16,0},{20,4},{24,8},{28,12},{1,17},{... | collective-permute-start | bytes 1179656 | tf_op jit(solution)/shard_map/ppermute | solution.py:983
  27.6 17.3 %collective-permute-start.3 = (bf16[256,768]{1,0:T(8,128)(2,1)S(1)}, bf16[256,768]{1,0:T(8,128)(2,1)S(1)}, u32[]{:S(2)}, u32[]{:S(2)}) collective-permute-start(bf16[256,768]{1,0:T(8,128)(2,1)S(1)} %get-tuple-element.407), channel_id=1, source_target_pairs={{0,8},{4,12},{8,0},{12,4},{16,24},{20,28},{24,16},{28,20},{1,9},{5... | collective-permute-start | bytes 1179656 | tf_op jit(solution)/shard_map/ppermute | solution.py:983
  29.2 15.7 %collective-permute-start.2 = (bf16[192,768]{1,0:T(8,128)(2,1)S(1)}, bf16[192,768]{1,0:T(8,128)(2,1)S(1)}, u32[]{:S(2)}, u32[]{:S(2)}) collective-permute-start(bf16[192,768]{1,0:T(8,128)(2,1)S(1)} %pad_maximum_fusion.15), channel_id=1, source_target_pairs={{0,2},{1,3},{2,0},{3,1},{4,6},{5,7},{6,4},{7,5},{8,10},{9,11},{10,... | collective-permute-start | bytes 884744 | tf_op jit(solution)/shard_map/ppermute | solution.py:989
  45.0 22.8 %collective-permute-start.7 = (bf16[2,256,768]{2,1,0:T(8,128)(2,1)S(1)}, bf16[2,256,768]{2,1,0:T(8,128)(2,1)S(1)}, u32[]{:S(2)}, u32[]{:S(2)}) collective-permute-start(bf16[2,256,768]{2,1,0:T(8,128)(2,1)S(1)} %pad_maximum_fusion.9), channel_id=1, source_target_pairs={{0,8},{4,12},{8,0},{12,4},{16,24},{20,28},{24,16},{28,20},{1,9},{5... | collective-permute-start | bytes 2359304 | tf_op jit(solution)/shard_map/ppermute | solution.py:983
  45.7 22.1 %collective-permute-start.6 = (bf16[2,256,768]{2,1,0:T(8,128)(2,1)S(1)}, bf16[2,256,768]{2,1,0:T(8,128)(2,1)}, u32[]{:S(2)}, u32[]{:S(2)}) collective-permute-start(bf16[2,256,768]{2,1,0:T(8,128)(2,1)S(1)} %pad_maximum_fusion.8), channel_id=1, source_target_pairs={{0,16},{4,20},{8,24},{12,28},{16,0},{20,4},{24,8},{28,12},{1,17},{... | collective-permute-start | bytes 2359304 | tf_op jit(solution)/shard_map/ppermute | solution.py:983
  46.3 21.5 %collective-permute-start.5 = (bf16[192,1536]{1,0:T(8,128)(2,1)S(1)}, bf16[192,1536]{1,0:T(8,128)(2,1)}, u32[]{:S(2)}, u32[]{:S(2)}) collective-permute-start(bf16[192,1536]{1,0:T(8,128)(2,1)S(1)} %constant_dynamic-update-slice_fusion), channel_id=1, source_target_pairs={{0,1},{1,0},{2,3},{3,2},{4,5},{5,4},{6,7},{7,6},{8,9},{9,8},{10,11... | collective-permute-start | bytes 1769480 | tf_op jit(solution)/shard_map/ppermute | solution.py:989
  47.1 20.7 %collective-permute-start.8 = (bf16[256,768]{1,0:T(8,128)(2,1)}, bf16[256,768]{1,0:T(8,128)(2,1)S(1)}, u32[]{:S(2)}, u32[]{:S(2)}) collective-permute-start(bf16[256,768]{1,0:T(8,128)(2,1)} %get-tuple-element.176), channel_id=1, source_target_pairs={{0,2},{2,0},{3,1},{4,6},{5,7},{7,5},{8,10},{10,8},{11,9},{12,14},{... | collective-permute-start | bytes 1179656 | tf_op jit(solution)/shard_map/ppermute | solution.py:1015
  54.9 30.9 %copy-start.19 = (s32[1,1,4,256]{3,1,2,0:T(1,128)}, s32[1,1,4,256]{3,1,2,0:T(1,128)S(1)}, u32[]{:S(2)}) copy-start(s32[1,1,4,256]{3,1,2,0:T(1,128)S(1)} %copy.45) | copy-start | bytes 12292
  72.8 14.0 %collective-permute-start.13 = (bf16[8,256,768]{2,1,0:T(8,128)(2,1)}, bf16[8,256,768]{2,1,0:T(8,128)(2,1)}, u32[]{:S(2)}, u32[]{:S(2)}) collective-permute-start(bf16[8,256,768]{2,1,0:T(8,128)(2,1)} %constant_dynamic-update-slice_fusion.2.refs_0_.refs_2_.refs_8_.refs_10_.refs_12_.refs_9_.refs_11_), channel_id=1, source_target_pairs={{0,4},{4,0},{8,12},{12,8},{16,20},{20,16},{24,28},{28,24},{1,5},{5... | collective-permute-start | bytes 9437192 | tf_op jit(solution)/shard_map/ppermute | solution.py:983
  74.1 20.6 %collective-permute-start.12 = (bf16[96,3072]{1,0:T(8,128)(2,1)S(1)}, bf16[96,3072]{1,0:T(8,128)(2,1)}, u32[]{:S(2)}, u32[]{:S(2)}) collective-permute-start(bf16[96,3072]{1,0:T(8,128)(2,1)S(1)} %get-tuple-element.399), channel_id=1, source_target_pairs={{0,16},{4,20},{8,24},{12,28},{16,0},{20,4},{24,8},{28,12},{1,17},{... | collective-permute-start | bytes 1769480 | tf_op jit(solution)/shard_map/ppermute | solution.py:983
  75.8 18.9 %collective-permute-start.11 = (bf16[96,3072]{1,0:T(8,128)(2,1)S(1)}, bf16[96,3072]{1,0:T(8,128)(2,1)}, u32[]{:S(2)}, u32[]{:S(2)}) collective-permute-start(bf16[96,3072]{1,0:T(8,128)(2,1)S(1)} %get-tuple-element.401), channel_id=1, source_target_pairs={{0,8},{4,12},{8,0},{12,4},{16,24},{20,28},{24,16},{28,20},{1,9},{5... | collective-permute-start | bytes 1769480 | tf_op jit(solution)/shard_map/ppermute | solution.py:983
  77.4 13.2 %collective-permute-start.10 = (bf16[256,768]{1,0:T(8,128)(2,1)}, bf16[256,768]{1,0:T(8,128)(2,1)S(1)}, u32[]{:S(2)}, u32[]{:S(2)}) collective-permute-start(bf16[256,768]{1,0:T(8,128)(2,1)} %get-tuple-element.186), channel_id=1, source_target_pairs={{1,2},{2,1},{3,0},{4,7},{5,6},{6,5},{9,10},{10,9},{11,8},{12,15},{... | collective-permute-start | bytes 1179656 | tf_op jit(solution)/shard_map/ppermute | solution.py:1015
  78.7 16.0 %collective-permute-start.9 = (bf16[256,768]{1,0:T(8,128)(2,1)S(1)}, bf16[256,768]{1,0:T(8,128)(2,1)S(1)}, u32[]{:S(2)}, u32[]{:S(2)}) collective-permute-start(bf16[256,768]{1,0:T(8,128)(2,1)S(1)} %copy-done.48), channel_id=1, source_target_pairs={{0,1},{1,0},{3,2},{4,5},{6,7},{7,6},{8,9},{9,8},{11,10},{12,13},{1... | collective-permute-start | bytes 1179656 | tf_op jit(solution)/shard_map/ppermute | solution.py:1015
  97.1 45.2 %collective-permute-start.15 = (bf16[2,96,3072]{2,1,0:T(8,128)(2,1)}, bf16[2,96,3072]{2,1,0:T(8,128)(2,1)}, u32[]{:S(2)}, u32[]{:S(2)}) collective-permute-start(bf16[2,96,3072]{2,1,0:T(8,128)(2,1)} %pad_maximum_fusion.3.refs_9_.refs_11_), channel_id=1, source_target_pairs={{0,8},{4,12},{8,0},{12,4},{16,24},{20,28},{24,16},{28,20},{1,9},{5... | collective-permute-start | bytes 3538952 | tf_op jit(solution)/shard_map/ppermute | solution.py:983
  99.8 42.5 %collective-permute-start.14 = (bf16[2,96,3072]{2,1,0:T(8,128)(2,1)}, bf16[2,96,3072]{2,1,0:T(8,128)(2,1)}, u32[]{:S(2)}, u32[]{:S(2)}) collective-permute-start(bf16[2,96,3072]{2,1,0:T(8,128)(2,1)} %pad_maximum_fusion.2.refs_5_.refs_7_), channel_id=1, source_target_pairs={{0,16},{4,20},{8,24},{12,28},{16,0},{20,4},{24,8},{28,12},{1,17},{... | collective-permute-start | bytes 3538952 | tf_op jit(solution)/shard_map/ppermute | solution.py:983
  100.3 41.9 %collective-permute-start.16 = (bf16[256,768]{1,0:T(8,128)(2,1)S(1)}, bf16[256,768]{1,0:T(8,128)(2,1)S(1)}, u32[]{:S(2)}, u32[]{:S(2)}) collective-permute-start(bf16[256,768]{1,0:T(8,128)(2,1)S(1)} %copy-done.44), channel_id=1, source_target_pairs={{0,1},{1,0},{3,2},{4,5},{6,7},{7,6},{8,9},{9,8},{11,10},{12,13},{1... | collective-permute-start | bytes 1179656 | tf_op jit(solution)/shard_map/ppermute | solution.py:1015
  105.7 36.5 %collective-permute-start.17 = (bf16[256,768]{1,0:T(8,128)(2,1)S(1)}, bf16[256,768]{1,0:T(8,128)(2,1)S(1)}, u32[]{:S(2)}, u32[]{:S(2)}) collective-permute-start(bf16[256,768]{1,0:T(8,128)(2,1)S(1)} %copy-done.43), channel_id=1, source_target_pairs={{0,2},{2,0},{3,1},{4,6},{5,7},{7,5},{8,10},{10,8},{11,9},{12,14},{... | collective-permute-start | bytes 1179656 | tf_op jit(solution)/shard_map/ppermute | solution.py:1015
  107.6 34.6 %collective-permute-start.18 = (bf16[256,768]{1,0:T(8,128)(2,1)S(1)}, bf16[256,768]{1,0:T(8,128)(2,1)S(1)}, u32[]{:S(2)}, u32[]{:S(2)}) collective-permute-start(bf16[256,768]{1,0:T(8,128)(2,1)S(1)} %copy-done.42), channel_id=1, source_target_pairs={{1,2},{2,1},{3,0},{4,7},{5,6},{6,5},{9,10},{10,9},{11,8},{12,15},{... | collective-permute-start | bytes 1179656 | tf_op jit(solution)/shard_map/ppermute | solution.py:1015
  122.0 22.3 %copy-start.50 = (f32[4,768]{1,0:T(4,128)S(1)}, f32[4,768]{1,0:T(4,128)}, u32[]{:S(2)}) copy-start(f32[4,768]{1,0:T(4,128)} %get-tuple-element.229) | copy-start | bytes 36868
  142.3 11.7 %collective-permute-start.19 = (bf16[2,96,3072]{2,1,0:T(8,128)(2,1)}, bf16[2,96,3072]{2,1,0:T(8,128)(2,1)S(1)}, u32[]{:S(2)}, u32[]{:S(2)}) collective-permute-start(bf16[2,96,3072]{2,1,0:T(8,128)(2,1)} %pad_maximum_fusion.2.refs_5_.refs_7_), channel_id=1, source_target_pairs={{0,4},{4,0},{8,12},{12,8},{16,20},{20,16},{24,28},{28,24},{1,5},{5... | collective-permute-start | bytes 3538952 | tf_op jit(solution)/shard_map/ppermute | solution.py:983
  143.7 10.3 %collective-permute-start.20 = (bf16[2,96,3072]{2,1,0:T(8,128)(2,1)}, bf16[2,96,3072]{2,1,0:T(8,128)(2,1)}, u32[]{:S(2)}, u32[]{:S(2)}) collective-permute-start(bf16[2,96,3072]{2,1,0:T(8,128)(2,1)} %collective-permute-done.14.refs_6_.refs_8_), channel_id=1, source_target_pairs={{0,4},{4,0},{8,12},{12,8},{16,20},{20,16},{24,28},{28,24},{1,5},{5... | collective-permute-start | bytes 3538952 | tf_op jit(solution)/shard_map/ppermute | solution.py:983
  143.8 10.3 %collective-permute-start.21 = (bf16[2,96,3072]{2,1,0:T(8,128)(2,1)}, bf16[2,96,3072]{2,1,0:T(8,128)(2,1)}, u32[]{:S(2)}, u32[]{:S(2)}) collective-permute-start(bf16[2,96,3072]{2,1,0:T(8,128)(2,1)} %pad_maximum_fusion.3.refs_9_.refs_11_), channel_id=1, source_target_pairs={{0,4},{4,0},{8,12},{12,8},{16,20},{20,16},{24,28},{28,24},{1,5},{5... | collective-permute-start | bytes 3538952 | tf_op jit(solution)/shard_map/ppermute | solution.py:983
  144.2 9.8 %collective-permute-start.22 = (bf16[2,96,3072]{2,1,0:T(8,128)(2,1)}, bf16[2,96,3072]{2,1,0:T(8,128)(2,1)}, u32[]{:S(2)}, u32[]{:S(2)}) collective-permute-start(bf16[2,96,3072]{2,1,0:T(8,128)(2,1)} %collective-permute-done.15.refs_10_.refs_12_), channel_id=1, source_target_pairs={{0,4},{4,0},{8,12},{12,8},{16,20},{20,16},{24,28},{28,24},{1,5},{5... | collective-permute-start | bytes 3538952 | tf_op jit(solution)/shard_map/ppermute | solution.py:983
  177.5 25.7 %copy-start.22 = (f32[3,1,512]{2,1,0:T(1,128)}, f32[3,1,512]{2,1,0:T(1,128)S(1)}, u32[]{:S(2)}) copy-start(f32[3,1,512]{2,1,0:T(1,128)S(1)} %get-tuple-element.295.d_bias_a) | copy-start | bytes 18436
  177.5 25.9 %collective-permute-start.23 = (bf16[2,4,96,1536]{3,2,1,0:T(8,128)(2,1)}, bf16[2,4,96,1536]{3,2,1,0:T(8,128)(2,1)S(1)}, u32[]{:S(2)}, u32[]{:S(2)}) collective-permute-start(bf16[2,4,96,1536]{3,2,1,0:T(8,128)(2,1)} %get-tuple-element.237), channel_id=1, source_target_pairs={{0,4},{4,0},{8,12},{12,8},{16,20},{20,16},{24,28},{28,24},{1,5},{5... | collective-permute-start | bytes 7077896 | tf_op jit(solution)/shard_map/ppermute | solution.py:983
  178.0 25.4 %copy-start.33 = (bf16[2,4,96,1536]{3,2,1,0:T(8,128)(2,1)S(1)}, bf16[2,4,96,1536]{3,2,1,0:T(8,128)(2,1)}, u32[]{:S(2)}) copy-start(bf16[2,4,96,1536]{3,2,1,0:T(8,128)(2,1)} %get-tuple-element.245) | copy-start | bytes 7077892
  203.2 13.9 %collective-permute-start.26 = (bf16[2,4,96,1536]{3,2,1,0:T(8,128)(2,1)}, bf16[2,4,96,1536]{3,2,1,0:T(8,128)(2,1)S(1)}, u32[]{:S(2)}, u32[]{:S(2)}) collective-permute-start(bf16[2,4,96,1536]{3,2,1,0:T(8,128)(2,1)} %get-tuple-element.247), channel_id=1, source_target_pairs={{0,4},{4,0},{8,12},{12,8},{16,20},{20,16},{24,28},{28,24},{1,5},{5... | collective-permute-start | bytes 7077896 | tf_op jit(solution)/shard_map/ppermute | solution.py:983
  203.4 17.2 %copy-start.34 = (bf16[2,4,96,1536]{3,2,1,0:T(8,128)(2,1)}, bf16[2,4,96,1536]{3,2,1,0:T(8,128)(2,1)S(1)}, u32[]{:S(2)}) copy-start(bf16[2,4,96,1536]{3,2,1,0:T(8,128)(2,1)S(1)} %collective-permute-done.23) | copy-start | bytes 7077892
  203.8 15.7 %collective-permute-start.24 = (bf16[2,96,1536]{2,1,0:T(8,128)(2,1)S(1)}, bf16[2,96,1536]{2,1,0:T(8,128)(2,1)S(1)}, u32[]{:S(2)}, u32[]{:S(2)}) collective-permute-start(bf16[2,96,1536]{2,1,0:T(8,128)(2,1)S(1)} %get-tuple-element.379), channel_id=1, source_target_pairs={{0,8},{4,12},{8,0},{12,4},{16,24},{20,28},{24,16},{28,20},{1,9},{5... | collective-permute-start | bytes 1769480 | tf_op jit(solution)/shard_map/ppermute | solution.py:983
  205.2 15.4 %collective-permute-start.25 = (bf16[2,96,1536]{2,1,0:T(8,128)(2,1)S(1)}, bf16[2,96,1536]{2,1,0:T(8,128)(2,1)S(1)}, u32[]{:S(2)}, u32[]{:S(2)}) collective-permute-start(bf16[2,96,1536]{2,1,0:T(8,128)(2,1)S(1)} %get-tuple-element.378), channel_id=1, source_target_pairs={{0,16},{4,20},{8,24},{12,28},{16,0},{20,4},{24,8},{28,12},{1,17},{... | collective-permute-start | bytes 1769480 | tf_op jit(solution)/shard_map/ppermute | solution.py:983
  217.2 52.1 %copy-start.31 = (bf16[2,4,96,1536]{3,2,1,0:T(8,128)(2,1)}, bf16[2,4,96,1536]{3,2,1,0:T(8,128)(2,1)S(1)}, u32[]{:S(2)}) copy-start(bf16[2,4,96,1536]{3,2,1,0:T(8,128)(2,1)S(1)} %collective-permute-done.26) | copy-start | bytes 7077892
  221.5 45.9 %collective-permute-start.31 = (bf16[3,96,1536]{2,1,0:T(8,128)(2,1)S(1)}, bf16[3,96,1536]{2,1,0:T(8,128)(2,1)S(1)}, u32[]{:S(2)}, u32[]{:S(2)}) collective-permute-start(bf16[3,96,1536]{2,1,0:T(8,128)(2,1)S(1)} %pad_maximum_fusion.7), channel_id=1, source_target_pairs={{0,8},{4,12},{8,0},{12,4},{16,24},{20,28},{24,16},{28,20},{1,9},{5... | collective-permute-start | bytes 2654216 | tf_op jit(solution)/shard_map/ppermute | solution.py:983
  222.3 45.2 %collective-permute-start.30 = (bf16[3,96,1536]{2,1,0:T(8,128)(2,1)S(1)}, bf16[3,96,1536]{2,1,0:T(8,128)(2,1)S(1)}, u32[]{:S(2)}, u32[]{:S(2)}) collective-permute-start(bf16[3,96,1536]{2,1,0:T(8,128)(2,1)S(1)} %pad_maximum_fusion.6), channel_id=1, source_target_pairs={{0,16},{4,20},{8,24},{12,28},{16,0},{20,4},{24,8},{28,12},{1,17},{... | collective-permute-start | bytes 2654216 | tf_op jit(solution)/shard_map/ppermute | solution.py:983
  223.9 43.5 %collective-permute-start.27 = (bf16[256,768]{1,0:T(8,128)(2,1)S(1)}, bf16[256,768]{1,0:T(8,128)(2,1)S(1)}, u32[]{:S(2)}, u32[]{:S(2)}) collective-permute-start(bf16[256,768]{1,0:T(8,128)(2,1)S(1)} %get-tuple-element.254), channel_id=1, source_target_pairs={{0,1},{1,0},{2,3},{5,4},{6,7},{7,6},{8,9},{9,8},{10,11},{13,12},{1... | collective-permute-start | bytes 1179656 | tf_op jit(solution)/shard_map/ppermute | solution.py:1015
  228.7 38.8 %collective-permute-start.28 = (bf16[256,768]{1,0:T(8,128)(2,1)S(1)}, bf16[256,768]{1,0:T(8,128)(2,1)}, u32[]{:S(2)}, u32[]{:S(2)}) collective-permute-start(bf16[256,768]{1,0:T(8,128)(2,1)S(1)} %get-tuple-element.255), channel_id=1, source_target_pairs={{0,2},{1,3},{2,0},{5,7},{6,4},{7,5},{8,10},{9,11},{10,8},{13,15},{... | collective-permute-start | bytes 1179656 | tf_op jit(solution)/shard_map/ppermute | solution.py:1015
  231.5 35.9 %collective-permute-start.29 = (bf16[256,768]{1,0:T(8,128)(2,1)S(1)}, bf16[256,768]{1,0:T(8,128)(2,1)}, u32[]{:S(2)}, u32[]{:S(2)}) collective-permute-start(bf16[256,768]{1,0:T(8,128)(2,1)S(1)} %get-tuple-element.256), channel_id=1, source_target_pairs={{0,3},{1,2},{2,1},{5,6},{6,5},{7,4},{8,11},{9,10},{10,9},{13,14},{... | collective-permute-start | bytes 1179656 | tf_op jit(solution)/shard_map/ppermute | solution.py:1015
  233.6 33.9 %copy-start.41 = (bf16[2,96,1536]{2,1,0:T(8,128)(2,1)S(1)}, bf16[2,96,1536]{2,1,0:T(8,128)(2,1)}, u32[]{:S(2)}) copy-start(bf16[2,96,1536]{2,1,0:T(8,128)(2,1)} %copy-done.40) | copy-start | bytes 1769476
  271.0 12.0 %collective-permute-start.33 = (bf16[1,96,1536]{2,1,0:T(8,128)(2,1)S(1)}, bf16[1,96,1536]{2,1,0:T(8,128)(2,1)}, u32[]{:S(2)}, u32[]{:S(2)}) collective-permute-start(bf16[1,96,1536]{2,1,0:T(8,128)(2,1)S(1)} %get-tuple-element.373), channel_id=1, source_target_pairs={{0,16},{4,20},{8,24},{12,28},{16,0},{20,4},{24,8},{28,12},{1,17},{... | collective-permute-start | bytes 884744 | tf_op jit(solution)/shard_map/ppermute | solution.py:983
  271.6 11.5 %collective-permute-start.34 = (bf16[1,96,1536]{2,1,0:T(8,128)(2,1)S(1)}, bf16[1,96,1536]{2,1,0:T(8,128)(2,1)}, u32[]{:S(2)}, u32[]{:S(2)}) collective-permute-start(bf16[1,96,1536]{2,1,0:T(8,128)(2,1)S(1)} %get-tuple-element.372), channel_id=1, source_target_pairs={{0,8},{4,12},{8,0},{12,4},{16,24},{20,28},{24,16},{28,20},{1,9},{5... | collective-permute-start | bytes 884744 | tf_op jit(solution)/shard_map/ppermute | solution.py:983
  273.1 10.0 %collective-permute-start.32 = (bf16[96,1536]{1,0:T(8,128)(2,1)S(1)}, bf16[96,1536]{1,0:T(8,128)(2,1)}, u32[]{:S(2)}, u32[]{:S(2)}) collective-permute-start(bf16[96,1536]{1,0:T(8,128)(2,1)S(1)} %fusion.8), channel_id=1, source_target_pairs={{0,1},{1,0},{2,3},{3,2},{4,5},{5,4},{6,7},{7,6},{8,9},{9,8},{10,11... | collective-permute-start | bytes 884744 | tf_op jit(solution)/shard_map/ppermute | solution.py:989
  283.1 12.7 %collective-permute-start.36 = (bf16[2,4,4,96,384]{4,3,2,1,0:T(8,128)(2,1)}, bf16[2,4,4,96,384]{4,3,2,1,0:T(8,128)(2,1)}, u32[]{:S(2)}, u32[]{:S(2)}) collective-permute-start(bf16[2,4,4,96,384]{4,3,2,1,0:T(8,128)(2,1)} %get-tuple-element.288), channel_id=1, source_target_pairs={{0,4},{4,0},{8,12},{12,8},{16,20},{20,16},{24,28},{28,24},{1,5},{5... | collective-permute-start | bytes 7077896 | tf_op jit(solution)/shard_map/ppermute | solution.py:983
  284.1 11.7 %collective-permute-start.35 = (bf16[96,1536]{1,0:T(8,128)(2,1)S(1)}, bf16[96,1536]{1,0:T(8,128)(2,1)S(1)}, u32[]{:S(2)}, u32[]{:S(2)}) collective-permute-start(bf16[96,1536]{1,0:T(8,128)(2,1)S(1)} %convert_add_fusion.4), channel_id=1, source_target_pairs={{0,1},{1,0},{2,3},{3,2},{4,5},{5,4},{6,7},{7,6},{8,9},{9,8},{10,11... | collective-permute-start | bytes 884744 | tf_op jit(solution)/shard_map/ppermute | solution.py:989
  297.3 15.8 %collective-permute-start.37 = (bf16[2,4,96,384]{3,2,1,0:T(8,128)(2,1)S(1)}, bf16[2,4,96,384]{3,2,1,0:T(8,128)(2,1)S(1)}, u32[]{:S(2)}, u32[]{:S(2)}) collective-permute-start(bf16[2,4,96,384]{3,2,1,0:T(8,128)(2,1)S(1)} %get-tuple-element.369), channel_id=1, source_target_pairs={{0,8},{4,12},{8,0},{12,4},{16,24},{20,28},{24,16},{28,20},{1,9},{5... | collective-permute-start | bytes 1769480 | tf_op jit(solution)/shard_map/ppermute | solution.py:983
  297.9 15.4 %collective-permute-start.38 = (bf16[2,4,96,384]{3,2,1,0:T(8,128)(2,1)S(1)}, bf16[2,4,96,384]{3,2,1,0:T(8,128)(2,1)S(1)}, u32[]{:S(2)}, u32[]{:S(2)}) collective-permute-start(bf16[2,4,96,384]{3,2,1,0:T(8,128)(2,1)S(1)} %get-tuple-element.368), channel_id=1, source_target_pairs={{0,16},{4,20},{8,24},{12,28},{16,0},{20,4},{24,8},{28,12},{1,17},{... | collective-permute-start | bytes 1769480 | tf_op jit(solution)/shard_map/ppermute | solution.py:983
  301.1 25.1 %collective-permute-start.40 = (bf16[256,768]{1,0:T(8,128)(2,1)}, bf16[256,768]{1,0:T(8,128)(2,1)}, u32[]{:S(2)}, u32[]{:S(2)}) collective-permute-start(bf16[256,768]{1,0:T(8,128)(2,1)} %get-tuple-element.299), channel_id=1, source_target_pairs={{0,1},{1,0},{2,3},{5,4},{6,7},{7,6},{8,9},{9,8},{10,11},{13,12},{1... | collective-permute-start | bytes 1179656 | tf_op jit(solution)/shard_map/ppermute | solution.py:1015
  304.9 22.7 %collective-permute-start.41 = (bf16[256,768]{1,0:T(8,128)(2,1)}, bf16[256,768]{1,0:T(8,128)(2,1)}, u32[]{:S(2)}, u32[]{:S(2)}) collective-permute-start(bf16[256,768]{1,0:T(8,128)(2,1)} %get-tuple-element.300), channel_id=1, source_target_pairs={{0,2},{1,3},{2,0},{5,7},{6,4},{7,5},{8,10},{9,11},{10,8},{13,15},{... | collective-permute-start | bytes 1179656 | tf_op jit(solution)/shard_map/ppermute | solution.py:1015
  307.2 20.4 %collective-permute-start.42 = (bf16[256,768]{1,0:T(8,128)(2,1)}, bf16[256,768]{1,0:T(8,128)(2,1)}, u32[]{:S(2)}, u32[]{:S(2)}) collective-permute-start(bf16[256,768]{1,0:T(8,128)(2,1)} %get-tuple-element.301), channel_id=1, source_target_pairs={{0,3},{1,2},{2,1},{5,6},{6,5},{7,4},{8,11},{9,10},{10,9},{13,14},{... | collective-permute-start | bytes 1179656 | tf_op jit(solution)/shard_map/ppermute | solution.py:1015
  315.4 12.2 %collective-permute-start.43 = (bf16[1,4,96,384]{3,2,1,0:T(8,128)(2,1)}, bf16[1,4,96,384]{3,2,1,0:T(8,128)(2,1)}, u32[]{:S(2)}, u32[]{:S(2)}) collective-permute-start(bf16[1,4,96,384]{3,2,1,0:T(8,128)(2,1)} %get-tuple-element.367), channel_id=1, source_target_pairs={{0,16},{4,20},{8,24},{12,28},{16,0},{20,4},{24,8},{28,12},{1,17},{... | collective-permute-start | bytes 884744 | tf_op jit(solution)/shard_map/ppermute | solution.py:983
  316.9 10.7 %collective-permute-start.44 = (bf16[1,4,96,384]{3,2,1,0:T(8,128)(2,1)}, bf16[1,4,96,384]{3,2,1,0:T(8,128)(2,1)}, u32[]{:S(2)}, u32[]{:S(2)}) collective-permute-start(bf16[1,4,96,384]{3,2,1,0:T(8,128)(2,1)} %get-tuple-element.366), channel_id=1, source_target_pairs={{0,8},{4,12},{8,0},{12,4},{16,24},{20,28},{24,16},{28,20},{1,9},{5... | collective-permute-start | bytes 884744 | tf_op jit(solution)/shard_map/ppermute | solution.py:983
  326.2 1.4 collective-permute-start.39
  329.0 19.2 %collective-permute-start.48 = (bf16[4,96,384]{2,1,0:T(8,128)(2,1)S(1)}, bf16[4,96,384]{2,1,0:T(8,128)(2,1)S(1)}, u32[]{:S(2)}, u32[]{:S(2)}) collective-permute-start(bf16[4,96,384]{2,1,0:T(8,128)(2,1)S(1)} %fusion.7), channel_id=1, source_target_pairs={{0,1},{1,0},{2,3},{3,2},{4,5},{5,4},{6,7},{7,6},{8,9},{9,8},{10,11... | collective-permute-start | bytes 884744 | tf_op jit(solution)/shard_map/ppermute | solution.py:989
  335.4 12.7 %collective-permute-start.49 = (bf16[2,96,768]{2,1,0:T(8,128)(2,1)S(1)}, bf16[2,96,768]{2,1,0:T(8,128)(2,1)S(1)}, u32[]{:S(2)}, u32[]{:S(2)}) collective-permute-start(bf16[2,96,768]{2,1,0:T(8,128)(2,1)S(1)} %slice.523), channel_id=1, source_target_pairs={{0,2},{1,3},{2,0},{3,1},{4,6},{5,7},{6,4},{7,5},{8,10},{9,11},{10,... | collective-permute-start | bytes 884744 | tf_op jit(solution)/shard_map/ppermute | solution.py:989
  336.3 4.7 %collective-permute-start.45 = (f32[2,1408]{1,0:T(2,128)S(1)}, f32[2,1408]{1,0:T(2,128)S(1)}, u32[]{:S(2)}, u32[]{:S(2)}) collective-permute-start(f32[2,1408]{1,0:T(2,128)S(1)} %get-tuple-element.412), channel_id=1, source_target_pairs={{0,8},{4,12},{8,0},{12,4},{16,24},{20,28},{24,16},{28,20},{1,9},{5... | collective-permute-start | bytes 33800 | tf_op jit(solution)/shard_map/ppermute | solution.py:986
  337.8 3.7 collective-permute-start.46
  338.3 4.6 %collective-permute-start.47 = (f32[2,1408]{1,0:T(2,128)S(1)}, f32[2,1408]{1,0:T(2,128)S(1)}, u32[]{:S(2)}, u32[]{:S(2)}) collective-permute-start(f32[2,1408]{1,0:T(2,128)S(1)} %get-tuple-element.410), channel_id=1, source_target_pairs={{0,24},{4,28},{8,16},{12,20},{16,8},{20,12},{24,0},{28,4},{1,25},{... | collective-permute-start | bytes 33800 | tf_op jit(solution)/shard_map/ppermute | solution.py:986
  348.2 12.9 %collective-permute-start.50 = (f32[9,1408]{1,0:T(8,128)S(1)}, f32[9,1408]{1,0:T(8,128)S(1)}, u32[]{:S(2)}, u32[]{:S(2)}) collective-permute-start(f32[9,1408]{1,0:T(8,128)S(1)} %concatenate.60), channel_id=1, source_target_pairs={{0,1},{1,0},{2,3},{3,2},{4,5},{5,4},{6,7},{7,6},{8,9},{9,8},{10,11... | collective-permute-start | bytes 152072 | tf_op jit(solution)/shard_map/ppermute | solution.py:989
  351.6 13.5 %collective-permute-start.51 = (f32[9,1408]{1,0:T(8,128)S(1)}, f32[9,1408]{1,0:T(8,128)S(1)}, u32[]{:S(2)}, u32[]{:S(2)}) collective-permute-start(f32[9,1408]{1,0:T(8,128)S(1)} %concatenate.60), channel_id=1, source_target_pairs={{0,2},{1,3},{2,0},{3,1},{4,6},{5,7},{6,4},{7,5},{8,10},{9,11},{10,... | collective-permute-start | bytes 152072 | tf_op jit(solution)/shard_map/ppermute | solution.py:989
  354.4 10.7 %collective-permute-start.52 = (f32[9,1408]{1,0:T(8,128)S(1)}, f32[9,1408]{1,0:T(8,128)S(1)}, u32[]{:S(2)}, u32[]{:S(2)}) collective-permute-start(f32[9,1408]{1,0:T(8,128)S(1)} %concatenate.60), channel_id=1, source_target_pairs={{0,3},{1,2},{2,1},{3,0},{4,7},{5,6},{6,5},{7,4},{8,11},{9,10},{10,... | collective-permute-start | bytes 152072 | tf_op jit(solution)/shard_map/ppermute | solution.py:989
  356.8 13.4 %collective-permute-start.53 = (bf16[4,96,192]{2,1,0:T(8,128)(2,1)S(1)}, bf16[4,96,192]{2,1,0:T(8,128)(2,1)S(1)}, u32[]{:S(2)}, u32[]{:S(2)}) collective-permute-start(bf16[4,96,192]{2,1,0:T(8,128)(2,1)S(1)} %slice.524), channel_id=1, source_target_pairs={{0,2},{1,3},{2,0},{3,1},{4,6},{5,7},{6,4},{7,5},{8,10},{9,11},{10,... | collective-permute-start | bytes 442376 | tf_op jit(solution)/shard_map/ppermute | solution.py:989
  (44 other events, 250.7 us)
